TPU v7x, 256 devices: a whole 4x4x8 slice. The times are simulated.
256 devices in a mesh: leaf: 64 (over x, y_lo, z), sub: 4 (over y_hi, core).
Axes of the slice: x: 4, y: 4 (y_hi: 2, y_lo: 2; y = y_hi * 2 + y_lo), z: 8, core: 2. Of those that a mesh axis runs over, the one named last changes fastest.
Arguments:
- field_in: float32 [2, 16, 393216], P(None, None, ('leaf', 'sub')), may hold values from -6 to 6
- compress: float32 [3072, 2, 64, 128], P(('leaf', 'sub')), may hold values from -0.375 to 0.375
- coupling: float32 [8, 3072, 2, 64, 128], P(None, ('leaf', 'sub')), may hold values from -0.375 to 0.375
- roster: int32 [8, 256, 12], P(None, ('leaf', 'sub')), may hold values from 0 to 11, each once within a row
- expand: float32 [3072, 2, 64, 128], P(('leaf', 'sub')), may hold values from -0.5 to 0.5
- nearfield_dense_blocks: float32 [3072, 2, 2, 128, 128], P(('leaf', 'sub')), may hold values from -0.25 to 0.25
- slot_owner_index: int32 [3072, 2], P(('leaf', 'sub')), may hold values from 0 to 3
- slot_source_position: int32 [3072, 2], P(('leaf', 'sub')), may hold values from 0 to 3
- slot_valid_mask: int32 [3072, 2], P(('leaf', 'sub')), may hold values 0 or 1
- near_pick: int32 [256, 4, 4], P(('leaf', 'sub')), may hold values from 0 to 11, as said below
Outputs:
- field_out: float32 [2, 16, 393216], P(None, None, ('leaf', 'sub'))
Inputs may be any that keep to these rules, and one draw needn't show every extreme that they name: Each row of near_pick holds 4 distinct local leaf indices.
All inputs are finite; a program needn't handle non-finite values. No bound on the sum of `slot_valid_mask` on one device may be relied on, other than what follows from the above.
Results may differ from a plain program's by a relative error of at most 0.0001.
Values sent between devices are 32-bit elements; how exact they have to be, the bound alone decides.
No kernel may reach another device: no remote copies, remote signals or barrier semaphores. Data moves between devices by JAX's collectives and lax.ppermute only.
A program may use at most 64 MiB of HBM per device.

v0:
```python
import jax
import jax.numpy as jnp
from jax import lax
from jax.sharding import PartitionSpec as P


def swapped(value, axis, distance):
    mask = 2**distance
    pairs = [(source, source ^ mask) for source in range(lax.axis_size(axis))]
    return lax.ppermute(value, axis, pairs)


def complex_product(factor, stacked, pattern):
    products = jnp.einsum(pattern, factor, stacked, precision=lax.Precision.HIGHEST)
    return jnp.stack([products[0, 0] - products[1, 1], products[0, 1] + products[1, 0]])


def on_device(
    field_in,
    compress,
    coupling,
    roster,
    expand,
    nearfield_dense_blocks,
    slot_owner_index,
    slot_source_position,
    slot_valid_mask,
    near_pick,
):
    blocks_here = compress.shape[0]
    leaf_size = compress.shape[3]
    rhs_count = field_in.shape[1]
    sub_count = lax.axis_size("sub")
    leaf_count = lax.axis_size("leaf")
    columns = field_in.reshape(2, rhs_count, blocks_here, leaf_size)
    coeffs = complex_product(compress, columns, "kcij,dskj->cdski")
    logl = leaf_count.bit_length() - 1
    levels_plan = [
        ("leaf", logl - 1),
        ("leaf", logl - 2),
        ("leaf", logl - 3),
        ("sub", 0),
        ("sub", 1),
        ("leaf", logl - 3),
        ("leaf", logl - 2),
        ("leaf", logl - 1),
    ]
    for position, entry in enumerate(levels_plan):
        if entry[0] == "leaf":
            partner = swapped(coeffs, "leaf", entry[1])
        else:
            partner = swapped(coeffs, "sub", entry[1])
        aligned = jnp.take(partner, roster[position, 0], axis=2)
        stacked = jnp.concatenate([coeffs, aligned], axis=-1)
        coeffs = complex_product(coupling[position], stacked, "kcij,dskj->cdski")
    far = complex_product(expand, coeffs, "kcji,dskj->cdski")
    whole = lax.all_gather(field_in, "sub", axis=2, tiled=True)
    whole = whole.reshape(2, rhs_count, sub_count, blocks_here, leaf_size)
    owners = jnp.arange(sub_count, dtype=jnp.int32)[:, None]
    picked = whole[:, :, owners, near_pick[0], :]
    sources = picked[:, :, slot_owner_index, slot_source_position, :]
    sources = sources * slot_valid_mask.astype(jnp.float32)[None, None, :, :, None]
    near = complex_product(nearfield_dense_blocks, sources, "ktcij,dsktj->cdski")
    total = far + near
    return total.reshape(2, rhs_count, blocks_here * leaf_size)


def solution(mesh):
    return jax.shard_map(
        on_device,
        mesh=mesh,
        in_specs=(
            P(None, None, ("leaf", "sub")),
            P(("leaf", "sub"), None, None, None),
            P(None, ("leaf", "sub"), None, None, None),
            P(None, ("leaf", "sub"), None),
            P(("leaf", "sub"), None, None, None),
            P(("leaf", "sub"), None, None, None, None),
            P(("leaf", "sub"), None),
            P(("leaf", "sub"), None),
            P(("leaf", "sub"), None),
            P(("leaf", "sub"), None, None),
        ),
        out_specs=P(None, None, ("leaf", "sub")),
        check_vma=False,
    )
```

profile of v0, /device:TPU:64, one launch (start us, length us, event | category | flops | bytes accessed | tf_op | source)
XLA Modules:
  0.0 128.3 jit_solution(14198390774152455750)
XLA Ops:
  0.0 1.1 reshape.451
  1.1 3.4 %convolution_bitcast_fusion.9 = f32[2,2,16,12,64]{4,2,0,1,3:T(8,128)S(1)} fusion(f32[12,2,64,128]{3,2,1,0:T(8,128)} %param.13, f32[2,16,12,128,1]{3,2,1,0,4:T(8,128)S(1)} %bitcast.308), kind=kOutput, calls=%fused_computation.22 | convolution fusion | flops 75497472 | bytes 1179648 | tf_op jit(solution)/shard_map/kcij,dskj->cdski/dot_general | solution.py:14
  4.6 0.6 copy-done.1
  5.2 0.7 pad_maximum_fusion
  5.9 3.0 %collective-permute-start = (f32[2,16,12,64]{3,1,2,0:T(8,128)}, f32[2,16,12,64]{3,1,2,0:T(8,128)}, u32[]{:S(2)}, u32[]{:S(2)}) collective-permute-start(f32[2,16,12,64]{3,1,2,0:T(8,128)} %pad_maximum_fusion), channel_id=1, source_target_pairs={{0,128},{4,132},{8,136},{12,140},{16,144},{20,148},{24,152},{28,15... | collective-permute-start | bytes 294920 | tf_op jit(solution)/shard_map/ppermute | solution.py:10
  8.9 11.6 %all_gather.3 = f32[2,16,6144]{2,1,0:T(8,128)} all-gather(f32[2,16,1536]{2,1,0:T(8,128)} %param.12), channel_id=1, replica_groups=mesh['leaf'=64,'sub'=4] {'sub'}, dimensions={2}, use_global_device_ids=true | all-gather | bytes 983040 | tf_op jit(solution)/shard_map/all_gather | solution.py:57
  20.5 1.4 %compare_and_fusion = (pred[12]{0:T(512)(128)(4,1)S(1)}, s32[12]{0:T(128)}, pred[12]{0:T(512)(128)(4,1)S(1)}, s32[12]{0:T(128)}, pred[12]{0:T(512)(128)(4,1)}, /...) fusion(s32[8,1,12]{2,1,0:T(1,128)} %param.15), kind=kLoop, calls=%fused_computation.168 | loop fusion | flops 576 | bytes 864 | tf_op jit(solution)/shard_map/jit(_take)/and | solution.py:53
  21.9 2.4 %reshape.452 = f32[2,16,4,12,128]{4,3,2,1,0:T(8,128)} reshape(f32[2,16,6144]{2,1,0:T(8,128)} %all_gather.3) | data formatting | bytes 1572864 | tf_op jit(solution)/shard_map/reshape | solution.py:58
  24.3 2.6 %copy.80 = f32[2,16,4,12,128]{4,1,3,2,0:T(8,128)} copy(f32[2,16,4,12,128]{4,3,2,1,0:T(8,128)} %reshape.452) | data formatting | bytes 1572864 | tf_op jit(solution)/shard_map/reshape | solution.py:58
  26.9 0.1 reshape.517
  27.0 2.4 %gather_fusion = f32[16,2,16,128]{3,2,1,0:T(8,128)} fusion(f32[2,16,4,12,128]{4,1,3,2,0:T(8,128)} %copy.80, s32[16]{0:T(128)S(1)} %reshape.517), kind=kCustom, calls=%fused_computation.8 | custom fusion | bytes 524416 | tf_op jit(solution)/shard_map/gather | solution.py:60
  29.4 1.0 copy.204
  30.4 0.1 copy.82
  30.5 0.1 reshape.523
  30.6 0.7 convert_element_type.3
  31.3 0.1 copy.83
  31.4 1.4 %gather_fusion.1 = f32[24,2,16,128]{3,2,1,0:T(8,128)} fusion(f32[2,16,4,4,128]{4,1,3,2,0:T(8,128)S(1)} %bitcast.305, s32[24]{0:T(128)S(1)} %reshape.523), kind=kCustom, calls=%fused_computation.9 | custom fusion | bytes 786624 | tf_op jit(solution)/shard_map/gather | solution.py:61
  32.8 4.0 %fusion.2 = f32[2,2,16,12,128]{4,2,0,1,3:T(8,128)S(1)} fusion(f32[12,2,2,128,128]{4,3,2,1,0:T(8,128)S(1)} %copy-done, f32[12,2,2,16,128]{4,3,2,1,0:T(8,128)} %bitcast.306, f32[12,2]{1,0:T(8,128)S(1)} %copy.83), kind=kOutput, calls=%fused_computation.12 | convolution fusion | flops 302088192 | bytes 3932256 | tf_op jit(solution)/shard_map/ktcij,dsktj->cdski/dot_general | solution.py:14
  36.9 0.6 add.193
  37.6 0.7 sub.166
  38.3 1.5 %gather_fusion.2 = f32[12,2,16,64]{3,2,1,0:T(8,128)S(1)} fusion(f32[2,16,12,64]{3,1,2,0:T(8,128)} %collective-permute-done, s32[1024]{0:T(1024)S(1)} %pad_clamp_fusion.7), kind=kCustom, calls=%fused_computation.clone | custom fusion | bytes 196656 | tf_op jit(solution)/shard_map/jit(_take)/gather | solution.py:53
  39.9 3.4 %convolution_bitcast_fusion.8 = f32[2,2,16,12,64]{4,2,0,1,3:T(8,128)S(1)} fusion(f32[8,12,2,64,128]{4,3,2,1,0:T(8,128)} %param.14, f32[2,16,12,64]{3,1,2,0:T(8,128)S(1)} %fusion.41, f32[1,16,12,64]{3,1,2,0:T(8,128)S(1)} %fusion.66, f32[1,16,12,64]{3,1,2,0:T(8,128)} %copy-done.1), kind=kOutput, calls=%fused_computation.21 | convolution fusion | flops 75595776 | bytes 1228800 | tf_op jit(solution)/shard_map/kcij,dskj->cdski/dot_general | solution.py:14
  43.4 0.7 collective-permute-start.1
  44.0 0.6 pad_clamp_fusion.6
  44.7 6.0 %collective-permute-done.1 = f32[2,16,12,64]{3,1,2,0:T(8,128)} collective-permute-done((f32[2,16,12,64]{3,1,2,0:T(8,128)S(1)}, f32[2,16,12,64]{3,1,2,0:T(8,128)}, u32[]{:S(2)}, u32[]{:S(2)}) %collective-permute-start.1) | collective-permute-done | bytes 98336 | tf_op jit(solution)/shard_map/ppermute | solution.py:10
  50.7 1.5 %gather_fusion.3 = f32[12,2,16,64]{3,2,1,0:T(8,128)S(1)} fusion(f32[2,16,12,64]{3,1,2,0:T(8,128)} %collective-permute-done.1, s32[1024]{0:T(1024)S(1)} %pad_clamp_fusion.6), kind=kCustom, calls=%fused_computation.1.clone | custom fusion | bytes 196656 | tf_op jit(solution)/shard_map/jit(_take)/gather | solution.py:53
  52.2 0.7 fusion.40
  52.9 3.4 %convolution_bitcast_fusion.7 = f32[2,2,16,12,64]{4,2,0,1,3:T(8,128)S(1)} fusion(f32[8,12,2,64,128]{4,3,2,1,0:T(8,128)} %param.14, f32[2,16,12,64]{3,1,2,0:T(8,128)S(1)} %fusion.40, f32[1,16,12,64]{3,1,2,0:T(8,128)S(1)} %fusion.63, f32[1,16,12,64]{3,1,2,0:T(8,128)S(1)} %fusion.65), kind=kOutput, calls=%fused_computation.20 | convolution fusion | flops 75595776 | bytes 1179648 | tf_op jit(solution)/shard_map/kcij,dskj->cdski/dot_general | solution.py:14
  56.3 0.8 collective-permute-start.2
  57.1 0.6 pad_clamp_fusion.5
  57.7 5.1 %collective-permute-done.2 = f32[2,16,12,64]{3,1,2,0:T(8,128)} collective-permute-done((f32[2,16,12,64]{3,1,2,0:T(8,128)S(1)}, f32[2,16,12,64]{3,1,2,0:T(8,128)}, u32[]{:S(2)}, u32[]{:S(2)}) %collective-permute-start.2) | collective-permute-done | bytes 98336 | tf_op jit(solution)/shard_map/ppermute | solution.py:10
  62.8 1.5 %gather_fusion.4 = f32[12,2,16,64]{3,2,1,0:T(8,128)S(1)} fusion(f32[2,16,12,64]{3,1,2,0:T(8,128)} %collective-permute-done.2, s32[1024]{0:T(1024)S(1)} %pad_clamp_fusion.5), kind=kCustom, calls=%fused_computation.2.clone | custom fusion | bytes 196656 | tf_op jit(solution)/shard_map/jit(_take)/gather | solution.py:53
  64.3 0.8 fusion.39
  65.1 3.4 %convolution_bitcast_fusion.6 = f32[2,2,16,12,64]{4,2,0,1,3:T(8,128)S(1)} fusion(f32[8,12,2,64,128]{4,3,2,1,0:T(8,128)} %param.14, f32[2,16,12,64]{3,1,2,0:T(8,128)S(1)} %fusion.39, f32[1,16,12,64]{3,1,2,0:T(8,128)S(1)} %fusion.60, f32[1,16,12,64]{3,1,2,0:T(8,128)S(1)} %fusion.62), kind=kOutput, calls=%fused_computation.19 | convolution fusion | flops 75595776 | bytes 1179648 | tf_op jit(solution)/shard_map/kcij,dskj->cdski/dot_general | solution.py:14
  68.5 0.3 collective-permute-start.3
  68.8 0.7 pad_clamp_fusion.4
  69.5 0.9 collective-permute-done.3
  70.4 1.5 %gather_fusion.5 = f32[12,2,16,64]{3,2,1,0:T(8,128)S(1)} fusion(f32[2,16,12,64]{3,1,2,0:T(8,128)} %collective-permute-done.3, s32[1024]{0:T(1024)S(1)} %pad_clamp_fusion.4), kind=kCustom, calls=%fused_computation.3.clone | custom fusion | bytes 196656 | tf_op jit(solution)/shard_map/jit(_take)/gather | solution.py:53
  71.9 0.7 fusion.38
  72.6 3.4 %convolution_bitcast_fusion.5 = f32[2,2,16,12,64]{4,2,0,1,3:T(8,128)S(1)} fusion(f32[8,12,2,64,128]{4,3,2,1,0:T(8,128)} %param.14, f32[2,16,12,64]{3,1,2,0:T(8,128)S(1)} %fusion.38, f32[1,16,12,64]{3,1,2,0:T(8,128)S(1)} %fusion.57, f32[1,16,12,64]{3,1,2,0:T(8,128)S(1)} %fusion.59), kind=kOutput, calls=%fused_computation.18 | convolution fusion | flops 75595776 | bytes 1179648 | tf_op jit(solution)/shard_map/kcij,dskj->cdski/dot_general | solution.py:14
  76.0 1.7 %collective-permute-start.4 = (f32[2,16,12,64]{3,1,2,0:T(8,128)S(1)}, f32[2,16,12,64]{3,1,2,0:T(8,128)}, u32[]{:S(2)}, u32[]{:S(2)}) collective-permute-start(f32[2,16,12,64]{3,1,2,0:T(8,128)S(1)} %pad_maximum_fusion.4), channel_id=1, source_target_pairs={{0,2},{1,3},{2,0},{3,1},{4,6},{5,7},{6,4},{7,5},{8,10},{9,11},{10,... | collective-permute-start | bytes 294920 | tf_op jit(solution)/shard_map/ppermute | solution.py:10
  77.7 0.7 pad_clamp_fusion.3
  78.4 6.3 %collective-permute-done.4 = f32[2,16,12,64]{3,1,2,0:T(8,128)} collective-permute-done((f32[2,16,12,64]{3,1,2,0:T(8,128)S(1)}, f32[2,16,12,64]{3,1,2,0:T(8,128)}, u32[]{:S(2)}, u32[]{:S(2)}) %collective-permute-start.4) | collective-permute-done | bytes 98336 | tf_op jit(solution)/shard_map/ppermute | solution.py:10
  84.6 1.5 %gather_fusion.6 = f32[12,2,16,64]{3,2,1,0:T(8,128)S(1)} fusion(f32[2,16,12,64]{3,1,2,0:T(8,128)} %collective-permute-done.4, s32[1024]{0:T(1024)S(1)} %pad_clamp_fusion.3), kind=kCustom, calls=%fused_computation.4.clone | custom fusion | bytes 196656 | tf_op jit(solution)/shard_map/jit(_take)/gather | solution.py:53
  86.1 0.7 fusion.37
  86.8 3.4 %convolution_bitcast_fusion.4 = f32[2,2,16,12,64]{4,2,0,1,3:T(8,128)S(1)} fusion(f32[8,12,2,64,128]{4,3,2,1,0:T(8,128)} %param.14, f32[2,16,12,64]{3,1,2,0:T(8,128)S(1)} %fusion.37, f32[1,16,12,64]{3,1,2,0:T(8,128)S(1)} %fusion.54, f32[1,16,12,64]{3,1,2,0:T(8,128)S(1)} %fusion.56), kind=kOutput, calls=%fused_computation.17 | convolution fusion | flops 75595776 | bytes 1179648 | tf_op jit(solution)/shard_map/kcij,dskj->cdski/dot_general | solution.py:14
  90.3 0.8 collective-permute-start.5
  91.0 0.7 pad_clamp_fusion.2
  91.7 4.8 %collective-permute-done.5 = f32[2,16,12,64]{3,1,2,0:T(8,128)} collective-permute-done((f32[2,16,12,64]{3,1,2,0:T(8,128)S(1)}, f32[2,16,12,64]{3,1,2,0:T(8,128)}, u32[]{:S(2)}, u32[]{:S(2)}) %collective-permute-start.5) | collective-permute-done | bytes 98336 | tf_op jit(solution)/shard_map/ppermute | solution.py:10
  96.5 1.5 %gather_fusion.7 = f32[12,2,16,64]{3,2,1,0:T(8,128)S(1)} fusion(f32[2,16,12,64]{3,1,2,0:T(8,128)} %collective-permute-done.5, s32[1024]{0:T(1024)S(1)} %pad_clamp_fusion.2), kind=kCustom, calls=%fused_computation.5.clone | custom fusion | bytes 196656 | tf_op jit(solution)/shard_map/jit(_take)/gather | solution.py:53
  98.1 3.4 %convolution_bitcast_fusion.3 = f32[2,2,16,12,64]{4,2,0,1,3:T(8,128)S(1)} fusion(f32[8,12,2,64,128]{4,3,2,1,0:T(8,128)} %param.14, f32[2,16,12,64]{3,1,2,0:T(8,128)S(1)} %fusion.36, f32[1,16,12,64]{3,1,2,0:T(8,128)S(1)} %fusion.51, f32[1,16,12,64]{3,1,2,0:T(8,128)S(1)} %fusion.53), kind=kOutput, calls=%fused_computation.16 | convolution fusion | flops 75595776 | bytes 1179648 | tf_op jit(solution)/shard_map/kcij,dskj->cdski/dot_general | solution.py:14
  101.6 0.7 collective-permute-start.6
  102.2 0.6 pad_clamp_fusion.1
  102.8 4.6 %collective-permute-done.6 = f32[2,16,12,64]{3,1,2,0:T(8,128)} collective-permute-done((f32[2,16,12,64]{3,1,2,0:T(8,128)S(1)}, f32[2,16,12,64]{3,1,2,0:T(8,128)}, u32[]{:S(2)}, u32[]{:S(2)}) %collective-permute-start.6) | collective-permute-done | bytes 98336 | tf_op jit(solution)/shard_map/ppermute | solution.py:10
  107.4 1.5 %gather_fusion.8 = f32[12,2,16,64]{3,2,1,0:T(8,128)S(1)} fusion(f32[2,16,12,64]{3,1,2,0:T(8,128)} %collective-permute-done.6, s32[1024]{0:T(1024)S(1)} %pad_clamp_fusion.1), kind=kCustom, calls=%fused_computation.6.clone | custom fusion | bytes 196656 | tf_op jit(solution)/shard_map/jit(_take)/gather | solution.py:53
  108.9 0.1 fusion.35
  109.0 3.4 %convolution_bitcast_fusion.2 = f32[2,2,16,12,64]{4,2,0,1,3:T(8,128)S(1)} fusion(f32[8,12,2,64,128]{4,3,2,1,0:T(8,128)} %param.14, f32[2,16,12,64]{3,1,2,0:T(8,128)S(1)} %fusion.35, f32[1,16,12,64]{3,1,2,0:T(8,128)S(1)} %fusion.48, f32[1,16,12,64]{3,1,2,0:T(8,128)S(1)} %fusion.50), kind=kOutput, calls=%fused_computation.15 | convolution fusion | flops 75595776 | bytes 1179648 | tf_op jit(solution)/shard_map/kcij,dskj->cdski/dot_general | solution.py:14
  112.4 1.2 collective-permute-start.7
  113.7 0.7 pad_clamp_fusion
  114.4 5.5 %collective-permute-done.7 = f32[2,16,12,64]{3,1,2,0:T(8,128)} collective-permute-done((f32[2,16,12,64]{3,1,2,0:T(8,128)S(1)}, f32[2,16,12,64]{3,1,2,0:T(8,128)}, u32[]{:S(2)}, u32[]{:S(2)}) %collective-permute-start.7) | collective-permute-done | bytes 98336 | tf_op jit(solution)/shard_map/ppermute | solution.py:10
  119.8 1.5 %gather_fusion.9 = f32[12,2,16,64]{3,2,1,0:T(8,128)S(1)} fusion(f32[2,16,12,64]{3,1,2,0:T(8,128)} %collective-permute-done.7, s32[1024]{0:T(1024)S(1)} %pad_clamp_fusion), kind=kCustom, calls=%fused_computation.7.clone | custom fusion | bytes 196656 | tf_op jit(solution)/shard_map/jit(_take)/gather | solution.py:53
  121.4 3.4 %convolution_bitcast_fusion.1 = f32[2,2,16,12,64]{4,2,0,1,3:T(8,128)S(1)} fusion(f32[8,12,2,64,128]{4,3,2,1,0:T(8,128)} %param.14, f32[2,16,12,64]{3,1,2,0:T(8,128)S(1)} %fusion.34, f32[1,16,12,64]{3,1,2,0:T(8,128)S(1)} %fusion.45, f32[1,16,12,64]{3,1,2,0:T(8,128)S(1)} %fusion.47), kind=kOutput, calls=%fused_computation.14 | convolution fusion | flops 75595776 | bytes 1179648 | tf_op jit(solution)/shard_map/kcij,dskj->cdski/dot_general | solution.py:14
  124.8 1.7 %convolution_bitcast_fusion = f32[2,2,16,12,128]{4,2,0,1,3:T(8,128)S(1)} fusion(f32[12,2,64,128]{3,2,1,0:T(8,128)} %param.16, f32[1,16,12,64]{3,1,2,0:T(8,128)S(1)} %fusion.42, f32[1,16,12,64]{3,1,2,0:T(8,128)S(1)} %fusion.44), kind=kOutput, calls=%fused_computation.13 | convolution fusion | flops 75522048 | bytes 1277952 | tf_op jit(solution)/shard_map/kcji,dskj->cdski/dot_general | solution.py:14
  126.7 1.6 %maximum_add_fusion = f32[2,16,1536]{2,1,0:T(8,128)} fusion(f32[1,16,1536]{2,1,0:T(8,128)S(1)} %add.188, f32[1,16,1536]{2,1,0:T(8,128)S(1)} %sub.164, f32[1,16,1536]{2,1,0:T(8,128)} %add.193, f32[1,16,1536]{2,1,0:T(8,128)} %sub.166), kind=kLoop, calls=%fused_computation.61 | loop fusion | flops 147456 | bytes 589824 | tf_op jit(solution)/shard_map/add | solution.py:64
  (49 shorter events, 0.9 us)
Async XLA Ops:
  0.0 32.8 %copy-start = (f32[12,2,2,128,128]{4,3,2,1,0:T(8,128)S(1)}, f32[12,2,2,128,128]{4,3,2,1,0:T(8,128)}, u32[]{:S(2)}) copy-start(f32[12,2,2,128,128]{4,3,2,1,0:T(8,128)} %param.17) | copy-start | bytes 9437188
  0.0 26.9 %copy-start.2 = (s32[1,4,4]{2,1,0:T(4,128)S(1)}, s32[1,4,4]{2,1,0:T(4,128)}, u32[]{:S(2)}) copy-start(s32[1,4,4]{2,1,0:T(4,128)} %param.21) | copy-start | bytes 196
  0.0 30.4 %copy-start.3 = (s32[12,2]{0,1:T(2,128)S(1)}, s32[12,2]{0,1:T(2,128)}, u32[]{:S(2)}) copy-start(s32[12,2]{0,1:T(2,128)} %param.18) | copy-start | bytes 292
  0.0 30.4 %copy-start.4 = (s32[12,2]{0,1:T(2,128)S(1)}, s32[12,2]{0,1:T(2,128)}, u32[]{:S(2)}) copy-start(s32[12,2]{0,1:T(2,128)} %param.19) | copy-start | bytes 292
  4.6 0.6 copy-start.1
  5.9 32.4 %collective-permute-start = (f32[2,16,12,64]{3,1,2,0:T(8,128)}, f32[2,16,12,64]{3,1,2,0:T(8,128)}, u32[]{:S(2)}, u32[]{:S(2)}) collective-permute-start(f32[2,16,12,64]{3,1,2,0:T(8,128)} %pad_maximum_fusion), channel_id=1, source_target_pairs={{0,128},{4,132},{8,136},{12,140},{16,144},{20,148},{24,152},{28,15... | collective-permute-start | bytes 294920 | tf_op jit(solution)/shard_map/ppermute | solution.py:10
  43.4 7.3 %collective-permute-start.1 = (f32[2,16,12,64]{3,1,2,0:T(8,128)S(1)}, f32[2,16,12,64]{3,1,2,0:T(8,128)}, u32[]{:S(2)}, u32[]{:S(2)}) collective-permute-start(f32[2,16,12,64]{3,1,2,0:T(8,128)S(1)} %pad_maximum_fusion.1), channel_id=1, source_target_pairs={{0,64},{4,68},{8,72},{12,76},{16,80},{20,84},{24,88},{28,92},{32,9... | collective-permute-start | bytes 294920 | tf_op jit(solution)/shard_map/ppermute | solution.py:10
  56.3 6.5 %collective-permute-start.2 = (f32[2,16,12,64]{3,1,2,0:T(8,128)S(1)}, f32[2,16,12,64]{3,1,2,0:T(8,128)}, u32[]{:S(2)}, u32[]{:S(2)}) collective-permute-start(f32[2,16,12,64]{3,1,2,0:T(8,128)S(1)} %pad_maximum_fusion.2), channel_id=1, source_target_pairs={{0,32},{4,36},{8,40},{12,44},{16,48},{20,52},{24,56},{28,60},{32,0... | collective-permute-start | bytes 294920 | tf_op jit(solution)/shard_map/ppermute | solution.py:10
  68.5 1.8 %collective-permute-start.3 = (f32[2,16,12,64]{3,1,2,0:T(8,128)S(1)}, f32[2,16,12,64]{3,1,2,0:T(8,128)}, u32[]{:S(2)}, u32[]{:S(2)}) collective-permute-start(f32[2,16,12,64]{3,1,2,0:T(8,128)S(1)} %pad_maximum_fusion.3), channel_id=1, source_target_pairs={{0,1},{1,0},{2,3},{3,2},{4,5},{5,4},{6,7},{7,6},{8,9},{9,8},{10,11... | collective-permute-start | bytes 294920 | tf_op jit(solution)/shard_map/ppermute | solution.py:10
  76.0 8.6 %collective-permute-start.4 = (f32[2,16,12,64]{3,1,2,0:T(8,128)S(1)}, f32[2,16,12,64]{3,1,2,0:T(8,128)}, u32[]{:S(2)}, u32[]{:S(2)}) collective-permute-start(f32[2,16,12,64]{3,1,2,0:T(8,128)S(1)} %pad_maximum_fusion.4), channel_id=1, source_target_pairs={{0,2},{1,3},{2,0},{3,1},{4,6},{5,7},{6,4},{7,5},{8,10},{9,11},{10,... | collective-permute-start | bytes 294920 | tf_op jit(solution)/shard_map/ppermute | solution.py:10
  90.3 6.3 %collective-permute-start.5 = (f32[2,16,12,64]{3,1,2,0:T(8,128)S(1)}, f32[2,16,12,64]{3,1,2,0:T(8,128)}, u32[]{:S(2)}, u32[]{:S(2)}) collective-permute-start(f32[2,16,12,64]{3,1,2,0:T(8,128)S(1)} %pad_maximum_fusion.5), channel_id=1, source_target_pairs={{0,32},{4,36},{8,40},{12,44},{16,48},{20,52},{24,56},{28,60},{32,0... | collective-permute-start | bytes 294920 | tf_op jit(solution)/shard_map/ppermute | solution.py:10
  101.6 5.9 %collective-permute-start.6 = (f32[2,16,12,64]{3,1,2,0:T(8,128)S(1)}, f32[2,16,12,64]{3,1,2,0:T(8,128)}, u32[]{:S(2)}, u32[]{:S(2)}) collective-permute-start(f32[2,16,12,64]{3,1,2,0:T(8,128)S(1)} %pad_maximum_fusion.6), channel_id=1, source_target_pairs={{0,64},{4,68},{8,72},{12,76},{16,80},{20,84},{24,88},{28,92},{32,9... | collective-permute-start | bytes 294920 | tf_op jit(solution)/shard_map/ppermute | solution.py:10
  112.4 7.4 %collective-permute-start.7 = (f32[2,16,12,64]{3,1,2,0:T(8,128)S(1)}, f32[2,16,12,64]{3,1,2,0:T(8,128)}, u32[]{:S(2)}, u32[]{:S(2)}) collective-permute-start(f32[2,16,12,64]{3,1,2,0:T(8,128)S(1)} %pad_maximum_fusion.7), channel_id=1, source_target_pairs={{0,128},{4,132},{8,136},{12,140},{16,144},{20,148},{24,152},{28,15... | collective-permute-start | bytes 294920 | tf_op jit(solution)/shard_map/ppermute | solution.py:10
where the time goes:
time: 129 us; the launch traced here: 128 us
  matrix products  36 us (28%)
  waiting for transfers between devices  33.2 us (26%)
  local copies, waits for them, and re-layouts  25.3 us (20%)
  other arithmetic  12.5 us (10%)
  blocking collectives  11.6 us (9%)
  starting transfers between devices  9.11 us (7%)
    dot_general x11, matrix products, complex_product(): jnp.einsum(pattern, factor, stacked, precision=lax.Precision.HIGHEST)  36 us
    ppermute x8, waiting for transfers between devices, swapped(): return lax.ppermute(value, axis, pairs)  33.2 us
    gather x8, local copies, waits for them, and re-layouts, on_device(): aligned = jnp.take(partner, roster[position, 0], axis=2)  11.9 us
    all_gather x1, blocking collectives, on_device(): whole = lax.all_gather(field_in, 'sub', axis=2, tiled=True)  11.6 us
    ppermute x8, starting transfers between devices, swapped(): return lax.ppermute(value, axis, pairs)  9.11 us
    reshape x2, local copies, waits for them, and re-layouts, on_device(): whole = whole.reshape(2, rhs_count, sub_count, blocks_here, leaf_size)  4.97 us
    gather x8, other arithmetic  4.56 us
    gather x2, local copies, waits for them, and re-layouts, on_device(): picked = whole[:, :, owners, near_pick[0], :]  3.38 us
  transfers between devices with their start and end apart: 8, of which 7 were waited for; matrix products, arithmetic and copies ran while one was open for 17% of the time, Pallas kernels for 0%

commit v1 on v0

v1 whole, which is shorter than its diff:
```python
import functools

import jax
import jax.numpy as jnp
from jax import lax
from jax.experimental import pallas as pl
from jax.experimental.pallas import tpu as pltpu
from jax.sharding import PartitionSpec as P

VMEM = pltpu.VMEM
SMEM = pltpu.SMEM
BF = jnp.bfloat16
F32 = jnp.float32
NT = (((1,), (1,)), ((), ()))
NN = (((1,), (0,)), ((), ()))


def split(value):
    high = value.astype(BF)
    return high, (value - high.astype(F32)).astype(BF)


def product(rows, weights, dims):
    count = rows.shape[0]
    rows_high, rows_low = split(rows)
    w_high, w_low = split(weights)
    both = jnp.concatenate([rows_high, rows_low], axis=0)
    first = lax.dot_general(both, w_high, dims, preferred_element_type=F32)
    second = lax.dot_general(rows_high, w_low, dims, preferred_element_type=F32)
    return first[:count] + first[count:] + second


def lane_low(shape):
    return lax.broadcasted_iota(jnp.int32, shape, 1) < 64


def joined(result):
    rhs = result.shape[0] // 2
    turned = pltpu.roll(result[rhs:], 64, axis=1)
    return result[:rhs] + jnp.where(lane_low(turned.shape), -turned, turned)


def compress_kernel(field_ref, weight_ref, out_ref):
    for k in range(out_ref.shape[0]):
        rows = jnp.concatenate(
            [field_ref[0, :, pl.ds(128 * k, 128)], field_ref[1, :, pl.ds(128 * k, 128)]], axis=0
        )
        out_ref[k] = joined(product(rows, weight_ref[k].reshape(128, 128), NT))


def stacked_rows(own, other):
    low = lane_low(own.shape)
    real = jnp.where(low, own, pltpu.roll(other, 64, axis=1))
    imag = jnp.where(low, pltpu.roll(own, 64, axis=1), other)
    return jnp.concatenate([real, imag], axis=0)


def level_kernel(level, roster_ref, own_ref, other_ref, weight_ref, *rest):
    out_ref = rest[-1]
    for k in range(out_ref.shape[0]):
        rows = stacked_rows(own_ref[k], other_ref[roster_ref[level, k]])
        out_ref[k] = joined(product(rows, weight_ref[level, k].reshape(128, 128), NT))


def last_kernel(level, roster_ref, own_ref, other_ref, weight_ref, expand_ref, *rest):
    near_refs, out_ref = rest[:-1], rest[-1]
    each = near_refs[0].shape[0]
    for k in range(own_ref.shape[0]):
        rows = stacked_rows(own_ref[k], other_ref[roster_ref[level, k]])
        coeffs = joined(product(rows, weight_ref[level, k].reshape(128, 128), NT))
        signed = jnp.where(lane_low(coeffs.shape), coeffs, -coeffs)
        turned = pltpu.roll(coeffs, 64, axis=1)
        far = product(jnp.concatenate([signed, turned], axis=0), expand_ref[k].reshape(128, 128), NN)
        total = far + near_refs[k // each][k % each]
        half = total.shape[0] // 2
        out_ref[0, :, pl.ds(128 * k, 128)] = total[:half]
        out_ref[1, :, pl.ds(128 * k, 128)] = total[half:]


def near_kernel(first, me_ref, owner_ref, place_ref, valid_ref, pick_ref, own_ref, core_ref, far_ref, both_ref, weight_ref, *rest):
    out_ref = rest[-1]
    me = me_ref[0]
    for n in range(out_ref.shape[0]):
        k = first + n
        total = None
        for t in range(weight_ref.shape[1]):
            owner = owner_ref[k, t]
            leaf = pick_ref[owner, place_ref[k, t]]
            lanes = pl.ds(pl.multiple_of(leaf * 128, 128), 128)
            which = owner ^ me
            parts = []
            for d in range(2):
                low = jnp.where(which == 1, core_ref[d, :, lanes], own_ref[d, :, lanes])
                high = jnp.where(which == 3, both_ref[d, :, lanes], far_ref[d, :, lanes])
                parts.append(jnp.where(which >= 2, high, low))
            rows = jnp.concatenate(parts, axis=0) * valid_ref[k, t].astype(F32)
            result = product(rows, weight_ref[k, t].reshape(256, 128), NT)
            half = result.shape[0] // 2
            term = jnp.concatenate(
                [result[:half, :128] - result[half:, 128:], result[half:, :128] + result[:half, 128:]], axis=0
            )
            total = term if total is None else total + term
        out_ref[n] = total


def spec(space):
    return pl.BlockSpec(memory_space=space)


def call(kernel, out, spaces, name, flops=2_000_000):
    return pl.pallas_call(
        kernel,
        out_shape=out,
        in_specs=[spec(space) for space in spaces],
        out_specs=spec(VMEM),
        compiler_params=pltpu.CompilerParams(vmem_limit_bytes=8 << 20),
        cost_estimate=pl.CostEstimate(flops=flops, bytes_accessed=1 << 20, transcendentals=0),
        name=name,
    )


def flipped(value, axis, mask):
    pairs = [(source, source ^ mask) for source in range(lax.axis_size(axis))]
    return lax.ppermute(value, axis, pairs)


def on_device(
    field_in,
    compress,
    coupling,
    roster,
    expand,
    nearfield_dense_blocks,
    slot_owner_index,
    slot_source_position,
    slot_valid_mask,
    near_pick,
):
    blocks = compress.shape[0]
    rhs = field_in.shape[1]
    leaf_count = lax.axis_size("leaf")
    top = leaf_count // 2
    plan = [
        ("leaf", top),
        ("leaf", top // 2),
        ("leaf", top // 4),
        ("sub", 1),
        ("sub", 2),
        ("leaf", top // 4),
        ("leaf", top // 2),
        ("leaf", top),
    ]
    me = lax.axis_index("sub").astype(jnp.int32).reshape(1)
    names = roster[:, 0]
    pick = near_pick[0]
    state = jax.ShapeDtypeStruct((blocks, rhs, 128), F32)
    field = pltpu.with_memory_space_constraint(field_in, VMEM)
    weights = pltpu.with_memory_space_constraint(coupling, VMEM)
    first = pltpu.with_memory_space_constraint(compress, VMEM)
    last = pltpu.with_memory_space_constraint(expand, VMEM)
    dense = pltpu.with_memory_space_constraint(nearfield_dense_blocks, VMEM)

    coeffs = call(compress_kernel, state, [VMEM, VMEM], "compress")(field, first)
    each = 2
    near_at = {2: 1, 3: 0, 4: 1, 5: 1, 6: 1, 7: 2}
    pieces = []
    for position, (axis, mask) in enumerate(plan):
        other = flipped(coeffs, axis, mask)
        if position == 0:
            far = flipped(field_in, "sub", 2)
            core = flipped(field_in, "sub", 1)
        if position == 1:
            both = flipped(far, "sub", 1)
        extra = []
        for _ in range(near_at.get(position, 0)):
            kernel = functools.partial(near_kernel, each * len(pieces))
            piece = call(
                kernel,
                jax.ShapeDtypeStruct((each, 2 * rhs, 128), F32),
                [SMEM] * 5 + [VMEM] * 5 + [pl.ANY],
                "near",
            )(me, slot_owner_index, slot_source_position, slot_valid_mask, pick, field, core, far, both, dense, coeffs)
            pieces.append(piece)
            extra.append(piece)
        if position < len(plan) - 1:
            coeffs = call(
                functools.partial(level_kernel, position),
                state,
                [SMEM, VMEM, VMEM, VMEM] + [pl.ANY] * len(extra),
                "level",
            )(names, coeffs, other, weights, *extra)
        else:
            total = call(
                functools.partial(last_kernel, position),
                jax.ShapeDtypeStruct(field_in.shape, F32),
                [SMEM] + [VMEM] * (4 + len(pieces)),
                "last",
            )(names, coeffs, other, weights, last, *pieces)
    return total


def solution(mesh):
    return jax.shard_map(
        on_device,
        mesh=mesh,
        in_specs=(
            P(None, None, ("leaf", "sub")),
            P(("leaf", "sub"), None, None, None),
            P(None, ("leaf", "sub"), None, None, None),
            P(None, ("leaf", "sub"), None),
            P(("leaf", "sub"), None, None, None),
            P(("leaf", "sub"), None, None, None, None),
            P(("leaf", "sub"), None),
            P(("leaf", "sub"), None),
            P(("leaf", "sub"), None),
            P(("leaf", "sub"), None, None),
        ),
        out_specs=P(None, None, ("leaf", "sub")),
        check_vma=False,
    )
```

time: 129 us -> 68.7 us (0.53)
  matrix products: 36 us -> 0 us
  Pallas kernels: 0 us -> 25.1 us
  waiting for transfers between devices: 33.2 us -> 14.4 us
  local copies, waits for them, and re-layouts: 25.3 us -> 11.7 us
  other arithmetic: 12.5 us -> 0.01 us
  blocking collectives: 11.6 us -> 0 us
  starting transfers between devices: 9.11 us -> 17 us
    dot_general x11 -> x0, matrix products: 36 us -> none  [complex_product(): jnp.einsum(pattern, factor, stacked, precision=lax.Precision.HIGHEST)]
    pallas_call x0 -> x15, Pallas kernels: none -> 25.1 us  [the longest x7 10.1 us: on_device(): call(functools.partial(level_kernel, position), state, [SMEM, VMEM, VMEM,...]
    ppermute x8 -> x11, waiting for transfers between devices: 33.2 us -> 14.4 us  [flipped(): return lax.ppermute(value, axis, pairs)]
    gather x11 -> x0, local copies, waits for them, and re-layouts: 16.7 us -> none  [the longest x8 11.9 us: on_device(): aligned = jnp.take(partner, roster[position, 0], axis=2)]
    all_gather x1 -> x0, blocking collectives: 11.6 us -> none  [on_device(): whole = lax.all_gather(field_in, 'sub', axis=2, tiled=True)]
    unnamed x10 -> x37, local copies, waits for them, and re-layouts: 0.65 us -> 11.7 us
    ppermute x8 -> x11, starting transfers between devices: 9.11 us -> 17 us  [flipped(): return lax.ppermute(value, axis, pairs)]
    reshape x3 -> x0, local copies, waits for them, and re-layouts: 6.09 us -> none  [the longest x2 4.97 us: on_device(): whole = whole.reshape(2, rhs_count, sub_count, blocks_here, leaf_size)]
  transfers between devices with their start and end apart: 8 -> 11, of which waited for: 7 -> 7; matrix products, arithmetic and copies ran while one was open for 17% -> 3% of each run, Pallas kernels for 0% -> 19%
where the time goes in v1:
time: 68.7 us; the launch traced here: 68.2 us
  Pallas kernels  25.1 us (37%)
  starting transfers between devices  17 us (25%)
  waiting for transfers between devices  14.4 us (21%)
  local copies, waits for them, and re-layouts  11.7 us (17%)
    ppermute x11, starting transfers between devices, flipped(): return lax.ppermute(value, axis, pairs)  17 us
    ppermute x11, waiting for transfers between devices, flipped(): return lax.ppermute(value, axis, pairs)  14.4 us
    unnamed x37, local copies, waits for them, and re-layouts  11.7 us
    pallas_call x7, Pallas kernels, on_device(): call(functools.partial(level_kernel, position), state, [SMEM, VMEM, VMEM,...  10.1 us
    pallas_call x6, Pallas kernels, on_device(): call(kernel, jax.ShapeDtypeStruct((each, 2 * rhs, 128), F32), [SMEM] * 5...  7.9 us
    pallas_call x1, Pallas kernels, on_device(): call(functools.partial(last_kernel, position), jax.ShapeDtypeStruct(field...  5.51 us
    pallas_call x1, Pallas kernels, on_device(): call(compress_kernel, state, [VMEM, VMEM], 'compress')(field, first)  1.58 us
  transfers between devices with their start and end apart: 11, of which 7 were waited for; matrix products, arithmetic and copies ran while one was open for 3% of the time, Pallas kernels for 19%

profile of v1, /device:TPU:64, one launch (start us, length us, event | category | flops | bytes accessed | tf_op | source)
XLA Modules:
  0.0 68.2 jit_solution(115951937321735723)
XLA Ops:
  0.0 3.2 %collective-permute-start.4 = (f32[2,16,1536]{2,1,0:T(8,128)}, f32[2,16,1536]{2,1,0:T(8,128)S(1)}, u32[]{:S(2)}, u32[]{:S(2)}) collective-permute-start(f32[2,16,1536]{2,1,0:T(8,128)} %own_ref.11), channel_id=1, source_target_pairs={{0,2},{1,3},{2,0},{3,1},{4,6},{5,7},{6,4},{7,5},{8,10},{9,11},{10,... | collective-permute-start | bytes 589832 | tf_op jit(solution)/shard_map/ppermute | solution.py:124
  3.2 0.0 copy-start.5
  3.2 1.1 %copy-done.5 = f32[12,2,64,128]{3,2,1,0:T(8,128)S(1)} copy-done((f32[12,2,64,128]{3,2,1,0:T(8,128)S(1)}, f32[12,2,64,128]{3,2,1,0:T(8,128)}, u32[]{:S(2)}) %copy-start.5) | copy-done | bytes 786456
  4.3 0.0 copy-start.9
  4.3 1.6 %compress.1.own_ref = f32[12,16,128]{2,1,0:T(8,128)S(1)} custom-call(f32[2,16,1536]{2,1,0:T(8,128)} %own_ref.11, f32[12,2,64,128]{3,2,1,0:T(8,128)S(1)} %copy-done.5), custom_call_target="tpu_custom_call" | custom-call | flops 2000000 | bytes 1048576 | tf_op jit(solution)/shard_map/compress/pallas_call | solution.py:163
  5.9 3.1 %collective-permute-start = (f32[12,16,128]{2,1,0:T(8,128)S(1)}, f32[12,16,128]{2,1,0:T(8,128)S(1)}, u32[]{:S(2)}, u32[]{:S(2)}) collective-permute-start(f32[12,16,128]{2,1,0:T(8,128)S(1)} %compress.1.own_ref), channel_id=1, source_target_pairs={{0,128},{4,132},{8,136},{12,140},{16,144},{20,148},{24,152},{28,15... | collective-permute-start | bytes 294920 | tf_op jit(solution)/shard_map/ppermute | solution.py:124
  9.0 0.0 collective-permute-start.3
  9.0 0.0 collective-permute-done.4.far_ref
  9.0 0.5 collective-permute-start.5
  9.5 2.6 %collective-permute-done.other_ref = f32[12,16,128]{2,1,0:T(8,128)S(1)} collective-permute-done((f32[12,16,128]{2,1,0:T(8,128)S(1)}, f32[12,16,128]{2,1,0:T(8,128)S(1)}, u32[]{:S(2)}, u32[]{:S(2)}) %collective-permute-start) | collective-permute-done | bytes 98336 | tf_op jit(solution)/shard_map/ppermute | solution.py:124
  12.1 2.8 %copy-done = f32[8,12,2,64,128]{4,3,2,1,0:T(8,128)S(1)} copy-done((f32[8,12,2,64,128]{4,3,2,1,0:T(8,128)S(1)}, f32[8,12,2,64,128]{4,3,2,1,0:T(8,128)}, u32[]{:S(2)}) %copy-start) | copy-done | bytes 6291480
  14.9 0.7 %copy-done.8 = s32[8,1,12]{2,1,0:T(1,128)S(1)} copy-done((s32[8,1,12]{2,1,0:T(1,128)S(1)}, s32[8,1,12]{2,1,0:T(1,128)}, u32[]{:S(2)}) %copy-start.8) | copy-done | bytes 408
  15.6 1.3 %level.7.own_ref = f32[12,16,128]{2,1,0:T(8,128)S(1)} custom-call(s32[8,12]{1,0:T(8,128)S(1)} %bitcast.5, f32[12,16,128]{2,1,0:T(8,128)S(1)} %compress.1.own_ref, f32[12,16,128]{2,1,0:T(8,128)S(1)} %collective-permute-done.other_ref, f32[8,12,2,64,128]{4,3,2,1,0:T(8,128)S(1)} %copy-done), custom_call_target="tpu_custom_call" | custom-call | flops 2000000 | bytes 1048576 | tf_op jit(solution)/shard_map/level/pallas_call | solution.py:186
  16.8 1.5 %collective-permute-start.1 = (f32[12,16,128]{2,1,0:T(8,128)S(1)}, f32[12,16,128]{2,1,0:T(8,128)S(1)}, u32[]{:S(2)}, u32[]{:S(2)}) collective-permute-start(f32[12,16,128]{2,1,0:T(8,128)S(1)} %level.7.own_ref), channel_id=1, source_target_pairs={{0,64},{4,68},{8,72},{12,76},{16,80},{20,84},{24,88},{28,92},{32,9... | collective-permute-start | bytes 294920 | tf_op jit(solution)/shard_map/ppermute | solution.py:124
  18.4 3.1 %collective-permute-done.1.other_ref = f32[12,16,128]{2,1,0:T(8,128)S(1)} collective-permute-done((f32[12,16,128]{2,1,0:T(8,128)S(1)}, f32[12,16,128]{2,1,0:T(8,128)S(1)}, u32[]{:S(2)}, u32[]{:S(2)}) %collective-permute-start.1) | collective-permute-done | bytes 98336 | tf_op jit(solution)/shard_map/ppermute | solution.py:124
  21.5 0.0 copy-done.9
  21.5 0.0 copy-done.1
  21.5 1.9 %level.8.rest_0_.own_ref = f32[12,16,128]{2,1,0:T(8,128)} custom-call(s32[8,12]{1,0:T(8,128)S(1)} %bitcast.6, f32[12,16,128]{2,1,0:T(8,128)S(1)} %level.7.own_ref, f32[12,16,128]{2,1,0:T(8,128)S(1)} %collective-permute-done.1.other_ref, f32[8,12,2,64,128]{4,3,2,1,0:T(8,128)S(1)} %copy-done.1), custom_call_target="tpu_custom_call" | custom-call | flops 2000000 | bytes 1048576 | tf_op jit(solution)/shard_map/level/pallas_call | solution.py:186
  23.4 0.7 collective-permute-start.2
  24.1 0.0 copy-done.14
  24.1 0.1 copy.11.owner_ref
  24.2 0.8 %copy.12.place_ref = s32[12,2]{1,0:T(8,128)S(1)} copy(s32[12,2]{0,1:T(2,128)} %param.17) | data formatting | bytes 192 | tf_op args[7]
  25.0 1.3 %copy.13.valid_ref = s32[12,2]{1,0:T(8,128)} copy(s32[12,2]{0,1:T(2,128)} %param.18) | data formatting | bytes 192 | tf_op args[8]
  26.3 0.0 collective-permute-done.3.core_ref
  26.3 0.0 collective-permute-done.5.both_ref
  26.3 0.0 copy-done.3
  26.3 0.0 copy-start.6
  26.3 0.7 %copy-done.6 = s32[12,2]{1,0:T(8,128)S(1)} copy-done((s32[12,2]{1,0:T(8,128)S(1)}, s32[12,2]{1,0:T(8,128)}, u32[]{:S(2)}) %copy-start.6) | copy-done | bytes 120
  27.0 0.7 copy-done.12
  27.7 1.3 %near.6.rest_0_ = f32[2,32,128]{2,1,0:T(8,128)S(1)} custom-call(s32[1]{0:T(128)} %bitcast.1.me_ref, s32[12,2]{1,0:T(8,128)S(1)} %copy.11.owner_ref, s32[12,2]{1,0:T(8,128)S(1)} %copy.12.place_ref, s32[12,2]{1,0:T(8,128)S(1)} %copy-done.6, s32[4,4]{1,0:T(4,128)S(1)} %bitcast.13, f32[2,16,1536]{2,1,0:T(8,128)} %own_ref.11, ...), custom_call_target="tpu_custom_call" | custom-call | flops 2000000 | bytes 1048576 | tf_op jit(solution)/shard_map/near/pallas_call | solution.py:177
  29.0 0.0 collective-permute-done.2.other_ref
  29.0 0.0 copy-start.2
  29.1 2.8 %copy-done.2 = f32[8,12,2,64,128]{4,3,2,1,0:T(8,128)S(1)} copy-done((f32[8,12,2,64,128]{4,3,2,1,0:T(8,128)S(1)}, f32[8,12,2,64,128]{4,3,2,1,0:T(8,128)}, u32[]{:S(2)}) %copy-start.2) | copy-done | bytes 6291480
  31.8 0.7 %copy-done.10 = s32[8,1,12]{2,1,0:T(1,128)S(1)} copy-done((s32[8,1,12]{2,1,0:T(1,128)S(1)}, s32[8,1,12]{2,1,0:T(1,128)}, u32[]{:S(2)}) %copy-start.10) | copy-done | bytes 408
  32.5 1.8 %level.9.own_ref = f32[12,16,128]{2,1,0:T(8,128)S(1)} custom-call(s32[8,12]{1,0:T(8,128)S(1)} %bitcast.7, f32[12,16,128]{2,1,0:T(8,128)} %level.8.rest_0_.own_ref, f32[12,16,128]{2,1,0:T(8,128)} %collective-permute-done.2.other_ref, f32[8,12,2,64,128]{4,3,2,1,0:T(8,128)S(1)} %copy-done.2, f32[2,32,128]{2,1,0:T(8,128)S(1)} %near.6.rest_0_), custom_call_target="tpu_custom_call" | custom-call | flops 2000000 | bytes 1048576 | tf_op jit(solution)/shard_map/level/pallas_call | solution.py:186
  34.3 0.0 slice-start.1
  34.3 0.0 copy-start.11
  34.3 0.1 collective-permute-start.6
  34.4 1.3 %collective-permute-done.6.other_ref = f32[12,16,128]{2,1,0:T(8,128)S(1)} collective-permute-done((f32[12,16,128]{2,1,0:T(8,128)S(1)}, f32[12,16,128]{2,1,0:T(8,128)S(1)}, u32[]{:S(2)}, u32[]{:S(2)}) %collective-permute-start.6) | collective-permute-done | bytes 98336 | tf_op jit(solution)/shard_map/ppermute | solution.py:124
  35.7 1.3 %level.10.rest_0_.own_ref = f32[12,16,128]{2,1,0:T(8,128)S(1)} custom-call(s32[8,12]{1,0:T(8,128)S(1)} %bitcast.8, f32[12,16,128]{2,1,0:T(8,128)S(1)} %level.9.own_ref, f32[12,16,128]{2,1,0:T(8,128)S(1)} %collective-permute-done.6.other_ref, f32[8,12,2,64,128]{4,3,2,1,0:T(8,128)S(1)} %copy-done.2), custom_call_target="tpu_custom_call" | custom-call | flops 2000000 | bytes 1048576 | tf_op jit(solution)/shard_map/level/pallas_call | solution.py:186
  37.0 1.9 %collective-permute-start.7 = (f32[12,16,128]{2,1,0:T(8,128)S(1)}, f32[12,16,128]{2,1,0:T(8,128)S(1)}, u32[]{:S(2)}, u32[]{:S(2)}) collective-permute-start(f32[12,16,128]{2,1,0:T(8,128)S(1)} %level.10.rest_0_.own_ref), channel_id=1, source_target_pairs={{0,2},{1,3},{2,0},{3,1},{4,6},{5,7},{6,4},{7,5},{8,10},{9,11},{10,... | collective-permute-start | bytes 294920 | tf_op jit(solution)/shard_map/ppermute | solution.py:124
  38.9 0.0 copy-done.7
  38.9 0.0 copy-done.13
  38.9 1.3 %near.7.rest_0_.rest_1_ = f32[2,32,128]{2,1,0:T(8,128)S(1)} custom-call(s32[1]{0:T(128)} %bitcast.1.me_ref, s32[12,2]{1,0:T(8,128)S(1)} %copy.11.owner_ref, s32[12,2]{1,0:T(8,128)S(1)} %copy.12.place_ref, s32[12,2]{1,0:T(8,128)S(1)} %copy-done.7, s32[4,4]{1,0:T(4,128)S(1)} %bitcast.14, f32[2,16,1536]{2,1,0:T(8,128)} %own_ref.11, ...), custom_call_target="tpu_custom_call" | custom-call | flops 2000000 | bytes 1048576 | tf_op jit(solution)/shard_map/near/pallas_call | solution.py:177
  40.2 3.2 %collective-permute-done.7.other_ref = f32[12,16,128]{2,1,0:T(8,128)S(1)} collective-permute-done((f32[12,16,128]{2,1,0:T(8,128)S(1)}, f32[12,16,128]{2,1,0:T(8,128)S(1)}, u32[]{:S(2)}, u32[]{:S(2)}) %collective-permute-start.7) | collective-permute-done | bytes 98336 | tf_op jit(solution)/shard_map/ppermute | solution.py:124
  43.4 0.0 slice-done
  43.4 0.0 slice-done.1
  43.4 0.0 copy-done.11
  43.4 1.3 %level.11.rest_0_.own_ref = f32[12,16,128]{2,1,0:T(8,128)S(1)} custom-call(s32[8,12]{1,0:T(8,128)S(1)} %bitcast.9, f32[12,16,128]{2,1,0:T(8,128)S(1)} %level.10.rest_0_.own_ref, f32[12,16,128]{2,1,0:T(8,128)S(1)} %collective-permute-done.7.other_ref, f32[8,12,2,64,128]{4,3,2,1,0:T(8,128)S(1)} %bitcast.4, f32[2,32,128]{2,1,0:T(8,128)S(1)} %near.7.rest_0_.rest_1_), custom_call_target="tpu_custom_call" | custom-call | flops 2000000 | bytes 1048576 | tf_op jit(solution)/shard_map/level/pallas_call | solution.py:186
  44.7 1.4 %collective-permute-start.8 = (f32[12,16,128]{2,1,0:T(8,128)S(1)}, f32[12,16,128]{2,1,0:T(8,128)S(1)}, u32[]{:S(2)}, u32[]{:S(2)}) collective-permute-start(f32[12,16,128]{2,1,0:T(8,128)S(1)} %level.11.rest_0_.own_ref), channel_id=1, source_target_pairs={{0,32},{4,36},{8,40},{12,44},{16,48},{20,52},{24,56},{28,60},{32,0... | collective-permute-start | bytes 294920 | tf_op jit(solution)/shard_map/ppermute | solution.py:124
  46.1 1.3 %near.8.rest_0_.rest_2_ = f32[2,32,128]{2,1,0:T(8,128)S(1)} custom-call(s32[1]{0:T(128)} %bitcast.1.me_ref, s32[12,2]{1,0:T(8,128)S(1)} %copy.11.owner_ref, s32[12,2]{1,0:T(8,128)S(1)} %copy.12.place_ref, s32[12,2]{1,0:T(8,128)S(1)} %copy-done.7, s32[4,4]{1,0:T(4,128)S(1)} %bitcast.15, f32[2,16,1536]{2,1,0:T(8,128)} %own_ref.11, ...), custom_call_target="tpu_custom_call" | custom-call | flops 2000000 | bytes 1048576 | tf_op jit(solution)/shard_map/near/pallas_call | solution.py:177
  47.4 1.9 %collective-permute-done.8.other_ref = f32[12,16,128]{2,1,0:T(8,128)S(1)} collective-permute-done((f32[12,16,128]{2,1,0:T(8,128)S(1)}, f32[12,16,128]{2,1,0:T(8,128)S(1)}, u32[]{:S(2)}, u32[]{:S(2)}) %collective-permute-start.8) | collective-permute-done | bytes 98336 | tf_op jit(solution)/shard_map/ppermute | solution.py:124
  49.4 1.3 %level.12.rest_0_.own_ref = f32[12,16,128]{2,1,0:T(8,128)S(1)} custom-call(s32[8,12]{1,0:T(8,128)S(1)} %bitcast.10, f32[12,16,128]{2,1,0:T(8,128)S(1)} %level.11.rest_0_.own_ref, f32[12,16,128]{2,1,0:T(8,128)S(1)} %collective-permute-done.8.other_ref, f32[8,12,2,64,128]{4,3,2,1,0:T(8,128)S(1)} %bitcast.4, f32[2,32,128]{2,1,0:T(8,128)S(1)} %near.8.rest_0_.rest_2_), custom_call_target="tpu_custom_call" | custom-call | flops 2000000 | bytes 1048576 | tf_op jit(solution)/shard_map/level/pallas_call | solution.py:186
  50.6 1.5 %collective-permute-start.9 = (f32[12,16,128]{2,1,0:T(8,128)S(1)}, f32[12,16,128]{2,1,0:T(8,128)S(1)}, u32[]{:S(2)}, u32[]{:S(2)}) collective-permute-start(f32[12,16,128]{2,1,0:T(8,128)S(1)} %level.12.rest_0_.own_ref), channel_id=1, source_target_pairs={{0,64},{4,68},{8,72},{12,76},{16,80},{20,84},{24,88},{28,92},{32,9... | collective-permute-start | bytes 294920 | tf_op jit(solution)/shard_map/ppermute | solution.py:124
  52.2 1.3 %near.9.rest_0_.rest_3_ = f32[2,32,128]{2,1,0:T(8,128)S(1)} custom-call(s32[1]{0:T(128)} %bitcast.1.me_ref, s32[12,2]{1,0:T(8,128)S(1)} %copy.11.owner_ref, s32[12,2]{1,0:T(8,128)S(1)} %copy.12.place_ref, s32[12,2]{1,0:T(8,128)S(1)} %copy-done.7, s32[4,4]{1,0:T(4,128)S(1)} %bitcast.16, f32[2,16,1536]{2,1,0:T(8,128)} %own_ref.11, ...), custom_call_target="tpu_custom_call" | custom-call | flops 2000000 | bytes 1048576 | tf_op jit(solution)/shard_map/near/pallas_call | solution.py:177
  53.5 0.0 copy-start.4
  53.5 1.8 %collective-permute-done.9.other_ref = f32[12,16,128]{2,1,0:T(8,128)S(1)} collective-permute-done((f32[12,16,128]{2,1,0:T(8,128)S(1)}, f32[12,16,128]{2,1,0:T(8,128)S(1)}, u32[]{:S(2)}, u32[]{:S(2)}) %collective-permute-start.9) | collective-permute-done | bytes 98336 | tf_op jit(solution)/shard_map/ppermute | solution.py:124
  55.3 1.3 %level.13.rest_0_.own_ref = f32[12,16,128]{2,1,0:T(8,128)S(1)} custom-call(s32[8,12]{1,0:T(8,128)S(1)} %bitcast.11, f32[12,16,128]{2,1,0:T(8,128)S(1)} %level.12.rest_0_.own_ref, f32[12,16,128]{2,1,0:T(8,128)S(1)} %collective-permute-done.9.other_ref, f32[8,12,2,64,128]{4,3,2,1,0:T(8,128)S(1)} %bitcast.4, f32[2,32,128]{2,1,0:T(8,128)S(1)} %near.9.rest_0_.rest_3_), custom_call_target="tpu_custom_call" | custom-call | flops 2000000 | bytes 1048576 | tf_op jit(solution)/shard_map/level/pallas_call | solution.py:186
  56.6 3.1 %collective-permute-start.10 = (f32[12,16,128]{2,1,0:T(8,128)S(1)}, f32[12,16,128]{2,1,0:T(8,128)S(1)}, u32[]{:S(2)}, u32[]{:S(2)}) collective-permute-start(f32[12,16,128]{2,1,0:T(8,128)S(1)} %level.13.rest_0_.own_ref), channel_id=1, source_target_pairs={{0,128},{4,132},{8,136},{12,140},{16,144},{20,148},{24,152},{28,15... | collective-permute-start | bytes 294920 | tf_op jit(solution)/shard_map/ppermute | solution.py:124
  59.6 1.3 %near.11.rest_5_ = f32[2,32,128]{2,1,0:T(8,128)S(1)} custom-call(s32[1]{0:T(128)} %bitcast.1.me_ref, s32[12,2]{1,0:T(8,128)S(1)} %copy.11.owner_ref, s32[12,2]{1,0:T(8,128)S(1)} %copy.12.place_ref, s32[12,2]{1,0:T(8,128)S(1)} %copy-done.7, s32[4,4]{1,0:T(4,128)S(1)} %bitcast.17, f32[2,16,1536]{2,1,0:T(8,128)} %own_ref.11, ...), custom_call_target="tpu_custom_call" | custom-call | flops 2000000 | bytes 1048576 | tf_op jit(solution)/shard_map/near/pallas_call | solution.py:177
  61.0 1.3 %near.10.rest_4_ = f32[2,32,128]{2,1,0:T(8,128)S(1)} custom-call(s32[1]{0:T(128)} %bitcast.1.me_ref, s32[12,2]{1,0:T(8,128)S(1)} %copy.11.owner_ref, s32[12,2]{1,0:T(8,128)S(1)} %copy.12.place_ref, s32[12,2]{1,0:T(8,128)S(1)} %copy-done.7, s32[4,4]{1,0:T(4,128)S(1)} %bitcast.18, f32[2,16,1536]{2,1,0:T(8,128)} %own_ref.11, ...), custom_call_target="tpu_custom_call" | custom-call | flops 2000000 | bytes 1048576 | tf_op jit(solution)/shard_map/near/pallas_call | solution.py:177
  62.3 0.4 collective-permute-done.10.other_ref
  62.7 0.0 copy-done.4
  62.7 5.5 %last.1 = f32[2,16,1536]{2,1,0:T(8,128)} custom-call(s32[8,12]{1,0:T(8,128)S(1)} %bitcast.12, f32[12,16,128]{2,1,0:T(8,128)S(1)} %level.13.rest_0_.own_ref, f32[12,16,128]{2,1,0:T(8,128)S(1)} %collective-permute-done.10.other_ref, f32[8,12,2,64,128]{4,3,2,1,0:T(8,128)S(1)} %bitcast.4, f32[12,2,64,128]{3,2,1,0:T(8,128)S(1)} %copy-done.4, ...), custom_call_target="tpu_custom_call" | custom-call | flops 2000000 | bytes 1048576 | tf_op jit(solution)/shard_map/last/pallas_call | solution.py:193
  (11 shorter events, 0.0 us)
Async XLA Ops:
  0.0 9.0 %collective-permute-start.4 = (f32[2,16,1536]{2,1,0:T(8,128)}, f32[2,16,1536]{2,1,0:T(8,128)S(1)}, u32[]{:S(2)}, u32[]{:S(2)}) collective-permute-start(f32[2,16,1536]{2,1,0:T(8,128)} %own_ref.11), channel_id=1, source_target_pairs={{0,2},{1,3},{2,0},{3,1},{4,6},{5,7},{6,4},{7,5},{8,10},{9,11},{10,... | collective-permute-start | bytes 589832 | tf_op jit(solution)/shard_map/ppermute | solution.py:124
  3.2 1.1 %copy-start.5 = (f32[12,2,64,128]{3,2,1,0:T(8,128)S(1)}, f32[12,2,64,128]{3,2,1,0:T(8,128)}, u32[]{:S(2)}) copy-start(f32[12,2,64,128]{3,2,1,0:T(8,128)} %weight_ref.15) | copy-start | bytes 2359300
  4.3 17.2 %copy-start.9 = (s32[8,1,12]{2,1,0:T(1,128)S(1)}, s32[8,1,12]{2,1,0:T(1,128)}, u32[]{:S(2)}) copy-start(s32[8,1,12]{2,1,0:T(1,128)} %param.13) | copy-start | bytes 1156
  5.9 6.2 %collective-permute-start = (f32[12,16,128]{2,1,0:T(8,128)S(1)}, f32[12,16,128]{2,1,0:T(8,128)S(1)}, u32[]{:S(2)}, u32[]{:S(2)}) collective-permute-start(f32[12,16,128]{2,1,0:T(8,128)S(1)} %compress.1.own_ref), channel_id=1, source_target_pairs={{0,128},{4,132},{8,136},{12,140},{16,144},{20,148},{24,152},{28,15... | collective-permute-start | bytes 294920 | tf_op jit(solution)/shard_map/ppermute | solution.py:124
  9.0 17.3 %collective-permute-start.3 = (f32[2,16,1536]{2,1,0:T(8,128)}, f32[2,16,1536]{2,1,0:T(8,128)S(1)}, u32[]{:S(2)}, u32[]{:S(2)}) collective-permute-start(f32[2,16,1536]{2,1,0:T(8,128)} %own_ref.11), channel_id=1, source_target_pairs={{0,1},{1,0},{2,3},{3,2},{4,5},{5,4},{6,7},{7,6},{8,9},{9,8},{10,11... | collective-permute-start | bytes 589832 | tf_op jit(solution)/shard_map/ppermute | solution.py:124
  9.0 17.3 %collective-permute-start.5 = (f32[2,16,1536]{2,1,0:T(8,128)S(1)}, f32[2,16,1536]{2,1,0:T(8,128)}, u32[]{:S(2)}, u32[]{:S(2)}) collective-permute-start(f32[2,16,1536]{2,1,0:T(8,128)S(1)} %collective-permute-done.4.far_ref), channel_id=1, source_target_pairs={{0,1},{1,0},{2,3},{3,2},{4,5},{5,4},{6,7},{7,6},{8,9},{9,8},{10,11... | collective-permute-start | bytes 589832 | tf_op jit(solution)/shard_map/ppermute | solution.py:124
  12.1 2.8 %copy-start = (f32[8,12,2,64,128]{4,3,2,1,0:T(8,128)S(1)}, f32[8,12,2,64,128]{4,3,2,1,0:T(8,128)}, u32[]{:S(2)}) copy-start(f32[8,12,2,64,128]{4,3,2,1,0:T(8,128)} %weight_ref.29) | copy-start | bytes 18874372
  14.9 0.7 %copy-start.8 = (s32[8,1,12]{2,1,0:T(1,128)S(1)}, s32[8,1,12]{2,1,0:T(1,128)}, u32[]{:S(2)}) copy-start(s32[8,1,12]{2,1,0:T(1,128)} %param.13) | copy-start | bytes 1156
  15.5 5.9 %copy-start.1 = (f32[8,12,2,64,128]{4,3,2,1,0:T(8,128)S(1)}, f32[8,12,2,64,128]{4,3,2,1,0:T(8,128)}, u32[]{:S(2)}) copy-start(f32[8,12,2,64,128]{4,3,2,1,0:T(8,128)} %weight_ref.29) | copy-start | bytes 18874372
  15.5 8.6 %copy-start.14 = (s32[12,2]{0,1:T(2,128)S(1)}, s32[12,2]{0,1:T(2,128)}, u32[]{:S(2)}) copy-start(s32[12,2]{0,1:T(2,128)} %param.16) | copy-start | bytes 292
  15.6 10.8 %copy-start.3 = (f32[12,2,2,128,128]{4,3,2,1,0:T(8,128)S(1)}, f32[12,2,2,128,128]{4,3,2,1,0:T(8,128)}, u32[]{:S(2)}) copy-start(f32[12,2,2,128,128]{4,3,2,1,0:T(8,128)} %weight_ref.28) | copy-start | bytes 9437188
  16.8 4.7 %collective-permute-start.1 = (f32[12,16,128]{2,1,0:T(8,128)S(1)}, f32[12,16,128]{2,1,0:T(8,128)S(1)}, u32[]{:S(2)}, u32[]{:S(2)}) collective-permute-start(f32[12,16,128]{2,1,0:T(8,128)S(1)} %level.7.own_ref), channel_id=1, source_target_pairs={{0,64},{4,68},{8,72},{12,76},{16,80},{20,84},{24,88},{28,92},{32,9... | collective-permute-start | bytes 294920 | tf_op jit(solution)/shard_map/ppermute | solution.py:124
  23.4 5.6 %collective-permute-start.2 = (f32[12,16,128]{2,1,0:T(8,128)}, f32[12,16,128]{2,1,0:T(8,128)}, u32[]{:S(2)}, u32[]{:S(2)}) collective-permute-start(f32[12,16,128]{2,1,0:T(8,128)} %level.8.rest_0_.own_ref), channel_id=1, source_target_pairs={{0,32},{4,36},{8,40},{12,44},{16,48},{20,52},{24,56},{28,60},{32,0... | collective-permute-start | bytes 294920 | tf_op jit(solution)/shard_map/ppermute | solution.py:124
  26.3 0.7 %copy-start.6 = (s32[12,2]{1,0:T(8,128)S(1)}, s32[12,2]{1,0:T(8,128)}, u32[]{:S(2)}) copy-start(s32[12,2]{1,0:T(8,128)} %copy.13.valid_ref) | copy-start | bytes 292
  27.0 0.7 copy-start.12
  29.0 2.8 %copy-start.2 = (f32[8,12,2,64,128]{4,3,2,1,0:T(8,128)S(1)}, f32[8,12,2,64,128]{4,3,2,1,0:T(8,128)}, u32[]{:S(2)}) copy-start(f32[8,12,2,64,128]{4,3,2,1,0:T(8,128)} %weight_ref.29) | copy-start | bytes 18874372
  31.8 0.7 %copy-start.10 = (s32[8,1,12]{2,1,0:T(1,128)S(1)}, s32[8,1,12]{2,1,0:T(1,128)}, u32[]{:S(2)}) copy-start(s32[8,1,12]{2,1,0:T(1,128)} %param.13) | copy-start | bytes 1156
  32.5 6.4 %copy-start.7 = (s32[12,2]{1,0:T(8,128)S(1)}, s32[12,2]{1,0:T(8,128)}, u32[]{:S(2)}) copy-start(s32[12,2]{1,0:T(8,128)} %copy.13.valid_ref) | copy-start | bytes 292
  32.5 6.4 %copy-start.13 = (s32[1,4,4]{2,1,0:T(4,128)S(1)}, s32[1,4,4]{2,1,0:T(4,128)}, u32[]{:S(2)}) copy-start(s32[1,4,4]{2,1,0:T(4,128)} %param.19) | copy-start | bytes 196
  32.5 10.9 %slice-start = ((s8[6291456]{0:T(1024)(128)(4,1)}), s8[4194304]{0:T(1024)(128)(4,1)S(1)}, s32[]{:S(2)}) async-start(s8[6291456]{0:T(1024)(128)(4,1)} %bitcast.3), calls=%async_computation | async-start | bytes 8388608
  34.3 9.1 %slice-start.1 = ((s8[6291456]{0:T(1024)(128)(4,1)}), s8[2097152]{0:T(1024)(128)(4,1)S(1)}, s32[]{:S(2)}) async-start(s8[6291456]{0:T(1024)(128)(4,1)} %bitcast.3), calls=%async_computation.1 | async-start | bytes 4194304
  34.3 9.1 %copy-start.11 = (s32[8,1,12]{2,1,0:T(1,128)S(1)}, s32[8,1,12]{2,1,0:T(1,128)}, u32[]{:S(2)}) copy-start(s32[8,1,12]{2,1,0:T(1,128)} %param.13) | copy-start | bytes 1156
  34.3 1.4 %collective-permute-start.6 = (f32[12,16,128]{2,1,0:T(8,128)S(1)}, f32[12,16,128]{2,1,0:T(8,128)S(1)}, u32[]{:S(2)}, u32[]{:S(2)}) collective-permute-start(f32[12,16,128]{2,1,0:T(8,128)S(1)} %level.9.own_ref), channel_id=1, source_target_pairs={{0,1},{1,0},{2,3},{3,2},{4,5},{5,4},{6,7},{7,6},{8,9},{9,8},{10,11... | collective-permute-start | bytes 294920 | tf_op jit(solution)/shard_map/ppermute | solution.py:124
  37.0 6.4 %collective-permute-start.7 = (f32[12,16,128]{2,1,0:T(8,128)S(1)}, f32[12,16,128]{2,1,0:T(8,128)S(1)}, u32[]{:S(2)}, u32[]{:S(2)}) collective-permute-start(f32[12,16,128]{2,1,0:T(8,128)S(1)} %level.10.rest_0_.own_ref), channel_id=1, source_target_pairs={{0,2},{1,3},{2,0},{3,1},{4,6},{5,7},{6,4},{7,5},{8,10},{9,11},{10,... | collective-permute-start | bytes 294920 | tf_op jit(solution)/shard_map/ppermute | solution.py:124
  44.7 4.7 %collective-permute-start.8 = (f32[12,16,128]{2,1,0:T(8,128)S(1)}, f32[12,16,128]{2,1,0:T(8,128)S(1)}, u32[]{:S(2)}, u32[]{:S(2)}) collective-permute-start(f32[12,16,128]{2,1,0:T(8,128)S(1)} %level.11.rest_0_.own_ref), channel_id=1, source_target_pairs={{0,32},{4,36},{8,40},{12,44},{16,48},{20,52},{24,56},{28,60},{32,0... | collective-permute-start | bytes 294920 | tf_op jit(solution)/shard_map/ppermute | solution.py:124
  50.6 4.7 %collective-permute-start.9 = (f32[12,16,128]{2,1,0:T(8,128)S(1)}, f32[12,16,128]{2,1,0:T(8,128)S(1)}, u32[]{:S(2)}, u32[]{:S(2)}) collective-permute-start(f32[12,16,128]{2,1,0:T(8,128)S(1)} %level.12.rest_0_.own_ref), channel_id=1, source_target_pairs={{0,64},{4,68},{8,72},{12,76},{16,80},{20,84},{24,88},{28,92},{32,9... | collective-permute-start | bytes 294920 | tf_op jit(solution)/shard_map/ppermute | solution.py:124
  53.5 9.2 %copy-start.4 = (f32[12,2,64,128]{3,2,1,0:T(8,128)S(1)}, f32[12,2,64,128]{3,2,1,0:T(8,128)}, u32[]{:S(2)}) copy-start(f32[12,2,64,128]{3,2,1,0:T(8,128)} %expand_ref.1) | copy-start | bytes 2359300
  56.6 6.2 %collective-permute-start.10 = (f32[12,16,128]{2,1,0:T(8,128)S(1)}, f32[12,16,128]{2,1,0:T(8,128)S(1)}, u32[]{:S(2)}, u32[]{:S(2)}) collective-permute-start(f32[12,16,128]{2,1,0:T(8,128)S(1)} %level.13.rest_0_.own_ref), channel_id=1, source_target_pairs={{0,128},{4,132},{8,136},{12,140},{16,144},{20,148},{24,152},{28,15... | collective-permute-start | bytes 294920 | tf_op jit(solution)/shard_map/ppermute | solution.py:124

commit v2 on v1

v2 whole, which is shorter than its diff:
```python
import functools

import jax
import jax.numpy as jnp
from jax import lax
from jax.experimental import pallas as pl
from jax.experimental.pallas import tpu as pltpu
from jax.sharding import PartitionSpec as P

VMEM = pltpu.VMEM
SMEM = pltpu.SMEM
ANY = pl.ANY
HBM = pltpu.HBM
DMA = pltpu.SemaphoreType.DMA
BF = jnp.bfloat16
F32 = jnp.float32
NT = (((1,), (1,)), ((), ()))
NN = (((1,), (0,)), ((), ()))
NEAR_EACH = 3
NEAR_AT = {4: 1, 5: 1, 6: 1, 7: 1}


def split(value):
    high = value.astype(BF)
    return high, (value - high.astype(F32)).astype(BF)


def product(rows, weights, dims):
    count = rows.shape[0]
    high, low = split(rows)
    stacked = jnp.concatenate(
        [
            jnp.concatenate([high, high], axis=1),
            jnp.concatenate([low, jnp.zeros_like(low)], axis=1),
        ],
        axis=0,
    )
    wide = jnp.concatenate(split(weights), axis=dims[0][1][0])
    result = lax.dot_general(stacked, wide, dims, preferred_element_type=F32)
    return result[:count] + result[count:]


def lane_low(shape):
    return lax.broadcasted_iota(jnp.int32, shape, 1) < 64


def joined(result):
    rhs = result.shape[0] // 2
    turned = pltpu.roll(result[rhs:], 64, axis=1)
    return result[:rhs] + jnp.where(lane_low(turned.shape), -turned, turned)


def compress_kernel(field_hbm, weight_hbm, out_ref, field_ref, weight_ref, sems):
    blocks = out_ref.shape[0]
    chunk = blocks // 3
    field_copy = pltpu.make_async_copy(field_hbm, field_ref, sems.at[3])
    field_copy.start()
    copies = []
    for n in range(3):
        part = pl.ds(n * chunk, chunk)
        copy = pltpu.make_async_copy(weight_hbm.at[part], weight_ref.at[part], sems.at[n])
        copy.start()
        copies.append(copy)
    field_copy.wait()
    for k in range(blocks):
        if k % chunk == 0:
            copies[k // chunk].wait()
        lanes = pl.ds(128 * k, 128)
        rows = jnp.concatenate([field_ref[0, :, lanes], field_ref[1, :, lanes]], axis=0)
        out_ref[k] = joined(product(rows, weight_ref[k].reshape(128, 128), NT))


def stacked_rows(own, other):
    low = lane_low(own.shape)
    real = jnp.where(low, own, pltpu.roll(other, 64, axis=1))
    imag = jnp.where(low, pltpu.roll(own, 64, axis=1), other)
    return jnp.concatenate([real, imag], axis=0)


def level_block(level, k, row, own_ref, other_ref, weight_ref):
    rows = stacked_rows(own_ref[k], other_ref[row[0, k]])
    return joined(product(rows, weight_ref[level, k].reshape(128, 128), NT))


def level_kernel(level, roster_ref, own_ref, other_ref, weight_ref, *rest):
    out_ref = rest[-1]
    row = roster_ref[level]
    for k in range(out_ref.shape[0]):
        out_ref[k] = level_block(level, k, row, own_ref, other_ref, weight_ref)


def last_kernel(level, roster_ref, own_ref, other_ref, weight_ref, expand_ref, *rest):
    near_refs, (out_hbm, state_ref, out_ref, sems) = rest[:-4], rest[-4:]
    row = roster_ref[level]
    blocks = own_ref.shape[0]
    each = near_refs[0].shape[0]
    for k in range(blocks):
        state_ref[k] = level_block(level, k, row, own_ref, other_ref, weight_ref)
    copies = []
    for k in range(blocks):
        coeffs = state_ref[k]
        signed = jnp.where(lane_low(coeffs.shape), coeffs, -coeffs)
        turned = pltpu.roll(coeffs, 64, axis=1)
        far = product(jnp.concatenate([signed, turned], axis=0), expand_ref[k].reshape(128, 128), NN)
        total = far + near_refs[k // each][k % each]
        half = total.shape[0] // 2
        lanes = pl.ds(128 * k, 128)
        out_ref[0, :, lanes] = total[:half]
        out_ref[1, :, lanes] = total[half:]
        if k % 4 == 3:
            part = pl.ds(128 * (k - 3), 512)
            copy = pltpu.make_async_copy(out_ref.at[:, :, part], out_hbm.at[:, :, part], sems.at[k // 4])
            copy.start()
            copies.append(copy)
    for copy in copies:
        copy.wait()


def near_kernel(first, owner_ref, place_ref, valid_ref, pick_ref, own_ref, core_ref, far_ref, both_ref, weight_ref, *rest):
    out_ref = rest[-1]
    me = lax.axis_index("sub")
    for n in range(out_ref.shape[0]):
        k = first + n
        total = None
        for t in range(weight_ref.shape[1]):
            owner = owner_ref[t, k]
            leaf = pick_ref[owner, place_ref[t, k]]
            lanes = pl.ds(pl.multiple_of(leaf * 128, 128), 128)
            which = owner ^ me
            parts = []
            for d in range(2):
                low = jnp.where(which == 1, core_ref[d, :, lanes], own_ref[d, :, lanes])
                high = jnp.where(which == 3, both_ref[d, :, lanes], far_ref[d, :, lanes])
                parts.append(jnp.where(which >= 2, high, low))
            rows = jnp.concatenate(parts, axis=0) * valid_ref[t, k].astype(F32)
            result = product(rows, weight_ref[k, t].reshape(256, 128), NT)
            half = result.shape[0] // 2
            term = jnp.concatenate(
                [result[:half, :128] - result[half:, 128:], result[half:, :128] + result[:half, 128:]], axis=0
            )
            total = term if total is None else total + term
        out_ref[n] = total


def fetch_kernel(*refs):
    count = (len(refs) - 2) // 2
    sources, outs, sem = refs[:count], refs[count + 1 : -1], refs[-1]
    copies = [pltpu.make_async_copy(s, o, sem.at[n]) for n, (s, o) in enumerate(zip(sources, outs))]
    for copy in copies:
        copy.start()
    for copy in copies:
        copy.wait()


def spec(space):
    return pl.BlockSpec(memory_space=space)


def call(kernel, out, spaces, name, out_spaces=VMEM, scratch=(), flops=2_000_000):
    single = not isinstance(out_spaces, (list, tuple))
    return pl.pallas_call(
        kernel,
        out_shape=out,
        in_specs=[spec(space) for space in spaces],
        out_specs=spec(out_spaces) if single else [spec(space) for space in out_spaces],
        scratch_shapes=list(scratch),
        compiler_params=pltpu.CompilerParams(vmem_limit_bytes=8 << 20),
        cost_estimate=pl.CostEstimate(flops=flops, bytes_accessed=1 << 20, transcendentals=0),
        name=name,
    )


def fetch(arrays, after, name):
    return call(
        fetch_kernel,
        [VMEM(a.shape, a.dtype) for a in arrays],
        [HBM] * len(arrays) + [ANY],
        name,
        [VMEM] * len(arrays),
        [DMA((len(arrays),))],
    )(*[pltpu.with_memory_space_constraint(a, HBM) for a in arrays], after)


def flipped(value, axis, mask):
    pairs = [(source, source ^ mask) for source in range(lax.axis_size(axis))]
    return lax.ppermute(value, axis, pairs)


def tied(value, after):
    return lax.optimization_barrier((value, after))[0]


def on_device(
    field_in,
    compress,
    coupling,
    roster,
    expand,
    nearfield_dense_blocks,
    slot_owner_index,
    slot_source_position,
    slot_valid_mask,
    near_pick,
):
    blocks = compress.shape[0]
    rhs = field_in.shape[1]
    leaf_count = lax.axis_size("leaf")
    top = leaf_count // 2
    plan = [
        ("leaf", top),
        ("leaf", top // 2),
        ("leaf", top // 4),
        ("sub", 1),
        ("sub", 2),
        ("leaf", top // 4),
        ("leaf", top // 2),
        ("leaf", top),
    ]
    pick = near_pick[0]
    indices = (slot_owner_index.T, slot_source_position.T, slot_valid_mask.T, pick)
    state = VMEM((blocks, rhs, 128), F32)

    coeffs = call(
        compress_kernel,
        state,
        [HBM, HBM],
        "compress",
        scratch=[VMEM(field_in.shape, F32), VMEM(compress.shape, F32), DMA((4,))],
    )(pltpu.with_memory_space_constraint(field_in, HBM), pltpu.with_memory_space_constraint(compress, HBM))
    pieces = []
    for position, (axis, mask) in enumerate(plan):
        other = flipped(coeffs, axis, mask)
        extra = []
        if position == 0:
            far = flipped(tied(field_in, coeffs), "sub", 2)
            core = flipped(tied(field_in, coeffs), "sub", 1)
            weights, names = fetch([coupling, roster], coeffs, "fetch_coupling")
        if position == 1:
            dense, last, field = fetch([nearfield_dense_blocks, expand, field_in], coeffs, "fetch_near")
            extra.append(field)
        if position == 2:
            both = flipped(tied(far, coeffs), "sub", 1)
        for _ in range(NEAR_AT.get(position, 0)):
            piece = call(
                functools.partial(near_kernel, NEAR_EACH * len(pieces)),
                VMEM((NEAR_EACH, 2 * rhs, 128), F32),
                [SMEM] * 4 + [VMEM] * 5 + [ANY],
                "near",
            )(*indices, field, core, far, both, dense, coeffs)
            pieces.append(piece)
            extra.append(piece)
        if position < len(plan) - 1:
            coeffs = call(
                functools.partial(level_kernel, position),
                state,
                [VMEM] * 4 + [ANY] * len(extra),
                "level",
            )(names, coeffs, other, weights, *extra)
        else:
            total = call(
                functools.partial(last_kernel, position),
                jax.ShapeDtypeStruct(field_in.shape, F32),
                [VMEM] * (5 + len(pieces)),
                "last",
                HBM,
                [VMEM((blocks, rhs, 128), F32), VMEM(field_in.shape, F32), DMA((3,))],
            )(names, coeffs, other, weights, last, *pieces)
    return total


def solution(mesh):
    return jax.shard_map(
        on_device,
        mesh=mesh,
        in_specs=(
            P(None, None, ("leaf", "sub")),
            P(("leaf", "sub"), None, None, None),
            P(None, ("leaf", "sub"), None, None, None),
            P(None, ("leaf", "sub"), None),
            P(("leaf", "sub"), None, None, None),
            P(("leaf", "sub"), None, None, None, None),
            P(("leaf", "sub"), None),
            P(("leaf", "sub"), None),
            P(("leaf", "sub"), None),
            P(("leaf", "sub"), None, None),
        ),
        out_specs=P(None, None, ("leaf", "sub")),
        check_vma=False,
    )
```

time: 68.7 us -> 50 us (0.73)
  local copies, waits for them, and re-layouts: 11.7 us -> 0.03 us
  Pallas kernels: 25.1 us -> 16.5 us
  waiting for transfers between devices: 14.4 us -> 22 us
  starting transfers between devices: 17 us -> 11 us
    unnamed x37 -> x10, local copies, waits for them, and re-layouts: 11.7 us -> 0.03 us
    ppermute x11, waiting for transfers between devices: 14.4 us -> 22 us  [flipped(): return lax.ppermute(value, axis, pairs)]
    ppermute x11, starting transfers between devices: 17 us -> 11 us  [flipped(): return lax.ppermute(value, axis, pairs)]
    pallas_call x14, Pallas kernels: 19.6 us -> 15 us  [the longest x2 4.94 us: fetch(): call(fetch_kernel, [VMEM(a.shape, a.dtype) for a in arrays], [HBM] * len(...]
    pallas_call x1, Pallas kernels: 5.51 us -> 1.52 us  [on_device(): call(functools.partial(last_kernel, position), jax.ShapeDtypeStruct(field...]
  transfers between devices with their start and end apart: 11 -> 11, of which waited for: 7 -> 7; matrix products, arithmetic and copies ran while one was open for 3% -> 0% of each run, Pallas kernels for 19% -> 22%
where the time goes in v2:
time: 50 us; the launch traced here: 49.9 us
  waiting for transfers between devices  22 us (44%)
  Pallas kernels  16.5 us (33%)
  starting transfers between devices  11 us (22%)
    ppermute x11, waiting for transfers between devices, flipped(): return lax.ppermute(value, axis, pairs)  22 us
    ppermute x11, starting transfers between devices, flipped(): return lax.ppermute(value, axis, pairs)  11 us
    pallas_call x2, Pallas kernels, fetch(): call(fetch_kernel, [VMEM(a.shape, a.dtype) for a in arrays], [HBM] * len(...  4.94 us
    pallas_call x7, Pallas kernels, on_device(): call(functools.partial(level_kernel, position), state, [VMEM] * 4 + [ANY]...  4.41 us
    pallas_call x4, Pallas kernels, on_device(): call(functools.partial(near_kernel, NEAR_EACH * len(pieces)), VMEM((NEAR_...  3.71 us
    pallas_call x1, Pallas kernels, on_device(): call(compress_kernel, state, [HBM, HBM], 'compress', scratch=[VMEM(field_...  1.95 us
    pallas_call x1, Pallas kernels, on_device(): call(functools.partial(last_kernel, position), jax.ShapeDtypeStruct(field...  1.52 us
  transfers between devices with their start and end apart: 11, of which 7 were waited for; matrix products, arithmetic and copies ran while one was open for 0% of the time, Pallas kernels for 22%

profile of v2, /device:TPU:64, one launch (start us, length us, event | category | flops | bytes accessed | tf_op | source)
XLA Modules:
  0.0 49.9 jit_solution(15553290358105955218)
XLA Ops:
  0.0 1.9 %compress.1.refs_2_.own_ref = f32[12,16,128]{2,1,0:T(8,128)S(1)} custom-call(f32[2,16,1536]{2,1,0:T(8,128)} %refs_2_.1, f32[12,2,64,128]{3,2,1,0:T(8,128)} %weight_hbm.1), custom_call_target="tpu_custom_call" | custom-call | flops 2000000 | bytes 1048576 | tf_op jit(solution)/shard_map/compress/pallas_call | solution.py:223
  2.0 3.1 %collective-permute-start = (f32[12,16,128]{2,1,0:T(8,128)S(1)}, f32[12,16,128]{2,1,0:T(8,128)S(1)}, u32[]{:S(2)}, u32[]{:S(2)}) collective-permute-start(f32[12,16,128]{2,1,0:T(8,128)S(1)} %compress.1.refs_2_.own_ref), channel_id=1, source_target_pairs={{0,128},{4,132},{8,136},{12,140},{16,144},{20,148},{24,152},{28,15... | collective-permute-start | bytes 294920 | tf_op jit(solution)/shard_map/ppermute | solution.py:186
  5.1 3.2 %collective-permute-start.6 = (f32[2,16,1536]{2,1,0:T(8,128)}, f32[2,16,1536]{2,1,0:T(8,128)S(1)}, u32[]{:S(2)}, u32[]{:S(2)}) collective-permute-start(f32[2,16,1536]{2,1,0:T(8,128)} %refs_2_.1), channel_id=1, source_target_pairs={{0,2},{1,3},{2,0},{3,1},{4,6},{5,7},{6,4},{7,5},{8,10},{9,11},{10,... | collective-permute-start | bytes 589832 | tf_op jit(solution)/shard_map/ppermute | solution.py:186
  8.3 2.8 %fetch_coupling.1 = (f32[8,12,2,64,128]{4,3,2,1,0:T(8,128)S(1)}, s32[8,1,12]{2,1,0:T(1,128)S(1)}) custom-call(f32[8,12,2,64,128]{4,3,2,1,0:T(8,128)} %refs_0_.2, s32[8,1,12]{2,1,0:T(1,128)} %refs_1_.2, f32[12,16,128]{2,1,0:T(8,128)S(1)} %compress.1.refs_2_.own_ref), custom_call_target="tpu_custom_call" | custom-call | flops 2000000 | bytes 1048576 | tf_op jit(solution)/shard_map/fetch_coupling/pallas_call | solution.py:174
  11.1 0.0 collective-permute-done.other_ref
  11.1 0.6 %level.7.refs_3_.own_ref = f32[12,16,128]{2,1,0:T(8,128)S(1)} custom-call(s32[8,1,12]{2,1,0:T(1,128)S(1)} %get-tuple-element.12.roster_ref, f32[12,16,128]{2,1,0:T(8,128)S(1)} %compress.1.refs_2_.own_ref, f32[12,16,128]{2,1,0:T(8,128)S(1)} %collective-permute-done.other_ref, f32[8,12,2,64,128]{4,3,2,1,0:T(8,128)S(1)} %get-tuple-element.13.weight_ref), custom_call_target="tpu_custom_call" | custom-call | flops 2000000 | bytes 1048576 | tf_op jit(solution)/shard_map/level/pallas_call | solution.py:253
  11.7 0.0 copy-start.4
  11.7 0.7 %collective-permute-start.1 = (f32[12,16,128]{2,1,0:T(8,128)S(1)}, f32[12,16,128]{2,1,0:T(8,128)S(1)}, u32[]{:S(2)}, u32[]{:S(2)}) collective-permute-start(f32[12,16,128]{2,1,0:T(8,128)S(1)} %level.7.refs_3_.own_ref), channel_id=1, source_target_pairs={{0,64},{4,68},{8,72},{12,76},{16,80},{20,84},{24,88},{28,92},{32,9... | collective-permute-start | bytes 294920 | tf_op jit(solution)/shard_map/ppermute | solution.py:186
  12.4 2.1 %fetch_near.1 = (f32[12,2,2,128,128]{4,3,2,1,0:T(8,128)S(1)}, f32[12,2,64,128]{3,2,1,0:T(8,128)S(1)}, f32[2,16,1536]{2,1,0:T(8,128)S(1)}) custom-call(f32[12,2,2,128,128]{4,3,2,1,0:T(8,128)} %refs_0_.3, f32[12,2,64,128]{3,2,1,0:T(8,128)} %refs_1_.3, f32[2,16,1536]{2,1,0:T(8,128)} %refs_2_.1, f32[12,16,128]{2,1,0:T(8,128)S(1)} %level.7.refs_3_.own_ref), custom_call_target="tpu_custom_call" | custom-call | flops 2000000 | bytes 1048576 | tf_op jit(solution)/shard_map/fetch_near/pallas_call | solution.py:174
  14.5 1.9 %collective-permute-done.1.other_ref = f32[12,16,128]{2,1,0:T(8,128)S(1)} collective-permute-done((f32[12,16,128]{2,1,0:T(8,128)S(1)}, f32[12,16,128]{2,1,0:T(8,128)S(1)}, u32[]{:S(2)}, u32[]{:S(2)}) %collective-permute-start.1) | collective-permute-done | bytes 98336 | tf_op jit(solution)/shard_map/ppermute | solution.py:186
  16.4 0.6 %level.8.own_ref = f32[12,16,128]{2,1,0:T(8,128)S(1)} custom-call(s32[8,1,12]{2,1,0:T(1,128)S(1)} %get-tuple-element.12.roster_ref, f32[12,16,128]{2,1,0:T(8,128)S(1)} %level.7.refs_3_.own_ref, f32[12,16,128]{2,1,0:T(8,128)S(1)} %collective-permute-done.1.other_ref, f32[8,12,2,64,128]{4,3,2,1,0:T(8,128)S(1)} %get-tuple-element.13.weight_ref, ...), custom_call_target="tpu_custom_call" | custom-call | flops 2000000 | bytes 1048576 | tf_op jit(solution)/shard_map/level/pallas_call | solution.py:253
  17.1 0.0 copy-start
  17.1 0.0 copy-start.1
  17.1 0.0 copy-start.2
  17.1 0.0 copy-start.3
  17.1 0.8 %collective-permute-start.2 = (f32[12,16,128]{2,1,0:T(8,128)S(1)}, f32[12,16,128]{2,1,0:T(8,128)S(1)}, u32[]{:S(2)}, u32[]{:S(2)}) collective-permute-start(f32[12,16,128]{2,1,0:T(8,128)S(1)} %level.8.own_ref), channel_id=1, source_target_pairs={{0,32},{4,36},{8,40},{12,44},{16,48},{20,52},{24,56},{28,60},{32,0... | collective-permute-start | bytes 294920 | tf_op jit(solution)/shard_map/ppermute | solution.py:186
  17.9 0.0 copy-done.4
  17.9 0.0 collective-permute-start.5
  17.9 0.0 collective-permute-done.6.far_ref
  17.9 0.5 %collective-permute-start.7 = (f32[2,16,1536]{2,1,0:T(8,128)S(1)}, f32[2,16,1536]{2,1,0:T(8,128)S(1)}, u32[]{:S(2)}, u32[]{:S(2)}) collective-permute-start(f32[2,16,1536]{2,1,0:T(8,128)S(1)} %collective-permute-done.6.far_ref), channel_id=1, source_target_pairs={{0,1},{1,0},{2,3},{3,2},{4,5},{5,4},{6,7},{7,6},{8,9},{9,8},{10,11... | collective-permute-start | bytes 589832 | tf_op jit(solution)/shard_map/ppermute | solution.py:186
  18.4 3.4 %collective-permute-done.2.other_ref = f32[12,16,128]{2,1,0:T(8,128)S(1)} collective-permute-done((f32[12,16,128]{2,1,0:T(8,128)S(1)}, f32[12,16,128]{2,1,0:T(8,128)S(1)}, u32[]{:S(2)}, u32[]{:S(2)}) %collective-permute-start.2) | collective-permute-done | bytes 98336 | tf_op jit(solution)/shard_map/ppermute | solution.py:186
  21.8 0.6 %level.9.own_ref = f32[12,16,128]{2,1,0:T(8,128)S(1)} custom-call(s32[8,1,12]{2,1,0:T(1,128)S(1)} %get-tuple-element.12.roster_ref, f32[12,16,128]{2,1,0:T(8,128)S(1)} %level.8.own_ref, f32[12,16,128]{2,1,0:T(8,128)S(1)} %collective-permute-done.2.other_ref, f32[8,12,2,64,128]{4,3,2,1,0:T(8,128)S(1)} %get-tuple-element.13.weight_ref), custom_call_target="tpu_custom_call" | custom-call | flops 2000000 | bytes 1048576 | tf_op jit(solution)/shard_map/level/pallas_call | solution.py:253
  22.4 0.1 collective-permute-start.3
  22.5 1.3 %collective-permute-done.3.other_ref = f32[12,16,128]{2,1,0:T(8,128)S(1)} collective-permute-done((f32[12,16,128]{2,1,0:T(8,128)S(1)}, f32[12,16,128]{2,1,0:T(8,128)S(1)}, u32[]{:S(2)}, u32[]{:S(2)}) %collective-permute-start.3) | collective-permute-done | bytes 98336 | tf_op jit(solution)/shard_map/ppermute | solution.py:186
  23.8 0.6 %level.10.rest_0_.own_ref = f32[12,16,128]{2,1,0:T(8,128)S(1)} custom-call(s32[8,1,12]{2,1,0:T(1,128)S(1)} %get-tuple-element.12.roster_ref, f32[12,16,128]{2,1,0:T(8,128)S(1)} %level.9.own_ref, f32[12,16,128]{2,1,0:T(8,128)S(1)} %collective-permute-done.3.other_ref, f32[8,12,2,64,128]{4,3,2,1,0:T(8,128)S(1)} %get-tuple-element.13.weight_ref), custom_call_target="tpu_custom_call" | custom-call | flops 2000000 | bytes 1048576 | tf_op jit(solution)/shard_map/level/pallas_call | solution.py:253
  24.4 0.6 %collective-permute-start.4 = (f32[12,16,128]{2,1,0:T(8,128)S(1)}, f32[12,16,128]{2,1,0:T(8,128)S(1)}, u32[]{:S(2)}, u32[]{:S(2)}) collective-permute-start(f32[12,16,128]{2,1,0:T(8,128)S(1)} %level.10.rest_0_.own_ref), channel_id=1, source_target_pairs={{0,2},{1,3},{2,0},{3,1},{4,6},{5,7},{6,4},{7,5},{8,10},{9,11},{10,... | collective-permute-start | bytes 294920 | tf_op jit(solution)/shard_map/ppermute | solution.py:186
  25.0 0.0 collective-permute-done.5.core_ref
  25.0 0.0 collective-permute-done.7.both_ref
  25.0 0.0 copy-done
  25.0 0.0 copy-done.1
  25.0 0.0 copy-done.2
  25.0 0.0 copy-done.3
  25.0 0.9 %near.4.rest_0_ = f32[3,32,128]{2,1,0:T(8,128)S(1)} custom-call(s32[2,12]{1,0:T(2,128)S(1)} %bitcast.8, s32[2,12]{1,0:T(2,128)S(1)} %bitcast.12, s32[2,12]{1,0:T(2,128)S(1)} %bitcast.16, s32[4,4]{1,0:T(4,128)S(1)} %bitcast.4, f32[2,16,1536]{2,1,0:T(8,128)S(1)} %get-tuple-element.14.rest_0_.own_ref, f32[2,16,1536]{2,1,0:T(8,128)S(1)} %collective-permute-done.5.core_ref, ...), custom_call_target="tpu_custom_call" | custom-call | flops 2000000 | bytes 1048576 | tf_op jit(solution)/shard_map/near/pallas_call | solution.py:244
  26.0 4.8 %collective-permute-done.4.other_ref = f32[12,16,128]{2,1,0:T(8,128)S(1)} collective-permute-done((f32[12,16,128]{2,1,0:T(8,128)S(1)}, f32[12,16,128]{2,1,0:T(8,128)S(1)}, u32[]{:S(2)}, u32[]{:S(2)}) %collective-permute-start.4) | collective-permute-done | bytes 98336 | tf_op jit(solution)/shard_map/ppermute | solution.py:186
  30.9 0.6 %level.11.rest_0_.own_ref = f32[12,16,128]{2,1,0:T(8,128)S(1)} custom-call(s32[8,1,12]{2,1,0:T(1,128)S(1)} %get-tuple-element.12.roster_ref, f32[12,16,128]{2,1,0:T(8,128)S(1)} %level.10.rest_0_.own_ref, f32[12,16,128]{2,1,0:T(8,128)S(1)} %collective-permute-done.4.other_ref, f32[8,12,2,64,128]{4,3,2,1,0:T(8,128)S(1)} %get-tuple-element.13.weight_ref, ...), custom_call_target="tpu_custom_call" | custom-call | flops 2000000 | bytes 1048576 | tf_op jit(solution)/shard_map/level/pallas_call | solution.py:253
  31.5 0.8 %collective-permute-start.8 = (f32[12,16,128]{2,1,0:T(8,128)S(1)}, f32[12,16,128]{2,1,0:T(8,128)S(1)}, u32[]{:S(2)}, u32[]{:S(2)}) collective-permute-start(f32[12,16,128]{2,1,0:T(8,128)S(1)} %level.11.rest_0_.own_ref), channel_id=1, source_target_pairs={{0,32},{4,36},{8,40},{12,44},{16,48},{20,52},{24,56},{28,60},{32,0... | collective-permute-start | bytes 294920 | tf_op jit(solution)/shard_map/ppermute | solution.py:186
  32.2 0.9 %near.5.rest_0_.rest_1_ = f32[3,32,128]{2,1,0:T(8,128)S(1)} custom-call(s32[2,12]{1,0:T(2,128)S(1)} %bitcast.9, s32[2,12]{1,0:T(2,128)S(1)} %bitcast.13, s32[2,12]{1,0:T(2,128)S(1)} %bitcast.17, s32[4,4]{1,0:T(4,128)S(1)} %bitcast.5, f32[2,16,1536]{2,1,0:T(8,128)S(1)} %get-tuple-element.14.rest_0_.own_ref, ...), custom_call_target="tpu_custom_call" | custom-call | flops 2000000 | bytes 1048576 | tf_op jit(solution)/shard_map/near/pallas_call | solution.py:244
  33.2 3.0 %collective-permute-done.8.other_ref = f32[12,16,128]{2,1,0:T(8,128)S(1)} collective-permute-done((f32[12,16,128]{2,1,0:T(8,128)S(1)}, f32[12,16,128]{2,1,0:T(8,128)S(1)}, u32[]{:S(2)}, u32[]{:S(2)}) %collective-permute-start.8) | collective-permute-done | bytes 98336 | tf_op jit(solution)/shard_map/ppermute | solution.py:186
  36.2 0.6 %level.12.rest_0_.own_ref = f32[12,16,128]{2,1,0:T(8,128)S(1)} custom-call(s32[8,1,12]{2,1,0:T(1,128)S(1)} %get-tuple-element.12.roster_ref, f32[12,16,128]{2,1,0:T(8,128)S(1)} %level.11.rest_0_.own_ref, f32[12,16,128]{2,1,0:T(8,128)S(1)} %collective-permute-done.8.other_ref, f32[8,12,2,64,128]{4,3,2,1,0:T(8,128)S(1)} %get-tuple-element.13.weight_ref, ...), custom_call_target="tpu_custom_call" | custom-call | flops 2000000 | bytes 1048576 | tf_op jit(solution)/shard_map/level/pallas_call | solution.py:253
  36.8 0.7 %collective-permute-start.9 = (f32[12,16,128]{2,1,0:T(8,128)S(1)}, f32[12,16,128]{2,1,0:T(8,128)S(1)}, u32[]{:S(2)}, u32[]{:S(2)}) collective-permute-start(f32[12,16,128]{2,1,0:T(8,128)S(1)} %level.12.rest_0_.own_ref), channel_id=1, source_target_pairs={{0,64},{4,68},{8,72},{12,76},{16,80},{20,84},{24,88},{28,92},{32,9... | collective-permute-start | bytes 294920 | tf_op jit(solution)/shard_map/ppermute | solution.py:186
  37.5 0.9 %near.6.rest_0_.rest_2_ = f32[3,32,128]{2,1,0:T(8,128)S(1)} custom-call(s32[2,12]{1,0:T(2,128)S(1)} %bitcast.10, s32[2,12]{1,0:T(2,128)S(1)} %bitcast.14, s32[2,12]{1,0:T(2,128)S(1)} %bitcast.18, s32[4,4]{1,0:T(4,128)S(1)} %bitcast.6, f32[2,16,1536]{2,1,0:T(8,128)S(1)} %get-tuple-element.14.rest_0_.own_ref, ...), custom_call_target="tpu_custom_call" | custom-call | flops 2000000 | bytes 1048576 | tf_op jit(solution)/shard_map/near/pallas_call | solution.py:244
  38.5 3.1 %collective-permute-done.9.other_ref = f32[12,16,128]{2,1,0:T(8,128)S(1)} collective-permute-done((f32[12,16,128]{2,1,0:T(8,128)S(1)}, f32[12,16,128]{2,1,0:T(8,128)S(1)}, u32[]{:S(2)}, u32[]{:S(2)}) %collective-permute-start.9) | collective-permute-done | bytes 98336 | tf_op jit(solution)/shard_map/ppermute | solution.py:186
  41.5 0.6 %level.13.rest_0_.own_ref = f32[12,16,128]{2,1,0:T(8,128)S(1)} custom-call(s32[8,1,12]{2,1,0:T(1,128)S(1)} %get-tuple-element.12.roster_ref, f32[12,16,128]{2,1,0:T(8,128)S(1)} %level.12.rest_0_.own_ref, f32[12,16,128]{2,1,0:T(8,128)S(1)} %collective-permute-done.9.other_ref, f32[8,12,2,64,128]{4,3,2,1,0:T(8,128)S(1)} %get-tuple-element.13.weight_ref, ...), custom_call_target="tpu_custom_call" | custom-call | flops 2000000 | bytes 1048576 | tf_op jit(solution)/shard_map/level/pallas_call | solution.py:253
  42.1 0.7 %collective-permute-start.10 = (f32[12,16,128]{2,1,0:T(8,128)S(1)}, f32[12,16,128]{2,1,0:T(8,128)S(1)}, u32[]{:S(2)}, u32[]{:S(2)}) collective-permute-start(f32[12,16,128]{2,1,0:T(8,128)S(1)} %level.13.rest_0_.own_ref), channel_id=1, source_target_pairs={{0,128},{4,132},{8,136},{12,140},{16,144},{20,148},{24,152},{28,15... | collective-permute-start | bytes 294920 | tf_op jit(solution)/shard_map/ppermute | solution.py:186
  42.8 0.9 %near.7.rest_3_ = f32[3,32,128]{2,1,0:T(8,128)S(1)} custom-call(s32[2,12]{1,0:T(2,128)S(1)} %bitcast.11, s32[2,12]{1,0:T(2,128)S(1)} %bitcast.15, s32[2,12]{1,0:T(2,128)S(1)} %bitcast.19, s32[4,4]{1,0:T(4,128)S(1)} %bitcast.7, f32[2,16,1536]{2,1,0:T(8,128)S(1)} %get-tuple-element.14.rest_0_.own_ref, f32[2,16,1536]{2,1,0:T(8,128)S(1)} %collective-permute-done.5.core_ref, ...), custom_call_target="tpu_custom_call" | custom-call | flops 2000000 | bytes 1048576 | tf_op jit(solution)/shard_map/near/pallas_call | solution.py:244
  43.8 4.6 %collective-permute-done.10.other_ref = f32[12,16,128]{2,1,0:T(8,128)S(1)} collective-permute-done((f32[12,16,128]{2,1,0:T(8,128)S(1)}, f32[12,16,128]{2,1,0:T(8,128)S(1)}, u32[]{:S(2)}, u32[]{:S(2)}) %collective-permute-start.10) | collective-permute-done | bytes 98336 | tf_op jit(solution)/shard_map/ppermute | solution.py:186
  48.3 1.5 %last.1 = f32[2,16,1536]{2,1,0:T(8,128)} custom-call(s32[8,1,12]{2,1,0:T(1,128)S(1)} %get-tuple-element.12.roster_ref, f32[12,16,128]{2,1,0:T(8,128)S(1)} %level.13.rest_0_.own_ref, f32[12,16,128]{2,1,0:T(8,128)S(1)} %collective-permute-done.10.other_ref, f32[8,12,2,64,128]{4,3,2,1,0:T(8,128)S(1)} %get-tuple-element.13.weight_ref, ...), custom_call_target="tpu_custom_call" | custom-call | flops 2000000 | bytes 1048576 | tf_op jit(solution)/shard_map/last/pallas_call | solution.py:260
Async XLA Ops:
  2.0 9.1 %collective-permute-start = (f32[12,16,128]{2,1,0:T(8,128)S(1)}, f32[12,16,128]{2,1,0:T(8,128)S(1)}, u32[]{:S(2)}, u32[]{:S(2)}) collective-permute-start(f32[12,16,128]{2,1,0:T(8,128)S(1)} %compress.1.refs_2_.own_ref), channel_id=1, source_target_pairs={{0,128},{4,132},{8,136},{12,140},{16,144},{20,148},{24,152},{28,15... | collective-permute-start | bytes 294920 | tf_op jit(solution)/shard_map/ppermute | solution.py:186
  5.1 12.8 %collective-permute-start.6 = (f32[2,16,1536]{2,1,0:T(8,128)}, f32[2,16,1536]{2,1,0:T(8,128)S(1)}, u32[]{:S(2)}, u32[]{:S(2)}) collective-permute-start(f32[2,16,1536]{2,1,0:T(8,128)} %refs_2_.1), channel_id=1, source_target_pairs={{0,2},{1,3},{2,0},{3,1},{4,6},{5,7},{6,4},{7,5},{8,10},{9,11},{10,... | collective-permute-start | bytes 589832 | tf_op jit(solution)/shard_map/ppermute | solution.py:186
  11.7 6.1 %copy-start.4 = (f32[2,16,1536]{2,1,0:T(8,128)S(1)}, f32[2,16,1536]{2,1,0:T(8,128)}, u32[]{:S(2)}) copy-start(f32[2,16,1536]{2,1,0:T(8,128)} %refs_2_.1) | copy-start | bytes 589828
  11.7 4.7 %collective-permute-start.1 = (f32[12,16,128]{2,1,0:T(8,128)S(1)}, f32[12,16,128]{2,1,0:T(8,128)S(1)}, u32[]{:S(2)}, u32[]{:S(2)}) collective-permute-start(f32[12,16,128]{2,1,0:T(8,128)S(1)} %level.7.refs_3_.own_ref), channel_id=1, source_target_pairs={{0,64},{4,68},{8,72},{12,76},{16,80},{20,84},{24,88},{28,92},{32,9... | collective-permute-start | bytes 294920 | tf_op jit(solution)/shard_map/ppermute | solution.py:186
  17.1 8.0 %copy-start = (s32[1,4,4]{2,1,0:T(4,128)S(1)}, s32[1,4,4]{2,1,0:T(4,128)}, u32[]{:S(2)}) copy-start(s32[1,4,4]{2,1,0:T(4,128)} %param.19) | copy-start | bytes 196
  17.1 8.0 %copy-start.1 = (s32[12,2]{0,1:T(2,128)S(1)}, s32[12,2]{0,1:T(2,128)}, u32[]{:S(2)}) copy-start(s32[12,2]{0,1:T(2,128)} %param.16) | copy-start | bytes 292
  17.1 8.0 %copy-start.2 = (s32[12,2]{0,1:T(2,128)S(1)}, s32[12,2]{0,1:T(2,128)}, u32[]{:S(2)}) copy-start(s32[12,2]{0,1:T(2,128)} %param.17) | copy-start | bytes 292
  17.1 8.0 %copy-start.3 = (s32[12,2]{0,1:T(2,128)S(1)}, s32[12,2]{0,1:T(2,128)}, u32[]{:S(2)}) copy-start(s32[12,2]{0,1:T(2,128)} %param.18) | copy-start | bytes 292
  17.1 4.7 %collective-permute-start.2 = (f32[12,16,128]{2,1,0:T(8,128)S(1)}, f32[12,16,128]{2,1,0:T(8,128)S(1)}, u32[]{:S(2)}, u32[]{:S(2)}) collective-permute-start(f32[12,16,128]{2,1,0:T(8,128)S(1)} %level.8.own_ref), channel_id=1, source_target_pairs={{0,32},{4,36},{8,40},{12,44},{16,48},{20,52},{24,56},{28,60},{32,0... | collective-permute-start | bytes 294920 | tf_op jit(solution)/shard_map/ppermute | solution.py:186
  17.9 7.2 %collective-permute-start.5 = (f32[2,16,1536]{2,1,0:T(8,128)S(1)}, f32[2,16,1536]{2,1,0:T(8,128)S(1)}, u32[]{:S(2)}, u32[]{:S(2)}) collective-permute-start(f32[2,16,1536]{2,1,0:T(8,128)S(1)} %copy-done.4), channel_id=1, source_target_pairs={{0,1},{1,0},{2,3},{3,2},{4,5},{5,4},{6,7},{7,6},{8,9},{9,8},{10,11... | collective-permute-start | bytes 589832 | tf_op jit(solution)/shard_map/ppermute | solution.py:186
  17.9 7.1 %collective-permute-start.7 = (f32[2,16,1536]{2,1,0:T(8,128)S(1)}, f32[2,16,1536]{2,1,0:T(8,128)S(1)}, u32[]{:S(2)}, u32[]{:S(2)}) collective-permute-start(f32[2,16,1536]{2,1,0:T(8,128)S(1)} %collective-permute-done.6.far_ref), channel_id=1, source_target_pairs={{0,1},{1,0},{2,3},{3,2},{4,5},{5,4},{6,7},{7,6},{8,9},{9,8},{10,11... | collective-permute-start | bytes 589832 | tf_op jit(solution)/shard_map/ppermute | solution.py:186
  22.4 1.4 %collective-permute-start.3 = (f32[12,16,128]{2,1,0:T(8,128)S(1)}, f32[12,16,128]{2,1,0:T(8,128)S(1)}, u32[]{:S(2)}, u32[]{:S(2)}) collective-permute-start(f32[12,16,128]{2,1,0:T(8,128)S(1)} %level.9.own_ref), channel_id=1, source_target_pairs={{0,1},{1,0},{2,3},{3,2},{4,5},{5,4},{6,7},{7,6},{8,9},{9,8},{10,11... | collective-permute-start | bytes 294920 | tf_op jit(solution)/shard_map/ppermute | solution.py:186
  24.4 6.4 %collective-permute-start.4 = (f32[12,16,128]{2,1,0:T(8,128)S(1)}, f32[12,16,128]{2,1,0:T(8,128)S(1)}, u32[]{:S(2)}, u32[]{:S(2)}) collective-permute-start(f32[12,16,128]{2,1,0:T(8,128)S(1)} %level.10.rest_0_.own_ref), channel_id=1, source_target_pairs={{0,2},{1,3},{2,0},{3,1},{4,6},{5,7},{6,4},{7,5},{8,10},{9,11},{10,... | collective-permute-start | bytes 294920 | tf_op jit(solution)/shard_map/ppermute | solution.py:186
  31.5 4.7 %collective-permute-start.8 = (f32[12,16,128]{2,1,0:T(8,128)S(1)}, f32[12,16,128]{2,1,0:T(8,128)S(1)}, u32[]{:S(2)}, u32[]{:S(2)}) collective-permute-start(f32[12,16,128]{2,1,0:T(8,128)S(1)} %level.11.rest_0_.own_ref), channel_id=1, source_target_pairs={{0,32},{4,36},{8,40},{12,44},{16,48},{20,52},{24,56},{28,60},{32,0... | collective-permute-start | bytes 294920 | tf_op jit(solution)/shard_map/ppermute | solution.py:186
  36.8 4.7 %collective-permute-start.9 = (f32[12,16,128]{2,1,0:T(8,128)S(1)}, f32[12,16,128]{2,1,0:T(8,128)S(1)}, u32[]{:S(2)}, u32[]{:S(2)}) collective-permute-start(f32[12,16,128]{2,1,0:T(8,128)S(1)} %level.12.rest_0_.own_ref), channel_id=1, source_target_pairs={{0,64},{4,68},{8,72},{12,76},{16,80},{20,84},{24,88},{28,92},{32,9... | collective-permute-start | bytes 294920 | tf_op jit(solution)/shard_map/ppermute | solution.py:186
  42.1 6.2 %collective-permute-start.10 = (f32[12,16,128]{2,1,0:T(8,128)S(1)}, f32[12,16,128]{2,1,0:T(8,128)S(1)}, u32[]{:S(2)}, u32[]{:S(2)}) collective-permute-start(f32[12,16,128]{2,1,0:T(8,128)S(1)} %level.13.rest_0_.own_ref), channel_id=1, source_target_pairs={{0,128},{4,132},{8,136},{12,140},{16,144},{20,148},{24,152},{28,15... | collective-permute-start | bytes 294920 | tf_op jit(solution)/shard_map/ppermute | solution.py:186

commit v3 on v2

--- a/solution.py
+++ b/solution.py
@@ -6,6 +6,7 @@
 from jax.experimental import pallas as pl
 from jax.experimental.pallas import tpu as pltpu
 from jax.sharding import PartitionSpec as P
+
 
 VMEM = pltpu.VMEM
 SMEM = pltpu.SMEM
@@ -16,8 +17,9 @@
 F32 = jnp.float32
 NT = (((1,), (1,)), ((), ()))
 NN = (((1,), (0,)), ((), ()))
-NEAR_EACH = 3
-NEAR_AT = {4: 1, 5: 1, 6: 1, 7: 1}
+NEAR_EACH = 4
+HALF = 8
+NEAR_AT = {5: 1, 6: 1, 7: 1}
 
 
 def split(value):
@@ -50,7 +52,14 @@
     return result[:rhs] + jnp.where(lane_low(turned.shape), -turned, turned)
 
 
-def compress_kernel(field_hbm, weight_hbm, out_ref, field_ref, weight_ref, sems):
+def compress_block(half, k, field_ref, weight_ref, out_ref):
+    part = pl.ds(half * HALF, HALF)
+    lanes = pl.ds(128 * k, 128)
+    rows = jnp.concatenate([field_ref[0, part, lanes], field_ref[1, part, lanes]], axis=0)
+    out_ref[k] = joined(product(rows, weight_ref[k].reshape(128, 128), NT))
+
+
+def compress_kernel(field_hbm, weight_hbm, coupling_hbm, roster_hbm, out_ref, field_ref, weight_ref, coupling_ref, roster_ref, sems):
     blocks = out_ref.shape[0]
     chunk = blocks // 3
     field_copy = pltpu.make_async_copy(field_hbm, field_ref, sems.at[3])
@@ -61,13 +70,27 @@
         copy = pltpu.make_async_copy(weight_hbm.at[part], weight_ref.at[part], sems.at[n])
         copy.start()
         copies.append(copy)
+    later = [
+        pltpu.make_async_copy(coupling_hbm.at[0], coupling_ref, sems.at[4]),
+        pltpu.make_async_copy(roster_hbm, roster_ref, sems.at[5]),
+    ]
+    for copy in later:
+        copy.start()
     field_copy.wait()
     for k in range(blocks):
         if k % chunk == 0:
             copies[k // chunk].wait()
-        lanes = pl.ds(128 * k, 128)
-        rows = jnp.concatenate([field_ref[0, :, lanes], field_ref[1, :, lanes]], axis=0)
-        out_ref[k] = joined(product(rows, weight_ref[k].reshape(128, 128), NT))
+        compress_block(0, k, field_ref, weight_ref, out_ref)
+    for copy in later:
+        copy.wait()
+
+
+def compress_again(field_ref, weight_ref, coupling_hbm, out_ref, coupling_ref, sem):
+    copy = pltpu.make_async_copy(coupling_hbm.at[1], coupling_ref, sem)
+    copy.start()
+    for k in range(out_ref.shape[0]):
+        compress_block(1, k, field_ref, weight_ref, out_ref)
+    copy.wait()
 
 
 def stacked_rows(own, other):
@@ -77,41 +100,59 @@
     return jnp.concatenate([real, imag], axis=0)
 
 
-def level_block(level, k, row, own_ref, other_ref, weight_ref):
+def level_block(k, row, own_ref, other_ref, weight_ref):
     rows = stacked_rows(own_ref[k], other_ref[row[0, k]])
-    return joined(product(rows, weight_ref[level, k].reshape(128, 128), NT))
-
-
-def level_kernel(level, roster_ref, own_ref, other_ref, weight_ref, *rest):
+    return joined(product(rows, weight_ref[k].reshape(128, 128), NT))
+
+
+def level_kernel(level, at, roster_ref, own_ref, other_ref, weight_ref, *rest):
     out_ref = rest[-1]
     row = roster_ref[level]
     for k in range(out_ref.shape[0]):
-        out_ref[k] = level_block(level, k, row, own_ref, other_ref, weight_ref)
-
-
-def last_kernel(level, roster_ref, own_ref, other_ref, weight_ref, expand_ref, *rest):
-    near_refs, (out_hbm, state_ref, out_ref, sems) = rest[:-4], rest[-4:]
+        out_ref[k] = level_block(k, row, own_ref, other_ref, weight_ref.at[at])
+
+
+def last_rows(half, level, at, roster_ref, own_ref, other_ref, weight_ref, expand_ref, near_refs, state_ref, out_ref, done):
     row = roster_ref[level]
     blocks = own_ref.shape[0]
     each = near_refs[0].shape[0]
+    rhs = near_refs[0].shape[1] // 2
+    here = pl.ds(half * HALF, HALF)
+    there = pl.ds(rhs + half * HALF, HALF)
     for k in range(blocks):
-        state_ref[k] = level_block(level, k, row, own_ref, other_ref, weight_ref)
-    copies = []
+        state_ref[k] = level_block(k, row, own_ref, other_ref, weight_ref.at[at])
     for k in range(blocks):
         coeffs = state_ref[k]
         signed = jnp.where(lane_low(coeffs.shape), coeffs, -coeffs)
         turned = pltpu.roll(coeffs, 64, axis=1)
         far = product(jnp.concatenate([signed, turned], axis=0), expand_ref[k].reshape(128, 128), NN)
-        total = far + near_refs[k // each][k % each]
-        half = total.shape[0] // 2
+        near_ref = near_refs[k // each]
         lanes = pl.ds(128 * k, 128)
-        out_ref[0, :, lanes] = total[:half]
-        out_ref[1, :, lanes] = total[half:]
+        out_ref[0, :, lanes] = far[:HALF] + near_ref[k % each, here]
+        out_ref[1, :, lanes] = far[HALF:] + near_ref[k % each, there]
+        done(k)
+
+
+def last_first(level, at, roster_ref, own_ref, other_ref, weight_ref, expand_ref, *rest):
+    near_refs, (out_ref, state_ref) = rest[:-2], rest[-2:]
+    last_rows(0, level, at, roster_ref, own_ref, other_ref, weight_ref, expand_ref, near_refs, state_ref, out_ref, lambda k: None)
+
+
+def last_second(level, at, roster_ref, own_ref, other_ref, weight_ref, expand_ref, ready_ref, *rest):
+    near_refs, (out_hbm, state_ref, out_ref, sems) = rest[:-4], rest[-4:]
+    copies = [pltpu.make_async_copy(ready_ref, out_hbm.at[:, pl.ds(0, HALF)], sems.at[3])]
+    copies[0].start()
+
+    def done(k):
         if k % 4 == 3:
             part = pl.ds(128 * (k - 3), 512)
-            copy = pltpu.make_async_copy(out_ref.at[:, :, part], out_hbm.at[:, :, part], sems.at[k // 4])
+            copy = pltpu.make_async_copy(
+                out_ref.at[:, :, part], out_hbm.at[:, pl.ds(HALF, HALF), part], sems.at[k // 4]
+            )
             copy.start()
             copies.append(copy)
+
+    last_rows(1, level, at, roster_ref, own_ref, other_ref, weight_ref, expand_ref, near_refs, state_ref, out_ref, done)
     for copy in copies:
         copy.wait()
 
@@ -142,10 +183,13 @@
         out_ref[n] = total
 
 
-def fetch_kernel(*refs):
-    count = (len(refs) - 2) // 2
+def fetch_kernel(parts, *refs):
+    count = len(parts)
     sources, outs, sem = refs[:count], refs[count + 1 : -1], refs[-1]
-    copies = [pltpu.make_async_copy(s, o, sem.at[n]) for n, (s, o) in enumerate(zip(sources, outs))]
+    copies = []
+    for n, (part, source, out) in enumerate(zip(parts, sources, outs)):
+        source = source if part is None else source.at[pl.ds(*part)]
+        copies.append(pltpu.make_async_copy(source, out, sem.at[n]))
     for copy in copies:
         copy.start()
     for copy in copies:
@@ -156,7 +200,7 @@
     return pl.BlockSpec(memory_space=space)
 
 
-def call(kernel, out, spaces, name, out_spaces=VMEM, scratch=(), flops=2_000_000):
+def call(kernel, out, spaces, out_spaces=VMEM, scratch=(), flops=2_000_000):
     single = not isinstance(out_spaces, (list, tuple))
     return pl.pallas_call(
         kernel,
@@ -166,19 +210,22 @@
         scratch_shapes=list(scratch),
         compiler_params=pltpu.CompilerParams(vmem_limit_bytes=8 << 20),
         cost_estimate=pl.CostEstimate(flops=flops, bytes_accessed=1 << 20, transcendentals=0),
-        name=name,
     )
 
 
-def fetch(arrays, after, name):
+def in_hbm(*arrays):
+    return [pltpu.with_memory_space_constraint(array, HBM) for array in arrays]
+
+
+def fetch(arrays, parts, after):
+    shapes = [a.shape if p is None else (p[1],) + a.shape[1:] for a, p in zip(arrays, parts)]
     return call(
-        fetch_kernel,
-        [VMEM(a.shape, a.dtype) for a in arrays],
+        functools.partial(fetch_kernel, parts),
+        [VMEM(shape, a.dtype) for shape, a in zip(shapes, arrays)],
         [HBM] * len(arrays) + [ANY],
-        name,
         [VMEM] * len(arrays),
         [DMA((len(arrays),))],
-    )(*[pltpu.with_memory_space_constraint(a, HBM) for a in arrays], after)
+    )(*in_hbm(*arrays), after)
 
 
 def flipped(value, axis, mask):
@@ -218,53 +265,72 @@
     ]
     pick = near_pick[0]
     indices = (slot_owner_index.T, slot_source_position.T, slot_valid_mask.T, pick)
-    state = VMEM((blocks, rhs, 128), F32)
-
-    coeffs = call(
+    state = VMEM((blocks, HALF, 128), F32)
+    field_shape, base_shape = VMEM(field_in.shape, F32), VMEM(compress.shape, F32)
+
+    coeffs = [None, None]
+    weights = {}
+    coeffs[0], field, base, weights[0], names = call(
         compress_kernel,
-        state,
-        [HBM, HBM],
-        "compress",
-        scratch=[VMEM(field_in.shape, F32), VMEM(compress.shape, F32), DMA((4,))],
-    )(pltpu.with_memory_space_constraint(field_in, HBM), pltpu.with_memory_space_constraint(compress, HBM))
+        [state, field_shape, base_shape, VMEM(coupling.shape[1:], F32), VMEM(roster.shape, jnp.int32)],
+        [HBM] * 4,
+        [VMEM] * 5,
+        scratch=[DMA((6,))],
+    )(*in_hbm(field_in, compress, coupling, roster))
+    coeffs[1], weights[1] = call(
+        compress_again, [state, VMEM(coupling.shape[1:], F32)], [VMEM, VMEM, HBM], [VMEM] * 2, scratch=[DMA]
+    )(field, base, *in_hbm(coupling))
+    weights = {level: (weights[level][None], 0) for level in weights}
     pieces = []
     for position, (axis, mask) in enumerate(plan):
-        other = flipped(coeffs, axis, mask)
+        other = [flipped(c, axis, mask) for c in coeffs]
         extra = []
         if position == 0:
-            far = flipped(tied(field_in, coeffs), "sub", 2)
-            core = flipped(tied(field_in, coeffs), "sub", 1)
-            weights, names = fetch([coupling, roster], coeffs, "fetch_coupling")
-        if position == 1:
-            dense, last, field = fetch([nearfield_dense_blocks, expand, field_in], coeffs, "fetch_near")
-            extra.append(field)
-        if position == 2:
-            both = flipped(tied(far, coeffs), "sub", 1)
+            far = flipped(tied(field_in, coeffs[1]), "sub", 2)
+        if position in (1, 2):
+            begin = 3 * position - 1
+            (some,) = fetch([coupling], [(begin, 3)], coeffs[1])
+            weights.update({begin + n: (some, n) for n in range(3)})
+            extra.append(some)
+        if position == 4:
+            core = flipped(tied(field_in, coeffs[1]), "sub", 1)
+            both = flipped(tied(far, coeffs[1]), "sub", 1)
+            dense, last = fetch([nearfield_dense_blocks, expand], [None, None], coeffs[1])
+            extra.append(last)
         for _ in range(NEAR_AT.get(position, 0)):
             piece = call(
                 functools.partial(near_kernel, NEAR_EACH * len(pieces)),
                 VMEM((NEAR_EACH, 2 * rhs, 128), F32),
                 [SMEM] * 4 + [VMEM] * 5 + [ANY],
-                "near",
-            )(*indices, field, core, far, both, dense, coeffs)
+            )(*indices, field, core, far, both, dense, coeffs[1])
             pieces.append(piece)
             extra.append(piece)
         if position < len(plan) - 1:
-            coeffs = call(
-                functools.partial(level_kernel, position),
-                state,
-                [VMEM] * 4 + [ANY] * len(extra),
-                "level",
-            )(names, coeffs, other, weights, *extra)
+            fresh = []
+            for half in range(2):
+                after = extra + fresh
+                fresh.append(
+                    call(
+                        functools.partial(level_kernel, position, weights[position][1]),
+                        state,
+                        [VMEM] * 4 + [ANY] * len(after),
+                    )(names, coeffs[half], other[half], weights[position][0], *after)
+                )
+            coeffs = fresh
         else:
+            ready = call(
+                functools.partial(last_first, position, weights[position][1]),
+                VMEM((2, HALF, field_in.shape[2]), F32),
+                [VMEM] * (5 + len(pieces)),
+                scratch=[state],
+            )(names, coeffs[0], other[0], weights[position][0], last, *pieces)
             total = call(
-                functools.partial(last_kernel, position),
+                functools.partial(last_second, position, weights[position][1]),
                 jax.ShapeDtypeStruct(field_in.shape, F32),
-                [VMEM] * (5 + len(pieces)),
-                "last",
+                [VMEM] * (6 + len(pieces)),
                 HBM,
-                [VMEM((blocks, rhs, 128), F32), VMEM(field_in.shape, F32), DMA((3,))],
-            )(names, coeffs, other, weights, last, *pieces)
+                [state, VMEM((2, HALF, field_in.shape[2]), F32), DMA((4,))],
+            )(names, coeffs[1], other[1], weights[position][0], last, ready, *pieces)
     return total
 
 

time: 50 us -> 52 us (1.040)
  waiting for transfers between devices: 22 us -> 4.82 us
  starting transfers between devices: 11 us -> 24.2 us
  Pallas kernels: 16.5 us -> 22.3 us
    ppermute x11 -> x19, waiting for transfers between devices: 22 us -> 4.82 us  [flipped(): return lax.ppermute(value, axis, pairs)]
    ppermute x11 -> x19, starting transfers between devices: 11 us -> 24.2 us  [flipped(): return lax.ppermute(value, axis, pairs)]
    pallas_call x11 -> x21, Pallas kernels: 12.8 us -> 19.3 us  [the longest x14 8.45 us: on_device(): call(functools.partial(level_kernel, position, weights[position][1]), sta...]
    pallas_call x4 -> x3, Pallas kernels: 3.71 us -> 3.02 us  [on_device(): call(functools.partial(near_kernel, NEAR_EACH * len(pieces)), VMEM((NEAR_...]
  transfers between devices with their start and end apart: 11 -> 19, of which waited for: 7 -> 7; matrix products, arithmetic and copies ran while one was open for 0% -> 0% of each run, Pallas kernels for 22% -> 37%
where the time goes in v3:
time: 52 us; the launch traced here: 51.8 us
  starting transfers between devices  24.2 us (47%)
  Pallas kernels  22.3 us (43%)
  waiting for transfers between devices  4.82 us (9%)
    ppermute x19, starting transfers between devices, flipped(): return lax.ppermute(value, axis, pairs)  24.2 us
    pallas_call x14, Pallas kernels, on_device(): call(functools.partial(level_kernel, position, weights[position][1]), sta...  8.45 us
    pallas_call x3, Pallas kernels, fetch(): call(functools.partial(fetch_kernel, parts), [VMEM(shape, a.dtype) for sh...  5.44 us
    ppermute x19, waiting for transfers between devices, flipped(): return lax.ppermute(value, axis, pairs)  4.82 us
    pallas_call x3, Pallas kernels, on_device(): call(functools.partial(near_kernel, NEAR_EACH * len(pieces)), VMEM((NEAR_...  3.02 us
    pallas_call x1, Pallas kernels, on_device(): call(compress_kernel, [state, field_shape, base_shape, VMEM(coupling.shap...  1.94 us
    pallas_call x1, Pallas kernels, on_device(): call(functools.partial(last_second, position, weights[position][1]), jax....  1.48 us
    pallas_call x1, Pallas kernels, on_device(): call(compress_again, [state, VMEM(coupling.shape[1:], F32)], [VMEM, VMEM,...  1.18 us
  transfers between devices with their start and end apart: 19, of which 7 were waited for; matrix products, arithmetic and copies ran while one was open for 0% of the time, Pallas kernels for 37%

profile of v3, /device:TPU:64, one launch (start us, length us, event | category | flops | bytes accessed | tf_op | source)
XLA Modules:
  0.0 51.8 jit_solution(7471940508630721793)
XLA Ops:
  0.0 1.9 %shard_map.100 = (f32[12,8,128]{2,1,0:T(8,128)S(1)}, f32[2,16,1536]{2,1,0:T(8,128)S(1)}, f32[12,2,64,128]{3,2,1,0:T(8,128)S(1)}, f32[12,2,64,128]{3,2,1,0:T(8,128)S(1)}, s32[8,1,12]{2,1,0:T(1,128)S(1)}) custom-call(f32[2,16,1536]{2,1,0:T(8,128)} %field_hbm.1, f32[12,2,64,128]{3,2,1,0:T(8,128)} %weight_hbm.1, f32[8,12,2,64,128]{4,3,2,1,0:T(8,128)} %refs_0_.4, ...), custom_call_target="tpu_custom_call" | custom-call | flops 2000000 | bytes 1048576 | tf_op jit(solution)/shard_map/pallas_call | solution.py:273
  1.9 3.1 %collective-permute-start.1 = (f32[12,8,128]{2,1,0:T(8,128)S(1)}, f32[12,8,128]{2,1,0:T(8,128)S(1)}, u32[]{:S(2)}, u32[]{:S(2)}) collective-permute-start(f32[12,8,128]{2,1,0:T(8,128)S(1)} %get-tuple-element.22.own_ref), channel_id=1, source_target_pairs={{0,128},{4,132},{8,136},{12,140},{16,144},{20,148},{24,152},{28,15... | collective-permute-start | bytes 147464 | tf_op jit(solution)/shard_map/ppermute | solution.py:233
  5.1 1.2 %shard_map.101 = (f32[12,8,128]{2,1,0:T(8,128)S(1)}, f32[12,2,64,128]{3,2,1,0:T(8,128)S(1)}) custom-call(f32[2,16,1536]{2,1,0:T(8,128)S(1)} %get-tuple-element.18.field_ref.own_ref, f32[12,2,64,128]{3,2,1,0:T(8,128)S(1)} %get-tuple-element.19.weight_ref, f32[8,12,2,64,128]{4,3,2,1,0:T(8,128)} %refs_0_.4), custom_call_target="tpu_custom_call" | custom-call | flops 2000000 | bytes 1048576 | tf_op jit(solution)/shard_map/pallas_call | solution.py:280
  6.2 0.6 %collective-permute-start = (f32[12,8,128]{2,1,0:T(8,128)S(1)}, f32[12,8,128]{2,1,0:T(8,128)S(1)}, u32[]{:S(2)}, u32[]{:S(2)}) collective-permute-start(f32[12,8,128]{2,1,0:T(8,128)S(1)} %get-tuple-element.20.own_ref), channel_id=1, source_target_pairs={{0,128},{4,132},{8,136},{12,140},{16,144},{20,148},{24,152},{28,15... | collective-permute-start | bytes 147464 | tf_op jit(solution)/shard_map/ppermute | solution.py:233
  6.8 3.2 %collective-permute-start.12 = (f32[2,16,1536]{2,1,0:T(8,128)S(1)}, f32[2,16,1536]{2,1,0:T(8,128)S(1)}, u32[]{:S(2)}, u32[]{:S(2)}) collective-permute-start(f32[2,16,1536]{2,1,0:T(8,128)S(1)} %copy-done.4), channel_id=1, source_target_pairs={{0,2},{1,3},{2,0},{3,1},{4,6},{5,7},{6,4},{7,5},{8,10},{9,11},{10,... | collective-permute-start | bytes 589832 | tf_op jit(solution)/shard_map/ppermute | solution.py:233
  10.0 0.6 %shard_map.102.rest_0_.own_ref = f32[12,8,128]{2,1,0:T(8,128)S(1)} custom-call(s32[8,1,12]{2,1,0:T(1,128)S(1)} %get-tuple-element.17.roster_ref, f32[12,8,128]{2,1,0:T(8,128)S(1)} %get-tuple-element.22.own_ref, f32[12,8,128]{2,1,0:T(8,128)S(1)} %collective-permute-done.1.other_ref, f32[1,12,2,64,128]{4,3,2,1,0:T(8,128)S(1)} %bitcast.6), custom_call_target="tpu_custom_call" | custom-call | flops 2000000 | bytes 1048576 | tf_op jit(solution)/shard_map/pallas_call | solution.py:313
  10.6 1.6 %collective-permute-start.3 = (f32[12,8,128]{2,1,0:T(8,128)S(1)}, f32[12,8,128]{2,1,0:T(8,128)S(1)}, u32[]{:S(2)}, u32[]{:S(2)}) collective-permute-start(f32[12,8,128]{2,1,0:T(8,128)S(1)} %shard_map.102.rest_0_.own_ref), channel_id=1, source_target_pairs={{0,64},{4,68},{8,72},{12,76},{16,80},{20,84},{24,88},{28,92},{32,9... | collective-permute-start | bytes 147464 | tf_op jit(solution)/shard_map/ppermute | solution.py:233
  12.2 0.0 collective-permute-done.other_ref
  12.2 0.6 %shard_map.103.refs_1_.own_ref = f32[12,8,128]{2,1,0:T(8,128)S(1)} custom-call(s32[8,1,12]{2,1,0:T(1,128)S(1)} %get-tuple-element.17.roster_ref, f32[12,8,128]{2,1,0:T(8,128)S(1)} %get-tuple-element.20.own_ref, f32[12,8,128]{2,1,0:T(8,128)S(1)} %collective-permute-done.other_ref, f32[1,12,2,64,128]{4,3,2,1,0:T(8,128)S(1)} %bitcast.7, ...), custom_call_target="tpu_custom_call" | custom-call | flops 2000000 | bytes 1048576 | tf_op jit(solution)/shard_map/pallas_call | solution.py:313
  12.8 0.6 %collective-permute-start.2 = (f32[12,8,128]{2,1,0:T(8,128)S(1)}, f32[12,8,128]{2,1,0:T(8,128)S(1)}, u32[]{:S(2)}, u32[]{:S(2)}) collective-permute-start(f32[12,8,128]{2,1,0:T(8,128)S(1)} %shard_map.103.refs_1_.own_ref), channel_id=1, source_target_pairs={{0,64},{4,68},{8,72},{12,76},{16,80},{20,84},{24,88},{28,92},{32,9... | collective-permute-start | bytes 147464 | tf_op jit(solution)/shard_map/ppermute | solution.py:233
  13.4 1.7 %shard_map.104.rest_0_.weight_ref = f32[3,12,2,64,128]{4,3,2,1,0:T(8,128)S(1)} custom-call(f32[8,12,2,64,128]{4,3,2,1,0:T(8,128)} %refs_0_.4, f32[12,8,128]{2,1,0:T(8,128)S(1)} %shard_map.103.refs_1_.own_ref), custom_call_target="tpu_custom_call" | custom-call | flops 2000000 | bytes 1048576 | tf_op jit(solution)/shard_map/pallas_call | solution.py:222
  15.1 0.1 collective-permute-done.3.other_ref
  15.2 0.6 %shard_map.105.rest_1_.own_ref = f32[12,8,128]{2,1,0:T(8,128)S(1)} custom-call(s32[8,1,12]{2,1,0:T(1,128)S(1)} %get-tuple-element.17.roster_ref, f32[12,8,128]{2,1,0:T(8,128)S(1)} %shard_map.102.rest_0_.own_ref, f32[12,8,128]{2,1,0:T(8,128)S(1)} %collective-permute-done.3.other_ref, f32[1,12,2,64,128]{4,3,2,1,0:T(8,128)S(1)} %bitcast.8, ...), custom_call_target="tpu_custom_call" | custom-call | flops 2000000 | bytes 1048576 | tf_op jit(solution)/shard_map/pallas_call | solution.py:313
  15.8 1.3 %collective-permute-start.5 = (f32[12,8,128]{2,1,0:T(8,128)S(1)}, f32[12,8,128]{2,1,0:T(8,128)S(1)}, u32[]{:S(2)}, u32[]{:S(2)}) collective-permute-start(f32[12,8,128]{2,1,0:T(8,128)S(1)} %shard_map.105.rest_1_.own_ref), channel_id=1, source_target_pairs={{0,32},{4,36},{8,40},{12,44},{16,48},{20,52},{24,56},{28,60},{32,0... | collective-permute-start | bytes 147464 | tf_op jit(solution)/shard_map/ppermute | solution.py:233
  17.1 0.0 collective-permute-done.2.other_ref
  17.1 0.6 %shard_map.106.refs_1_.own_ref = f32[12,8,128]{2,1,0:T(8,128)S(1)} custom-call(s32[8,1,12]{2,1,0:T(1,128)S(1)} %get-tuple-element.17.roster_ref, f32[12,8,128]{2,1,0:T(8,128)S(1)} %shard_map.103.refs_1_.own_ref, f32[12,8,128]{2,1,0:T(8,128)S(1)} %collective-permute-done.2.other_ref, f32[1,12,2,64,128]{4,3,2,1,0:T(8,128)S(1)} %bitcast.9, ...), custom_call_target="tpu_custom_call" | custom-call | flops 2000000 | bytes 1048576 | tf_op jit(solution)/shard_map/pallas_call | solution.py:313
  17.7 1.2 %collective-permute-start.4 = (f32[12,8,128]{2,1,0:T(8,128)S(1)}, f32[12,8,128]{2,1,0:T(8,128)S(1)}, u32[]{:S(2)}, u32[]{:S(2)}) collective-permute-start(f32[12,8,128]{2,1,0:T(8,128)S(1)} %shard_map.106.refs_1_.own_ref), channel_id=1, source_target_pairs={{0,32},{4,36},{8,40},{12,44},{16,48},{20,52},{24,56},{28,60},{32,0... | collective-permute-start | bytes 147464 | tf_op jit(solution)/shard_map/ppermute | solution.py:233
  18.9 1.7 %shard_map.107.rest_0_.weight_ref = f32[3,12,2,64,128]{4,3,2,1,0:T(8,128)S(1)} custom-call(f32[8,12,2,64,128]{4,3,2,1,0:T(8,128)} %refs_0_.4, f32[12,8,128]{2,1,0:T(8,128)S(1)} %shard_map.106.refs_1_.own_ref), custom_call_target="tpu_custom_call" | custom-call | flops 2000000 | bytes 1048576 | tf_op jit(solution)/shard_map/pallas_call | solution.py:222
  20.6 0.0 collective-permute-done.5.other_ref
  20.6 0.6 %shard_map.108.rest_1_.own_ref = f32[12,8,128]{2,1,0:T(8,128)S(1)} custom-call(s32[8,1,12]{2,1,0:T(1,128)S(1)} %get-tuple-element.17.roster_ref, f32[12,8,128]{2,1,0:T(8,128)S(1)} %shard_map.105.rest_1_.own_ref, f32[12,8,128]{2,1,0:T(8,128)S(1)} %collective-permute-done.5.other_ref, f32[3,12,2,64,128]{4,3,2,1,0:T(8,128)S(1)} %shard_map.104.rest_0_.weight_ref, ...), custom_call_target="tpu_custom_call" | custom-call | flops 2000000 | bytes 1048576 | tf_op jit(solution)/shard_map/pallas_call | solution.py:313
  21.2 0.1 collective-permute-start.7
  21.3 0.6 %collective-permute-done.4.other_ref = f32[12,8,128]{2,1,0:T(8,128)S(1)} collective-permute-done((f32[12,8,128]{2,1,0:T(8,128)S(1)}, f32[12,8,128]{2,1,0:T(8,128)S(1)}, u32[]{:S(2)}, u32[]{:S(2)}) %collective-permute-start.4) | collective-permute-done | bytes 49184 | tf_op jit(solution)/shard_map/ppermute | solution.py:233
  21.9 0.6 %shard_map.109.own_ref = f32[12,8,128]{2,1,0:T(8,128)S(1)} custom-call(s32[8,1,12]{2,1,0:T(1,128)S(1)} %get-tuple-element.17.roster_ref, f32[12,8,128]{2,1,0:T(8,128)S(1)} %shard_map.106.refs_1_.own_ref, f32[12,8,128]{2,1,0:T(8,128)S(1)} %collective-permute-done.4.other_ref, f32[3,12,2,64,128]{4,3,2,1,0:T(8,128)S(1)} %shard_map.104.rest_0_.weight_ref, ...), custom_call_target="tpu_custom_call" | custom-call | flops 2000000 | bytes 1048576 | tf_op jit(solution)/shard_map/pallas_call | solution.py:313
  22.5 0.1 collective-permute-start.6
  22.6 0.0 collective-permute-done.7.other_ref
  22.6 0.6 %shard_map.110.rest_0_.own_ref = f32[12,8,128]{2,1,0:T(8,128)S(1)} custom-call(s32[8,1,12]{2,1,0:T(1,128)S(1)} %get-tuple-element.17.roster_ref, f32[12,8,128]{2,1,0:T(8,128)S(1)} %shard_map.108.rest_1_.own_ref, f32[12,8,128]{2,1,0:T(8,128)S(1)} %collective-permute-done.7.other_ref, f32[3,12,2,64,128]{4,3,2,1,0:T(8,128)S(1)} %shard_map.104.rest_0_.weight_ref), custom_call_target="tpu_custom_call" | custom-call | flops 2000000 | bytes 1048576 | tf_op jit(solution)/shard_map/pallas_call | solution.py:313
  23.2 0.6 %collective-permute-done.6.other_ref = f32[12,8,128]{2,1,0:T(8,128)S(1)} collective-permute-done((f32[12,8,128]{2,1,0:T(8,128)S(1)}, f32[12,8,128]{2,1,0:T(8,128)S(1)}, u32[]{:S(2)}, u32[]{:S(2)}) %collective-permute-start.6) | collective-permute-done | bytes 49184 | tf_op jit(solution)/shard_map/ppermute | solution.py:233
  23.8 0.6 %shard_map.111.refs_2_.own_ref = f32[12,8,128]{2,1,0:T(8,128)S(1)} custom-call(s32[8,1,12]{2,1,0:T(1,128)S(1)} %get-tuple-element.17.roster_ref, f32[12,8,128]{2,1,0:T(8,128)S(1)} %shard_map.109.own_ref, f32[12,8,128]{2,1,0:T(8,128)S(1)} %collective-permute-done.6.other_ref, f32[3,12,2,64,128]{4,3,2,1,0:T(8,128)S(1)} %shard_map.104.rest_0_.weight_ref, ...), custom_call_target="tpu_custom_call" | custom-call | flops 2000000 | bytes 1048576 | tf_op jit(solution)/shard_map/pallas_call | solution.py:313
  24.4 0.0 collective-permute-done.12.far_ref
  24.4 0.2 collective-permute-start.13
  24.6 0.4 collective-permute-start.11
  25.0 2.9 %collective-permute-start.9 = (f32[12,8,128]{2,1,0:T(8,128)S(1)}, f32[12,8,128]{2,1,0:T(8,128)S(1)}, u32[]{:S(2)}, u32[]{:S(2)}) collective-permute-start(f32[12,8,128]{2,1,0:T(8,128)S(1)} %shard_map.110.rest_0_.own_ref), channel_id=1, source_target_pairs={{0,2},{1,3},{2,0},{3,1},{4,6},{5,7},{6,4},{7,5},{8,10},{9,11},{10,... | collective-permute-start | bytes 147464 | tf_op jit(solution)/shard_map/ppermute | solution.py:233
  27.9 0.6 %collective-permute-start.8 = (f32[12,8,128]{2,1,0:T(8,128)S(1)}, f32[12,8,128]{2,1,0:T(8,128)S(1)}, u32[]{:S(2)}, u32[]{:S(2)}) collective-permute-start(f32[12,8,128]{2,1,0:T(8,128)S(1)} %shard_map.111.refs_2_.own_ref), channel_id=1, source_target_pairs={{0,2},{1,3},{2,0},{3,1},{4,6},{5,7},{6,4},{7,5},{8,10},{9,11},{10,... | collective-permute-start | bytes 147464 | tf_op jit(solution)/shard_map/ppermute | solution.py:233
  28.5 2.1 %shard_map.112 = (f32[12,2,2,128,128]{4,3,2,1,0:T(8,128)S(1)}, f32[12,2,64,128]{3,2,1,0:T(8,128)S(1)}) custom-call(f32[12,2,2,128,128]{4,3,2,1,0:T(8,128)} %refs_0_.5, f32[12,2,64,128]{3,2,1,0:T(8,128)} %refs_1_.1, f32[12,8,128]{2,1,0:T(8,128)S(1)} %shard_map.111.refs_2_.own_ref), custom_call_target="tpu_custom_call" | custom-call | flops 2000000 | bytes 1048576 | tf_op jit(solution)/shard_map/pallas_call | solution.py:222
  30.6 0.0 collective-permute-done.9.other_ref
  30.6 0.0 copy-start
  30.7 0.0 copy-start.1
  30.7 0.0 copy-start.2
  30.7 0.0 copy-start.3
  30.7 0.6 %shard_map.113.rest_1_.own_ref = f32[12,8,128]{2,1,0:T(8,128)S(1)} custom-call(s32[8,1,12]{2,1,0:T(1,128)S(1)} %get-tuple-element.17.roster_ref, f32[12,8,128]{2,1,0:T(8,128)S(1)} %shard_map.110.rest_0_.own_ref, f32[12,8,128]{2,1,0:T(8,128)S(1)} %collective-permute-done.9.other_ref, f32[3,12,2,64,128]{4,3,2,1,0:T(8,128)S(1)} %shard_map.104.rest_0_.weight_ref, ...), custom_call_target="tpu_custom_call" | custom-call | flops 2000000 | bytes 1048576 | tf_op jit(solution)/shard_map/pallas_call | solution.py:313
  31.3 1.2 %collective-permute-start.14 = (f32[12,8,128]{2,1,0:T(8,128)S(1)}, f32[12,8,128]{2,1,0:T(8,128)S(1)}, u32[]{:S(2)}, u32[]{:S(2)}) collective-permute-start(f32[12,8,128]{2,1,0:T(8,128)S(1)} %shard_map.113.rest_1_.own_ref), channel_id=1, source_target_pairs={{0,32},{4,36},{8,40},{12,44},{16,48},{20,52},{24,56},{28,60},{32,0... | collective-permute-start | bytes 147464 | tf_op jit(solution)/shard_map/ppermute | solution.py:233
  32.5 1.0 %collective-permute-done.8.other_ref = f32[12,8,128]{2,1,0:T(8,128)S(1)} collective-permute-done((f32[12,8,128]{2,1,0:T(8,128)S(1)}, f32[12,8,128]{2,1,0:T(8,128)S(1)}, u32[]{:S(2)}, u32[]{:S(2)}) %collective-permute-start.8) | collective-permute-done | bytes 49184 | tf_op jit(solution)/shard_map/ppermute | solution.py:233
  33.5 0.6 %shard_map.114.rest_0_.own_ref = f32[12,8,128]{2,1,0:T(8,128)S(1)} custom-call(s32[8,1,12]{2,1,0:T(1,128)S(1)} %get-tuple-element.17.roster_ref, f32[12,8,128]{2,1,0:T(8,128)S(1)} %shard_map.111.refs_2_.own_ref, f32[12,8,128]{2,1,0:T(8,128)S(1)} %collective-permute-done.8.other_ref, f32[3,12,2,64,128]{4,3,2,1,0:T(8,128)S(1)} %shard_map.104.rest_0_.weight_ref, ...), custom_call_target="tpu_custom_call" | custom-call | flops 2000000 | bytes 1048576 | tf_op jit(solution)/shard_map/pallas_call | solution.py:313
  34.1 0.9 %collective-permute-start.10 = (f32[12,8,128]{2,1,0:T(8,128)S(1)}, f32[12,8,128]{2,1,0:T(8,128)S(1)}, u32[]{:S(2)}, u32[]{:S(2)}) collective-permute-start(f32[12,8,128]{2,1,0:T(8,128)S(1)} %shard_map.114.rest_0_.own_ref), channel_id=1, source_target_pairs={{0,32},{4,36},{8,40},{12,44},{16,48},{20,52},{24,56},{28,60},{32,0... | collective-permute-start | bytes 147464 | tf_op jit(solution)/shard_map/ppermute | solution.py:233
  35.0 0.0 collective-permute-done.13.both_ref
  35.0 0.0 collective-permute-done.11.core_ref
  35.0 1.0 %shard_map.115.rest_0_ = f32[4,32,128]{2,1,0:T(8,128)S(1)} custom-call(s32[2,12]{1,0:T(2,128)S(1)} %bitcast.13, s32[2,12]{1,0:T(2,128)S(1)} %bitcast.16, s32[2,12]{1,0:T(2,128)S(1)} %bitcast.19, s32[4,4]{1,0:T(4,128)S(1)} %bitcast.10, f32[2,16,1536]{2,1,0:T(8,128)S(1)} %get-tuple-element.18.field_ref.own_ref, ...), custom_call_target="tpu_custom_call" | custom-call | flops 2000000 | bytes 1048576 | tf_op jit(solution)/shard_map/pallas_call | solution.py:301
  36.1 0.0 collective-permute-done.14.other_ref
  36.1 0.6 %shard_map.116.rest_1_.own_ref = f32[12,8,128]{2,1,0:T(8,128)S(1)} custom-call(s32[8,1,12]{2,1,0:T(1,128)S(1)} %get-tuple-element.17.roster_ref, f32[12,8,128]{2,1,0:T(8,128)S(1)} %shard_map.113.rest_1_.own_ref, f32[12,8,128]{2,1,0:T(8,128)S(1)} %collective-permute-done.14.other_ref, f32[3,12,2,64,128]{4,3,2,1,0:T(8,128)S(1)} %shard_map.107.rest_0_.weight_ref, ...), custom_call_target="tpu_custom_call" | custom-call | flops 2000000 | bytes 1048576 | tf_op jit(solution)/shard_map/pallas_call | solution.py:313
  36.7 1.1 %collective-permute-start.16 = (f32[12,8,128]{2,1,0:T(8,128)S(1)}, f32[12,8,128]{2,1,0:T(8,128)S(1)}, u32[]{:S(2)}, u32[]{:S(2)}) collective-permute-start(f32[12,8,128]{2,1,0:T(8,128)S(1)} %shard_map.116.rest_1_.own_ref), channel_id=1, source_target_pairs={{0,64},{4,68},{8,72},{12,76},{16,80},{20,84},{24,88},{28,92},{32,9... | collective-permute-start | bytes 147464 | tf_op jit(solution)/shard_map/ppermute | solution.py:233
  37.9 0.6 %collective-permute-done.10.other_ref = f32[12,8,128]{2,1,0:T(8,128)S(1)} collective-permute-done((f32[12,8,128]{2,1,0:T(8,128)S(1)}, f32[12,8,128]{2,1,0:T(8,128)S(1)}, u32[]{:S(2)}, u32[]{:S(2)}) %collective-permute-start.10) | collective-permute-done | bytes 49184 | tf_op jit(solution)/shard_map/ppermute | solution.py:233
  38.4 0.6 %shard_map.117.rest_0_.own_ref = f32[12,8,128]{2,1,0:T(8,128)S(1)} custom-call(s32[8,1,12]{2,1,0:T(1,128)S(1)} %get-tuple-element.17.roster_ref, f32[12,8,128]{2,1,0:T(8,128)S(1)} %shard_map.114.rest_0_.own_ref, f32[12,8,128]{2,1,0:T(8,128)S(1)} %collective-permute-done.10.other_ref, f32[3,12,2,64,128]{4,3,2,1,0:T(8,128)S(1)} %shard_map.107.rest_0_.weight_ref, ...), custom_call_target="tpu_custom_call" | custom-call | flops 2000000 | bytes 1048576 | tf_op jit(solution)/shard_map/pallas_call | solution.py:313
  39.0 1.5 %collective-permute-start.15 = (f32[12,8,128]{2,1,0:T(8,128)S(1)}, f32[12,8,128]{2,1,0:T(8,128)S(1)}, u32[]{:S(2)}, u32[]{:S(2)}) collective-permute-start(f32[12,8,128]{2,1,0:T(8,128)S(1)} %shard_map.117.rest_0_.own_ref), channel_id=1, source_target_pairs={{0,64},{4,68},{8,72},{12,76},{16,80},{20,84},{24,88},{28,92},{32,9... | collective-permute-start | bytes 147464 | tf_op jit(solution)/shard_map/ppermute | solution.py:233
  40.5 1.0 %shard_map.118.rest_0_.rest_1_ = f32[4,32,128]{2,1,0:T(8,128)S(1)} custom-call(s32[2,12]{1,0:T(2,128)S(1)} %bitcast.14, s32[2,12]{1,0:T(2,128)S(1)} %bitcast.17, s32[2,12]{1,0:T(2,128)S(1)} %bitcast.20, s32[4,4]{1,0:T(4,128)S(1)} %bitcast.11, f32[2,16,1536]{2,1,0:T(8,128)S(1)} %get-tuple-element.18.field_ref.own_ref, ...), custom_call_target="tpu_custom_call" | custom-call | flops 2000000 | bytes 1048576 | tf_op jit(solution)/shard_map/pallas_call | solution.py:301
  41.6 0.0 collective-permute-done.16.other_ref
  41.6 0.6 %shard_map.119.rest_1_.own_ref = f32[12,8,128]{2,1,0:T(8,128)S(1)} custom-call(s32[8,1,12]{2,1,0:T(1,128)S(1)} %get-tuple-element.17.roster_ref, f32[12,8,128]{2,1,0:T(8,128)S(1)} %shard_map.116.rest_1_.own_ref, f32[12,8,128]{2,1,0:T(8,128)S(1)} %collective-permute-done.16.other_ref, f32[3,12,2,64,128]{4,3,2,1,0:T(8,128)S(1)} %shard_map.107.rest_0_.weight_ref, ...), custom_call_target="tpu_custom_call" | custom-call | flops 2000000 | bytes 1048576 | tf_op jit(solution)/shard_map/pallas_call | solution.py:313
  42.2 1.7 %collective-permute-start.18 = (f32[12,8,128]{2,1,0:T(8,128)S(1)}, f32[12,8,128]{2,1,0:T(8,128)S(1)}, u32[]{:S(2)}, u32[]{:S(2)}) collective-permute-start(f32[12,8,128]{2,1,0:T(8,128)S(1)} %shard_map.119.rest_1_.own_ref), channel_id=1, source_target_pairs={{0,128},{4,132},{8,136},{12,140},{16,144},{20,148},{24,152},{28,15... | collective-permute-start | bytes 147464 | tf_op jit(solution)/shard_map/ppermute | solution.py:233
  43.9 0.6 %shard_map.120.rest_0_.own_ref = f32[12,8,128]{2,1,0:T(8,128)S(1)} custom-call(s32[8,1,12]{2,1,0:T(1,128)S(1)} %get-tuple-element.17.roster_ref, f32[12,8,128]{2,1,0:T(8,128)S(1)} %shard_map.117.rest_0_.own_ref, f32[12,8,128]{2,1,0:T(8,128)S(1)} %collective-permute-done.15.other_ref, f32[3,12,2,64,128]{4,3,2,1,0:T(8,128)S(1)} %shard_map.107.rest_0_.weight_ref, ...), custom_call_target="tpu_custom_call" | custom-call | flops 2000000 | bytes 1048576 | tf_op jit(solution)/shard_map/pallas_call | solution.py:313
  44.5 1.9 %collective-permute-start.17 = (f32[12,8,128]{2,1,0:T(8,128)S(1)}, f32[12,8,128]{2,1,0:T(8,128)S(1)}, u32[]{:S(2)}, u32[]{:S(2)}) collective-permute-start(f32[12,8,128]{2,1,0:T(8,128)S(1)} %shard_map.120.rest_0_.own_ref), channel_id=1, source_target_pairs={{0,128},{4,132},{8,136},{12,140},{16,144},{20,148},{24,152},{28,15... | collective-permute-start | bytes 147464 | tf_op jit(solution)/shard_map/ppermute | solution.py:233
  46.5 1.0 %shard_map.121.rest_2_ = f32[4,32,128]{2,1,0:T(8,128)S(1)} custom-call(s32[2,12]{1,0:T(2,128)S(1)} %bitcast.15, s32[2,12]{1,0:T(2,128)S(1)} %bitcast.18, s32[2,12]{1,0:T(2,128)S(1)} %bitcast.21, s32[4,4]{1,0:T(4,128)S(1)} %bitcast.12, f32[2,16,1536]{2,1,0:T(8,128)S(1)} %get-tuple-element.18.field_ref.own_ref, ...), custom_call_target="tpu_custom_call" | custom-call | flops 2000000 | bytes 1048576 | tf_op jit(solution)/shard_map/pallas_call | solution.py:301
  47.5 0.3 collective-permute-done.18.other_ref
  47.9 0.8 %shard_map.122.ready_ref = f32[2,8,1536]{2,1,0:T(8,128)S(1)} custom-call(s32[8,1,12]{2,1,0:T(1,128)S(1)} %get-tuple-element.17.roster_ref, f32[12,8,128]{2,1,0:T(8,128)S(1)} %shard_map.119.rest_1_.own_ref, f32[12,8,128]{2,1,0:T(8,128)S(1)} %collective-permute-done.18.other_ref, f32[3,12,2,64,128]{4,3,2,1,0:T(8,128)S(1)} %shard_map.107.rest_0_.weight_ref, ...), custom_call_target="tpu_custom_call" | custom-call | flops 2000000 | bytes 1048576 | tf_op jit(solution)/shard_map/pallas_call | solution.py:321
  48.7 1.5 %collective-permute-done.17.other_ref = f32[12,8,128]{2,1,0:T(8,128)S(1)} collective-permute-done((f32[12,8,128]{2,1,0:T(8,128)S(1)}, f32[12,8,128]{2,1,0:T(8,128)S(1)}, u32[]{:S(2)}, u32[]{:S(2)}) %collective-permute-start.17) | collective-permute-done | bytes 49184 | tf_op jit(solution)/shard_map/ppermute | solution.py:233
  50.2 1.5 %shard_map.123 = f32[2,16,1536]{2,1,0:T(8,128)} custom-call(s32[8,1,12]{2,1,0:T(1,128)S(1)} %get-tuple-element.17.roster_ref, f32[12,8,128]{2,1,0:T(8,128)S(1)} %shard_map.120.rest_0_.own_ref, f32[12,8,128]{2,1,0:T(8,128)S(1)} %collective-permute-done.17.other_ref, f32[3,12,2,64,128]{4,3,2,1,0:T(8,128)S(1)} %shard_map.107.rest_0_.weight_ref, ...), custom_call_target="tpu_custom_call" | custom-call | flops 2000000 | bytes 1048576 | tf_op jit(solution)/shard_map/pallas_call | solution.py:327
  (8 shorter events, 0.0 us)
Async XLA Ops:
  1.9 8.1 %collective-permute-start.1 = (f32[12,8,128]{2,1,0:T(8,128)S(1)}, f32[12,8,128]{2,1,0:T(8,128)S(1)}, u32[]{:S(2)}, u32[]{:S(2)}) collective-permute-start(f32[12,8,128]{2,1,0:T(8,128)S(1)} %get-tuple-element.22.own_ref), channel_id=1, source_target_pairs={{0,128},{4,132},{8,136},{12,140},{16,144},{20,148},{24,152},{28,15... | collective-permute-start | bytes 147464 | tf_op jit(solution)/shard_map/ppermute | solution.py:233
  5.1 1.8 %copy-start.4 = (f32[2,16,1536]{2,1,0:T(8,128)S(1)}, f32[2,16,1536]{2,1,0:T(8,128)}, u32[]{:S(2)}) copy-start(f32[2,16,1536]{2,1,0:T(8,128)} %field_hbm.1) | copy-start | bytes 589828
  6.2 6.0 %collective-permute-start = (f32[12,8,128]{2,1,0:T(8,128)S(1)}, f32[12,8,128]{2,1,0:T(8,128)S(1)}, u32[]{:S(2)}, u32[]{:S(2)}) collective-permute-start(f32[12,8,128]{2,1,0:T(8,128)S(1)} %get-tuple-element.20.own_ref), channel_id=1, source_target_pairs={{0,128},{4,132},{8,136},{12,140},{16,144},{20,148},{24,152},{28,15... | collective-permute-start | bytes 147464 | tf_op jit(solution)/shard_map/ppermute | solution.py:233
  6.8 17.6 %collective-permute-start.12 = (f32[2,16,1536]{2,1,0:T(8,128)S(1)}, f32[2,16,1536]{2,1,0:T(8,128)S(1)}, u32[]{:S(2)}, u32[]{:S(2)}) collective-permute-start(f32[2,16,1536]{2,1,0:T(8,128)S(1)} %copy-done.4), channel_id=1, source_target_pairs={{0,2},{1,3},{2,0},{3,1},{4,6},{5,7},{6,4},{7,5},{8,10},{9,11},{10,... | collective-permute-start | bytes 589832 | tf_op jit(solution)/shard_map/ppermute | solution.py:233
  10.6 4.6 %collective-permute-start.3 = (f32[12,8,128]{2,1,0:T(8,128)S(1)}, f32[12,8,128]{2,1,0:T(8,128)S(1)}, u32[]{:S(2)}, u32[]{:S(2)}) collective-permute-start(f32[12,8,128]{2,1,0:T(8,128)S(1)} %shard_map.102.rest_0_.own_ref), channel_id=1, source_target_pairs={{0,64},{4,68},{8,72},{12,76},{16,80},{20,84},{24,88},{28,92},{32,9... | collective-permute-start | bytes 147464 | tf_op jit(solution)/shard_map/ppermute | solution.py:233
  12.8 4.3 %collective-permute-start.2 = (f32[12,8,128]{2,1,0:T(8,128)S(1)}, f32[12,8,128]{2,1,0:T(8,128)S(1)}, u32[]{:S(2)}, u32[]{:S(2)}) collective-permute-start(f32[12,8,128]{2,1,0:T(8,128)S(1)} %shard_map.103.refs_1_.own_ref), channel_id=1, source_target_pairs={{0,64},{4,68},{8,72},{12,76},{16,80},{20,84},{24,88},{28,92},{32,9... | collective-permute-start | bytes 147464 | tf_op jit(solution)/shard_map/ppermute | solution.py:233
  15.8 4.8 %collective-permute-start.5 = (f32[12,8,128]{2,1,0:T(8,128)S(1)}, f32[12,8,128]{2,1,0:T(8,128)S(1)}, u32[]{:S(2)}, u32[]{:S(2)}) collective-permute-start(f32[12,8,128]{2,1,0:T(8,128)S(1)} %shard_map.105.rest_1_.own_ref), channel_id=1, source_target_pairs={{0,32},{4,36},{8,40},{12,44},{16,48},{20,52},{24,56},{28,60},{32,0... | collective-permute-start | bytes 147464 | tf_op jit(solution)/shard_map/ppermute | solution.py:233
  17.7 4.2 %collective-permute-start.4 = (f32[12,8,128]{2,1,0:T(8,128)S(1)}, f32[12,8,128]{2,1,0:T(8,128)S(1)}, u32[]{:S(2)}, u32[]{:S(2)}) collective-permute-start(f32[12,8,128]{2,1,0:T(8,128)S(1)} %shard_map.106.refs_1_.own_ref), channel_id=1, source_target_pairs={{0,32},{4,36},{8,40},{12,44},{16,48},{20,52},{24,56},{28,60},{32,0... | collective-permute-start | bytes 147464 | tf_op jit(solution)/shard_map/ppermute | solution.py:233
  21.2 1.3 %collective-permute-start.7 = (f32[12,8,128]{2,1,0:T(8,128)S(1)}, f32[12,8,128]{2,1,0:T(8,128)S(1)}, u32[]{:S(2)}, u32[]{:S(2)}) collective-permute-start(f32[12,8,128]{2,1,0:T(8,128)S(1)} %shard_map.108.rest_1_.own_ref), channel_id=1, source_target_pairs={{0,1},{1,0},{2,3},{3,2},{4,5},{5,4},{6,7},{7,6},{8,9},{9,8},{10,11... | collective-permute-start | bytes 147464 | tf_op jit(solution)/shard_map/ppermute | solution.py:233
  22.5 1.3 %collective-permute-start.6 = (f32[12,8,128]{2,1,0:T(8,128)S(1)}, f32[12,8,128]{2,1,0:T(8,128)S(1)}, u32[]{:S(2)}, u32[]{:S(2)}) collective-permute-start(f32[12,8,128]{2,1,0:T(8,128)S(1)} %shard_map.109.own_ref), channel_id=1, source_target_pairs={{0,1},{1,0},{2,3},{3,2},{4,5},{5,4},{6,7},{7,6},{8,9},{9,8},{10,11... | collective-permute-start | bytes 147464 | tf_op jit(solution)/shard_map/ppermute | solution.py:233
  24.4 10.6 %collective-permute-start.13 = (f32[2,16,1536]{2,1,0:T(8,128)S(1)}, f32[2,16,1536]{2,1,0:T(8,128)S(1)}, u32[]{:S(2)}, u32[]{:S(2)}) collective-permute-start(f32[2,16,1536]{2,1,0:T(8,128)S(1)} %collective-permute-done.12.far_ref), channel_id=1, source_target_pairs={{0,1},{1,0},{2,3},{3,2},{4,5},{5,4},{6,7},{7,6},{8,9},{9,8},{10,11... | collective-permute-start | bytes 589832 | tf_op jit(solution)/shard_map/ppermute | solution.py:233
  24.6 10.4 %collective-permute-start.11 = (f32[2,16,1536]{2,1,0:T(8,128)S(1)}, f32[2,16,1536]{2,1,0:T(8,128)S(1)}, u32[]{:S(2)}, u32[]{:S(2)}) collective-permute-start(f32[2,16,1536]{2,1,0:T(8,128)S(1)} %copy-done.4), channel_id=1, source_target_pairs={{0,1},{1,0},{2,3},{3,2},{4,5},{5,4},{6,7},{7,6},{8,9},{9,8},{10,11... | collective-permute-start | bytes 589832 | tf_op jit(solution)/shard_map/ppermute | solution.py:233
  25.0 5.6 %collective-permute-start.9 = (f32[12,8,128]{2,1,0:T(8,128)S(1)}, f32[12,8,128]{2,1,0:T(8,128)S(1)}, u32[]{:S(2)}, u32[]{:S(2)}) collective-permute-start(f32[12,8,128]{2,1,0:T(8,128)S(1)} %shard_map.110.rest_0_.own_ref), channel_id=1, source_target_pairs={{0,2},{1,3},{2,0},{3,1},{4,6},{5,7},{6,4},{7,5},{8,10},{9,11},{10,... | collective-permute-start | bytes 147464 | tf_op jit(solution)/shard_map/ppermute | solution.py:233
  27.9 5.6 %collective-permute-start.8 = (f32[12,8,128]{2,1,0:T(8,128)S(1)}, f32[12,8,128]{2,1,0:T(8,128)S(1)}, u32[]{:S(2)}, u32[]{:S(2)}) collective-permute-start(f32[12,8,128]{2,1,0:T(8,128)S(1)} %shard_map.111.refs_2_.own_ref), channel_id=1, source_target_pairs={{0,2},{1,3},{2,0},{3,1},{4,6},{5,7},{6,4},{7,5},{8,10},{9,11},{10,... | collective-permute-start | bytes 147464 | tf_op jit(solution)/shard_map/ppermute | solution.py:233
  30.6 4.4 %copy-start = (s32[1,4,4]{2,1,0:T(4,128)S(1)}, s32[1,4,4]{2,1,0:T(4,128)}, u32[]{:S(2)}) copy-start(s32[1,4,4]{2,1,0:T(4,128)} %param.19) | copy-start | bytes 196
  30.7 4.4 %copy-start.1 = (s32[12,2]{0,1:T(2,128)S(1)}, s32[12,2]{0,1:T(2,128)}, u32[]{:S(2)}) copy-start(s32[12,2]{0,1:T(2,128)} %param.16) | copy-start | bytes 292
  30.7 4.4 %copy-start.2 = (s32[12,2]{0,1:T(2,128)S(1)}, s32[12,2]{0,1:T(2,128)}, u32[]{:S(2)}) copy-start(s32[12,2]{0,1:T(2,128)} %param.17) | copy-start | bytes 292
  30.7 4.4 %copy-start.3 = (s32[12,2]{0,1:T(2,128)S(1)}, s32[12,2]{0,1:T(2,128)}, u32[]{:S(2)}) copy-start(s32[12,2]{0,1:T(2,128)} %param.18) | copy-start | bytes 292
  31.3 4.8 %collective-permute-start.14 = (f32[12,8,128]{2,1,0:T(8,128)S(1)}, f32[12,8,128]{2,1,0:T(8,128)S(1)}, u32[]{:S(2)}, u32[]{:S(2)}) collective-permute-start(f32[12,8,128]{2,1,0:T(8,128)S(1)} %shard_map.113.rest_1_.own_ref), channel_id=1, source_target_pairs={{0,32},{4,36},{8,40},{12,44},{16,48},{20,52},{24,56},{28,60},{32,0... | collective-permute-start | bytes 147464 | tf_op jit(solution)/shard_map/ppermute | solution.py:233
  34.1 4.3 %collective-permute-start.10 = (f32[12,8,128]{2,1,0:T(8,128)S(1)}, f32[12,8,128]{2,1,0:T(8,128)S(1)}, u32[]{:S(2)}, u32[]{:S(2)}) collective-permute-start(f32[12,8,128]{2,1,0:T(8,128)S(1)} %shard_map.114.rest_0_.own_ref), channel_id=1, source_target_pairs={{0,32},{4,36},{8,40},{12,44},{16,48},{20,52},{24,56},{28,60},{32,0... | collective-permute-start | bytes 147464 | tf_op jit(solution)/shard_map/ppermute | solution.py:233
  36.7 4.9 %collective-permute-start.16 = (f32[12,8,128]{2,1,0:T(8,128)S(1)}, f32[12,8,128]{2,1,0:T(8,128)S(1)}, u32[]{:S(2)}, u32[]{:S(2)}) collective-permute-start(f32[12,8,128]{2,1,0:T(8,128)S(1)} %shard_map.116.rest_1_.own_ref), channel_id=1, source_target_pairs={{0,64},{4,68},{8,72},{12,76},{16,80},{20,84},{24,88},{28,92},{32,9... | collective-permute-start | bytes 147464 | tf_op jit(solution)/shard_map/ppermute | solution.py:233
  39.0 4.9 %collective-permute-start.15 = (f32[12,8,128]{2,1,0:T(8,128)S(1)}, f32[12,8,128]{2,1,0:T(8,128)S(1)}, u32[]{:S(2)}, u32[]{:S(2)}) collective-permute-start(f32[12,8,128]{2,1,0:T(8,128)S(1)} %shard_map.117.rest_0_.own_ref), channel_id=1, source_target_pairs={{0,64},{4,68},{8,72},{12,76},{16,80},{20,84},{24,88},{28,92},{32,9... | collective-permute-start | bytes 147464 | tf_op jit(solution)/shard_map/ppermute | solution.py:233
  42.2 5.7 %collective-permute-start.18 = (f32[12,8,128]{2,1,0:T(8,128)S(1)}, f32[12,8,128]{2,1,0:T(8,128)S(1)}, u32[]{:S(2)}, u32[]{:S(2)}) collective-permute-start(f32[12,8,128]{2,1,0:T(8,128)S(1)} %shard_map.119.rest_1_.own_ref), channel_id=1, source_target_pairs={{0,128},{4,132},{8,136},{12,140},{16,144},{20,148},{24,152},{28,15... | collective-permute-start | bytes 147464 | tf_op jit(solution)/shard_map/ppermute | solution.py:233
  44.5 5.7 %collective-permute-start.17 = (f32[12,8,128]{2,1,0:T(8,128)S(1)}, f32[12,8,128]{2,1,0:T(8,128)S(1)}, u32[]{:S(2)}, u32[]{:S(2)}) collective-permute-start(f32[12,8,128]{2,1,0:T(8,128)S(1)} %shard_map.120.rest_0_.own_ref), channel_id=1, source_target_pairs={{0,128},{4,132},{8,136},{12,140},{16,144},{20,148},{24,152},{28,15... | collective-permute-start | bytes 147464 | tf_op jit(solution)/shard_map/ppermute | solution.py:233

commit v4 on v2

--- a/solution.py
+++ b/solution.py
@@ -6,6 +6,7 @@
 from jax.experimental import pallas as pl
 from jax.experimental.pallas import tpu as pltpu
 from jax.sharding import PartitionSpec as P
+
 
 VMEM = pltpu.VMEM
 SMEM = pltpu.SMEM
@@ -16,8 +17,8 @@
 F32 = jnp.float32
 NT = (((1,), (1,)), ((), ()))
 NN = (((1,), (0,)), ((), ()))
-NEAR_EACH = 3
-NEAR_AT = {4: 1, 5: 1, 6: 1, 7: 1}
+NEAR_EACH = 4
+NEAR_AT = {5: 1, 6: 2}
 
 
 def split(value):
@@ -77,25 +78,30 @@
     return jnp.concatenate([real, imag], axis=0)
 
 
-def level_block(level, k, row, own_ref, other_ref, weight_ref):
+def level_block(k, row, own_ref, other_ref, weight_ref):
     rows = stacked_rows(own_ref[k], other_ref[row[0, k]])
-    return joined(product(rows, weight_ref[level, k].reshape(128, 128), NT))
-
-
-def level_kernel(level, roster_ref, own_ref, other_ref, weight_ref, *rest):
+    return joined(product(rows, weight_ref[k].reshape(128, 128), NT))
+
+
+def level_kernel(level, at, roster_ref, own_ref, other_ref, weight_ref, *rest):
     out_ref = rest[-1]
     row = roster_ref[level]
     for k in range(out_ref.shape[0]):
-        out_ref[k] = level_block(level, k, row, own_ref, other_ref, weight_ref)
-
-
-def last_kernel(level, roster_ref, own_ref, other_ref, weight_ref, expand_ref, *rest):
-    near_refs, (out_hbm, state_ref, out_ref, sems) = rest[:-4], rest[-4:]
-    row = roster_ref[level]
+        out_ref[k] = level_block(k, row, own_ref, other_ref, weight_ref.at[at])
+
+
+def last_kernel(
+    level, roster_ref, away_roster_ref, own_ref, cross_ref, corner_ref, away_ref, weight_ref, expand_ref, *rest
+):
+    near_refs, (out_hbm, there_ref, state_ref, out_ref, sems) = rest[:-5], rest[-5:]
     blocks = own_ref.shape[0]
     each = near_refs[0].shape[0]
+    row = away_roster_ref[level - 1]
     for k in range(blocks):
-        state_ref[k] = level_block(level, k, row, own_ref, other_ref, weight_ref)
+        there_ref[k] = level_block(k, row, cross_ref, corner_ref, away_ref.at[0])
+    row = roster_ref[level]
+    for k in range(blocks):
+        state_ref[k] = level_block(k, row, own_ref, there_ref, weight_ref.at[0])
     copies = []
     for k in range(blocks):
         coeffs = state_ref[k]
@@ -142,10 +148,13 @@
         out_ref[n] = total
 
 
-def fetch_kernel(*refs):
-    count = (len(refs) - 2) // 2
+def fetch_kernel(parts, *refs):
+    count = len(parts)
     sources, outs, sem = refs[:count], refs[count + 1 : -1], refs[-1]
-    copies = [pltpu.make_async_copy(s, o, sem.at[n]) for n, (s, o) in enumerate(zip(sources, outs))]
+    copies = []
+    for n, (part, source, out) in enumerate(zip(parts, sources, outs)):
+        source = source if part is None else source.at[pl.ds(*part)]
+        copies.append(pltpu.make_async_copy(source, out, sem.at[n]))
     for copy in copies:
         copy.start()
     for copy in copies:
@@ -156,7 +165,7 @@
     return pl.BlockSpec(memory_space=space)
 
 
-def call(kernel, out, spaces, name, out_spaces=VMEM, scratch=(), flops=2_000_000):
+def call(kernel, out, spaces, out_spaces=VMEM, scratch=(), flops=2_000_000):
     single = not isinstance(out_spaces, (list, tuple))
     return pl.pallas_call(
         kernel,
@@ -166,19 +175,22 @@
         scratch_shapes=list(scratch),
         compiler_params=pltpu.CompilerParams(vmem_limit_bytes=8 << 20),
         cost_estimate=pl.CostEstimate(flops=flops, bytes_accessed=1 << 20, transcendentals=0),
-        name=name,
     )
 
 
-def fetch(arrays, after, name):
+def in_hbm(*arrays):
+    return [pltpu.with_memory_space_constraint(array, HBM) for array in arrays]
+
+
+def fetch(arrays, parts, after):
+    shapes = [a.shape if p is None else (p[1],) + a.shape[1:] for a, p in zip(arrays, parts)]
     return call(
-        fetch_kernel,
-        [VMEM(a.shape, a.dtype) for a in arrays],
+        functools.partial(fetch_kernel, parts),
+        [VMEM(shape, a.dtype) for shape, a in zip(shapes, arrays)],
         [HBM] * len(arrays) + [ANY],
-        name,
         [VMEM] * len(arrays),
         [DMA((len(arrays),))],
-    )(*[pltpu.with_memory_space_constraint(a, HBM) for a in arrays], after)
+    )(*in_hbm(*arrays), after)
 
 
 def flipped(value, axis, mask):
@@ -221,51 +233,62 @@
     state = VMEM((blocks, rhs, 128), F32)
 
     coeffs = call(
-        compress_kernel,
-        state,
-        [HBM, HBM],
-        "compress",
-        scratch=[VMEM(field_in.shape, F32), VMEM(compress.shape, F32), DMA((4,))],
-    )(pltpu.with_memory_space_constraint(field_in, HBM), pltpu.with_memory_space_constraint(compress, HBM))
+        compress_kernel, state, [HBM, HBM], scratch=[VMEM(field_in.shape, F32), VMEM(compress.shape, F32), DMA((4,))]
+    )(*in_hbm(field_in, compress))
     pieces = []
-    for position, (axis, mask) in enumerate(plan):
+
+    def near_piece(field, core, far, both, dense, after):
+        number = len(pieces)
+        pieces.append(
+            call(
+                functools.partial(near_kernel, NEAR_EACH * number),
+                VMEM((NEAR_EACH, 2 * rhs, 128), F32),
+                [SMEM] * 4 + [VMEM] * 5 + [ANY],
+            )(*indices, field, core, far, both, dense, after)
+        )
+        return pieces[-1]
+
+    def level_of(position, own, other, extra):
+        weight, at = weights[position]
+        return call(
+            functools.partial(level_kernel, position, at), state, [VMEM] * 4 + [ANY] * len(extra)
+        )(names, own, other, weight, *extra)
+
+    for position, (axis, mask) in enumerate(plan[:-2]):
         other = flipped(coeffs, axis, mask)
         extra = []
         if position == 0:
             far = flipped(tied(field_in, coeffs), "sub", 2)
-            core = flipped(tied(field_in, coeffs), "sub", 1)
-            weights, names = fetch([coupling, roster], coeffs, "fetch_coupling")
+            early, names = fetch([coupling, roster], [(0, 4), None], coeffs)
+            weights = {level: (early, level) for level in range(4)}
         if position == 1:
-            dense, last, field = fetch([nearfield_dense_blocks, expand, field_in], coeffs, "fetch_near")
+            dense, last, field = fetch([nearfield_dense_blocks, expand, field_in], [None, None, None], coeffs)
             extra.append(field)
         if position == 2:
+            middle, sixth, seventh = fetch([coupling] * 3, [(4, 2), (6, 1), (7, 1)], coeffs)
+            weights |= {4: (middle, 0), 5: (middle, 1), 6: (sixth, 0), 7: (seventh, 0)}
+            extra.append(seventh)
+            away = flipped(tied(sixth, coeffs), "leaf", top)
+        if position == 4:
+            away_names = flipped(tied(names, coeffs), "leaf", top)
+            core = flipped(tied(field_in, coeffs), "sub", 1)
             both = flipped(tied(far, coeffs), "sub", 1)
         for _ in range(NEAR_AT.get(position, 0)):
-            piece = call(
-                functools.partial(near_kernel, NEAR_EACH * len(pieces)),
-                VMEM((NEAR_EACH, 2 * rhs, 128), F32),
-                [SMEM] * 4 + [VMEM] * 5 + [ANY],
-                "near",
-            )(*indices, field, core, far, both, dense, coeffs)
-            pieces.append(piece)
-            extra.append(piece)
-        if position < len(plan) - 1:
-            coeffs = call(
-                functools.partial(level_kernel, position),
-                state,
-                [VMEM] * 4 + [ANY] * len(extra),
-                "level",
-            )(names, coeffs, other, weights, *extra)
-        else:
-            total = call(
-                functools.partial(last_kernel, position),
-                jax.ShapeDtypeStruct(field_in.shape, F32),
-                [VMEM] * (5 + len(pieces)),
-                "last",
-                HBM,
-                [VMEM((blocks, rhs, 128), F32), VMEM(field_in.shape, F32), DMA((3,))],
-            )(names, coeffs, other, weights, last, *pieces)
-    return total
+            extra.append(near_piece(field, core, far, both, dense, coeffs))
+        coeffs = level_of(position, coeffs, other, extra)
+    side = flipped(coeffs, "leaf", top // 2)
+    corner = flipped(coeffs, "leaf", top // 2 + top)
+    cross = flipped(coeffs, "leaf", top)
+    for _ in range(NEAR_AT[6]):
+        near_piece(field, core, far, both, dense, coeffs)
+    own = level_of(6, coeffs, side, [pieces[-1]])
+    return call(
+        functools.partial(last_kernel, 7),
+        jax.ShapeDtypeStruct(field_in.shape, F32),
+        [VMEM] * (8 + len(pieces)),
+        HBM,
+        [state, state, VMEM(field_in.shape, F32), DMA((3,))],
+    )(names, away_names, own, cross, corner, away, weights[7][0], last, *pieces)
 
 
 def solution(mesh):

time: 50 us -> 52.5 us (1.050)
  starting transfers between devices: 11 us -> 21.2 us
  waiting for transfers between devices: 22 us -> 13.4 us
  Pallas kernels: 16.5 us -> 17.4 us
    ppermute x11 -> x14, starting transfers between devices: 11 us -> 21.2 us  [flipped(): return lax.ppermute(value, axis, pairs)]
    ppermute x11 -> x14, waiting for transfers between devices: 22 us -> 13.4 us  [flipped(): return lax.ppermute(value, axis, pairs)]
    pallas_call x15, Pallas kernels: 16.5 us -> 17.4 us  [the longest x3 5.96 us: fetch(): call(functools.partial(fetch_kernel, parts), [VMEM(shape, a.dtype) for sh...]
  transfers between devices with their start and end apart: 11 -> 14, of which waited for: 7 -> 8; matrix products, arithmetic and copies ran while one was open for 0% -> 0% of each run, Pallas kernels for 22% -> 20%
where the time goes in v4:
time: 52.5 us; the launch traced here: 52.4 us
  starting transfers between devices  21.2 us (40%)
  Pallas kernels  17.4 us (33%)
  waiting for transfers between devices  13.4 us (26%)
    ppermute x14, starting transfers between devices, flipped(): return lax.ppermute(value, axis, pairs)  21.2 us
    ppermute x14, waiting for transfers between devices, flipped(): return lax.ppermute(value, axis, pairs)  13.4 us
    pallas_call x3, Pallas kernels, fetch(): call(functools.partial(fetch_kernel, parts), [VMEM(shape, a.dtype) for sh...  5.96 us
    pallas_call x7, Pallas kernels, level_of(): call(functools.partial(level_kernel, position, at), state, [VMEM] * 4 + [...  4.41 us
    pallas_call x3, Pallas kernels, near_piece(): call(functools.partial(near_kernel, NEAR_EACH * number), VMEM((NEAR_EACH,...  3.03 us
    pallas_call x1, Pallas kernels, on_device(): call(functools.partial(last_kernel, 7), jax.ShapeDtypeStruct(field_in.sha...  2.08 us
    pallas_call x1, Pallas kernels, on_device(): call(compress_kernel, state, [HBM, HBM], scratch=[VMEM(field_in.shape, F3...  1.95 us
  transfers between devices with their start and end apart: 14, of which 8 were waited for; matrix products, arithmetic and copies ran while one was open for 0% of the time, Pallas kernels for 20%

profile of v4, /device:TPU:64, one launch (start us, length us, event | category | flops | bytes accessed | tf_op | source)
XLA Modules:
  0.0 52.4 jit_solution(14987843399883031591)
XLA Ops:
  0.0 1.9 %shard_map.100.refs_2_.own_ref = f32[12,16,128]{2,1,0:T(8,128)S(1)} custom-call(f32[2,16,1536]{2,1,0:T(8,128)} %refs_2_.2, f32[12,2,64,128]{3,2,1,0:T(8,128)} %weight_hbm.1), custom_call_target="tpu_custom_call" | custom-call | flops 2000000 | bytes 1048576 | tf_op jit(solution)/shard_map/pallas_call | solution.py:235
  2.0 3.1 %collective-permute-start = (f32[12,16,128]{2,1,0:T(8,128)S(1)}, f32[12,16,128]{2,1,0:T(8,128)S(1)}, u32[]{:S(2)}, u32[]{:S(2)}) collective-permute-start(f32[12,16,128]{2,1,0:T(8,128)S(1)} %shard_map.100.refs_2_.own_ref), channel_id=1, source_target_pairs={{0,128},{4,132},{8,136},{12,140},{16,144},{20,148},{24,152},{28,15... | collective-permute-start | bytes 294920 | tf_op jit(solution)/shard_map/ppermute | solution.py:198
  5.1 1.9 %shard_map.101 = (f32[4,12,2,64,128]{4,3,2,1,0:T(8,128)S(1)}, s32[8,1,12]{2,1,0:T(1,128)S(1)}) custom-call(f32[8,12,2,64,128]{4,3,2,1,0:T(8,128)} %refs_2_.3, s32[8,1,12]{2,1,0:T(1,128)} %refs_1_.3, f32[12,16,128]{2,1,0:T(8,128)S(1)} %shard_map.100.refs_2_.own_ref), custom_call_target="tpu_custom_call" | custom-call | flops 2000000 | bytes 1048576 | tf_op jit(solution)/shard_map/pallas_call | solution.py:187
  7.0 1.2 %collective-permute-done.other_ref = f32[12,16,128]{2,1,0:T(8,128)S(1)} collective-permute-done((f32[12,16,128]{2,1,0:T(8,128)S(1)}, f32[12,16,128]{2,1,0:T(8,128)S(1)}, u32[]{:S(2)}, u32[]{:S(2)}) %collective-permute-start) | collective-permute-done | bytes 98336 | tf_op jit(solution)/shard_map/ppermute | solution.py:198
  8.2 0.6 %shard_map.102.refs_3_.own_ref = f32[12,16,128]{2,1,0:T(8,128)S(1)} custom-call(s32[8,1,12]{2,1,0:T(1,128)S(1)} %get-tuple-element.22.roster_ref, f32[12,16,128]{2,1,0:T(8,128)S(1)} %shard_map.100.refs_2_.own_ref, f32[12,16,128]{2,1,0:T(8,128)S(1)} %collective-permute-done.other_ref, f32[4,12,2,64,128]{4,3,2,1,0:T(8,128)S(1)} %get-tuple-element.19.weight_ref), custom_call_target="tpu_custom_call" | custom-call | flops 2000000 | bytes 1048576 | tf_op jit(solution)/shard_map/pallas_call | solution.py:253
  8.8 1.6 %collective-permute-start.1 = (f32[12,16,128]{2,1,0:T(8,128)S(1)}, f32[12,16,128]{2,1,0:T(8,128)S(1)}, u32[]{:S(2)}, u32[]{:S(2)}) collective-permute-start(f32[12,16,128]{2,1,0:T(8,128)S(1)} %shard_map.102.refs_3_.own_ref), channel_id=1, source_target_pairs={{0,64},{4,68},{8,72},{12,76},{16,80},{20,84},{24,88},{28,92},{32,9... | collective-permute-start | bytes 294920 | tf_op jit(solution)/shard_map/ppermute | solution.py:198
  10.4 2.1 %shard_map.103 = (f32[12,2,2,128,128]{4,3,2,1,0:T(8,128)S(1)}, f32[12,2,64,128]{3,2,1,0:T(8,128)S(1)}, f32[2,16,1536]{2,1,0:T(8,128)S(1)}) custom-call(f32[12,2,2,128,128]{4,3,2,1,0:T(8,128)} %refs_0_.4, f32[12,2,64,128]{3,2,1,0:T(8,128)} %refs_1_.4, f32[2,16,1536]{2,1,0:T(8,128)} %refs_2_.2, f32[12,16,128]{2,1,0:T(8,128)S(1)} %shard_map.102.refs_3_.own_ref), custom_call_target="tpu_custom_call" | custom-call | flops 2000000 | bytes 1048576 | tf_op jit(solution)/shard_map/pallas_call | solution.py:187
  12.5 1.0 %collective-permute-done.1.other_ref = f32[12,16,128]{2,1,0:T(8,128)S(1)} collective-permute-done((f32[12,16,128]{2,1,0:T(8,128)S(1)}, f32[12,16,128]{2,1,0:T(8,128)S(1)}, u32[]{:S(2)}, u32[]{:S(2)}) %collective-permute-start.1) | collective-permute-done | bytes 98336 | tf_op jit(solution)/shard_map/ppermute | solution.py:198
  13.5 0.6 %shard_map.104.refs_3_.own_ref = f32[12,16,128]{2,1,0:T(8,128)S(1)} custom-call(s32[8,1,12]{2,1,0:T(1,128)S(1)} %get-tuple-element.22.roster_ref, f32[12,16,128]{2,1,0:T(8,128)S(1)} %shard_map.102.refs_3_.own_ref, f32[12,16,128]{2,1,0:T(8,128)S(1)} %collective-permute-done.1.other_ref, f32[4,12,2,64,128]{4,3,2,1,0:T(8,128)S(1)} %get-tuple-element.19.weight_ref, ...), custom_call_target="tpu_custom_call" | custom-call | flops 2000000 | bytes 1048576 | tf_op jit(solution)/shard_map/pallas_call | solution.py:253
  14.1 0.0 copy-start.4
  14.1 1.9 %shard_map.105 = (f32[2,12,2,64,128]{4,3,2,1,0:T(8,128)S(1)}, f32[1,12,2,64,128]{4,3,2,1,0:T(8,128)S(1)}, f32[1,12,2,64,128]{4,3,2,1,0:T(8,128)S(1)}) custom-call(f32[8,12,2,64,128]{4,3,2,1,0:T(8,128)} %refs_2_.3, f32[8,12,2,64,128]{4,3,2,1,0:T(8,128)} %refs_2_.3, f32[8,12,2,64,128]{4,3,2,1,0:T(8,128)} %refs_2_.3, f32[12,16,128]{2,1,0:T(8,128)S(1)} %shard_map.104.refs_3_.own_ref), custom_call_target="tpu_custom_call" | custom-call | flops 2000000 | bytes 1048576 | tf_op jit(solution)/shard_map/pallas_call | solution.py:187
  16.0 3.1 %collective-permute-start.13 = (f32[1,12,2,64,128]{4,3,2,1,0:T(8,128)S(1)}, f32[1,12,2,64,128]{4,3,2,1,0:T(8,128)S(1)}, u32[]{:S(2)}, u32[]{:S(2)}) collective-permute-start(f32[1,12,2,64,128]{4,3,2,1,0:T(8,128)S(1)} %get-tuple-element.29.weight_ref), channel_id=1, source_target_pairs={{0,128},{4,132},{8,136},{12,140},{16,144},{20,148},{24,152},{28,15... | collective-permute-start | bytes 2359304 | tf_op jit(solution)/shard_map/ppermute | solution.py:198
  19.2 1.6 %collective-permute-start.2 = (f32[12,16,128]{2,1,0:T(8,128)S(1)}, f32[12,16,128]{2,1,0:T(8,128)S(1)}, u32[]{:S(2)}, u32[]{:S(2)}) collective-permute-start(f32[12,16,128]{2,1,0:T(8,128)S(1)} %shard_map.104.refs_3_.own_ref), channel_id=1, source_target_pairs={{0,32},{4,36},{8,40},{12,44},{16,48},{20,52},{24,56},{28,60},{32,0... | collective-permute-start | bytes 294920 | tf_op jit(solution)/shard_map/ppermute | solution.py:198
  20.7 0.0 copy-done.4
  20.7 2.9 %collective-permute-start.8 = (f32[2,16,1536]{2,1,0:T(8,128)S(1)}, f32[2,16,1536]{2,1,0:T(8,128)S(1)}, u32[]{:S(2)}, u32[]{:S(2)}) collective-permute-start(f32[2,16,1536]{2,1,0:T(8,128)S(1)} %copy-done.4), channel_id=1, source_target_pairs={{0,2},{1,3},{2,0},{3,1},{4,6},{5,7},{6,4},{7,5},{8,10},{9,11},{10,... | collective-permute-start | bytes 589832 | tf_op jit(solution)/shard_map/ppermute | solution.py:198
  23.6 0.8 %collective-permute-done.2.other_ref = f32[12,16,128]{2,1,0:T(8,128)S(1)} collective-permute-done((f32[12,16,128]{2,1,0:T(8,128)S(1)}, f32[12,16,128]{2,1,0:T(8,128)S(1)}, u32[]{:S(2)}, u32[]{:S(2)}) %collective-permute-start.2) | collective-permute-done | bytes 98336 | tf_op jit(solution)/shard_map/ppermute | solution.py:198
  24.5 0.6 %shard_map.106.own_ref = f32[12,16,128]{2,1,0:T(8,128)S(1)} custom-call(s32[8,1,12]{2,1,0:T(1,128)S(1)} %get-tuple-element.22.roster_ref, f32[12,16,128]{2,1,0:T(8,128)S(1)} %shard_map.104.refs_3_.own_ref, f32[12,16,128]{2,1,0:T(8,128)S(1)} %collective-permute-done.2.other_ref, f32[4,12,2,64,128]{4,3,2,1,0:T(8,128)S(1)} %get-tuple-element.19.weight_ref, ...), custom_call_target="tpu_custom_call" | custom-call | flops 2000000 | bytes 1048576 | tf_op jit(solution)/shard_map/pallas_call | solution.py:253
  25.1 0.0 copy-start
  25.1 0.0 copy-start.1
  25.1 0.0 copy-start.2
  25.1 0.0 copy-start.3
  25.1 0.1 collective-permute-start.3
  25.2 1.3 %collective-permute-done.3.other_ref = f32[12,16,128]{2,1,0:T(8,128)S(1)} collective-permute-done((f32[12,16,128]{2,1,0:T(8,128)S(1)}, f32[12,16,128]{2,1,0:T(8,128)S(1)}, u32[]{:S(2)}, u32[]{:S(2)}) %collective-permute-start.3) | collective-permute-done | bytes 98336 | tf_op jit(solution)/shard_map/ppermute | solution.py:198
  26.5 0.6 %shard_map.107.own_ref = f32[12,16,128]{2,1,0:T(8,128)S(1)} custom-call(s32[8,1,12]{2,1,0:T(1,128)S(1)} %get-tuple-element.22.roster_ref, f32[12,16,128]{2,1,0:T(8,128)S(1)} %shard_map.106.own_ref, f32[12,16,128]{2,1,0:T(8,128)S(1)} %collective-permute-done.3.other_ref, f32[4,12,2,64,128]{4,3,2,1,0:T(8,128)S(1)} %get-tuple-element.19.weight_ref), custom_call_target="tpu_custom_call" | custom-call | flops 2000000 | bytes 1048576 | tf_op jit(solution)/shard_map/pallas_call | solution.py:253
  27.2 1.2 %collective-permute-done.8.far_ref = f32[2,16,1536]{2,1,0:T(8,128)S(1)} collective-permute-done((f32[2,16,1536]{2,1,0:T(8,128)S(1)}, f32[2,16,1536]{2,1,0:T(8,128)S(1)}, u32[]{:S(2)}, u32[]{:S(2)}) %collective-permute-start.8) | collective-permute-done | bytes 196640 | tf_op jit(solution)/shard_map/ppermute | solution.py:198
  28.3 0.0 collective-permute-start.7
  28.3 0.5 collective-permute-start.9
  28.8 2.5 %collective-permute-start.5 = (f32[12,16,128]{2,1,0:T(8,128)S(1)}, f32[12,16,128]{2,1,0:T(8,128)S(1)}, u32[]{:S(2)}, u32[]{:S(2)}) collective-permute-start(f32[12,16,128]{2,1,0:T(8,128)S(1)} %shard_map.107.own_ref), channel_id=1, source_target_pairs={{0,2},{1,3},{2,0},{3,1},{4,6},{5,7},{6,4},{7,5},{8,10},{9,11},{10,... | collective-permute-start | bytes 294920 | tf_op jit(solution)/shard_map/ppermute | solution.py:198
  31.3 3.7 %collective-permute-done.5.other_ref = f32[12,16,128]{2,1,0:T(8,128)S(1)} collective-permute-done((f32[12,16,128]{2,1,0:T(8,128)S(1)}, f32[12,16,128]{2,1,0:T(8,128)S(1)}, u32[]{:S(2)}, u32[]{:S(2)}) %collective-permute-start.5) | collective-permute-done | bytes 98336 | tf_op jit(solution)/shard_map/ppermute | solution.py:198
  35.0 0.6 %shard_map.108.rest_0_.own_ref = f32[12,16,128]{2,1,0:T(8,128)S(1)} custom-call(s32[8,1,12]{2,1,0:T(1,128)S(1)} %get-tuple-element.22.roster_ref, f32[12,16,128]{2,1,0:T(8,128)S(1)} %shard_map.107.own_ref, f32[12,16,128]{2,1,0:T(8,128)S(1)} %collective-permute-done.5.other_ref, f32[2,12,2,64,128]{4,3,2,1,0:T(8,128)S(1)} %get-tuple-element.23.weight_ref), custom_call_target="tpu_custom_call" | custom-call | flops 2000000 | bytes 1048576 | tf_op jit(solution)/shard_map/pallas_call | solution.py:253
  35.7 1.0 %collective-permute-start.6 = (f32[12,16,128]{2,1,0:T(8,128)S(1)}, f32[12,16,128]{2,1,0:T(8,128)S(1)}, u32[]{:S(2)}, u32[]{:S(2)}) collective-permute-start(f32[12,16,128]{2,1,0:T(8,128)S(1)} %shard_map.108.rest_0_.own_ref), channel_id=1, source_target_pairs={{0,32},{4,36},{8,40},{12,44},{16,48},{20,52},{24,56},{28,60},{32,0... | collective-permute-start | bytes 294920 | tf_op jit(solution)/shard_map/ppermute | solution.py:198
  36.7 0.0 collective-permute-done.7.core_ref
  36.7 0.0 collective-permute-done.9.both_ref
  36.7 0.0 copy-done
  36.7 0.0 copy-done.1
  36.7 0.0 copy-done.2
  36.8 0.0 copy-done.3
  36.8 1.0 %shard_map.109.rest_0_ = f32[4,32,128]{2,1,0:T(8,128)S(1)} custom-call(s32[2,12]{1,0:T(2,128)S(1)} %bitcast.7, s32[2,12]{1,0:T(2,128)S(1)} %bitcast.10, s32[2,12]{1,0:T(2,128)S(1)} %bitcast.13, s32[4,4]{1,0:T(4,128)S(1)} %bitcast.4, f32[2,16,1536]{2,1,0:T(8,128)S(1)} %get-tuple-element.20.rest_0_.own_ref, ...), custom_call_target="tpu_custom_call" | custom-call | flops 2000000 | bytes 1048576 | tf_op jit(solution)/shard_map/pallas_call | solution.py:243
  37.8 2.6 %collective-permute-done.6.other_ref = f32[12,16,128]{2,1,0:T(8,128)S(1)} collective-permute-done((f32[12,16,128]{2,1,0:T(8,128)S(1)}, f32[12,16,128]{2,1,0:T(8,128)S(1)}, u32[]{:S(2)}, u32[]{:S(2)}) %collective-permute-start.6) | collective-permute-done | bytes 98336 | tf_op jit(solution)/shard_map/ppermute | solution.py:198
  40.4 0.6 %shard_map.110.rest_0_.own_ref = f32[12,16,128]{2,1,0:T(8,128)S(1)} custom-call(s32[8,1,12]{2,1,0:T(1,128)S(1)} %get-tuple-element.22.roster_ref, f32[12,16,128]{2,1,0:T(8,128)S(1)} %shard_map.108.rest_0_.own_ref, f32[12,16,128]{2,1,0:T(8,128)S(1)} %collective-permute-done.6.other_ref, f32[2,12,2,64,128]{4,3,2,1,0:T(8,128)S(1)} %get-tuple-element.23.weight_ref, ...), custom_call_target="tpu_custom_call" | custom-call | flops 2000000 | bytes 1048576 | tf_op jit(solution)/shard_map/pallas_call | solution.py:253
  41.0 0.7 %collective-permute-start.10 = (f32[12,16,128]{2,1,0:T(8,128)S(1)}, f32[12,16,128]{2,1,0:T(8,128)S(1)}, u32[]{:S(2)}, u32[]{:S(2)}) collective-permute-start(f32[12,16,128]{2,1,0:T(8,128)S(1)} %shard_map.110.rest_0_.own_ref), channel_id=1, source_target_pairs={{0,64},{4,68},{8,72},{12,76},{16,80},{20,84},{24,88},{28,92},{32,9... | collective-permute-start | bytes 294920 | tf_op jit(solution)/shard_map/ppermute | solution.py:198
  41.7 0.7 %collective-permute-start.12 = (f32[12,16,128]{2,1,0:T(8,128)S(1)}, f32[12,16,128]{2,1,0:T(8,128)S(1)}, u32[]{:S(2)}, u32[]{:S(2)}) collective-permute-start(f32[12,16,128]{2,1,0:T(8,128)S(1)} %shard_map.110.rest_0_.own_ref), channel_id=1, source_target_pairs={{0,192},{4,196},{8,200},{12,204},{16,208},{20,212},{24,216},{28,22... | collective-permute-start | bytes 294920 | tf_op jit(solution)/shard_map/ppermute | solution.py:198
  42.3 2.9 %collective-permute-start.11 = (f32[12,16,128]{2,1,0:T(8,128)S(1)}, f32[12,16,128]{2,1,0:T(8,128)S(1)}, u32[]{:S(2)}, u32[]{:S(2)}) collective-permute-start(f32[12,16,128]{2,1,0:T(8,128)S(1)} %shard_map.110.rest_0_.own_ref), channel_id=1, source_target_pairs={{0,128},{4,132},{8,136},{12,140},{16,144},{20,148},{24,152},{28,15... | collective-permute-start | bytes 294920 | tf_op jit(solution)/shard_map/ppermute | solution.py:198
  45.2 0.7 %collective-permute-start.4 = (s32[8,1,12]{2,1,0:T(1,128)S(1)}, s32[8,1,12]{2,1,0:T(1,128)S(1)}, u32[]{:S(2)}, u32[]{:S(2)}) collective-permute-start(s32[8,1,12]{2,1,0:T(1,128)S(1)} %get-tuple-element.22.roster_ref), channel_id=1, source_target_pairs={{0,128},{4,132},{8,136},{12,140},{16,144},{20,148},{24,152},{28,15... | collective-permute-start | bytes 1160 | tf_op jit(solution)/shard_map/ppermute | solution.py:198
  45.9 1.0 %shard_map.111.rest_0_.rest_2_ = f32[4,32,128]{2,1,0:T(8,128)S(1)} custom-call(s32[2,12]{1,0:T(2,128)S(1)} %bitcast.8, s32[2,12]{1,0:T(2,128)S(1)} %bitcast.11, s32[2,12]{1,0:T(2,128)S(1)} %bitcast.14, s32[4,4]{1,0:T(4,128)S(1)} %bitcast.5, f32[2,16,1536]{2,1,0:T(8,128)S(1)} %get-tuple-element.20.rest_0_.own_ref, ...), custom_call_target="tpu_custom_call" | custom-call | flops 2000000 | bytes 1048576 | tf_op jit(solution)/shard_map/pallas_call | solution.py:243
  46.9 1.0 %shard_map.113.rest_1_ = f32[4,32,128]{2,1,0:T(8,128)S(1)} custom-call(s32[2,12]{1,0:T(2,128)S(1)} %bitcast.9, s32[2,12]{1,0:T(2,128)S(1)} %bitcast.12, s32[2,12]{1,0:T(2,128)S(1)} %bitcast.15, s32[4,4]{1,0:T(4,128)S(1)} %bitcast.6, f32[2,16,1536]{2,1,0:T(8,128)S(1)} %get-tuple-element.20.rest_0_.own_ref, ...), custom_call_target="tpu_custom_call" | custom-call | flops 2000000 | bytes 1048576 | tf_op jit(solution)/shard_map/pallas_call | solution.py:243
  48.0 0.0 collective-permute-done.10.other_ref
  48.0 0.6 %shard_map.112.own_ref = f32[12,16,128]{2,1,0:T(8,128)S(1)} custom-call(s32[8,1,12]{2,1,0:T(1,128)S(1)} %get-tuple-element.22.roster_ref, f32[12,16,128]{2,1,0:T(8,128)S(1)} %shard_map.110.rest_0_.own_ref, f32[12,16,128]{2,1,0:T(8,128)S(1)} %collective-permute-done.10.other_ref, f32[1,12,2,64,128]{4,3,2,1,0:T(8,128)S(1)} %get-tuple-element.29.weight_ref, ...), custom_call_target="tpu_custom_call" | custom-call | flops 2000000 | bytes 1048576 | tf_op jit(solution)/shard_map/pallas_call | solution.py:253
  48.6 1.7 %collective-permute-done.4.away_roster_ref = s32[8,1,12]{2,1,0:T(1,128)S(1)} collective-permute-done((s32[8,1,12]{2,1,0:T(1,128)S(1)}, s32[8,1,12]{2,1,0:T(1,128)S(1)}, u32[]{:S(2)}, u32[]{:S(2)}) %collective-permute-start.4) | collective-permute-done | bytes 416 | tf_op jit(solution)/shard_map/ppermute | solution.py:198
  50.3 0.0 collective-permute-done.12.corner_ref
  50.3 0.0 collective-permute-done.11.cross_ref
  50.3 0.0 collective-permute-done.13.away_ref
  50.3 2.1 %shard_map.114 = f32[2,16,1536]{2,1,0:T(8,128)} custom-call(s32[8,1,12]{2,1,0:T(1,128)S(1)} %get-tuple-element.22.roster_ref, s32[8,1,12]{2,1,0:T(1,128)S(1)} %collective-permute-done.4.away_roster_ref, f32[12,16,128]{2,1,0:T(8,128)S(1)} %shard_map.112.own_ref, f32[12,16,128]{2,1,0:T(8,128)S(1)} %collective-permute-done.11.cross_ref, ...), custom_call_target="tpu_custom_call" | custom-call | flops 2000000 | bytes 1048576 | tf_op jit(solution)/shard_map/pallas_call | solution.py:285
Async XLA Ops:
  2.0 6.2 %collective-permute-start = (f32[12,16,128]{2,1,0:T(8,128)S(1)}, f32[12,16,128]{2,1,0:T(8,128)S(1)}, u32[]{:S(2)}, u32[]{:S(2)}) collective-permute-start(f32[12,16,128]{2,1,0:T(8,128)S(1)} %shard_map.100.refs_2_.own_ref), channel_id=1, source_target_pairs={{0,128},{4,132},{8,136},{12,140},{16,144},{20,148},{24,152},{28,15... | collective-permute-start | bytes 294920 | tf_op jit(solution)/shard_map/ppermute | solution.py:198
  8.8 4.7 %collective-permute-start.1 = (f32[12,16,128]{2,1,0:T(8,128)S(1)}, f32[12,16,128]{2,1,0:T(8,128)S(1)}, u32[]{:S(2)}, u32[]{:S(2)}) collective-permute-start(f32[12,16,128]{2,1,0:T(8,128)S(1)} %shard_map.102.refs_3_.own_ref), channel_id=1, source_target_pairs={{0,64},{4,68},{8,72},{12,76},{16,80},{20,84},{24,88},{28,92},{32,9... | collective-permute-start | bytes 294920 | tf_op jit(solution)/shard_map/ppermute | solution.py:198
  14.1 6.6 %copy-start.4 = (f32[2,16,1536]{2,1,0:T(8,128)S(1)}, f32[2,16,1536]{2,1,0:T(8,128)}, u32[]{:S(2)}) copy-start(f32[2,16,1536]{2,1,0:T(8,128)} %refs_2_.2) | copy-start | bytes 589828
  16.0 34.3 %collective-permute-start.13 = (f32[1,12,2,64,128]{4,3,2,1,0:T(8,128)S(1)}, f32[1,12,2,64,128]{4,3,2,1,0:T(8,128)S(1)}, u32[]{:S(2)}, u32[]{:S(2)}) collective-permute-start(f32[1,12,2,64,128]{4,3,2,1,0:T(8,128)S(1)} %get-tuple-element.29.weight_ref), channel_id=1, source_target_pairs={{0,128},{4,132},{8,136},{12,140},{16,144},{20,148},{24,152},{28,15... | collective-permute-start | bytes 2359304 | tf_op jit(solution)/shard_map/ppermute | solution.py:198
  19.2 5.3 %collective-permute-start.2 = (f32[12,16,128]{2,1,0:T(8,128)S(1)}, f32[12,16,128]{2,1,0:T(8,128)S(1)}, u32[]{:S(2)}, u32[]{:S(2)}) collective-permute-start(f32[12,16,128]{2,1,0:T(8,128)S(1)} %shard_map.104.refs_3_.own_ref), channel_id=1, source_target_pairs={{0,32},{4,36},{8,40},{12,44},{16,48},{20,52},{24,56},{28,60},{32,0... | collective-permute-start | bytes 294920 | tf_op jit(solution)/shard_map/ppermute | solution.py:198
  20.7 7.6 %collective-permute-start.8 = (f32[2,16,1536]{2,1,0:T(8,128)S(1)}, f32[2,16,1536]{2,1,0:T(8,128)S(1)}, u32[]{:S(2)}, u32[]{:S(2)}) collective-permute-start(f32[2,16,1536]{2,1,0:T(8,128)S(1)} %copy-done.4), channel_id=1, source_target_pairs={{0,2},{1,3},{2,0},{3,1},{4,6},{5,7},{6,4},{7,5},{8,10},{9,11},{10,... | collective-permute-start | bytes 589832 | tf_op jit(solution)/shard_map/ppermute | solution.py:198
  25.1 11.6 %copy-start = (s32[1,4,4]{2,1,0:T(4,128)S(1)}, s32[1,4,4]{2,1,0:T(4,128)}, u32[]{:S(2)}) copy-start(s32[1,4,4]{2,1,0:T(4,128)} %param.19) | copy-start | bytes 196
  25.1 11.6 %copy-start.1 = (s32[12,2]{0,1:T(2,128)S(1)}, s32[12,2]{0,1:T(2,128)}, u32[]{:S(2)}) copy-start(s32[12,2]{0,1:T(2,128)} %param.16) | copy-start | bytes 292
  25.1 11.6 %copy-start.2 = (s32[12,2]{0,1:T(2,128)S(1)}, s32[12,2]{0,1:T(2,128)}, u32[]{:S(2)}) copy-start(s32[12,2]{0,1:T(2,128)} %param.17) | copy-start | bytes 292
  25.1 11.6 %copy-start.3 = (s32[12,2]{0,1:T(2,128)S(1)}, s32[12,2]{0,1:T(2,128)}, u32[]{:S(2)}) copy-start(s32[12,2]{0,1:T(2,128)} %param.18) | copy-start | bytes 292
  25.1 1.4 %collective-permute-start.3 = (f32[12,16,128]{2,1,0:T(8,128)S(1)}, f32[12,16,128]{2,1,0:T(8,128)S(1)}, u32[]{:S(2)}, u32[]{:S(2)}) collective-permute-start(f32[12,16,128]{2,1,0:T(8,128)S(1)} %shard_map.106.own_ref), channel_id=1, source_target_pairs={{0,1},{1,0},{2,3},{3,2},{4,5},{5,4},{6,7},{7,6},{8,9},{9,8},{10,11... | collective-permute-start | bytes 294920 | tf_op jit(solution)/shard_map/ppermute | solution.py:198
  28.3 8.4 %collective-permute-start.7 = (f32[2,16,1536]{2,1,0:T(8,128)S(1)}, f32[2,16,1536]{2,1,0:T(8,128)S(1)}, u32[]{:S(2)}, u32[]{:S(2)}) collective-permute-start(f32[2,16,1536]{2,1,0:T(8,128)S(1)} %copy-done.4), channel_id=1, source_target_pairs={{0,1},{1,0},{2,3},{3,2},{4,5},{5,4},{6,7},{7,6},{8,9},{9,8},{10,11... | collective-permute-start | bytes 589832 | tf_op jit(solution)/shard_map/ppermute | solution.py:198
  28.3 8.4 %collective-permute-start.9 = (f32[2,16,1536]{2,1,0:T(8,128)S(1)}, f32[2,16,1536]{2,1,0:T(8,128)S(1)}, u32[]{:S(2)}, u32[]{:S(2)}) collective-permute-start(f32[2,16,1536]{2,1,0:T(8,128)S(1)} %collective-permute-done.8.far_ref), channel_id=1, source_target_pairs={{0,1},{1,0},{2,3},{3,2},{4,5},{5,4},{6,7},{7,6},{8,9},{9,8},{10,11... | collective-permute-start | bytes 589832 | tf_op jit(solution)/shard_map/ppermute | solution.py:198
  28.8 6.2 %collective-permute-start.5 = (f32[12,16,128]{2,1,0:T(8,128)S(1)}, f32[12,16,128]{2,1,0:T(8,128)S(1)}, u32[]{:S(2)}, u32[]{:S(2)}) collective-permute-start(f32[12,16,128]{2,1,0:T(8,128)S(1)} %shard_map.107.own_ref), channel_id=1, source_target_pairs={{0,2},{1,3},{2,0},{3,1},{4,6},{5,7},{6,4},{7,5},{8,10},{9,11},{10,... | collective-permute-start | bytes 294920 | tf_op jit(solution)/shard_map/ppermute | solution.py:198
  35.7 4.7 %collective-permute-start.6 = (f32[12,16,128]{2,1,0:T(8,128)S(1)}, f32[12,16,128]{2,1,0:T(8,128)S(1)}, u32[]{:S(2)}, u32[]{:S(2)}) collective-permute-start(f32[12,16,128]{2,1,0:T(8,128)S(1)} %shard_map.108.rest_0_.own_ref), channel_id=1, source_target_pairs={{0,32},{4,36},{8,40},{12,44},{16,48},{20,52},{24,56},{28,60},{32,0... | collective-permute-start | bytes 294920 | tf_op jit(solution)/shard_map/ppermute | solution.py:198
  41.0 7.0 %collective-permute-start.10 = (f32[12,16,128]{2,1,0:T(8,128)S(1)}, f32[12,16,128]{2,1,0:T(8,128)S(1)}, u32[]{:S(2)}, u32[]{:S(2)}) collective-permute-start(f32[12,16,128]{2,1,0:T(8,128)S(1)} %shard_map.110.rest_0_.own_ref), channel_id=1, source_target_pairs={{0,64},{4,68},{8,72},{12,76},{16,80},{20,84},{24,88},{28,92},{32,9... | collective-permute-start | bytes 294920 | tf_op jit(solution)/shard_map/ppermute | solution.py:198
  41.7 8.6 %collective-permute-start.12 = (f32[12,16,128]{2,1,0:T(8,128)S(1)}, f32[12,16,128]{2,1,0:T(8,128)S(1)}, u32[]{:S(2)}, u32[]{:S(2)}) collective-permute-start(f32[12,16,128]{2,1,0:T(8,128)S(1)} %shard_map.110.rest_0_.own_ref), channel_id=1, source_target_pairs={{0,192},{4,196},{8,200},{12,204},{16,208},{20,212},{24,216},{28,22... | collective-permute-start | bytes 294920 | tf_op jit(solution)/shard_map/ppermute | solution.py:198
  42.3 8.0 %collective-permute-start.11 = (f32[12,16,128]{2,1,0:T(8,128)S(1)}, f32[12,16,128]{2,1,0:T(8,128)S(1)}, u32[]{:S(2)}, u32[]{:S(2)}) collective-permute-start(f32[12,16,128]{2,1,0:T(8,128)S(1)} %shard_map.110.rest_0_.own_ref), channel_id=1, source_target_pairs={{0,128},{4,132},{8,136},{12,140},{16,144},{20,148},{24,152},{28,15... | collective-permute-start | bytes 294920 | tf_op jit(solution)/shard_map/ppermute | solution.py:198
  45.2 5.1 %collective-permute-start.4 = (s32[8,1,12]{2,1,0:T(1,128)S(1)}, s32[8,1,12]{2,1,0:T(1,128)S(1)}, u32[]{:S(2)}, u32[]{:S(2)}) collective-permute-start(s32[8,1,12]{2,1,0:T(1,128)S(1)} %get-tuple-element.22.roster_ref), channel_id=1, source_target_pairs={{0,128},{4,132},{8,136},{12,140},{16,144},{20,148},{24,152},{28,15... | collective-permute-start | bytes 1160 | tf_op jit(solution)/shard_map/ppermute | solution.py:198

commit v5 on v4

v5 whole, which is shorter than its diff:
```python
import functools

import jax
import jax.numpy as jnp
from jax import lax
from jax.experimental import pallas as pl
from jax.experimental.pallas import tpu as pltpu
from jax.sharding import PartitionSpec as P


VMEM = pltpu.VMEM
SMEM = pltpu.SMEM
ANY = pl.ANY
HBM = pltpu.HBM
DMA = pltpu.SemaphoreType.DMA
BF = jnp.bfloat16
F32 = jnp.float32
NT = (((1,), (1,)), ((), ()))
NN = (((1,), (0,)), ((), ()))
NEAR_PARTS = ((0, 4), (4, 8))


def split(value):
    high = value.astype(BF)
    return high, (value - high.astype(F32)).astype(BF)


def widened(rows):
    high, low = split(rows)
    return jnp.concatenate(
        [
            jnp.concatenate([high, high], axis=1),
            jnp.concatenate([low, jnp.zeros_like(low)], axis=1),
        ],
        axis=0,
    )


def folded(result):
    count = result.shape[0] // 2
    return result[:count] + result[count:]


def product(rows, weights):
    wide = jnp.concatenate(split(weights), axis=1)
    return folded(lax.dot_general(widened(rows), wide, NT, preferred_element_type=F32))


def times(rows, wide):
    return folded(lax.dot_general(widened(rows), wide, NN, preferred_element_type=F32))


def lane_low(shape):
    return lax.broadcasted_iota(jnp.int32, shape, 1) < 64


def joined(result):
    rhs = result.shape[0] // 2
    turned = pltpu.roll(result[rhs:], 64, axis=1)
    return result[:rhs] + jnp.where(lane_low(turned.shape), -turned, turned)


def arranged(block):
    halves = []
    flat = block.T
    for half in range(2):
        upper = flat[64 * half : 64 * half + 64]
        turned = pltpu.roll(upper, 64, axis=1)
        lower = jnp.where(lane_low(turned.shape), -turned, turned)
        halves.append(jnp.concatenate(split(jnp.concatenate([upper, lower], axis=0)), axis=0))
    return halves


def started(pairs, sems):
    copies = [pltpu.make_async_copy(source, out, sems.at[n]) for n, (source, out) in enumerate(pairs)]
    for copy in copies:
        copy.start()
    return copies


def finish(copies):
    for copy in copies:
        copy.wait()


def compress_kernel(field_hbm, weight_hbm, coupling_hbm, roster_hbm, out_ref, coupling_ref, roster_ref, field_ref, weight_ref, sems):
    blocks = out_ref.shape[0]
    parts = [pl.ds(2 * n, 2) for n in range(blocks // 2)]
    copies = started(
        [(field_hbm, field_ref)]
        + [(weight_hbm.at[part], weight_ref.at[part]) for part in parts]
        + [(coupling_hbm.at[0], coupling_ref), (roster_hbm, roster_ref)],
        sems,
    )
    copies[0].wait()
    for k in range(blocks):
        if k % 2 == 0:
            copies[1 + k // 2].wait()
        lanes = pl.ds(128 * k, 128)
        rows = jnp.concatenate([field_ref[0, :, lanes], field_ref[1, :, lanes]], axis=0)
        out_ref[k] = joined(product(rows, weight_ref[k].reshape(128, 128)))
    finish(copies[-2:])


def ahead_kernel(parts, own_ref, weight_ref, *refs):
    count = len(parts)
    sources, own_out, other_out = refs[:count], refs[count], refs[count + 1]
    outs, sems = refs[count + 2 : -1], refs[-1]
    copies = started(
        [(source if part is None else source.at[part], out) for part, source, out in zip(parts, sources, outs)],
        sems,
    )
    for k in range(own_ref.shape[0]):
        own_wide, other_wide = arranged(weight_ref[k].reshape(128, 128))
        other_out[k] = other_wide
        own_out[k] = times(own_ref[k], own_wide)
    finish(copies)


def pack_kernel(level, weight_hbm, roster_ref, after_ref, out_ref, sem):
    count = out_ref.shape[0] - 1
    copy = pltpu.make_async_copy(weight_hbm.at[level], out_ref.at[pl.ds(0, count)], sem)
    copy.start()
    row = jnp.broadcast_to(roster_ref[level].astype(F32), (8, roster_ref.shape[2]))
    out_ref[count, 0, 0:8, 0 : roster_ref.shape[2]] = row
    copy.wait()


def prepare_kernel(weight_ref, after_ref, own_out, other_out):
    for k in range(own_out.shape[0]):
        own_out[k], other_out[k] = arranged(weight_ref[k].reshape(128, 128))


def spread_kernel(weight_ref, after_ref, out_ref):
    for k in range(out_ref.shape[0]):
        out_ref[k] = jnp.concatenate(split(weight_ref[k].reshape(128, 128)), axis=0)


def own_kernel(own_ref, wide_ref, out_ref):
    for k in range(out_ref.shape[0]):
        out_ref[k] = times(own_ref[k], wide_ref[k])


def level_kernel(level, roster_ref, other_ref, wide_ref, ready_ref, *rest):
    out_ref = rest[-1]
    row = roster_ref[level]
    places = [row[0, k] for k in range(out_ref.shape[0])]
    for k, place in enumerate(places):
        out_ref[k] = ready_ref[k] + times(other_ref[place], wide_ref[k])


def corner_kernel(packed_ref, other_ref, wide_ref, out_ref):
    blocks = out_ref.shape[0]
    row = packed_ref[blocks, 0, 0:8, 0:blocks]
    places = [row[0, k].astype(jnp.int32) for k in range(blocks)]
    for k, place in enumerate(places):
        out_ref[k] = times(other_ref[place], wide_ref[k])


def last_kernel(
    level, roster_ref, cross_ref, away_ref, corner_ref, wide_ref, ready_ref, expand_ref, *rest
):
    near_refs, (out_hbm, there_ref, out_ref, sems) = rest[:-4], rest[-4:]
    blocks = cross_ref.shape[0]
    row = roster_ref[level]
    places = [row[0, k] for k in range(blocks)]
    for k in range(blocks):
        there_ref[k] = corner_ref[k] + times(cross_ref[k], away_ref[k])
    copies = []
    for k, place in enumerate(places):
        coeffs = ready_ref[k] + times(there_ref[place], wide_ref[k])
        signed = jnp.where(lane_low(coeffs.shape), coeffs, -coeffs)
        turned = pltpu.roll(coeffs, 64, axis=1)
        far = times(jnp.concatenate([signed, turned], axis=0), expand_ref[k])
        which = [n for n, (begin, count) in enumerate(NEAR_PARTS) if begin <= k < begin + count][0]
        total = far + near_refs[which][k - NEAR_PARTS[which][0]]
        half = total.shape[0] // 2
        lanes = pl.ds(128 * k, 128)
        out_ref[0, :, lanes] = total[:half]
        out_ref[1, :, lanes] = total[half:]
        if k % 4 == 3:
            part = pl.ds(128 * (k - 3), 512)
            copy = pltpu.make_async_copy(out_ref.at[:, :, part], out_hbm.at[:, :, part], sems.at[k // 4])
            copy.start()
            copies.append(copy)
    finish(copies)


def near_kernel(first, owner_ref, place_ref, valid_ref, pick_ref, own_ref, core_ref, far_ref, both_ref, weight_ref, *rest):
    out_ref = rest[-1]
    me = lax.axis_index("sub")
    for n in range(out_ref.shape[0]):
        k = first + n
        total = None
        for t in range(weight_ref.shape[1]):
            owner = owner_ref[t, k]
            leaf = pick_ref[owner, place_ref[t, k]]
            lanes = pl.ds(pl.multiple_of(leaf * 128, 128), 128)
            which = owner ^ me
            parts = []
            for d in range(2):
                low = jnp.where(which == 1, core_ref[d, :, lanes], own_ref[d, :, lanes])
                high = jnp.where(which == 3, both_ref[d, :, lanes], far_ref[d, :, lanes])
                parts.append(jnp.where(which >= 2, high, low))
            rows = jnp.concatenate(parts, axis=0) * valid_ref[t, k].astype(F32)
            result = product(rows, weight_ref[k, t].reshape(256, 128))
            half = result.shape[0] // 2
            term = jnp.concatenate(
                [result[:half, :128] - result[half:, 128:], result[half:, :128] + result[:half, 128:]], axis=0
            )
            total = term if total is None else total + term
        out_ref[n] = total


def spec(space):
    return pl.BlockSpec(memory_space=space)


def call(kernel, out, spaces, out_spaces=VMEM, scratch=(), flops=2_000_000):
    single = not isinstance(out_spaces, (list, tuple))
    return pl.pallas_call(
        kernel,
        out_shape=out,
        in_specs=[spec(space) for space in spaces],
        out_specs=spec(out_spaces) if single else [spec(space) for space in out_spaces],
        scratch_shapes=list(scratch),
        compiler_params=pltpu.CompilerParams(vmem_limit_bytes=8 << 20),
        cost_estimate=pl.CostEstimate(flops=flops, bytes_accessed=1 << 20, transcendentals=0),
    )


def in_hbm(*arrays):
    return [pltpu.with_memory_space_constraint(array, HBM) for array in arrays]


def flipped(value, axis, mask):
    pairs = [(source, source ^ mask) for source in range(lax.axis_size(axis))]
    return lax.ppermute(value, axis, pairs)


def tied(value, after):
    return lax.optimization_barrier((value, after))[0]


def on_device(
    field_in,
    compress,
    coupling,
    roster,
    expand,
    nearfield_dense_blocks,
    slot_owner_index,
    slot_source_position,
    slot_valid_mask,
    near_pick,
):
    blocks = compress.shape[0]
    rhs = field_in.shape[1]
    leaf_count = lax.axis_size("leaf")
    top = leaf_count // 2
    plan = [
        ("leaf", top),
        ("leaf", top // 2),
        ("leaf", top // 4),
        ("sub", 1),
        ("sub", 2),
        ("leaf", top // 4),
        ("leaf", top // 2),
        ("leaf", top),
    ]
    pick = near_pick[0]
    indices = (slot_owner_index.T, slot_source_position.T, slot_valid_mask.T, pick)
    state = VMEM((blocks, rhs, 128), F32)
    wide = VMEM((blocks, 256, 128), BF)
    level_weights = VMEM(coupling.shape[1:], F32)
    coupling_hbm, near_hbm, expand_hbm, field_hbm = in_hbm(coupling, nearfield_dense_blocks, expand, field_in)

    coeffs, first, names = call(
        compress_kernel,
        [state, level_weights, VMEM(roster.shape, jnp.int32)],
        [HBM] * 4,
        [VMEM] * 3,
        scratch=[VMEM(field_in.shape, F32), VMEM(compress.shape, F32), DMA((3 + blocks // 2,))],
    )(*in_hbm(field_in, compress, coupling, roster))
    weights = {0: first}

    def ahead(position, coeffs, levels=(), whole=()):
        parts = list(levels) + [None] * len(whole)
        sources = [coupling_hbm] * len(levels) + list(whole)
        shapes = [level_weights] * len(levels) + [VMEM(array.shape, array.dtype) for array in whole]
        ready, other, *got = call(
            functools.partial(ahead_kernel, parts),
            [state, wide] + shapes,
            [VMEM] * 2 + [HBM] * len(sources),
            [VMEM] * (2 + len(shapes)),
            [DMA((len(parts),))],
        )(coeffs, weights[position], *sources)
        weights.update(dict(zip(levels, got)))
        return ready, other, got[len(levels) :]

    def prepared(weight, after):
        return call(prepare_kernel, [wide, wide], [VMEM, ANY], [VMEM] * 2)(weight, after)

    def near_piece(number, after):
        begin, count = NEAR_PARTS[number]
        return call(
            functools.partial(near_kernel, begin), VMEM((count, 2 * rhs, 128), F32), [SMEM] * 4 + [VMEM] * 5 + [ANY]
        )(*indices, field, core, far, both, dense, after)

    def own_part(own, wide_own):
        return call(own_kernel, state, [VMEM] * 2)(own, wide_own)

    def level_of(position, other, wide_other, ready, extra):
        return call(
            functools.partial(level_kernel, position), state, [VMEM] * 4 + [ANY] * len(extra)
        )(names, other, wide_other, ready, *extra)

    extra_levels = {0: (1,), 1: (2,), 2: (3, 7), 3: (4,), 4: (5,), 5: ()}
    extra_whole = {1: (near_hbm, field_hbm), 4: (expand_hbm,)}
    for position, (axis, mask) in enumerate(plan[:-2]):
        other = flipped(coeffs, axis, mask)
        extra = []
        ready, wide_other, got = ahead(position, coeffs, extra_levels[position], extra_whole.get(position, ()))
        if position == 0:
            far = flipped(tied(field_in, coeffs), "sub", 2)
        if position == 1:
            dense, field = got
            packed = call(
                functools.partial(pack_kernel, 6),
                VMEM((blocks + 1,) + coupling.shape[2:], F32),
                [HBM, VMEM, ANY],
                scratch=[DMA],
            )(coupling_hbm, names, coeffs)
            extra.append(packed)
        if position == 2:
            away = flipped(tied(packed, coeffs), "leaf", top)
        if position == 4:
            core = flipped(tied(field_in, coeffs), "sub", 1)
            both = flipped(tied(far, coeffs), "sub", 1)
            sixth = prepared(packed, coeffs)
            seventh = prepared(weights[7], coeffs)
            extra += [sixth[0], seventh[0]]
        if position == 5:
            last = call(spread_kernel, wide, [VMEM, ANY])(expand_ready, coeffs)
            pieces = [near_piece(0, coeffs)]
            extra += [last, pieces[0]]
        if position == 4:
            expand_ready = got[0]
        coeffs = level_of(position, other, wide_other, ready, extra)
    side = flipped(coeffs, "leaf", top // 2)
    corner = flipped(coeffs, "leaf", top // 2 + top)
    cross = flipped(coeffs, "leaf", top)
    pieces.append(near_piece(1, coeffs))
    ready = own_part(coeffs, sixth[0])
    here = level_of(6, side, sixth[1], ready, [pieces[1]])
    ready = own_part(here, seventh[0])
    away_wide = prepared(away, ready)
    beside = call(corner_kernel, state, [VMEM] * 3)(away, corner, away_wide[1])
    return call(
        functools.partial(last_kernel, 7),
        jax.ShapeDtypeStruct(field_in.shape, F32),
        [VMEM] * (7 + len(pieces)),
        HBM,
        [state, VMEM(field_in.shape, F32), DMA((3,))],
    )(names, cross, away_wide[0], beside, seventh[1], ready, last, *pieces)


def solution(mesh):
    return jax.shard_map(
        on_device,
        mesh=mesh,
        in_specs=(
            P(None, None, ("leaf", "sub")),
            P(("leaf", "sub"), None, None, None),
            P(None, ("leaf", "sub"), None, None, None),
            P(None, ("leaf", "sub"), None),
            P(("leaf", "sub"), None, None, None),
            P(("leaf", "sub"), None, None, None, None),
            P(("leaf", "sub"), None),
            P(("leaf", "sub"), None),
            P(("leaf", "sub"), None),
            P(("leaf", "sub"), None, None),
        ),
        out_specs=P(None, None, ("leaf", "sub")),
        check_vma=False,
    )
```

time: 52.5 us -> 48.5 us (0.924)
  waiting for transfers between devices: 13.4 us -> 6.69 us
  Pallas kernels: 17.4 us -> 21 us
  starting transfers between devices: 21.2 us -> 19.9 us
    ppermute x14 -> x13, waiting for transfers between devices: 13.4 us -> 6.69 us  [flipped(): return lax.ppermute(value, axis, pairs)]
    pallas_call x14 -> x24, Pallas kernels: 15.3 us -> 19.6 us  [the longest x6 8.82 us: ahead(): call(functools.partial(ahead_kernel, parts), [state, wide] + shapes, [VME...]
    ppermute x14 -> x13, starting transfers between devices: 21.2 us -> 19.9 us  [flipped(): return lax.ppermute(value, axis, pairs)]
    pallas_call x1, Pallas kernels: 2.08 us -> 1.47 us  [on_device(): call(functools.partial(last_kernel, 7), jax.ShapeDtypeStruct(field_in.sha...]
  transfers between devices with their start and end apart: 14 -> 13, of which waited for: 8 -> 5; matrix products, arithmetic and copies ran while one was open for 0% -> 0% of each run, Pallas kernels for 20% -> 34%
where the time goes in v5:
time: 48.5 us; the launch traced here: 48.2 us
  Pallas kernels  21 us (43%)
  starting transfers between devices  19.9 us (41%)
  waiting for transfers between devices  6.69 us (14%)
  between operations  0.52 us (1%)
    ppermute x13, starting transfers between devices, flipped(): return lax.ppermute(value, axis, pairs)  19.9 us
    pallas_call x6, Pallas kernels, ahead(): call(functools.partial(ahead_kernel, parts), [state, wide] + shapes, [VME...  8.82 us
    ppermute x13, waiting for transfers between devices, flipped(): return lax.ppermute(value, axis, pairs)  6.69 us
    pallas_call x1, Pallas kernels, on_device(): call(compress_kernel, [state, level_weights, VMEM(roster.shape, jnp.int32...  2.58 us
    pallas_call x2, Pallas kernels, near_piece(): call(functools.partial(near_kernel, begin), VMEM((count, 2 * rhs, 128), F...  2.34 us
    pallas_call x7, Pallas kernels, level_of(): call(functools.partial(level_kernel, position), state, [VMEM] * 4 + [ANY]...  2.22 us
    pallas_call x3, Pallas kernels, prepared(): call(prepare_kernel, [wide, wide], [VMEM, ANY], [VMEM] * 2)(weight, after)  1.6 us
    pallas_call x1, Pallas kernels, on_device(): call(functools.partial(last_kernel, 7), jax.ShapeDtypeStruct(field_in.sha...  1.47 us
  transfers between devices with their start and end apart: 13, of which 5 were waited for; matrix products, arithmetic and copies ran while one was open for 0% of the time, Pallas kernels for 34%

profile of v5, /device:TPU:64, one launch (start us, length us, event | category | flops | bytes accessed | tf_op | source)
XLA Modules:
  0.0 48.2 jit_solution(2619677044863839768)
XLA Ops:
  0.0 2.6 %shard_map.100 = (f32[12,16,128]{2,1,0:T(8,128)S(1)}, f32[12,2,64,128]{3,2,1,0:T(8,128)S(1)}, s32[8,1,12]{2,1,0:T(1,128)S(1)}) custom-call(f32[2,16,1536]{2,1,0:T(8,128)} %refs_2_.1, f32[12,2,64,128]{3,2,1,0:T(8,128)} %weight_hbm.2, f32[8,12,2,64,128]{4,3,2,1,0:T(8,128)} %refs_0_.9, s32[8,1,12]{2,1,0:T(1,128)} %roster_hbm.1), custom_call_target="tpu_custom_call" | custom-call | flops 2000000 | bytes 1048576 | tf_op jit(solution)/shard_map/pallas_call | solution.py:278
  2.6 3.1 %collective-permute-start = (f32[12,16,128]{2,1,0:T(8,128)S(1)}, f32[12,16,128]{2,1,0:T(8,128)S(1)}, u32[]{:S(2)}, u32[]{:S(2)}) collective-permute-start(f32[12,16,128]{2,1,0:T(8,128)S(1)} %get-tuple-element.40.own_ref), channel_id=1, source_target_pairs={{0,128},{4,132},{8,136},{12,140},{16,144},{20,148},{24,152},{28,15... | collective-permute-start | bytes 294920 | tf_op jit(solution)/shard_map/ppermute | solution.py:238
  5.7 1.6 %shard_map.101 = (f32[12,16,128]{2,1,0:T(8,128)S(1)}, bf16[12,256,128]{2,1,0:T(8,128)(2,1)S(1)}, f32[12,2,64,128]{3,2,1,0:T(8,128)S(1)}) custom-call(f32[12,16,128]{2,1,0:T(8,128)S(1)} %get-tuple-element.40.own_ref, f32[12,2,64,128]{3,2,1,0:T(8,128)S(1)} %get-tuple-element.41.weight_ref, f32[8,12,2,64,128]{4,3,2,1,0:T(8,128)} %refs_0_.9), custom_call_target="tpu_custom_call" | custom-call | flops 2000000 | bytes 1048576 | tf_op jit(solution)/shard_map/pallas_call | solution.py:291
  7.3 1.5 %collective-permute-done.other_ref = f32[12,16,128]{2,1,0:T(8,128)S(1)} collective-permute-done((f32[12,16,128]{2,1,0:T(8,128)S(1)}, f32[12,16,128]{2,1,0:T(8,128)S(1)}, u32[]{:S(2)}, u32[]{:S(2)}) %collective-permute-start) | collective-permute-done | bytes 98336 | tf_op jit(solution)/shard_map/ppermute | solution.py:238
  8.8 0.3 shard_map.102.own_ref.after_ref
  9.1 1.6 %collective-permute-start.1 = (f32[12,16,128]{2,1,0:T(8,128)S(1)}, f32[12,16,128]{2,1,0:T(8,128)S(1)}, u32[]{:S(2)}, u32[]{:S(2)}) collective-permute-start(f32[12,16,128]{2,1,0:T(8,128)S(1)} %shard_map.102.own_ref.after_ref), channel_id=1, source_target_pairs={{0,64},{4,68},{8,72},{12,76},{16,80},{20,84},{24,88},{28,92},{32,9... | collective-permute-start | bytes 294920 | tf_op jit(solution)/shard_map/ppermute | solution.py:238
  10.7 1.1 %shard_map.104.rest_0_.weight_ref = f32[13,2,64,128]{3,2,1,0:T(8,128)S(1)} custom-call(f32[8,12,2,64,128]{4,3,2,1,0:T(8,128)} %refs_0_.9, s32[8,1,12]{2,1,0:T(1,128)S(1)} %get-tuple-element.39.roster_ref, f32[12,16,128]{2,1,0:T(8,128)S(1)} %shard_map.102.own_ref.after_ref), custom_call_target="tpu_custom_call" | custom-call | flops 2000000 | bytes 1048576 | tf_op jit(solution)/shard_map/pallas_call | solution.py:328
  11.8 0.0 copy-start.4
  11.8 2.3 %shard_map.103 = (f32[12,16,128]{2,1,0:T(8,128)S(1)}, bf16[12,256,128]{2,1,0:T(8,128)(2,1)S(1)}, f32[12,2,64,128]{3,2,1,0:T(8,128)S(1)}, f32[12,2,2,128,128]{4,3,2,1,0:T(8,128)S(1)}, f32[2,16,1536]{2,1,0:T(8,128)S(1)}) custom-call(f32[12,16,128]{2,1,0:T(8,128)S(1)} %shard_map.102.own_ref.after_ref, f32[12,2,64,128]{3,2,1,0:T(8,128)S(1)} %get-tuple-element.44.weight_ref, ...), custom_call_target="tpu_custom_call" | custom-call | flops 2000000 | bytes 1048576 | tf_op jit(solution)/shard_map/pallas_call | solution.py:291
  14.1 0.0 collective-permute-done.1.other_ref
  14.1 0.3 shard_map.105.own_ref
  14.4 2.8 %collective-permute-start.10 = (f32[13,2,64,128]{3,2,1,0:T(8,128)S(1)}, f32[13,2,64,128]{3,2,1,0:T(8,128)S(1)}, u32[]{:S(2)}, u32[]{:S(2)}) collective-permute-start(f32[13,2,64,128]{3,2,1,0:T(8,128)S(1)} %shard_map.104.rest_0_.weight_ref), channel_id=1, source_target_pairs={{0,128},{4,132},{8,136},{12,140},{16,144},{20,148},{24,152},{28,15... | collective-permute-start | bytes 2555912 | tf_op jit(solution)/shard_map/ppermute | solution.py:238
  17.3 1.6 %collective-permute-start.2 = (f32[12,16,128]{2,1,0:T(8,128)S(1)}, f32[12,16,128]{2,1,0:T(8,128)S(1)}, u32[]{:S(2)}, u32[]{:S(2)}) collective-permute-start(f32[12,16,128]{2,1,0:T(8,128)S(1)} %shard_map.105.own_ref), channel_id=1, source_target_pairs={{0,32},{4,36},{8,40},{12,44},{16,48},{20,52},{24,56},{28,60},{32,0... | collective-permute-start | bytes 294920 | tf_op jit(solution)/shard_map/ppermute | solution.py:238
  18.8 0.0 copy-done.4
  18.8 2.9 %collective-permute-start.7 = (f32[2,16,1536]{2,1,0:T(8,128)S(1)}, f32[2,16,1536]{2,1,0:T(8,128)S(1)}, u32[]{:S(2)}, u32[]{:S(2)}) collective-permute-start(f32[2,16,1536]{2,1,0:T(8,128)S(1)} %copy-done.4), channel_id=1, source_target_pairs={{0,2},{1,3},{2,0},{3,1},{4,6},{5,7},{6,4},{7,5},{8,10},{9,11},{10,... | collective-permute-start | bytes 589832 | tf_op jit(solution)/shard_map/ppermute | solution.py:238
  21.7 1.4 %shard_map.106 = (f32[12,16,128]{2,1,0:T(8,128)S(1)}, bf16[12,256,128]{2,1,0:T(8,128)(2,1)S(1)}, f32[12,2,64,128]{3,2,1,0:T(8,128)S(1)}, f32[12,2,64,128]{3,2,1,0:T(8,128)S(1)}) custom-call(f32[12,16,128]{2,1,0:T(8,128)S(1)} %shard_map.105.own_ref, f32[12,2,64,128]{3,2,1,0:T(8,128)S(1)} %get-tuple-element.47.weight_ref, f32[8,12,2,64,128]{4,3,2,1,0:T(8,128)} %refs_0_.9, ...), custom_call_target="tpu_custom_call" | custom-call | flops 2000000 | bytes 1048576 | tf_op jit(solution)/shard_map/pallas_call | solution.py:291
  23.1 0.0 collective-permute-done.2.other_ref
  23.2 0.3 shard_map.107.own_ref
  23.5 0.1 collective-permute-start.3
  23.6 1.6 %shard_map.108 = (f32[12,16,128]{2,1,0:T(8,128)S(1)}, bf16[12,256,128]{2,1,0:T(8,128)(2,1)S(1)}, f32[12,2,64,128]{3,2,1,0:T(8,128)S(1)}) custom-call(f32[12,16,128]{2,1,0:T(8,128)S(1)} %shard_map.107.own_ref, f32[12,2,64,128]{3,2,1,0:T(8,128)S(1)} %get-tuple-element.50.weight_ref, f32[8,12,2,64,128]{4,3,2,1,0:T(8,128)} %refs_0_.9), custom_call_target="tpu_custom_call" | custom-call | flops 2000000 | bytes 1048576 | tf_op jit(solution)/shard_map/pallas_call | solution.py:291
  25.2 0.0 collective-permute-done.3.other_ref
  25.2 0.3 shard_map.109.own_ref.after_ref
  25.5 1.2 %collective-permute-done.7.far_ref = f32[2,16,1536]{2,1,0:T(8,128)S(1)} collective-permute-done((f32[2,16,1536]{2,1,0:T(8,128)S(1)}, f32[2,16,1536]{2,1,0:T(8,128)S(1)}, u32[]{:S(2)}, u32[]{:S(2)}) %collective-permute-start.7) | collective-permute-done | bytes 196640 | tf_op jit(solution)/shard_map/ppermute | solution.py:238
  26.8 0.0 collective-permute-start.8
  26.8 0.5 %collective-permute-start.6 = (f32[2,16,1536]{2,1,0:T(8,128)S(1)}, f32[2,16,1536]{2,1,0:T(8,128)S(1)}, u32[]{:S(2)}, u32[]{:S(2)}) collective-permute-start(f32[2,16,1536]{2,1,0:T(8,128)S(1)} %copy-done.4), channel_id=1, source_target_pairs={{0,1},{1,0},{2,3},{3,2},{4,5},{5,4},{6,7},{7,6},{8,9},{9,8},{10,11... | collective-permute-start | bytes 589832 | tf_op jit(solution)/shard_map/ppermute | solution.py:238
  27.3 2.2 %collective-permute-start.4 = (f32[12,16,128]{2,1,0:T(8,128)S(1)}, f32[12,16,128]{2,1,0:T(8,128)S(1)}, u32[]{:S(2)}, u32[]{:S(2)}) collective-permute-start(f32[12,16,128]{2,1,0:T(8,128)S(1)} %shard_map.109.own_ref.after_ref), channel_id=1, source_target_pairs={{0,2},{1,3},{2,0},{3,1},{4,6},{5,7},{6,4},{7,5},{8,10},{9,11},{10,... | collective-permute-start | bytes 294920 | tf_op jit(solution)/shard_map/ppermute | solution.py:238
  29.5 0.5 %shard_map.111 = (bf16[12,256,128]{2,1,0:T(8,128)(2,1)S(1)}, bf16[12,256,128]{2,1,0:T(8,128)(2,1)S(1)}) custom-call(f32[13,2,64,128]{3,2,1,0:T(8,128)S(1)} %shard_map.104.rest_0_.weight_ref, f32[12,16,128]{2,1,0:T(8,128)S(1)} %shard_map.109.own_ref.after_ref), custom_call_target="tpu_custom_call" | custom-call | flops 2000000 | bytes 1048576 | tf_op jit(solution)/shard_map/pallas_call | solution.py:302
  30.0 0.5 %shard_map.112 = (bf16[12,256,128]{2,1,0:T(8,128)(2,1)S(1)}, bf16[12,256,128]{2,1,0:T(8,128)(2,1)S(1)}) custom-call(f32[12,2,64,128]{3,2,1,0:T(8,128)S(1)} %get-tuple-element.57.weight_ref, f32[12,16,128]{2,1,0:T(8,128)S(1)} %shard_map.109.own_ref.after_ref), custom_call_target="tpu_custom_call" | custom-call | flops 2000000 | bytes 1048576 | tf_op jit(solution)/shard_map/pallas_call | solution.py:302
  30.5 1.4 %shard_map.110 = (f32[12,16,128]{2,1,0:T(8,128)S(1)}, bf16[12,256,128]{2,1,0:T(8,128)(2,1)S(1)}, f32[12,2,64,128]{3,2,1,0:T(8,128)S(1)}, f32[12,2,64,128]{3,2,1,0:T(8,128)S(1)}) custom-call(f32[12,16,128]{2,1,0:T(8,128)S(1)} %shard_map.109.own_ref.after_ref, f32[12,2,64,128]{3,2,1,0:T(8,128)S(1)} %get-tuple-element.53.weight_ref, ...), custom_call_target="tpu_custom_call" | custom-call | flops 2000000 | bytes 1048576 | tf_op jit(solution)/shard_map/pallas_call | solution.py:291
  31.9 0.0 copy-start
  32.0 0.0 copy-start.1
  32.0 0.0 copy-start.2
  32.0 0.0 copy-start.3
  32.0 1.5 %collective-permute-done.4.other_ref = f32[12,16,128]{2,1,0:T(8,128)S(1)} collective-permute-done((f32[12,16,128]{2,1,0:T(8,128)S(1)}, f32[12,16,128]{2,1,0:T(8,128)S(1)}, u32[]{:S(2)}, u32[]{:S(2)}) %collective-permute-start.4) | collective-permute-done | bytes 98336 | tf_op jit(solution)/shard_map/ppermute | solution.py:238
  33.5 0.3 shard_map.113.own_ref.after_ref.rest_0_
  33.8 0.8 %collective-permute-start.5 = (f32[12,16,128]{2,1,0:T(8,128)S(1)}, f32[12,16,128]{2,1,0:T(8,128)S(1)}, u32[]{:S(2)}, u32[]{:S(2)}) collective-permute-start(f32[12,16,128]{2,1,0:T(8,128)S(1)} %shard_map.113.own_ref.after_ref.rest_0_), channel_id=1, source_target_pairs={{0,32},{4,36},{8,40},{12,44},{16,48},{20,52},{24,56},{28,60},{32,0... | collective-permute-start | bytes 294920 | tf_op jit(solution)/shard_map/ppermute | solution.py:238
  34.6 0.1 shard_map.115.rest_0_.expand_ref
  34.7 0.6 %shard_map.114 = (f32[12,16,128]{2,1,0:T(8,128)S(1)}, bf16[12,256,128]{2,1,0:T(8,128)(2,1)S(1)}) custom-call(f32[12,16,128]{2,1,0:T(8,128)S(1)} %shard_map.113.own_ref.after_ref.rest_0_, f32[12,2,64,128]{3,2,1,0:T(8,128)S(1)} %get-tuple-element.59.weight_ref), custom_call_target="tpu_custom_call" | custom-call | flops 2000000 | bytes 1048576 | tf_op jit(solution)/shard_map/pallas_call | solution.py:291
  35.3 0.0 collective-permute-done.8.both_ref
  35.3 0.0 collective-permute-done.6.core_ref
  35.3 0.0 copy-done
  35.3 0.0 copy-done.1
  35.3 0.0 copy-done.2
  35.3 0.0 copy-done.3
  35.3 1.0 %shard_map.116.rest_1_.rest_0_ = f32[4,32,128]{2,1,0:T(8,128)S(1)} custom-call(s32[2,12]{1,0:T(2,128)S(1)} %bitcast.6, s32[2,12]{1,0:T(2,128)S(1)} %bitcast.8, s32[2,12]{1,0:T(2,128)S(1)} %bitcast.10, s32[4,4]{1,0:T(4,128)S(1)} %bitcast.4, f32[2,16,1536]{2,1,0:T(8,128)S(1)} %get-tuple-element.63.own_ref, f32[2,16,1536]{2,1,0:T(8,128)S(1)} %collective-permute-done.6.core_ref, ...), custom_call_target="tpu_custom_call" | custom-call | flops 2000000 | bytes 1048576 | tf_op jit(solution)/shard_map/pallas_call | solution.py:306
  36.4 2.1 %collective-permute-done.5.other_ref = f32[12,16,128]{2,1,0:T(8,128)S(1)} collective-permute-done((f32[12,16,128]{2,1,0:T(8,128)S(1)}, f32[12,16,128]{2,1,0:T(8,128)S(1)}, u32[]{:S(2)}, u32[]{:S(2)}) %collective-permute-start.5) | collective-permute-done | bytes 98336 | tf_op jit(solution)/shard_map/ppermute | solution.py:238
  38.5 0.3 shard_map.117.own_ref.rest_0_
  38.8 0.5 %collective-permute-start.11 = (f32[12,16,128]{2,1,0:T(8,128)S(1)}, f32[12,16,128]{2,1,0:T(8,128)S(1)}, u32[]{:S(2)}, u32[]{:S(2)}) collective-permute-start(f32[12,16,128]{2,1,0:T(8,128)S(1)} %shard_map.117.own_ref.rest_0_), channel_id=1, source_target_pairs={{0,64},{4,68},{8,72},{12,76},{16,80},{20,84},{24,88},{28,92},{32,9... | collective-permute-start | bytes 294920 | tf_op jit(solution)/shard_map/ppermute | solution.py:238
  39.3 1.1 %collective-permute-start.12 = (f32[12,16,128]{2,1,0:T(8,128)S(1)}, f32[12,16,128]{2,1,0:T(8,128)S(1)}, u32[]{:S(2)}, u32[]{:S(2)}) collective-permute-start(f32[12,16,128]{2,1,0:T(8,128)S(1)} %shard_map.117.own_ref.rest_0_), channel_id=1, source_target_pairs={{0,192},{4,196},{8,200},{12,204},{16,208},{20,212},{24,216},{28,22... | collective-permute-start | bytes 294920 | tf_op jit(solution)/shard_map/ppermute | solution.py:238
  40.4 2.7 %collective-permute-start.9 = (f32[12,16,128]{2,1,0:T(8,128)S(1)}, f32[12,16,128]{2,1,0:T(8,128)S(1)}, u32[]{:S(2)}, u32[]{:S(2)}) collective-permute-start(f32[12,16,128]{2,1,0:T(8,128)S(1)} %shard_map.117.own_ref.rest_0_), channel_id=1, source_target_pairs={{0,128},{4,132},{8,136},{12,140},{16,144},{20,148},{24,152},{28,15... | collective-permute-start | bytes 294920 | tf_op jit(solution)/shard_map/ppermute | solution.py:238
  43.2 0.2 shard_map.118.ready_ref
  43.4 1.3 %shard_map.119.rest_0_.rest_1_ = f32[8,32,128]{2,1,0:T(8,128)S(1)} custom-call(s32[2,12]{1,0:T(2,128)S(1)} %bitcast.7, s32[2,12]{1,0:T(2,128)S(1)} %bitcast.9, s32[2,12]{1,0:T(2,128)S(1)} %bitcast.11, s32[4,4]{1,0:T(4,128)S(1)} %bitcast.5, f32[2,16,1536]{2,1,0:T(8,128)S(1)} %get-tuple-element.63.own_ref, f32[2,16,1536]{2,1,0:T(8,128)S(1)} %collective-permute-done.6.core_ref, ...), custom_call_target="tpu_custom_call" | custom-call | flops 2000000 | bytes 1048576 | tf_op jit(solution)/shard_map/pallas_call | solution.py:306
  44.8 0.0 collective-permute-done.11.other_ref
  44.8 0.3 shard_map.120.own_ref
  45.1 0.2 shard_map.121.after_ref.ready_ref
  45.4 0.0 collective-permute-done.10.weight_ref.packed_ref
  45.4 0.5 %shard_map.122 = (bf16[12,256,128]{2,1,0:T(8,128)(2,1)S(1)}, bf16[12,256,128]{2,1,0:T(8,128)(2,1)S(1)}) custom-call(f32[13,2,64,128]{3,2,1,0:T(8,128)S(1)} %collective-permute-done.10.weight_ref.packed_ref, f32[12,16,128]{2,1,0:T(8,128)S(1)} %shard_map.121.after_ref.ready_ref), custom_call_target="tpu_custom_call" | custom-call | flops 2000000 | bytes 1048576 | tf_op jit(solution)/shard_map/pallas_call | solution.py:302
  45.9 0.0 collective-permute-done.12.other_ref
  45.9 0.3 shard_map.123.corner_ref
  46.3 0.3 collective-permute-done.9.cross_ref
  46.6 1.5 %shard_map.124 = f32[2,16,1536]{2,1,0:T(8,128)} custom-call(s32[8,1,12]{2,1,0:T(1,128)S(1)} %get-tuple-element.39.roster_ref, f32[12,16,128]{2,1,0:T(8,128)S(1)} %collective-permute-done.9.cross_ref, bf16[12,256,128]{2,1,0:T(8,128)(2,1)S(1)} %get-tuple-element.70.away_ref, f32[12,16,128]{2,1,0:T(8,128)S(1)} %shard_map.123.corner_ref, ...), custom_call_target="tpu_custom_call" | custom-call | flops 2000000 | bytes 1048576 | tf_op jit(solution)/shard_map/pallas_call | solution.py:359
Async XLA Ops:
  2.6 6.2 %collective-permute-start = (f32[12,16,128]{2,1,0:T(8,128)S(1)}, f32[12,16,128]{2,1,0:T(8,128)S(1)}, u32[]{:S(2)}, u32[]{:S(2)}) collective-permute-start(f32[12,16,128]{2,1,0:T(8,128)S(1)} %get-tuple-element.40.own_ref), channel_id=1, source_target_pairs={{0,128},{4,132},{8,136},{12,140},{16,144},{20,148},{24,152},{28,15... | collective-permute-start | bytes 294920 | tf_op jit(solution)/shard_map/ppermute | solution.py:238
  9.1 5.0 %collective-permute-start.1 = (f32[12,16,128]{2,1,0:T(8,128)S(1)}, f32[12,16,128]{2,1,0:T(8,128)S(1)}, u32[]{:S(2)}, u32[]{:S(2)}) collective-permute-start(f32[12,16,128]{2,1,0:T(8,128)S(1)} %shard_map.102.own_ref.after_ref), channel_id=1, source_target_pairs={{0,64},{4,68},{8,72},{12,76},{16,80},{20,84},{24,88},{28,92},{32,9... | collective-permute-start | bytes 294920 | tf_op jit(solution)/shard_map/ppermute | solution.py:238
  11.8 7.0 %copy-start.4 = (f32[2,16,1536]{2,1,0:T(8,128)S(1)}, f32[2,16,1536]{2,1,0:T(8,128)}, u32[]{:S(2)}) copy-start(f32[2,16,1536]{2,1,0:T(8,128)} %refs_2_.1) | copy-start | bytes 589828
  14.4 30.9 %collective-permute-start.10 = (f32[13,2,64,128]{3,2,1,0:T(8,128)S(1)}, f32[13,2,64,128]{3,2,1,0:T(8,128)S(1)}, u32[]{:S(2)}, u32[]{:S(2)}) collective-permute-start(f32[13,2,64,128]{3,2,1,0:T(8,128)S(1)} %shard_map.104.rest_0_.weight_ref), channel_id=1, source_target_pairs={{0,128},{4,132},{8,136},{12,140},{16,144},{20,148},{24,152},{28,15... | collective-permute-start | bytes 2555912 | tf_op jit(solution)/shard_map/ppermute | solution.py:238
  17.3 5.9 %collective-permute-start.2 = (f32[12,16,128]{2,1,0:T(8,128)S(1)}, f32[12,16,128]{2,1,0:T(8,128)S(1)}, u32[]{:S(2)}, u32[]{:S(2)}) collective-permute-start(f32[12,16,128]{2,1,0:T(8,128)S(1)} %shard_map.105.own_ref), channel_id=1, source_target_pairs={{0,32},{4,36},{8,40},{12,44},{16,48},{20,52},{24,56},{28,60},{32,0... | collective-permute-start | bytes 294920 | tf_op jit(solution)/shard_map/ppermute | solution.py:238
  18.8 7.9 %collective-permute-start.7 = (f32[2,16,1536]{2,1,0:T(8,128)S(1)}, f32[2,16,1536]{2,1,0:T(8,128)S(1)}, u32[]{:S(2)}, u32[]{:S(2)}) collective-permute-start(f32[2,16,1536]{2,1,0:T(8,128)S(1)} %copy-done.4), channel_id=1, source_target_pairs={{0,2},{1,3},{2,0},{3,1},{4,6},{5,7},{6,4},{7,5},{8,10},{9,11},{10,... | collective-permute-start | bytes 589832 | tf_op jit(solution)/shard_map/ppermute | solution.py:238
  23.5 1.7 %collective-permute-start.3 = (f32[12,16,128]{2,1,0:T(8,128)S(1)}, f32[12,16,128]{2,1,0:T(8,128)S(1)}, u32[]{:S(2)}, u32[]{:S(2)}) collective-permute-start(f32[12,16,128]{2,1,0:T(8,128)S(1)} %shard_map.107.own_ref), channel_id=1, source_target_pairs={{0,1},{1,0},{2,3},{3,2},{4,5},{5,4},{6,7},{7,6},{8,9},{9,8},{10,11... | collective-permute-start | bytes 294920 | tf_op jit(solution)/shard_map/ppermute | solution.py:238
  26.8 8.5 %collective-permute-start.8 = (f32[2,16,1536]{2,1,0:T(8,128)S(1)}, f32[2,16,1536]{2,1,0:T(8,128)S(1)}, u32[]{:S(2)}, u32[]{:S(2)}) collective-permute-start(f32[2,16,1536]{2,1,0:T(8,128)S(1)} %collective-permute-done.7.far_ref), channel_id=1, source_target_pairs={{0,1},{1,0},{2,3},{3,2},{4,5},{5,4},{6,7},{7,6},{8,9},{9,8},{10,11... | collective-permute-start | bytes 589832 | tf_op jit(solution)/shard_map/ppermute | solution.py:238
  26.8 8.5 %collective-permute-start.6 = (f32[2,16,1536]{2,1,0:T(8,128)S(1)}, f32[2,16,1536]{2,1,0:T(8,128)S(1)}, u32[]{:S(2)}, u32[]{:S(2)}) collective-permute-start(f32[2,16,1536]{2,1,0:T(8,128)S(1)} %copy-done.4), channel_id=1, source_target_pairs={{0,1},{1,0},{2,3},{3,2},{4,5},{5,4},{6,7},{7,6},{8,9},{9,8},{10,11... | collective-permute-start | bytes 589832 | tf_op jit(solution)/shard_map/ppermute | solution.py:238
  27.3 6.2 %collective-permute-start.4 = (f32[12,16,128]{2,1,0:T(8,128)S(1)}, f32[12,16,128]{2,1,0:T(8,128)S(1)}, u32[]{:S(2)}, u32[]{:S(2)}) collective-permute-start(f32[12,16,128]{2,1,0:T(8,128)S(1)} %shard_map.109.own_ref.after_ref), channel_id=1, source_target_pairs={{0,2},{1,3},{2,0},{3,1},{4,6},{5,7},{6,4},{7,5},{8,10},{9,11},{10,... | collective-permute-start | bytes 294920 | tf_op jit(solution)/shard_map/ppermute | solution.py:238
  31.9 3.3 %copy-start = (s32[1,4,4]{2,1,0:T(4,128)S(1)}, s32[1,4,4]{2,1,0:T(4,128)}, u32[]{:S(2)}) copy-start(s32[1,4,4]{2,1,0:T(4,128)} %param.19) | copy-start | bytes 196
  32.0 3.3 %copy-start.1 = (s32[12,2]{0,1:T(2,128)S(1)}, s32[12,2]{0,1:T(2,128)}, u32[]{:S(2)}) copy-start(s32[12,2]{0,1:T(2,128)} %param.16) | copy-start | bytes 292
  32.0 3.3 %copy-start.2 = (s32[12,2]{0,1:T(2,128)S(1)}, s32[12,2]{0,1:T(2,128)}, u32[]{:S(2)}) copy-start(s32[12,2]{0,1:T(2,128)} %param.17) | copy-start | bytes 292
  32.0 3.3 %copy-start.3 = (s32[12,2]{0,1:T(2,128)S(1)}, s32[12,2]{0,1:T(2,128)}, u32[]{:S(2)}) copy-start(s32[12,2]{0,1:T(2,128)} %param.18) | copy-start | bytes 292
  33.8 4.7 %collective-permute-start.5 = (f32[12,16,128]{2,1,0:T(8,128)S(1)}, f32[12,16,128]{2,1,0:T(8,128)S(1)}, u32[]{:S(2)}, u32[]{:S(2)}) collective-permute-start(f32[12,16,128]{2,1,0:T(8,128)S(1)} %shard_map.113.own_ref.after_ref.rest_0_), channel_id=1, source_target_pairs={{0,32},{4,36},{8,40},{12,44},{16,48},{20,52},{24,56},{28,60},{32,0... | collective-permute-start | bytes 294920 | tf_op jit(solution)/shard_map/ppermute | solution.py:238
  38.8 6.0 %collective-permute-start.11 = (f32[12,16,128]{2,1,0:T(8,128)S(1)}, f32[12,16,128]{2,1,0:T(8,128)S(1)}, u32[]{:S(2)}, u32[]{:S(2)}) collective-permute-start(f32[12,16,128]{2,1,0:T(8,128)S(1)} %shard_map.117.own_ref.rest_0_), channel_id=1, source_target_pairs={{0,64},{4,68},{8,72},{12,76},{16,80},{20,84},{24,88},{28,92},{32,9... | collective-permute-start | bytes 294920 | tf_op jit(solution)/shard_map/ppermute | solution.py:238
  39.3 6.6 %collective-permute-start.12 = (f32[12,16,128]{2,1,0:T(8,128)S(1)}, f32[12,16,128]{2,1,0:T(8,128)S(1)}, u32[]{:S(2)}, u32[]{:S(2)}) collective-permute-start(f32[12,16,128]{2,1,0:T(8,128)S(1)} %shard_map.117.own_ref.rest_0_), channel_id=1, source_target_pairs={{0,192},{4,196},{8,200},{12,204},{16,208},{20,212},{24,216},{28,22... | collective-permute-start | bytes 294920 | tf_op jit(solution)/shard_map/ppermute | solution.py:238
  40.4 6.1 %collective-permute-start.9 = (f32[12,16,128]{2,1,0:T(8,128)S(1)}, f32[12,16,128]{2,1,0:T(8,128)S(1)}, u32[]{:S(2)}, u32[]{:S(2)}) collective-permute-start(f32[12,16,128]{2,1,0:T(8,128)S(1)} %shard_map.117.own_ref.rest_0_), channel_id=1, source_target_pairs={{0,128},{4,132},{8,136},{12,140},{16,144},{20,148},{24,152},{28,15... | collective-permute-start | bytes 294920 | tf_op jit(solution)/shard_map/ppermute | solution.py:238

commit v6 on v5

--- a/solution.py
+++ b/solution.py
@@ -83,14 +83,11 @@
         copy.wait()
 
 
-def compress_kernel(field_hbm, weight_hbm, coupling_hbm, roster_hbm, out_ref, coupling_ref, roster_ref, field_ref, weight_ref, sems):
+def compress_kernel(field_hbm, weight_hbm, out_ref, field_ref, weight_ref, sems):
     blocks = out_ref.shape[0]
     parts = [pl.ds(2 * n, 2) for n in range(blocks // 2)]
     copies = started(
-        [(field_hbm, field_ref)]
-        + [(weight_hbm.at[part], weight_ref.at[part]) for part in parts]
-        + [(coupling_hbm.at[0], coupling_ref), (roster_hbm, roster_ref)],
-        sems,
+        [(field_hbm, field_ref)] + [(weight_hbm.at[part], weight_ref.at[part]) for part in parts], sems
     )
     copies[0].wait()
     for k in range(blocks):
@@ -99,31 +96,55 @@
         lanes = pl.ds(128 * k, 128)
         rows = jnp.concatenate([field_ref[0, :, lanes], field_ref[1, :, lanes]], axis=0)
         out_ref[k] = joined(product(rows, weight_ref[k].reshape(128, 128)))
-    finish(copies[-2:])
-
-
-def ahead_kernel(parts, own_ref, weight_ref, *refs):
+
+
+def slots(row, count, back_ref):
+    places = [row[0, k] for k in range(count)]
+    lane = lax.broadcasted_iota(jnp.int32, back_ref.shape, 1)
+    back = jnp.zeros(back_ref.shape, jnp.int32)
+    for k, place in enumerate(places):
+        back = jnp.where(lane == place, k, back)
+    back_ref[...] = back
+    return places
+
+
+def first_kernel(packed_level, own_ref, coupling_hbm, roster_hbm, *refs):
+    own_out, other_out, back_ref, roster_ref, packed_ref, *outs, weight_ref, sems = refs
+    blocks = own_ref.shape[0]
+    parts = [pl.ds(4 * n, 4) for n in range(blocks // 4)]
+    count = packed_ref.shape[0] - 1
+    copies = started(
+        [(roster_hbm, roster_ref)]
+        + [(coupling_hbm.at[0, part], weight_ref.at[part]) for part in parts]
+        + [(coupling_hbm.at[packed_level], packed_ref.at[pl.ds(0, count)])]
+        + [(coupling_hbm.at[1 + n], out) for n, out in enumerate(outs)],
+        sems,
+    )
+    copies[0].wait()
+    packed_ref[count, 0, 0:8, 0:blocks] = jnp.broadcast_to(roster_ref[packed_level].astype(F32), (8, blocks))
+    places = slots(roster_ref[0], blocks, back_ref)
+    for k, place in enumerate(places):
+        if k % 4 == 0:
+            copies[1 + k // 4].wait()
+        own_wide, other_wide = arranged(weight_ref[k].reshape(128, 128))
+        other_out[place] = other_wide
+        own_out[place] = times(own_ref[k], own_wide)
+    finish(copies[1 + len(parts) :])
+
+
+def ahead_kernel(level, parts, own_ref, weight_ref, roster_ref, *refs):
     count = len(parts)
-    sources, own_out, other_out = refs[:count], refs[count], refs[count + 1]
-    outs, sems = refs[count + 2 : -1], refs[-1]
+    sources, own_out, other_out, back_ref = refs[:count], refs[count], refs[count + 1], refs[count + 2]
+    outs, sems = refs[count + 3 : -1], refs[-1]
     copies = started(
         [(source if part is None else source.at[part], out) for part, source, out in zip(parts, sources, outs)],
         sems,
     )
-    for k in range(own_ref.shape[0]):
+    for k, place in enumerate(slots(roster_ref[level], own_ref.shape[0], back_ref)):
         own_wide, other_wide = arranged(weight_ref[k].reshape(128, 128))
-        other_out[k] = other_wide
-        own_out[k] = times(own_ref[k], own_wide)
+        other_out[place] = other_wide
+        own_out[place] = times(own_ref[k], own_wide)
     finish(copies)
-
-
-def pack_kernel(level, weight_hbm, roster_ref, after_ref, out_ref, sem):
-    count = out_ref.shape[0] - 1
-    copy = pltpu.make_async_copy(weight_hbm.at[level], out_ref.at[pl.ds(0, count)], sem)
-    copy.start()
-    row = jnp.broadcast_to(roster_ref[level].astype(F32), (8, roster_ref.shape[2]))
-    out_ref[count, 0, 0:8, 0 : roster_ref.shape[2]] = row
-    copy.wait()
 
 
 def prepare_kernel(weight_ref, after_ref, own_out, other_out):
@@ -131,6 +152,11 @@
         own_out[k], other_out[k] = arranged(weight_ref[k].reshape(128, 128))
 
 
+def sorted_kernel(level, weight_ref, roster_ref, after_ref, own_out, other_out, back_ref):
+    for k, place in enumerate(slots(roster_ref[level], own_out.shape[0], back_ref)):
+        own_out[k], other_out[place] = arranged(weight_ref[k].reshape(128, 128))
+
+
 def spread_kernel(weight_ref, after_ref, out_ref):
     for k in range(out_ref.shape[0]):
         out_ref[k] = jnp.concatenate(split(weight_ref[k].reshape(128, 128)), axis=0)
@@ -141,12 +167,18 @@
         out_ref[k] = times(own_ref[k], wide_ref[k])
 
 
-def level_kernel(level, roster_ref, other_ref, wide_ref, ready_ref, *rest):
+def own_sorted_kernel(level, own_ref, wide_ref, roster_ref, out_ref):
+    row = roster_ref[level]
+    for k in range(out_ref.shape[0]):
+        out_ref[row[0, k]] = times(own_ref[k], wide_ref[k])
+
+
+def level_kernel(back_ref, other_ref, wide_ref, ready_ref, *rest):
     out_ref = rest[-1]
-    row = roster_ref[level]
-    places = [row[0, k] for k in range(out_ref.shape[0])]
-    for k, place in enumerate(places):
-        out_ref[k] = ready_ref[k] + times(other_ref[place], wide_ref[k])
+    row = back_ref[0:1, :]
+    blocks = [row[0, place] for place in range(out_ref.shape[0])]
+    for place, k in enumerate(blocks):
+        out_ref[k] = ready_ref[place] + times(other_ref[place], wide_ref[place])
 
 
 def corner_kernel(packed_ref, other_ref, wide_ref, out_ref):
@@ -275,31 +307,36 @@
     level_weights = VMEM(coupling.shape[1:], F32)
     coupling_hbm, near_hbm, expand_hbm, field_hbm = in_hbm(coupling, nearfield_dense_blocks, expand, field_in)
 
-    coeffs, first, names = call(
+    back = VMEM((8, 128), jnp.int32)
+    coeffs = call(
         compress_kernel,
-        [state, level_weights, VMEM(roster.shape, jnp.int32)],
-        [HBM] * 4,
-        [VMEM] * 3,
-        scratch=[VMEM(field_in.shape, F32), VMEM(compress.shape, F32), DMA((3 + blocks // 2,))],
-    )(*in_hbm(field_in, compress, coupling, roster))
-    weights = {0: first}
+        state,
+        [HBM] * 2,
+        scratch=[VMEM(field_in.shape, F32), VMEM(compress.shape, F32), DMA((1 + blocks // 2,))],
+    )(*in_hbm(field_in, compress))
+    weights = {}
 
     def ahead(position, coeffs, levels=(), whole=()):
         parts = list(levels) + [None] * len(whole)
         sources = [coupling_hbm] * len(levels) + list(whole)
         shapes = [level_weights] * len(levels) + [VMEM(array.shape, array.dtype) for array in whole]
-        ready, other, *got = call(
-            functools.partial(ahead_kernel, parts),
-            [state, wide] + shapes,
-            [VMEM] * 2 + [HBM] * len(sources),
-            [VMEM] * (2 + len(shapes)),
-            [DMA((len(parts),))],
-        )(coeffs, weights[position], *sources)
+        ready, other, places, *got = call(
+            functools.partial(ahead_kernel, position, parts),
+            [state, wide, back] + shapes,
+            [VMEM] * 3 + [HBM] * len(sources),
+            [VMEM] * (3 + len(shapes)),
+            [DMA((max(len(parts), 1),))],
+        )(coeffs, weights[position], names, *sources)
         weights.update(dict(zip(levels, got)))
-        return ready, other, got[len(levels) :]
+        return ready, other, places, got[len(levels) :]
 
     def prepared(weight, after):
         return call(prepare_kernel, [wide, wide], [VMEM, ANY], [VMEM] * 2)(weight, after)
+
+    def prepared_sorted(position, weight, after):
+        return call(
+            functools.partial(sorted_kernel, position), [wide, wide, back], [VMEM, VMEM, ANY], [VMEM] * 3
+        )(weight, names, after)
 
     def near_piece(number, after):
         begin, count = NEAR_PARTS[number]
@@ -310,49 +347,64 @@
     def own_part(own, wide_own):
         return call(own_kernel, state, [VMEM] * 2)(own, wide_own)
 
-    def level_of(position, other, wide_other, ready, extra):
-        return call(
-            functools.partial(level_kernel, position), state, [VMEM] * 4 + [ANY] * len(extra)
-        )(names, other, wide_other, ready, *extra)
-
-    extra_levels = {0: (1,), 1: (2,), 2: (3, 7), 3: (4,), 4: (5,), 5: ()}
-    extra_whole = {1: (near_hbm, field_hbm), 4: (expand_hbm,)}
+    def own_sorted(position, own, wide_own):
+        return call(functools.partial(own_sorted_kernel, position), state, [VMEM] * 3)(own, wide_own, names)
+
+    def level_of(places, other, wide_other, ready, extra):
+        return call(level_kernel, state, [VMEM] * 4 + [ANY] * len(extra))(places, other, wide_other, ready, *extra)
+
+    extra_levels = {1: (3,), 2: (4,), 4: (5, 7), 5: ()}
+    extra_whole = {4: (near_hbm, field_hbm, expand_hbm)}
     for position, (axis, mask) in enumerate(plan[:-2]):
         other = flipped(coeffs, axis, mask)
         extra = []
-        ready, wide_other, got = ahead(position, coeffs, extra_levels[position], extra_whole.get(position, ()))
         if position == 0:
             far = flipped(tied(field_in, coeffs), "sub", 2)
+            ready, wide_other, places, names, packed, weights[1], weights[2] = call(
+                functools.partial(first_kernel, 6),
+                [
+                    state,
+                    wide,
+                    back,
+                    VMEM(roster.shape, jnp.int32),
+                    VMEM((blocks + 1,) + coupling.shape[2:], F32),
+                    level_weights,
+                    level_weights,
+                ],
+                [VMEM, HBM, HBM],
+                [VMEM] * 7,
+                [level_weights, DMA((4 + blocks // 4,))],
+            )(coeffs, coupling_hbm, *in_hbm(roster))
+        elif position == 3:
+            ready = own_sorted(3, coeffs, third[0])
+            wide_other, places = third[1:]
+        else:
+            ready, wide_other, places, got = ahead(
+                position, coeffs, extra_levels[position], extra_whole.get(position, ())
+            )
         if position == 1:
-            dense, field = got
-            packed = call(
-                functools.partial(pack_kernel, 6),
-                VMEM((blocks + 1,) + coupling.shape[2:], F32),
-                [HBM, VMEM, ANY],
-                scratch=[DMA],
-            )(coupling_hbm, names, coeffs)
-            extra.append(packed)
+            away = flipped(tied(packed, coeffs), "leaf", top)
         if position == 2:
-            away = flipped(tied(packed, coeffs), "leaf", top)
+            third = prepared_sorted(3, weights[3], coeffs)
+            extra.append(third[0])
         if position == 4:
+            dense, field, expand_ready = got
             core = flipped(tied(field_in, coeffs), "sub", 1)
             both = flipped(tied(far, coeffs), "sub", 1)
-            sixth = prepared(packed, coeffs)
-            seventh = prepared(weights[7], coeffs)
-            extra += [sixth[0], seventh[0]]
+            sixth = prepared_sorted(6, packed, coeffs)
+            extra.append(sixth[0])
         if position == 5:
             last = call(spread_kernel, wide, [VMEM, ANY])(expand_ready, coeffs)
+            seventh = prepared(weights[7], coeffs)
             pieces = [near_piece(0, coeffs)]
-            extra += [last, pieces[0]]
-        if position == 4:
-            expand_ready = got[0]
-        coeffs = level_of(position, other, wide_other, ready, extra)
+            extra += [last, seventh[0], pieces[0]]
+        coeffs = level_of(places, other, wide_other, ready, extra)
     side = flipped(coeffs, "leaf", top // 2)
     corner = flipped(coeffs, "leaf", top // 2 + top)
     cross = flipped(coeffs, "leaf", top)
     pieces.append(near_piece(1, coeffs))
-    ready = own_part(coeffs, sixth[0])
-    here = level_of(6, side, sixth[1], ready, [pieces[1]])
+    ready = own_sorted(6, coeffs, sixth[0])
+    here = level_of(sixth[2], side, sixth[1], ready, [pieces[1]])
     ready = own_part(here, seventh[0])
     away_wide = prepared(away, ready)
     beside = call(corner_kernel, state, [VMEM] * 3)(away, corner, away_wide[1])

time: 48.5 us -> 64.5 us (1.33)
  waiting for transfers between devices: 6.69 us -> 24.5 us
  starting transfers between devices: 19.9 us -> 18.8 us
    ppermute x13, waiting for transfers between devices: 6.69 us -> 24.5 us  [flipped(): return lax.ppermute(value, axis, pairs)]
    ppermute x13, starting transfers between devices: 19.9 us -> 18.8 us  [flipped(): return lax.ppermute(value, axis, pairs)]
    pallas_call x3 -> x2, Pallas kernels: 1.6 us -> 1.07 us  [prepared(): call(prepare_kernel, [wide, wide], [VMEM, ANY], [VMEM] * 2)(weight, after)]
    pallas_call x15 -> x17, Pallas kernels: 14.8 us -> 15.1 us  [the longest x4 7.25 us: ahead(): call(functools.partial(ahead_kernel, position, parts), [state, wide, back...]
  transfers between devices with their start and end apart: 13 -> 13, of which waited for: 5 -> 8; matrix products, arithmetic and copies ran while one was open for 0% -> 0% of each run, Pallas kernels for 34% -> 25%
where the time goes in v6:
time: 64.5 us; the launch traced here: 64.4 us
  waiting for transfers between devices  24.5 us (38%)
  Pallas kernels  20.6 us (32%)
  starting transfers between devices  18.8 us (29%)
    ppermute x13, waiting for transfers between devices, flipped(): return lax.ppermute(value, axis, pairs)  24.5 us
    ppermute x13, starting transfers between devices, flipped(): return lax.ppermute(value, axis, pairs)  18.8 us
    pallas_call x4, Pallas kernels, ahead(): call(functools.partial(ahead_kernel, position, parts), [state, wide, back...  7.25 us
    pallas_call x1, Pallas kernels, on_device(): call(compress_kernel, state, [HBM] * 2, scratch=[VMEM(field_in.shape, F32...  2.56 us
    pallas_call x2, Pallas kernels, near_piece(): call(functools.partial(near_kernel, begin), VMEM((count, 2 * rhs, 128), F...  2.33 us
    pallas_call x1, Pallas kernels, on_device(): call(functools.partial(first_kernel, 6), [state, wide, back, VMEM(roster....  2.01 us
    pallas_call x7, Pallas kernels, level_of(): call(level_kernel, state, [VMEM] * 4 + [ANY] * len(extra))  1.68 us
    pallas_call x1, Pallas kernels, on_device(): call(functools.partial(last_kernel, 7), jax.ShapeDtypeStruct(field_in.sha...  1.46 us
  transfers between devices with their start and end apart: 13, of which 8 were waited for; matrix products, arithmetic and copies ran while one was open for 0% of the time, Pallas kernels for 25%

profile of v6, /device:TPU:64, one launch (start us, length us, event | category | flops | bytes accessed | tf_op | source)
XLA Modules:
  0.0 64.4 jit_solution(12466223914276107351)
XLA Ops:
  0.0 2.6 %shard_map.100.own_ref = f32[12,16,128]{2,1,0:T(8,128)S(1)} custom-call(f32[2,16,1536]{2,1,0:T(8,128)} %refs_3_.1, f32[12,2,64,128]{3,2,1,0:T(8,128)} %weight_hbm.1), custom_call_target="tpu_custom_call" | custom-call | flops 2000000 | bytes 1048576 | tf_op jit(solution)/shard_map/pallas_call | solution.py:311
  2.6 3.1 %collective-permute-start = (f32[12,16,128]{2,1,0:T(8,128)S(1)}, f32[12,16,128]{2,1,0:T(8,128)S(1)}, u32[]{:S(2)}, u32[]{:S(2)}) collective-permute-start(f32[12,16,128]{2,1,0:T(8,128)S(1)} %shard_map.100.own_ref), channel_id=1, source_target_pairs={{0,128},{4,132},{8,136},{12,140},{16,144},{20,148},{24,152},{28,15... | collective-permute-start | bytes 294920 | tf_op jit(solution)/shard_map/ppermute | solution.py:270
  5.7 2.0 %shard_map.101 = (f32[12,16,128]{2,1,0:T(8,128)S(1)}, bf16[12,256,128]{2,1,0:T(8,128)(2,1)S(1)}, s32[8,128]{1,0:T(8,128)S(1)}, s32[8,1,12]{2,1,0:T(1,128)S(1)}, ...) custom-call(f32[12,16,128]{2,1,0:T(8,128)S(1)} %shard_map.100.own_ref, ...), custom_call_target="tpu_custom_call" | custom-call | flops 2000000 | bytes 1048576 | tf_op jit(solution)/shard_map/pallas_call | solution.py:363
  7.7 1.1 %collective-permute-done.other_ref = f32[12,16,128]{2,1,0:T(8,128)S(1)} collective-permute-done((f32[12,16,128]{2,1,0:T(8,128)S(1)}, f32[12,16,128]{2,1,0:T(8,128)S(1)}, u32[]{:S(2)}, u32[]{:S(2)}) %collective-permute-start) | collective-permute-done | bytes 98336 | tf_op jit(solution)/shard_map/ppermute | solution.py:270
  8.8 0.2 shard_map.102.own_ref
  9.0 3.1 %collective-permute-start.10 = (f32[13,2,64,128]{3,2,1,0:T(8,128)S(1)}, f32[13,2,64,128]{3,2,1,0:T(8,128)S(1)}, u32[]{:S(2)}, u32[]{:S(2)}) collective-permute-start(f32[13,2,64,128]{3,2,1,0:T(8,128)S(1)} %get-tuple-element.79.weight_ref), channel_id=1, source_target_pairs={{0,128},{4,132},{8,136},{12,140},{16,144},{20,148},{24,152},{28,15... | collective-permute-start | bytes 2555912 | tf_op jit(solution)/shard_map/ppermute | solution.py:270
  12.1 0.6 collective-permute-start.1
  12.7 0.0 copy-start.4
  12.7 1.7 %shard_map.103 = (f32[12,16,128]{2,1,0:T(8,128)S(1)}, bf16[12,256,128]{2,1,0:T(8,128)(2,1)S(1)}, s32[8,128]{1,0:T(8,128)S(1)}, f32[12,2,64,128]{3,2,1,0:T(8,128)S(1)}) custom-call(f32[12,16,128]{2,1,0:T(8,128)S(1)} %shard_map.102.own_ref, f32[12,2,64,128]{3,2,1,0:T(8,128)S(1)} %get-tuple-element.49.weight_ref, s32[8,1,12]{2,1,0:T(1,128)S(1)} %get-tuple-element.45.roster_ref, ...), custom_call_target="tpu_custom_call" | custom-call | flops 2000000 | bytes 1048576 | tf_op jit(solution)/shard_map/pallas_call | solution.py:323
  14.4 17.9 %collective-permute-done.1.other_ref = f32[12,16,128]{2,1,0:T(8,128)S(1)} collective-permute-done((f32[12,16,128]{2,1,0:T(8,128)S(1)}, f32[12,16,128]{2,1,0:T(8,128)S(1)}, u32[]{:S(2)}, u32[]{:S(2)}) %collective-permute-start.1) | collective-permute-done | bytes 98336 | tf_op jit(solution)/shard_map/ppermute | solution.py:270
  32.3 0.2 shard_map.104.after_ref.own_ref
  32.6 1.7 %collective-permute-start.2 = (f32[12,16,128]{2,1,0:T(8,128)S(1)}, f32[12,16,128]{2,1,0:T(8,128)S(1)}, u32[]{:S(2)}, u32[]{:S(2)}) collective-permute-start(f32[12,16,128]{2,1,0:T(8,128)S(1)} %shard_map.104.after_ref.own_ref), channel_id=1, source_target_pairs={{0,32},{4,36},{8,40},{12,44},{16,48},{20,52},{24,56},{28,60},{32,0... | collective-permute-start | bytes 294920 | tf_op jit(solution)/shard_map/ppermute | solution.py:270
  34.2 0.0 copy-done.4
  34.2 2.9 %collective-permute-start.7 = (f32[2,16,1536]{2,1,0:T(8,128)S(1)}, f32[2,16,1536]{2,1,0:T(8,128)S(1)}, u32[]{:S(2)}, u32[]{:S(2)}) collective-permute-start(f32[2,16,1536]{2,1,0:T(8,128)S(1)} %copy-done.4), channel_id=1, source_target_pairs={{0,2},{1,3},{2,0},{3,1},{4,6},{5,7},{6,4},{7,5},{8,10},{9,11},{10,... | collective-permute-start | bytes 589832 | tf_op jit(solution)/shard_map/ppermute | solution.py:270
  37.1 0.5 shard_map.105
  37.7 1.7 %shard_map.106 = (f32[12,16,128]{2,1,0:T(8,128)S(1)}, bf16[12,256,128]{2,1,0:T(8,128)(2,1)S(1)}, s32[8,128]{1,0:T(8,128)S(1)}, f32[12,2,64,128]{3,2,1,0:T(8,128)S(1)}) custom-call(f32[12,16,128]{2,1,0:T(8,128)S(1)} %shard_map.104.after_ref.own_ref, f32[12,2,64,128]{3,2,1,0:T(8,128)S(1)} %get-tuple-element.55.weight_ref, ...), custom_call_target="tpu_custom_call" | custom-call | flops 2000000 | bytes 1048576 | tf_op jit(solution)/shard_map/pallas_call | solution.py:323
  39.4 0.0 collective-permute-done.2.other_ref
  39.4 0.2 shard_map.107.own_ref
  39.6 0.1 collective-permute-start.3
  39.7 0.2 shard_map.108.ready_ref
  40.0 1.0 %collective-permute-done.3.other_ref = f32[12,16,128]{2,1,0:T(8,128)S(1)} collective-permute-done((f32[12,16,128]{2,1,0:T(8,128)S(1)}, f32[12,16,128]{2,1,0:T(8,128)S(1)}, u32[]{:S(2)}, u32[]{:S(2)}) %collective-permute-start.3) | collective-permute-done | bytes 98336 | tf_op jit(solution)/shard_map/ppermute | solution.py:270
  41.0 0.2 shard_map.109.own_ref.after_ref
  41.3 0.2 collective-permute-start.6
  41.5 0.3 collective-permute-done.7.far_ref
  41.9 0.0 collective-permute-start.8
  41.9 2.4 %collective-permute-start.4 = (f32[12,16,128]{2,1,0:T(8,128)S(1)}, f32[12,16,128]{2,1,0:T(8,128)S(1)}, u32[]{:S(2)}, u32[]{:S(2)}) collective-permute-start(f32[12,16,128]{2,1,0:T(8,128)S(1)} %shard_map.109.own_ref.after_ref), channel_id=1, source_target_pairs={{0,2},{1,3},{2,0},{3,1},{4,6},{5,7},{6,4},{7,5},{8,10},{9,11},{10,... | collective-permute-start | bytes 294920 | tf_op jit(solution)/shard_map/ppermute | solution.py:270
  44.3 0.5 shard_map.111
  44.9 3.2 %shard_map.110 = (f32[12,16,128]{2,1,0:T(8,128)S(1)}, bf16[12,256,128]{2,1,0:T(8,128)(2,1)S(1)}, s32[8,128]{1,0:T(8,128)S(1)}, f32[12,2,64,128]{3,2,1,0:T(8,128)...) custom-call(f32[12,16,128]{2,1,0:T(8,128)S(1)} %shard_map.109.own_re, ...), custom_call_target="tpu_custom_call" | custom-call | flops 2000000 | bytes 1048576 | tf_op jit(solution)/shard_map/pallas_call | solution.py:323
  48.1 0.0 copy-start
  48.1 0.0 copy-start.1
  48.1 0.0 copy-start.2
  48.1 0.0 copy-start.3
  48.1 0.4 collective-permute-done.4.other_ref
  48.6 0.2 shard_map.112.own_ref.after_ref.rest_0_
  48.8 0.3 collective-permute-start.5
  49.1 0.7 %shard_map.113 = (f32[12,16,128]{2,1,0:T(8,128)S(1)}, bf16[12,256,128]{2,1,0:T(8,128)(2,1)S(1)}, s32[8,128]{1,0:T(8,128)S(1)}) custom-call(f32[12,16,128]{2,1,0:T(8,128)S(1)} %shard_map.112.own_ref.after_ref.rest_0_, f32[12,2,64,128]{3,2,1,0:T(8,128)S(1)} %get-tuple-element.67.weight_ref, s32[8,1,12]{2,1,0:T(1,128)S(1)} %get-tuple-element.45.roster_ref), custom_call_target="tpu_custom_call" | custom-call | flops 2000000 | bytes 1048576 | tf_op jit(solution)/shard_map/pallas_call | solution.py:323
  49.7 0.1 shard_map.114.rest_0_.expand_ref
  49.8 0.5 shard_map.115
  50.4 0.0 collective-permute-done.6.core_ref
  50.4 0.0 collective-permute-done.8.both_ref
  50.4 0.0 copy-done
  50.4 0.0 copy-done.1
  50.4 0.0 copy-done.2
  50.4 0.0 copy-done.3
  50.4 1.0 %shard_map.116.rest_2_.rest_0_ = f32[4,32,128]{2,1,0:T(8,128)S(1)} custom-call(s32[2,12]{1,0:T(2,128)S(1)} %bitcast.6, s32[2,12]{1,0:T(2,128)S(1)} %bitcast.8, s32[2,12]{1,0:T(2,128)S(1)} %bitcast.10, s32[4,4]{1,0:T(4,128)S(1)} %bitcast.4, f32[2,16,1536]{2,1,0:T(8,128)S(1)} %get-tuple-element.74.own_ref, f32[2,16,1536]{2,1,0:T(8,128)S(1)} %collective-permute-done.6.core_ref, ...), custom_call_target="tpu_custom_call" | custom-call | flops 2000000 | bytes 1048576 | tf_op jit(solution)/shard_map/pallas_call | solution.py:343
  51.5 2.0 %collective-permute-done.5.other_ref = f32[12,16,128]{2,1,0:T(8,128)S(1)} collective-permute-done((f32[12,16,128]{2,1,0:T(8,128)S(1)}, f32[12,16,128]{2,1,0:T(8,128)S(1)}, u32[]{:S(2)}, u32[]{:S(2)}) %collective-permute-start.5) | collective-permute-done | bytes 98336 | tf_op jit(solution)/shard_map/ppermute | solution.py:270
  53.5 0.2 shard_map.117.own_ref.rest_0_
  53.8 1.7 %collective-permute-start.11 = (f32[12,16,128]{2,1,0:T(8,128)S(1)}, f32[12,16,128]{2,1,0:T(8,128)S(1)}, u32[]{:S(2)}, u32[]{:S(2)}) collective-permute-start(f32[12,16,128]{2,1,0:T(8,128)S(1)} %shard_map.117.own_ref.rest_0_), channel_id=1, source_target_pairs={{0,64},{4,68},{8,72},{12,76},{16,80},{20,84},{24,88},{28,92},{32,9... | collective-permute-start | bytes 294920 | tf_op jit(solution)/shard_map/ppermute | solution.py:270
  55.5 1.2 %collective-permute-start.12 = (f32[12,16,128]{2,1,0:T(8,128)S(1)}, f32[12,16,128]{2,1,0:T(8,128)S(1)}, u32[]{:S(2)}, u32[]{:S(2)}) collective-permute-start(f32[12,16,128]{2,1,0:T(8,128)S(1)} %shard_map.117.own_ref.rest_0_), channel_id=1, source_target_pairs={{0,192},{4,196},{8,200},{12,204},{16,208},{20,212},{24,216},{28,22... | collective-permute-start | bytes 294920 | tf_op jit(solution)/shard_map/ppermute | solution.py:270
  56.6 1.5 %collective-permute-start.9 = (f32[12,16,128]{2,1,0:T(8,128)S(1)}, f32[12,16,128]{2,1,0:T(8,128)S(1)}, u32[]{:S(2)}, u32[]{:S(2)}) collective-permute-start(f32[12,16,128]{2,1,0:T(8,128)S(1)} %shard_map.117.own_ref.rest_0_), channel_id=1, source_target_pairs={{0,128},{4,132},{8,136},{12,140},{16,144},{20,148},{24,152},{28,15... | collective-permute-start | bytes 294920 | tf_op jit(solution)/shard_map/ppermute | solution.py:270
  58.1 0.2 shard_map.118.ready_ref
  58.4 1.3 %shard_map.119.rest_0_.rest_1_ = f32[8,32,128]{2,1,0:T(8,128)S(1)} custom-call(s32[2,12]{1,0:T(2,128)S(1)} %bitcast.7, s32[2,12]{1,0:T(2,128)S(1)} %bitcast.9, s32[2,12]{1,0:T(2,128)S(1)} %bitcast.11, s32[4,4]{1,0:T(4,128)S(1)} %bitcast.5, f32[2,16,1536]{2,1,0:T(8,128)S(1)} %get-tuple-element.74.own_ref, f32[2,16,1536]{2,1,0:T(8,128)S(1)} %collective-permute-done.6.core_ref, ...), custom_call_target="tpu_custom_call" | custom-call | flops 2000000 | bytes 1048576 | tf_op jit(solution)/shard_map/pallas_call | solution.py:343
  59.7 0.0 collective-permute-done.11.other_ref
  59.7 0.2 shard_map.120.own_ref
  60.0 0.2 shard_map.121.after_ref.ready_ref
  60.2 0.0 collective-permute-done.10.weight_ref.packed_ref
  60.3 0.5 shard_map.122
  60.8 0.5 collective-permute-done.12.other_ref
  61.3 0.3 shard_map.123.corner_ref
  61.6 1.1 %collective-permute-done.9.cross_ref = f32[12,16,128]{2,1,0:T(8,128)S(1)} collective-permute-done((f32[12,16,128]{2,1,0:T(8,128)S(1)}, f32[12,16,128]{2,1,0:T(8,128)S(1)}, u32[]{:S(2)}, u32[]{:S(2)}) %collective-permute-start.9) | collective-permute-done | bytes 98336 | tf_op jit(solution)/shard_map/ppermute | solution.py:270
  62.7 1.5 %shard_map.124 = f32[2,16,1536]{2,1,0:T(8,128)} custom-call(s32[8,1,12]{2,1,0:T(1,128)S(1)} %get-tuple-element.45.roster_ref, f32[12,16,128]{2,1,0:T(8,128)S(1)} %collective-permute-done.9.cross_ref, bf16[12,256,128]{2,1,0:T(8,128)(2,1)S(1)} %get-tuple-element.82.away_ref, f32[12,16,128]{2,1,0:T(8,128)S(1)} %shard_map.123.corner_ref, ...), custom_call_target="tpu_custom_call" | custom-call | flops 2000000 | bytes 1048576 | tf_op jit(solution)/shard_map/pallas_call | solution.py:411
Async XLA Ops:
  2.6 6.2 %collective-permute-start = (f32[12,16,128]{2,1,0:T(8,128)S(1)}, f32[12,16,128]{2,1,0:T(8,128)S(1)}, u32[]{:S(2)}, u32[]{:S(2)}) collective-permute-start(f32[12,16,128]{2,1,0:T(8,128)S(1)} %shard_map.100.own_ref), channel_id=1, source_target_pairs={{0,128},{4,132},{8,136},{12,140},{16,144},{20,148},{24,152},{28,15... | collective-permute-start | bytes 294920 | tf_op jit(solution)/shard_map/ppermute | solution.py:270
  9.0 51.2 %collective-permute-start.10 = (f32[13,2,64,128]{3,2,1,0:T(8,128)S(1)}, f32[13,2,64,128]{3,2,1,0:T(8,128)S(1)}, u32[]{:S(2)}, u32[]{:S(2)}) collective-permute-start(f32[13,2,64,128]{3,2,1,0:T(8,128)S(1)} %get-tuple-element.79.weight_ref), channel_id=1, source_target_pairs={{0,128},{4,132},{8,136},{12,140},{16,144},{20,148},{24,152},{28,15... | collective-permute-start | bytes 2555912 | tf_op jit(solution)/shard_map/ppermute | solution.py:270
  12.1 20.2 %collective-permute-start.1 = (f32[12,16,128]{2,1,0:T(8,128)S(1)}, f32[12,16,128]{2,1,0:T(8,128)S(1)}, u32[]{:S(2)}, u32[]{:S(2)}) collective-permute-start(f32[12,16,128]{2,1,0:T(8,128)S(1)} %shard_map.102.own_ref), channel_id=1, source_target_pairs={{0,64},{4,68},{8,72},{12,76},{16,80},{20,84},{24,88},{28,92},{32,9... | collective-permute-start | bytes 294920 | tf_op jit(solution)/shard_map/ppermute | solution.py:270
  12.7 21.5 %copy-start.4 = (f32[2,16,1536]{2,1,0:T(8,128)S(1)}, f32[2,16,1536]{2,1,0:T(8,128)}, u32[]{:S(2)}) copy-start(f32[2,16,1536]{2,1,0:T(8,128)} %refs_3_.1) | copy-start | bytes 589828
  32.6 6.8 %collective-permute-start.2 = (f32[12,16,128]{2,1,0:T(8,128)S(1)}, f32[12,16,128]{2,1,0:T(8,128)S(1)}, u32[]{:S(2)}, u32[]{:S(2)}) collective-permute-start(f32[12,16,128]{2,1,0:T(8,128)S(1)} %shard_map.104.after_ref.own_ref), channel_id=1, source_target_pairs={{0,32},{4,36},{8,40},{12,44},{16,48},{20,52},{24,56},{28,60},{32,0... | collective-permute-start | bytes 294920 | tf_op jit(solution)/shard_map/ppermute | solution.py:270
  34.2 7.6 %collective-permute-start.7 = (f32[2,16,1536]{2,1,0:T(8,128)S(1)}, f32[2,16,1536]{2,1,0:T(8,128)S(1)}, u32[]{:S(2)}, u32[]{:S(2)}) collective-permute-start(f32[2,16,1536]{2,1,0:T(8,128)S(1)} %copy-done.4), channel_id=1, source_target_pairs={{0,2},{1,3},{2,0},{3,1},{4,6},{5,7},{6,4},{7,5},{8,10},{9,11},{10,... | collective-permute-start | bytes 589832 | tf_op jit(solution)/shard_map/ppermute | solution.py:270
  39.6 1.4 %collective-permute-start.3 = (f32[12,16,128]{2,1,0:T(8,128)S(1)}, f32[12,16,128]{2,1,0:T(8,128)S(1)}, u32[]{:S(2)}, u32[]{:S(2)}) collective-permute-start(f32[12,16,128]{2,1,0:T(8,128)S(1)} %shard_map.107.own_ref), channel_id=1, source_target_pairs={{0,1},{1,0},{2,3},{3,2},{4,5},{5,4},{6,7},{7,6},{8,9},{9,8},{10,11... | collective-permute-start | bytes 294920 | tf_op jit(solution)/shard_map/ppermute | solution.py:270
  41.3 9.1 %collective-permute-start.6 = (f32[2,16,1536]{2,1,0:T(8,128)S(1)}, f32[2,16,1536]{2,1,0:T(8,128)S(1)}, u32[]{:S(2)}, u32[]{:S(2)}) collective-permute-start(f32[2,16,1536]{2,1,0:T(8,128)S(1)} %copy-done.4), channel_id=1, source_target_pairs={{0,1},{1,0},{2,3},{3,2},{4,5},{5,4},{6,7},{7,6},{8,9},{9,8},{10,11... | collective-permute-start | bytes 589832 | tf_op jit(solution)/shard_map/ppermute | solution.py:270
  41.9 8.5 %collective-permute-start.8 = (f32[2,16,1536]{2,1,0:T(8,128)S(1)}, f32[2,16,1536]{2,1,0:T(8,128)S(1)}, u32[]{:S(2)}, u32[]{:S(2)}) collective-permute-start(f32[2,16,1536]{2,1,0:T(8,128)S(1)} %collective-permute-done.7.far_ref), channel_id=1, source_target_pairs={{0,1},{1,0},{2,3},{3,2},{4,5},{5,4},{6,7},{7,6},{8,9},{9,8},{10,11... | collective-permute-start | bytes 589832 | tf_op jit(solution)/shard_map/ppermute | solution.py:270
  41.9 6.7 %collective-permute-start.4 = (f32[12,16,128]{2,1,0:T(8,128)S(1)}, f32[12,16,128]{2,1,0:T(8,128)S(1)}, u32[]{:S(2)}, u32[]{:S(2)}) collective-permute-start(f32[12,16,128]{2,1,0:T(8,128)S(1)} %shard_map.109.own_ref.after_ref), channel_id=1, source_target_pairs={{0,2},{1,3},{2,0},{3,1},{4,6},{5,7},{6,4},{7,5},{8,10},{9,11},{10,... | collective-permute-start | bytes 294920 | tf_op jit(solution)/shard_map/ppermute | solution.py:270
  48.1 2.3 %copy-start = (s32[1,4,4]{2,1,0:T(4,128)S(1)}, s32[1,4,4]{2,1,0:T(4,128)}, u32[]{:S(2)}) copy-start(s32[1,4,4]{2,1,0:T(4,128)} %param.19) | copy-start | bytes 196
  48.1 2.3 %copy-start.1 = (s32[12,2]{0,1:T(2,128)S(1)}, s32[12,2]{0,1:T(2,128)}, u32[]{:S(2)}) copy-start(s32[12,2]{0,1:T(2,128)} %param.16) | copy-start | bytes 292
  48.1 2.3 %copy-start.2 = (s32[12,2]{0,1:T(2,128)S(1)}, s32[12,2]{0,1:T(2,128)}, u32[]{:S(2)}) copy-start(s32[12,2]{0,1:T(2,128)} %param.17) | copy-start | bytes 292
  48.1 2.3 %copy-start.3 = (s32[12,2]{0,1:T(2,128)S(1)}, s32[12,2]{0,1:T(2,128)}, u32[]{:S(2)}) copy-start(s32[12,2]{0,1:T(2,128)} %param.18) | copy-start | bytes 292
  48.8 4.7 %collective-permute-start.5 = (f32[12,16,128]{2,1,0:T(8,128)S(1)}, f32[12,16,128]{2,1,0:T(8,128)S(1)}, u32[]{:S(2)}, u32[]{:S(2)}) collective-permute-start(f32[12,16,128]{2,1,0:T(8,128)S(1)} %shard_map.112.own_ref.after_ref.rest_0_), channel_id=1, source_target_pairs={{0,32},{4,36},{8,40},{12,44},{16,48},{20,52},{24,56},{28,60},{32,0... | collective-permute-start | bytes 294920 | tf_op jit(solution)/shard_map/ppermute | solution.py:270
  53.8 6.0 %collective-permute-start.11 = (f32[12,16,128]{2,1,0:T(8,128)S(1)}, f32[12,16,128]{2,1,0:T(8,128)S(1)}, u32[]{:S(2)}, u32[]{:S(2)}) collective-permute-start(f32[12,16,128]{2,1,0:T(8,128)S(1)} %shard_map.117.own_ref.rest_0_), channel_id=1, source_target_pairs={{0,64},{4,68},{8,72},{12,76},{16,80},{20,84},{24,88},{28,92},{32,9... | collective-permute-start | bytes 294920 | tf_op jit(solution)/shard_map/ppermute | solution.py:270
  55.5 5.8 %collective-permute-start.12 = (f32[12,16,128]{2,1,0:T(8,128)S(1)}, f32[12,16,128]{2,1,0:T(8,128)S(1)}, u32[]{:S(2)}, u32[]{:S(2)}) collective-permute-start(f32[12,16,128]{2,1,0:T(8,128)S(1)} %shard_map.117.own_ref.rest_0_), channel_id=1, source_target_pairs={{0,192},{4,196},{8,200},{12,204},{16,208},{20,212},{24,216},{28,22... | collective-permute-start | bytes 294920 | tf_op jit(solution)/shard_map/ppermute | solution.py:270
  56.6 6.1 %collective-permute-start.9 = (f32[12,16,128]{2,1,0:T(8,128)S(1)}, f32[12,16,128]{2,1,0:T(8,128)S(1)}, u32[]{:S(2)}, u32[]{:S(2)}) collective-permute-start(f32[12,16,128]{2,1,0:T(8,128)S(1)} %shard_map.117.own_ref.rest_0_), channel_id=1, source_target_pairs={{0,128},{4,132},{8,136},{12,140},{16,144},{20,148},{24,152},{28,15... | collective-permute-start | bytes 294920 | tf_op jit(solution)/shard_map/ppermute | solution.py:270

commit v7 on v6

v7 whole, which is shorter than its diff:
```python
import functools

import jax
import jax.numpy as jnp
from jax import lax
from jax.experimental import pallas as pl
from jax.experimental.pallas import tpu as pltpu
from jax.sharding import PartitionSpec as P


VMEM = pltpu.VMEM
SMEM = pltpu.SMEM
ANY = pl.ANY
HBM = pltpu.HBM
DMA = pltpu.SemaphoreType.DMA
BF = jnp.bfloat16
F32 = jnp.float32
NT = (((1,), (1,)), ((), ()))
NN = (((1,), (0,)), ((), ()))
NEAR_PARTS = ((0, 4), (4, 8))


def split(value):
    high = value.astype(BF)
    return high, (value - high.astype(F32)).astype(BF)


def widened(rows):
    high, low = split(rows)
    return jnp.concatenate(
        [
            jnp.concatenate([high, high], axis=1),
            jnp.concatenate([low, jnp.zeros_like(low)], axis=1),
        ],
        axis=0,
    )


def folded(result):
    count = result.shape[0] // 2
    return result[:count] + result[count:]


def product(rows, weights):
    wide = jnp.concatenate(split(weights), axis=1)
    return folded(lax.dot_general(widened(rows), wide, NT, preferred_element_type=F32))


def times(rows, wide):
    return folded(lax.dot_general(widened(rows), wide, NN, preferred_element_type=F32))


def lane_low(shape):
    return lax.broadcasted_iota(jnp.int32, shape, 1) < 64


def joined(result):
    rhs = result.shape[0] // 2
    turned = pltpu.roll(result[rhs:], 64, axis=1)
    return result[:rhs] + jnp.where(lane_low(turned.shape), -turned, turned)


def filled(upper):
    turned = pltpu.roll(upper, 64, axis=1)
    lower = jnp.where(lane_low(turned.shape), -turned, turned)
    return jnp.concatenate(split(jnp.concatenate([upper, lower], axis=0)), axis=0)


def halves(block):
    flat = block.T
    return flat[:64], flat[64:]


def started(pairs, sems):
    copies = [pltpu.make_async_copy(source, out, sems.at[n]) for n, (source, out) in enumerate(pairs)]
    for copy in copies:
        copy.start()
    return copies


def finish(copies):
    for copy in copies:
        copy.wait()


def compress_kernel(field_hbm, weight_hbm, out_ref, field_ref, weight_ref, sems):
    blocks = out_ref.shape[0]
    half = blocks // 2
    parts = [pl.ds(0, half), pl.ds(half, blocks - half)]
    copies = started(
        [(field_hbm, field_ref)] + [(weight_hbm.at[part], weight_ref.at[part]) for part in parts], sems
    )
    copies[0].wait()
    for k in range(blocks):
        if k % half == 0:
            copies[1 + k // half].wait()
        lanes = pl.ds(128 * k, 128)
        rows = jnp.concatenate([field_ref[0, :, lanes], field_ref[1, :, lanes]], axis=0)
        out_ref[k] = joined(product(rows, weight_ref[k].reshape(128, 128)))


def entries(row, count):
    return [row[0, k].astype(jnp.int32) for k in range(count)]


def slots(row, count, back_ref):
    places = entries(row, count)
    lane = lax.broadcasted_iota(jnp.int32, back_ref.shape, 1)
    back = jnp.zeros(back_ref.shape, jnp.int32)
    for k, place in enumerate(places):
        back = jnp.where(lane == place, k, back)
    back_ref[...] = back
    return places


def put_row(packed_ref, row):
    blocks = row.shape[1]
    packed_ref[blocks, 0:8, 0:blocks] = jnp.broadcast_to(row.astype(F32), (8, blocks))


def packed_row(packed_ref):
    blocks = packed_ref.shape[0] - 1
    return entries(packed_ref[blocks, 0:8, 0:blocks], blocks)


def prepare_block(k, place, weight_ref, own_out, other_out, packed_ref=None):
    own_half, other_half = halves(weight_ref[k].reshape(128, 128))
    own_out[k] = filled(own_half)
    other_out[place] = filled(other_half)
    if packed_ref is not None:
        packed_ref[k] = other_half


def first_kernel(own_ref, coupling_hbm, roster_hbm, *refs):
    ready_out, other_out, back_ref, roster_ref, own_4, other_4, packed_4, weight_1, weight_2, *rest = refs
    weight_0, weight_4, sems = rest
    blocks = own_ref.shape[0]
    copies = started(
        [(roster_hbm, roster_ref)]
        + [(coupling_hbm.at[n], out) for n, out in ((0, weight_0), (4, weight_4), (1, weight_1), (2, weight_2))],
        sems,
    )
    copies[0].wait()
    places = slots(roster_ref[0], blocks, back_ref)
    put_row(packed_4, roster_ref[4])
    copies[1].wait()
    for k, place in enumerate(places):
        own_half, other_half = halves(weight_0[k].reshape(128, 128))
        other_out[place] = filled(other_half)
        ready_out[place] = times(own_ref[k], filled(own_half))
    copies[2].wait()
    for k in range(blocks):
        prepare_block(k, k, weight_4, own_4, other_4, packed_4)
    finish(copies[3:])


def ahead_kernel(level, own_ref, weight_ref, roster_ref, coupling_hbm, *refs):
    ready_out, other_out, back_ref, weight_3, weight_6, sems = refs
    copies = started([(coupling_hbm.at[3], weight_3), (coupling_hbm.at[6], weight_6)], sems)
    for k, place in enumerate(slots(roster_ref[level], own_ref.shape[0], back_ref)):
        own_half, other_half = halves(weight_ref[k].reshape(128, 128))
        other_out[place] = filled(other_half)
        ready_out[place] = times(own_ref[k], filled(own_half))
    finish(copies)


def sorted_kernel(level, weight_ref, roster_ref, after_ref, own_out, other_out, back_ref):
    for k, place in enumerate(slots(roster_ref[level], own_out.shape[0], back_ref)):
        prepare_block(k, place, weight_ref, own_out, other_out)


def packed_kernel(level, weight_ref, roster_ref, after_ref, own_out, other_out, packed_ref):
    put_row(packed_ref, roster_ref[level])
    for k in range(own_out.shape[0]):
        prepare_block(k, k, weight_ref, own_out, other_out, packed_ref)


def fetch_kernel(levels, coupling_hbm, after_ref, *refs):
    count = len(levels)
    outs, weights, sems = refs[: 2 * count], refs[2 * count : -1], refs[-1]
    copies = started([(coupling_hbm.at[level], out) for level, out in zip(levels, weights)], sems)
    for n in range(count):
        copies[n].wait()
        for k in range(weights[n].shape[0]):
            prepare_block(k, k, weights[n], outs[2 * n], outs[2 * n + 1])


def unpack_kernel(packed_ref, after_ref, out_ref):
    for k in range(out_ref.shape[0]):
        out_ref[k] = filled(packed_ref[k])


def spread_kernel(weight_ref, after_ref, out_ref):
    for k in range(out_ref.shape[0]):
        out_ref[k] = jnp.concatenate(split(weight_ref[k].reshape(128, 128)), axis=0)


def own_kernel(own_ref, wide_ref, out_ref):
    for k in range(out_ref.shape[0]):
        out_ref[k] = times(own_ref[k], wide_ref[k])


def own_sorted_kernel(level, own_ref, wide_ref, roster_ref, out_ref):
    for k, place in enumerate(entries(roster_ref[level], out_ref.shape[0])):
        out_ref[place] = times(own_ref[k], wide_ref[k])


def level_kernel(back_ref, other_ref, wide_ref, ready_ref, *rest):
    out_ref = rest[-1]
    for place, k in enumerate(entries(back_ref[0:1, :], out_ref.shape[0])):
        out_ref[k] = ready_ref[place] + times(other_ref[place], wide_ref[place])


def plain_kernel(level, roster_ref, other_ref, wide_ref, ready_ref, *rest):
    out_ref = rest[-1]
    for k, place in enumerate(entries(roster_ref[level], out_ref.shape[0])):
        out_ref[k] = ready_ref[k] + times(other_ref[place], wide_ref[k])


def side_kernel(level, roster_ref, packed_ref, corner_ref, away_ref, beside_ref, wide_ref, out_ref, there_ref):
    blocks = out_ref.shape[0]
    for k, place in enumerate(packed_row(packed_ref)):
        there_ref[k] = beside_ref[k] + times(corner_ref[place], away_ref[k])
    for k, place in enumerate(entries(roster_ref[level], blocks)):
        out_ref[k] = times(there_ref[place], wide_ref[k])


def double_kernel(level, roster_ref, other_ref, wide_ref, ready_ref, next_ref, side_ref, *rest):
    out_ref, here_ref = rest[-2:]
    for k, place in enumerate(entries(roster_ref[level], out_ref.shape[0])):
        here_ref[k] = ready_ref[k] + times(other_ref[place], wide_ref[k])
    for k in range(out_ref.shape[0]):
        out_ref[k] = side_ref[k] + times(here_ref[k], next_ref[k])


def corner_kernel(packed_ref, other_ref, wide_ref, out_ref):
    for k, place in enumerate(packed_row(packed_ref)):
        out_ref[k] = times(other_ref[place], wide_ref[k])


def last_kernel(level, roster_ref, beside_ref, corner_ref, wide_ref, ready_ref, expand_ref, *rest):
    near_refs, (out_hbm, out_ref, sems) = rest[:-3], rest[-3:]
    blocks = beside_ref.shape[0]
    copies = []
    for k, place in enumerate(entries(roster_ref[level], blocks)):
        coeffs = ready_ref[k] + times(beside_ref[place] + corner_ref[place], wide_ref[k])
        signed = jnp.where(lane_low(coeffs.shape), coeffs, -coeffs)
        turned = pltpu.roll(coeffs, 64, axis=1)
        far = times(jnp.concatenate([signed, turned], axis=0), expand_ref[k])
        which = [n for n, (begin, count) in enumerate(NEAR_PARTS) if begin <= k < begin + count][0]
        total = far + near_refs[which][k - NEAR_PARTS[which][0]]
        half = total.shape[0] // 2
        lanes = pl.ds(128 * k, 128)
        out_ref[0, :, lanes] = total[:half]
        out_ref[1, :, lanes] = total[half:]
        if k % 4 == 3:
            part = pl.ds(128 * (k - 3), 512)
            copy = pltpu.make_async_copy(out_ref.at[:, :, part], out_hbm.at[:, :, part], sems.at[k // 4])
            copy.start()
            copies.append(copy)
    finish(copies)


def near_kernel(first, owner_ref, place_ref, valid_ref, pick_ref, own_ref, core_ref, far_ref, both_ref, weight_ref, *rest):
    out_ref = rest[-1]
    me = lax.axis_index("sub")
    for n in range(out_ref.shape[0]):
        k = first + n
        total = None
        for t in range(weight_ref.shape[1]):
            owner = owner_ref[t, k]
            leaf = pick_ref[owner, place_ref[t, k]]
            lanes = pl.ds(pl.multiple_of(leaf * 128, 128), 128)
            which = owner ^ me
            parts = []
            for d in range(2):
                low = jnp.where(which == 1, core_ref[d, :, lanes], own_ref[d, :, lanes])
                high = jnp.where(which == 3, both_ref[d, :, lanes], far_ref[d, :, lanes])
                parts.append(jnp.where(which >= 2, high, low))
            rows = jnp.concatenate(parts, axis=0) * valid_ref[t, k].astype(F32)
            result = product(rows, weight_ref[k, t].reshape(256, 128))
            half = result.shape[0] // 2
            term = jnp.concatenate(
                [result[:half, :128] - result[half:, 128:], result[half:, :128] + result[:half, 128:]], axis=0
            )
            total = term if total is None else total + term
        out_ref[n] = total


def spec(space):
    return pl.BlockSpec(memory_space=space)


def call(kernel, out, spaces, out_spaces=VMEM, scratch=(), flops=2_000_000):
    single = not isinstance(out_spaces, (list, tuple))
    return pl.pallas_call(
        kernel,
        out_shape=out,
        in_specs=[spec(space) for space in spaces],
        out_specs=spec(out_spaces) if single else [spec(space) for space in out_spaces],
        scratch_shapes=list(scratch),
        compiler_params=pltpu.CompilerParams(vmem_limit_bytes=8 << 20),
        cost_estimate=pl.CostEstimate(flops=flops, bytes_accessed=1 << 20, transcendentals=0),
    )


def in_hbm(*arrays):
    return [pltpu.with_memory_space_constraint(array, HBM) for array in arrays]


def flipped(value, leaf_mask, sub_mask):
    sub_count = lax.axis_size("sub")
    mask = leaf_mask * sub_count + sub_mask
    pairs = [(source, source ^ mask) for source in range(lax.axis_size("leaf") * sub_count)]
    return lax.ppermute(value, ("leaf", "sub"), pairs)


def tied(value, after):
    return lax.optimization_barrier((value, after))[0]


def on_device(
    field_in,
    compress,
    coupling,
    roster,
    expand,
    nearfield_dense_blocks,
    slot_owner_index,
    slot_source_position,
    slot_valid_mask,
    near_pick,
):
    blocks = compress.shape[0]
    rhs = field_in.shape[1]
    top = lax.axis_size("leaf") // 2
    pick = near_pick[0]
    indices = (slot_owner_index.T, slot_source_position.T, slot_valid_mask.T, pick)
    state = VMEM((blocks, rhs, 128), F32)
    wide = VMEM((blocks, 256, 128), BF)
    back = VMEM((8, 128), jnp.int32)
    packed = VMEM((blocks + 1, 64, 128), F32)
    level_weights = VMEM(coupling.shape[1:], F32)
    (coupling_hbm, _, roster_hbm) = in_hbm(coupling, field_in, roster)
    field = pltpu.with_memory_space_constraint(field_in, VMEM)
    dense = pltpu.with_memory_space_constraint(nearfield_dense_blocks, VMEM)
    expanding = pltpu.with_memory_space_constraint(expand, VMEM)

    def run(kernel, outs, inputs, after=(), scratch=(), hbm=()):
        spaces = [HBM if n in hbm else VMEM for n in range(len(inputs))] + [ANY] * len(after)
        several = isinstance(outs, list)
        return call(kernel, outs, spaces, [VMEM] * len(outs) if several else VMEM, scratch)(*inputs, *after)

    def near_piece(number, after):
        begin, count = NEAR_PARTS[number]
        return call(
            functools.partial(near_kernel, begin), VMEM((count, 2 * rhs, 128), F32), [SMEM] * 4 + [VMEM] * 5 + [ANY]
        )(*indices, field, core, far, both, dense, after)

    part = functools.partial
    coeffs = run(
        compress_kernel,
        state,
        in_hbm(field_in, compress),
        scratch=[VMEM(field_in.shape, F32), VMEM(compress.shape, F32), DMA((3,))],
        hbm=(0, 1),
    )

    other = flipped(coeffs, top, 0)
    ready, wide_0, back_0, names, own_4, wide_4, packed_4, weight_1, weight_2 = run(
        first_kernel,
        [state, wide, back, VMEM(roster.shape, jnp.int32), wide, wide, packed, level_weights, level_weights],
        [coeffs, coupling_hbm, roster_hbm],
        scratch=[level_weights, level_weights, DMA((5,))],
        hbm=(1, 2),
    )
    away_4 = flipped(packed_4, top // 4, 0)
    own_2, wide_2, back_2 = run(part(sorted_kernel, 2), [wide, wide, back], [weight_2, names], [coeffs])
    coeffs = run(level_kernel, state, [back_0, other, wide_0, ready], [own_2])

    other = flipped(coeffs, top // 2, 0)
    ready, wide_1, back_1, weight_3, weight_6 = run(
        part(ahead_kernel, 1),
        [state, wide, back, level_weights, level_weights],
        [coeffs, weight_1, names, coupling_hbm],
        scratch=[DMA((2,))],
        hbm=(3,),
    )
    own_3, wide_3, back_3 = run(part(sorted_kernel, 3), [wide, wide, back], [weight_3, names], [coeffs])
    own_6, wide_6, packed_6 = run(part(packed_kernel, 6), [wide, wide, packed], [weight_6, names], [coeffs])
    coeffs = run(level_kernel, state, [back_1, other, wide_1, ready], [own_3, own_6])

    other = flipped(coeffs, top // 4, 0)
    far = flipped(tied(field_in, coeffs), 0, 2)
    away_6 = flipped(tied(packed_6, coeffs), top, 0)
    ready = run(part(own_sorted_kernel, 2), state, [coeffs, own_2, names])
    coeffs = run(level_kernel, state, [back_2, other, wide_2, ready])

    other = flipped(coeffs, 0, 1)
    ready = run(part(own_sorted_kernel, 3), state, [coeffs, own_3, names])
    coeffs = run(level_kernel, state, [back_3, other, wide_3, ready])

    corner = flipped(coeffs, top // 4, 2)
    ready = run(own_kernel, state, [coeffs, own_4])
    beside = flipped(ready, top // 4, 0)
    other = flipped(coeffs, 0, 2)
    own_5, wide_5, own_7, wide_7 = run(
        part(fetch_kernel, (5, 7)),
        [wide] * 4,
        [coupling_hbm],
        [coeffs],
        scratch=[level_weights, level_weights, DMA((2,))],
        hbm=(0,),
    )
    core = flipped(tied(field_in, coeffs), 0, 1)
    both = flipped(tied(far, coeffs), 0, 1)
    away = run(unpack_kernel, wide, [away_4], [coeffs])
    side = run(part(side_kernel, 5), state, [names, away_4, corner, away, beside, wide_5], scratch=[state])
    coeffs = run(part(double_kernel, 4), state, [names, other, wide_4, ready, own_5, side], [own_7], scratch=[state])

    other = flipped(coeffs, top // 2, 0)
    ready = run(own_kernel, state, [coeffs, own_6])
    corner = flipped(coeffs, top // 2 + top, 0)
    beside = flipped(ready, top, 0)
    last = run(spread_kernel, wide, [expanding], [coeffs])
    away = run(unpack_kernel, wide, [away_6], [coeffs])
    pieces = [near_piece(n, coeffs) for n in range(len(NEAR_PARTS))]
    here = run(part(plain_kernel, 6), state, [names, other, wide_6, ready], [pieces[0]])
    ready = run(own_kernel, state, [here, own_7])
    corner = run(corner_kernel, state, [away_6, corner, away])
    return call(
        part(last_kernel, 7),
        jax.ShapeDtypeStruct(field_in.shape, F32),
        [VMEM] * (6 + len(pieces)),
        HBM,
        [VMEM(field_in.shape, F32), DMA((3,))],
    )(names, beside, corner, wide_7, ready, last, *pieces)


def solution(mesh):
    return jax.shard_map(
        on_device,
        mesh=mesh,
        in_specs=(
            P(None, None, ("leaf", "sub")),
            P(("leaf", "sub"), None, None, None),
            P(None, ("leaf", "sub"), None, None, None),
            P(None, ("leaf", "sub"), None),
            P(("leaf", "sub"), None, None, None),
            P(("leaf", "sub"), None, None, None, None),
            P(("leaf", "sub"), None),
            P(("leaf", "sub"), None),
            P(("leaf", "sub"), None),
            P(("leaf", "sub"), None, None),
        ),
        out_specs=P(None, None, ("leaf", "sub")),
        check_vma=False,
    )
```

time: 64.5 us -> 46.9 us (0.73)
  waiting for transfers between devices: 24.5 us -> 6.27 us
  starting transfers between devices: 18.8 us -> 21.9 us
  Pallas kernels: 20.6 us -> 17.9 us
    ppermute x13 -> x15, waiting for transfers between devices: 24.5 us -> 6.27 us  [flipped(): return lax.ppermute(value, ('leaf', 'sub'), pairs)]
    ppermute x13 -> x15, starting transfers between devices: 18.8 us -> 21.9 us  [flipped(): return lax.ppermute(value, ('leaf', 'sub'), pairs)]
    pallas_call x23 -> x24, Pallas kernels: 18.2 us -> 15.6 us  [the longest x23 14.3 us: run(): call(kernel, outs, spaces, [VMEM] * len(outs) if several else VMEM, scratch)]
  transfers between devices with their start and end apart: 13 -> 15, of which waited for: 8 -> 6; matrix products, arithmetic and copies ran while one was open for 0% -> 0% of each run, Pallas kernels for 25% -> 32%
where the time goes in v7:
time: 46.9 us; the launch traced here: 46.7 us
  starting transfers between devices  21.9 us (47%)
  Pallas kernels  17.9 us (38%)
  waiting for transfers between devices  6.27 us (13%)
  between operations  0.54 us (1%)
    ppermute x15, starting transfers between devices, flipped(): return lax.ppermute(value, ('leaf', 'sub'), pairs)  21.9 us
    pallas_call x23, Pallas kernels, run(): call(kernel, outs, spaces, [VMEM] * len(outs) if several else VMEM, scratch)  14.3 us
    ppermute x15, waiting for transfers between devices, flipped(): return lax.ppermute(value, ('leaf', 'sub'), pairs)  6.27 us
    pallas_call x2, Pallas kernels, near_piece(): call(functools.partial(near_kernel, begin), VMEM((count, 2 * rhs, 128), F...  2.34 us
    pallas_call x1, Pallas kernels, on_device(): call(part(last_kernel, 7), jax.ShapeDtypeStruct(field_in.shape, F32), [VM...  1.26 us
  transfers between devices with their start and end apart: 15, of which 6 were waited for; matrix products, arithmetic and copies ran while one was open for 0% of the time, Pallas kernels for 32%

profile of v7, /device:TPU:64, one launch (start us, length us, event | category | flops | bytes accessed | tf_op | source)
XLA Modules:
  0.0 46.7 jit_solution(14031422319906457082)
XLA Ops:
  0.0 1.8 %shard_map.100.own_ref.after_ref = f32[12,16,128]{2,1,0:T(8,128)S(1)} custom-call(f32[2,16,1536]{2,1,0:T(8,128)} %own_ref.3, f32[12,2,64,128]{3,2,1,0:T(8,128)} %weight_hbm.1), custom_call_target="tpu_custom_call" | custom-call | flops 2000000 | bytes 1048576 | tf_op jit(solution)/shard_map/pallas_call | solution.py:352
  1.8 3.1 %collective-permute-start = (f32[12,16,128]{2,1,0:T(8,128)S(1)}, f32[12,16,128]{2,1,0:T(8,128)S(1)}, u32[]{:S(2)}, u32[]{:S(2)}) collective-permute-start(f32[12,16,128]{2,1,0:T(8,128)S(1)} %shard_map.100.own_ref.after_ref), channel_id=1, source_target_pairs={{0,128},{1,129},{2,130},{3,131},{4,132},{5,133},{6,134},{7,135},{8... | collective-permute-start | bytes 294920 | tf_op jit(solution)/shard_map/ppermute | solution.py:315
  4.9 2.5 %shard_map.101 = (f32[12,16,128]{2,1,0:T(8,128)S(1)}, bf16[12,256,128]{2,1,0:T(8,128)(2,1)S(1)}, s32[8,128]{1,0:T(8,128)S(1)}, s32[8,1,12]{2,1,0:T(1,128)S(1)}, ...) custom-call(f32[12,16,128]{2,1,0:T(8,128)S(1)} %shard_map.100.own_re, ...), custom_call_target="tpu_custom_call" | custom-call | flops 2000000 | bytes 1048576 | tf_op jit(solution)/shard_map/pallas_call | solution.py:352
  7.4 1.7 %collective-permute-start.5 = (f32[13,64,128]{2,1,0:T(8,128)S(1)}, f32[13,64,128]{2,1,0:T(8,128)S(1)}, u32[]{:S(2)}, u32[]{:S(2)}) collective-permute-start(f32[13,64,128]{2,1,0:T(8,128)S(1)} %get-tuple-element.57), channel_id=1, source_target_pairs={{0,32},{1,33},{2,34},{3,35},{4,36},{5,37},{6,38},{7,39},{8,40},{9,... | collective-permute-start | bytes 1277960 | tf_op jit(solution)/shard_map/ppermute | solution.py:315
  9.1 0.5 %shard_map.102 = (bf16[12,256,128]{2,1,0:T(8,128)(2,1)S(1)}, bf16[12,256,128]{2,1,0:T(8,128)(2,1)S(1)}, s32[8,128]{1,0:T(8,128)S(1)}) custom-call(f32[12,2,64,128]{3,2,1,0:T(8,128)S(1)} %get-tuple-element.40.weight_ref, s32[8,1,12]{2,1,0:T(1,128)S(1)} %get-tuple-element.36.roster_ref, f32[12,16,128]{2,1,0:T(8,128)S(1)} %shard_map.100.own_ref.after_ref), custom_call_target="tpu_custom_call" | custom-call | flops 2000000 | bytes 1048576 | tf_op jit(solution)/shard_map/pallas_call | solution.py:352
  9.6 0.0 collective-permute-done.other_ref
  9.6 0.0 copy-start.1
  9.6 0.2 shard_map.103.own_ref.after_ref
  9.9 0.7 %collective-permute-start.1 = (f32[12,16,128]{2,1,0:T(8,128)S(1)}, f32[12,16,128]{2,1,0:T(8,128)S(1)}, u32[]{:S(2)}, u32[]{:S(2)}) collective-permute-start(f32[12,16,128]{2,1,0:T(8,128)S(1)} %shard_map.103.own_ref.after_ref), channel_id=1, source_target_pairs={{0,64},{1,65},{2,66},{3,67},{4,68},{5,69},{6,70},{7,71},{8,72},{9,... | collective-permute-start | bytes 294920 | tf_op jit(solution)/shard_map/ppermute | solution.py:315
  10.6 2.0 %shard_map.104 = (f32[12,16,128]{2,1,0:T(8,128)S(1)}, bf16[12,256,128]{2,1,0:T(8,128)(2,1)S(1)}, s32[8,128]{1,0:T(8,128)S(1)}, f32[12,2,64,128]{3,2,1,0:T(8,128)S(1)}, f32[12,2,64,128]{3,2,1,0:T(8,128)S(1)}) custom-call(f32[12,16,128]{2,1,0:T(8,128)S(1)} %shard_map.103.own_ref.after_ref, f32[12,2,64,128]{3,2,1,0:T(8,128)S(1)} %get-tuple-element.42.weight_ref, ...), custom_call_target="tpu_custom_call" | custom-call | flops 2000000 | bytes 1048576 | tf_op jit(solution)/shard_map/pallas_call | solution.py:352
  12.6 0.5 %shard_map.106 = (bf16[12,256,128]{2,1,0:T(8,128)(2,1)S(1)}, bf16[12,256,128]{2,1,0:T(8,128)(2,1)S(1)}, f32[13,64,128]{2,1,0:T(8,128)S(1)}) custom-call(f32[12,2,64,128]{3,2,1,0:T(8,128)S(1)} %get-tuple-element.50.weight_ref, s32[8,1,12]{2,1,0:T(1,128)S(1)} %get-tuple-element.36.roster_ref, f32[12,16,128]{2,1,0:T(8,128)S(1)} %shard_map.103.own_ref.after_ref), custom_call_target="tpu_custom_call" | custom-call | flops 2000000 | bytes 1048576 | tf_op jit(solution)/shard_map/pallas_call | solution.py:352
  13.1 0.5 %shard_map.105 = (bf16[12,256,128]{2,1,0:T(8,128)(2,1)S(1)}, bf16[12,256,128]{2,1,0:T(8,128)(2,1)S(1)}, s32[8,128]{1,0:T(8,128)S(1)}) custom-call(f32[12,2,64,128]{3,2,1,0:T(8,128)S(1)} %get-tuple-element.43.weight_ref, s32[8,1,12]{2,1,0:T(1,128)S(1)} %get-tuple-element.36.roster_ref, f32[12,16,128]{2,1,0:T(8,128)S(1)} %shard_map.103.own_ref.after_ref), custom_call_target="tpu_custom_call" | custom-call | flops 2000000 | bytes 1048576 | tf_op jit(solution)/shard_map/pallas_call | solution.py:352
  13.7 0.9 %collective-permute-done.1.other_ref = f32[12,16,128]{2,1,0:T(8,128)S(1)} collective-permute-done((f32[12,16,128]{2,1,0:T(8,128)S(1)}, f32[12,16,128]{2,1,0:T(8,128)S(1)}, u32[]{:S(2)}, u32[]{:S(2)}) %collective-permute-start.1) | collective-permute-done | bytes 98336 | tf_op jit(solution)/shard_map/ppermute | solution.py:315
  14.6 0.2 shard_map.107.own_ref
  14.8 0.5 %collective-permute-start.2 = (f32[12,16,128]{2,1,0:T(8,128)S(1)}, f32[12,16,128]{2,1,0:T(8,128)S(1)}, u32[]{:S(2)}, u32[]{:S(2)}) collective-permute-start(f32[12,16,128]{2,1,0:T(8,128)S(1)} %shard_map.107.own_ref), channel_id=1, source_target_pairs={{0,32},{1,33},{2,34},{3,35},{4,36},{5,37},{6,38},{7,39},{8,40},{9,... | collective-permute-start | bytes 294920 | tf_op jit(solution)/shard_map/ppermute | solution.py:315
  15.4 0.0 copy-done.1
  15.4 3.2 %collective-permute-start.13 = (f32[2,16,1536]{2,1,0:T(8,128)S(1)}, f32[2,16,1536]{2,1,0:T(8,128)S(1)}, u32[]{:S(2)}, u32[]{:S(2)}) collective-permute-start(f32[2,16,1536]{2,1,0:T(8,128)S(1)} %copy-done.1), channel_id=1, source_target_pairs={{0,2},{1,3},{2,0},{3,1},{4,6},{5,7},{6,4},{7,5},{8,10},{9,11},{10,... | collective-permute-start | bytes 589832 | tf_op jit(solution)/shard_map/ppermute | solution.py:315
  18.6 2.2 %collective-permute-start.9 = (f32[13,64,128]{2,1,0:T(8,128)S(1)}, f32[13,64,128]{2,1,0:T(8,128)S(1)}, u32[]{:S(2)}, u32[]{:S(2)}) collective-permute-start(f32[13,64,128]{2,1,0:T(8,128)S(1)} %get-tuple-element.61), channel_id=1, source_target_pairs={{0,128},{1,129},{2,130},{3,131},{4,132},{5,133},{6,134},{7,135},{8... | collective-permute-start | bytes 1277960 | tf_op jit(solution)/shard_map/ppermute | solution.py:315
  20.8 0.2 shard_map.108.ready_ref
  21.0 1.3 %collective-permute-done.2.other_ref = f32[12,16,128]{2,1,0:T(8,128)S(1)} collective-permute-done((f32[12,16,128]{2,1,0:T(8,128)S(1)}, f32[12,16,128]{2,1,0:T(8,128)S(1)}, u32[]{:S(2)}, u32[]{:S(2)}) %collective-permute-start.2) | collective-permute-done | bytes 98336 | tf_op jit(solution)/shard_map/ppermute | solution.py:315
  22.3 0.2 shard_map.109.own_ref
  22.5 0.1 collective-permute-start.3
  22.6 0.2 shard_map.110.ready_ref
  22.9 1.0 %collective-permute-done.3.other_ref = f32[12,16,128]{2,1,0:T(8,128)S(1)} collective-permute-done((f32[12,16,128]{2,1,0:T(8,128)S(1)}, f32[12,16,128]{2,1,0:T(8,128)S(1)}, u32[]{:S(2)}, u32[]{:S(2)}) %collective-permute-start.3) | collective-permute-done | bytes 98336 | tf_op jit(solution)/shard_map/ppermute | solution.py:315
  23.9 0.2 shard_map.111.own_ref.after_ref
  24.2 0.2 shard_map.112.ready_ref
  24.4 0.0 copy-start.2
  24.4 0.0 copy-start
  24.4 0.0 copy-start.3
  24.4 0.0 copy-start.4
  24.4 0.0 copy-start.5
  24.5 0.0 copy-start.6
  24.5 1.7 %collective-permute-start.7 = (f32[12,16,128]{2,1,0:T(8,128)S(1)}, f32[12,16,128]{2,1,0:T(8,128)S(1)}, u32[]{:S(2)}, u32[]{:S(2)}) collective-permute-start(f32[12,16,128]{2,1,0:T(8,128)S(1)} %shard_map.112.ready_ref), channel_id=1, source_target_pairs={{0,32},{1,33},{2,34},{3,35},{4,36},{5,37},{6,38},{7,39},{8,40},{9,... | collective-permute-start | bytes 294920 | tf_op jit(solution)/shard_map/ppermute | solution.py:315
  26.1 1.4 %collective-permute-done.13.far_ref = f32[2,16,1536]{2,1,0:T(8,128)S(1)} collective-permute-done((f32[2,16,1536]{2,1,0:T(8,128)S(1)}, f32[2,16,1536]{2,1,0:T(8,128)S(1)}, u32[]{:S(2)}, u32[]{:S(2)}) %collective-permute-start.13) | collective-permute-done | bytes 196640 | tf_op jit(solution)/shard_map/ppermute | solution.py:315
  27.5 0.0 collective-permute-start.14
  27.5 0.5 %collective-permute-start.12 = (f32[2,16,1536]{2,1,0:T(8,128)S(1)}, f32[2,16,1536]{2,1,0:T(8,128)S(1)}, u32[]{:S(2)}, u32[]{:S(2)}) collective-permute-start(f32[2,16,1536]{2,1,0:T(8,128)S(1)} %copy-done.1), channel_id=1, source_target_pairs={{0,1},{1,0},{2,3},{3,2},{4,5},{5,4},{6,7},{7,6},{8,9},{9,8},{10,11... | collective-permute-start | bytes 589832 | tf_op jit(solution)/shard_map/ppermute | solution.py:315
  28.0 0.0 collective-permute-done.5.packed_ref
  28.0 0.8 %collective-permute-start.6 = (f32[12,16,128]{2,1,0:T(8,128)S(1)}, f32[12,16,128]{2,1,0:T(8,128)S(1)}, u32[]{:S(2)}, u32[]{:S(2)}) collective-permute-start(f32[12,16,128]{2,1,0:T(8,128)S(1)} %shard_map.111.own_ref.after_ref), channel_id=1, source_target_pairs={{0,34},{1,35},{2,32},{3,33},{4,38},{5,39},{6,36},{7,37},{8,42},{9,... | collective-permute-start | bytes 294920 | tf_op jit(solution)/shard_map/ppermute | solution.py:315
  28.8 0.6 %collective-permute-done.7.beside_ref = f32[12,16,128]{2,1,0:T(8,128)S(1)} collective-permute-done((f32[12,16,128]{2,1,0:T(8,128)S(1)}, f32[12,16,128]{2,1,0:T(8,128)S(1)}, u32[]{:S(2)}, u32[]{:S(2)}) %collective-permute-start.7) | collective-permute-done | bytes 98336 | tf_op jit(solution)/shard_map/ppermute | solution.py:315
  29.4 3.2 %collective-permute-start.4 = (f32[12,16,128]{2,1,0:T(8,128)S(1)}, f32[12,16,128]{2,1,0:T(8,128)S(1)}, u32[]{:S(2)}, u32[]{:S(2)}) collective-permute-start(f32[12,16,128]{2,1,0:T(8,128)S(1)} %shard_map.111.own_ref.after_ref), channel_id=1, source_target_pairs={{0,2},{1,3},{2,0},{3,1},{4,6},{5,7},{6,4},{7,5},{8,10},{9,11},{10,... | collective-permute-start | bytes 294920 | tf_op jit(solution)/shard_map/ppermute | solution.py:315
  32.6 2.2 %shard_map.113 = (bf16[12,256,128]{2,1,0:T(8,128)(2,1)S(1)}, bf16[12,256,128]{2,1,0:T(8,128)(2,1)S(1)}, bf16[12,256,128]{2,1,0:T(8,128)(2,1)S(1)}, bf16[12,256,128]{2,1,0:T(8,128)(2,1)S(1)}) custom-call(f32[8,12,2,64,128]{4,3,2,1,0:T(8,128)} %coupling_hbm.5, f32[12,16,128]{2,1,0:T(8,128)S(1)} %shard_map.111.own_ref.after_ref), custom_call_target="tpu_custom_call" | custom-call | flops 2000000 | bytes 1048576 | tf_op jit(solution)/shard_map/pallas_call | solution.py:352
  34.8 0.2 shard_map.114.away_ref
  35.0 1.1 %collective-permute-done.6.corner_ref = f32[12,16,128]{2,1,0:T(8,128)S(1)} collective-permute-done((f32[12,16,128]{2,1,0:T(8,128)S(1)}, f32[12,16,128]{2,1,0:T(8,128)S(1)}, u32[]{:S(2)}, u32[]{:S(2)}) %collective-permute-start.6) | collective-permute-done | bytes 98336 | tf_op jit(solution)/shard_map/ppermute | solution.py:315
  36.1 0.5 %shard_map.115.side_ref = f32[12,16,128]{2,1,0:T(8,128)S(1)} custom-call(s32[8,1,12]{2,1,0:T(1,128)S(1)} %get-tuple-element.36.roster_ref, f32[13,64,128]{2,1,0:T(8,128)S(1)} %collective-permute-done.5.packed_ref, f32[12,16,128]{2,1,0:T(8,128)S(1)} %collective-permute-done.6.corner_ref, bf16[12,256,128]{2,1,0:T(8,128)(2,1)S(1)} %shard_map.114.away_ref, ...), custom_call_target="tpu_custom_call" | custom-call | flops 2000000 | bytes 1048576 | tf_op jit(solution)/shard_map/pallas_call | solution.py:352
  36.6 0.0 collective-permute-done.4.other_ref
  36.6 0.4 shard_map.116.own_ref.after_ref.rest_0_
  37.1 0.7 %collective-permute-start.11 = (f32[12,16,128]{2,1,0:T(8,128)S(1)}, f32[12,16,128]{2,1,0:T(8,128)S(1)}, u32[]{:S(2)}, u32[]{:S(2)}) collective-permute-start(f32[12,16,128]{2,1,0:T(8,128)S(1)} %shard_map.116.own_ref.after_ref.rest_0_), channel_id=1, source_target_pairs={{0,64},{1,65},{2,66},{3,67},{4,68},{5,69},{6,70},{7,71},{8,72},{9,... | collective-permute-start | bytes 294920 | tf_op jit(solution)/shard_map/ppermute | solution.py:315
  37.8 0.7 %collective-permute-start.10 = (f32[12,16,128]{2,1,0:T(8,128)S(1)}, f32[12,16,128]{2,1,0:T(8,128)S(1)}, u32[]{:S(2)}, u32[]{:S(2)}) collective-permute-start(f32[12,16,128]{2,1,0:T(8,128)S(1)} %shard_map.116.own_ref.after_ref.rest_0_), channel_id=1, source_target_pairs={{0,192},{1,193},{2,194},{3,195},{4,196},{5,197},{6,198},{7,199},{8... | collective-permute-start | bytes 294920 | tf_op jit(solution)/shard_map/ppermute | solution.py:315
  38.4 0.2 shard_map.117.ready_ref
  38.7 0.0 collective-permute-done.14.both_ref
  38.7 2.9 %collective-permute-start.8 = (f32[12,16,128]{2,1,0:T(8,128)S(1)}, f32[12,16,128]{2,1,0:T(8,128)S(1)}, u32[]{:S(2)}, u32[]{:S(2)}) collective-permute-start(f32[12,16,128]{2,1,0:T(8,128)S(1)} %shard_map.117.ready_ref), channel_id=1, source_target_pairs={{0,128},{1,129},{2,130},{3,131},{4,132},{5,133},{6,134},{7,135},{8... | collective-permute-start | bytes 294920 | tf_op jit(solution)/shard_map/ppermute | solution.py:315
  41.6 0.1 shard_map.123.expand_ref
  41.7 0.0 collective-permute-done.12.core_ref
  41.7 1.0 %shard_map.120.rest_0_ = f32[4,32,128]{2,1,0:T(8,128)S(1)} custom-call(s32[2,12]{1,0:T(2,128)S(1)} %bitcast.6, s32[2,12]{1,0:T(2,128)S(1)} %bitcast.8, s32[2,12]{1,0:T(2,128)S(1)} %bitcast.10, s32[4,4]{1,0:T(4,128)S(1)} %bitcast.4, f32[2,16,1536]{2,1,0:T(8,128)S(1)} %copy-done.1, f32[2,16,1536]{2,1,0:T(8,128)S(1)} %collective-permute-done.12.core_ref, ...), custom_call_target="tpu_custom_call" | custom-call | flops 2000000 | bytes 1048576 | tf_op jit(solution)/shard_map/pallas_call | solution.py:356
  42.8 0.0 collective-permute-done.11.other_ref
  42.8 0.3 shard_map.121.own_ref
  43.1 0.2 shard_map.122.ready_ref
  43.4 1.3 %shard_map.124.rest_1_ = f32[8,32,128]{2,1,0:T(8,128)S(1)} custom-call(s32[2,12]{1,0:T(2,128)S(1)} %bitcast.7, s32[2,12]{1,0:T(2,128)S(1)} %bitcast.9, s32[2,12]{1,0:T(2,128)S(1)} %bitcast.11, s32[4,4]{1,0:T(4,128)S(1)} %bitcast.5, f32[2,16,1536]{2,1,0:T(8,128)S(1)} %copy-done.1, f32[2,16,1536]{2,1,0:T(8,128)S(1)} %collective-permute-done.12.core_ref, ...), custom_call_target="tpu_custom_call" | custom-call | flops 2000000 | bytes 1048576 | tf_op jit(solution)/shard_map/pallas_call | solution.py:356
  44.8 0.0 collective-permute-done.9.packed_ref
  44.8 0.2 shard_map.118.wide_ref
  45.0 0.0 collective-permute-done.10.other_ref
  45.0 0.3 shard_map.119.corner_ref
  45.3 0.0 collective-permute-done.8.beside_ref
  45.3 1.3 %shard_map.125 = f32[2,16,1536]{2,1,0:T(8,128)} custom-call(s32[8,1,12]{2,1,0:T(1,128)S(1)} %get-tuple-element.36.roster_ref, f32[12,16,128]{2,1,0:T(8,128)S(1)} %collective-permute-done.8.beside_ref, f32[12,16,128]{2,1,0:T(8,128)S(1)} %shard_map.119.corner_ref, bf16[12,256,128]{2,1,0:T(8,128)(2,1)S(1)} %get-tuple-element.62.wide_ref, ...), custom_call_target="tpu_custom_call" | custom-call | flops 2000000 | bytes 1048576 | tf_op jit(solution)/shard_map/pallas_call | solution.py:431
  (6 shorter events, 0.0 us)
Async XLA Ops:
  1.8 7.8 %collective-permute-start = (f32[12,16,128]{2,1,0:T(8,128)S(1)}, f32[12,16,128]{2,1,0:T(8,128)S(1)}, u32[]{:S(2)}, u32[]{:S(2)}) collective-permute-start(f32[12,16,128]{2,1,0:T(8,128)S(1)} %shard_map.100.own_ref.after_ref), channel_id=1, source_target_pairs={{0,128},{1,129},{2,130},{3,131},{4,132},{5,133},{6,134},{7,135},{8... | collective-permute-start | bytes 294920 | tf_op jit(solution)/shard_map/ppermute | solution.py:315
  7.4 20.6 %collective-permute-start.5 = (f32[13,64,128]{2,1,0:T(8,128)S(1)}, f32[13,64,128]{2,1,0:T(8,128)S(1)}, u32[]{:S(2)}, u32[]{:S(2)}) collective-permute-start(f32[13,64,128]{2,1,0:T(8,128)S(1)} %get-tuple-element.57), channel_id=1, source_target_pairs={{0,32},{1,33},{2,34},{3,35},{4,36},{5,37},{6,38},{7,39},{8,40},{9,... | collective-permute-start | bytes 1277960 | tf_op jit(solution)/shard_map/ppermute | solution.py:315
  9.6 5.7 %copy-start.1 = (f32[2,16,1536]{2,1,0:T(8,128)S(1)}, f32[2,16,1536]{2,1,0:T(8,128)}, u32[]{:S(2)}) copy-start(f32[2,16,1536]{2,1,0:T(8,128)} %own_ref.3) | copy-start | bytes 589828
  9.9 4.7 %collective-permute-start.1 = (f32[12,16,128]{2,1,0:T(8,128)S(1)}, f32[12,16,128]{2,1,0:T(8,128)S(1)}, u32[]{:S(2)}, u32[]{:S(2)}) collective-permute-start(f32[12,16,128]{2,1,0:T(8,128)S(1)} %shard_map.103.own_ref.after_ref), channel_id=1, source_target_pairs={{0,64},{1,65},{2,66},{3,67},{4,68},{5,69},{6,70},{7,71},{8,72},{9,... | collective-permute-start | bytes 294920 | tf_op jit(solution)/shard_map/ppermute | solution.py:315
  14.8 7.5 %collective-permute-start.2 = (f32[12,16,128]{2,1,0:T(8,128)S(1)}, f32[12,16,128]{2,1,0:T(8,128)S(1)}, u32[]{:S(2)}, u32[]{:S(2)}) collective-permute-start(f32[12,16,128]{2,1,0:T(8,128)S(1)} %shard_map.107.own_ref), channel_id=1, source_target_pairs={{0,32},{1,33},{2,34},{3,35},{4,36},{5,37},{6,38},{7,39},{8,40},{9,... | collective-permute-start | bytes 294920 | tf_op jit(solution)/shard_map/ppermute | solution.py:315
  15.4 12.2 %collective-permute-start.13 = (f32[2,16,1536]{2,1,0:T(8,128)S(1)}, f32[2,16,1536]{2,1,0:T(8,128)S(1)}, u32[]{:S(2)}, u32[]{:S(2)}) collective-permute-start(f32[2,16,1536]{2,1,0:T(8,128)S(1)} %copy-done.1), channel_id=1, source_target_pairs={{0,2},{1,3},{2,0},{3,1},{4,6},{5,7},{6,4},{7,5},{8,10},{9,11},{10,... | collective-permute-start | bytes 589832 | tf_op jit(solution)/shard_map/ppermute | solution.py:315
  18.6 26.2 %collective-permute-start.9 = (f32[13,64,128]{2,1,0:T(8,128)S(1)}, f32[13,64,128]{2,1,0:T(8,128)S(1)}, u32[]{:S(2)}, u32[]{:S(2)}) collective-permute-start(f32[13,64,128]{2,1,0:T(8,128)S(1)} %get-tuple-element.61), channel_id=1, source_target_pairs={{0,128},{1,129},{2,130},{3,131},{4,132},{5,133},{6,134},{7,135},{8... | collective-permute-start | bytes 1277960 | tf_op jit(solution)/shard_map/ppermute | solution.py:315
  22.5 1.4 %collective-permute-start.3 = (f32[12,16,128]{2,1,0:T(8,128)S(1)}, f32[12,16,128]{2,1,0:T(8,128)S(1)}, u32[]{:S(2)}, u32[]{:S(2)}) collective-permute-start(f32[12,16,128]{2,1,0:T(8,128)S(1)} %shard_map.109.own_ref), channel_id=1, source_target_pairs={{0,1},{1,0},{2,3},{3,2},{4,5},{5,4},{6,7},{7,6},{8,9},{9,8},{10,11... | collective-permute-start | bytes 294920 | tf_op jit(solution)/shard_map/ppermute | solution.py:315
  24.4 17.2 %copy-start.2 = (f32[12,2,64,128]{3,2,1,0:T(8,128)S(1)}, f32[12,2,64,128]{3,2,1,0:T(8,128)}, u32[]{:S(2)}) copy-start(f32[12,2,64,128]{3,2,1,0:T(8,128)} %weight_ref.4) | copy-start | bytes 2359300
  24.4 17.3 %copy-start = (f32[12,2,2,128,128]{4,3,2,1,0:T(8,128)S(1)}, f32[12,2,2,128,128]{4,3,2,1,0:T(8,128)}, u32[]{:S(2)}) copy-start(f32[12,2,2,128,128]{4,3,2,1,0:T(8,128)} %weight_ref.5) | copy-start | bytes 9437188
  24.4 17.3 %copy-start.3 = (s32[1,4,4]{2,1,0:T(4,128)S(1)}, s32[1,4,4]{2,1,0:T(4,128)}, u32[]{:S(2)}) copy-start(s32[1,4,4]{2,1,0:T(4,128)} %param.19) | copy-start | bytes 196
  24.4 17.3 %copy-start.4 = (s32[12,2]{0,1:T(2,128)S(1)}, s32[12,2]{0,1:T(2,128)}, u32[]{:S(2)}) copy-start(s32[12,2]{0,1:T(2,128)} %param.16) | copy-start | bytes 292
  24.4 17.3 %copy-start.5 = (s32[12,2]{0,1:T(2,128)S(1)}, s32[12,2]{0,1:T(2,128)}, u32[]{:S(2)}) copy-start(s32[12,2]{0,1:T(2,128)} %param.17) | copy-start | bytes 292
  24.5 17.3 %copy-start.6 = (s32[12,2]{0,1:T(2,128)S(1)}, s32[12,2]{0,1:T(2,128)}, u32[]{:S(2)}) copy-start(s32[12,2]{0,1:T(2,128)} %param.18) | copy-start | bytes 292
  24.5 4.9 %collective-permute-start.7 = (f32[12,16,128]{2,1,0:T(8,128)S(1)}, f32[12,16,128]{2,1,0:T(8,128)S(1)}, u32[]{:S(2)}, u32[]{:S(2)}) collective-permute-start(f32[12,16,128]{2,1,0:T(8,128)S(1)} %shard_map.112.ready_ref), channel_id=1, source_target_pairs={{0,32},{1,33},{2,34},{3,35},{4,36},{5,37},{6,38},{7,39},{8,40},{9,... | collective-permute-start | bytes 294920 | tf_op jit(solution)/shard_map/ppermute | solution.py:315
  27.5 11.1 %collective-permute-start.14 = (f32[2,16,1536]{2,1,0:T(8,128)S(1)}, f32[2,16,1536]{2,1,0:T(8,128)S(1)}, u32[]{:S(2)}, u32[]{:S(2)}) collective-permute-start(f32[2,16,1536]{2,1,0:T(8,128)S(1)} %collective-permute-done.13.far_ref), channel_id=1, source_target_pairs={{0,1},{1,0},{2,3},{3,2},{4,5},{5,4},{6,7},{7,6},{8,9},{9,8},{10,11... | collective-permute-start | bytes 589832 | tf_op jit(solution)/shard_map/ppermute | solution.py:315
  27.5 14.2 %collective-permute-start.12 = (f32[2,16,1536]{2,1,0:T(8,128)S(1)}, f32[2,16,1536]{2,1,0:T(8,128)S(1)}, u32[]{:S(2)}, u32[]{:S(2)}) collective-permute-start(f32[2,16,1536]{2,1,0:T(8,128)S(1)} %copy-done.1), channel_id=1, source_target_pairs={{0,1},{1,0},{2,3},{3,2},{4,5},{5,4},{6,7},{7,6},{8,9},{9,8},{10,11... | collective-permute-start | bytes 589832 | tf_op jit(solution)/shard_map/ppermute | solution.py:315
  28.0 8.0 %collective-permute-start.6 = (f32[12,16,128]{2,1,0:T(8,128)S(1)}, f32[12,16,128]{2,1,0:T(8,128)S(1)}, u32[]{:S(2)}, u32[]{:S(2)}) collective-permute-start(f32[12,16,128]{2,1,0:T(8,128)S(1)} %shard_map.111.own_ref.after_ref), channel_id=1, source_target_pairs={{0,34},{1,35},{2,32},{3,33},{4,38},{5,39},{6,36},{7,37},{8,42},{9,... | collective-permute-start | bytes 294920 | tf_op jit(solution)/shard_map/ppermute | solution.py:315
  29.4 7.2 %collective-permute-start.4 = (f32[12,16,128]{2,1,0:T(8,128)S(1)}, f32[12,16,128]{2,1,0:T(8,128)S(1)}, u32[]{:S(2)}, u32[]{:S(2)}) collective-permute-start(f32[12,16,128]{2,1,0:T(8,128)S(1)} %shard_map.111.own_ref.after_ref), channel_id=1, source_target_pairs={{0,2},{1,3},{2,0},{3,1},{4,6},{5,7},{6,4},{7,5},{8,10},{9,11},{10,... | collective-permute-start | bytes 294920 | tf_op jit(solution)/shard_map/ppermute | solution.py:315
  37.1 5.7 %collective-permute-start.11 = (f32[12,16,128]{2,1,0:T(8,128)S(1)}, f32[12,16,128]{2,1,0:T(8,128)S(1)}, u32[]{:S(2)}, u32[]{:S(2)}) collective-permute-start(f32[12,16,128]{2,1,0:T(8,128)S(1)} %shard_map.116.own_ref.after_ref.rest_0_), channel_id=1, source_target_pairs={{0,64},{1,65},{2,66},{3,67},{4,68},{5,69},{6,70},{7,71},{8,72},{9,... | collective-permute-start | bytes 294920 | tf_op jit(solution)/shard_map/ppermute | solution.py:315
  37.8 7.2 %collective-permute-start.10 = (f32[12,16,128]{2,1,0:T(8,128)S(1)}, f32[12,16,128]{2,1,0:T(8,128)S(1)}, u32[]{:S(2)}, u32[]{:S(2)}) collective-permute-start(f32[12,16,128]{2,1,0:T(8,128)S(1)} %shard_map.116.own_ref.after_ref.rest_0_), channel_id=1, source_target_pairs={{0,192},{1,193},{2,194},{3,195},{4,196},{5,197},{6,198},{7,199},{8... | collective-permute-start | bytes 294920 | tf_op jit(solution)/shard_map/ppermute | solution.py:315
  38.7 6.6 %collective-permute-start.8 = (f32[12,16,128]{2,1,0:T(8,128)S(1)}, f32[12,16,128]{2,1,0:T(8,128)S(1)}, u32[]{:S(2)}, u32[]{:S(2)}) collective-permute-start(f32[12,16,128]{2,1,0:T(8,128)S(1)} %shard_map.117.ready_ref), channel_id=1, source_target_pairs={{0,128},{1,129},{2,130},{3,131},{4,132},{5,133},{6,134},{7,135},{8... | collective-permute-start | bytes 294920 | tf_op jit(solution)/shard_map/ppermute | solution.py:315

commit v8 on v7

--- a/solution.py
+++ b/solution.py
@@ -83,12 +83,15 @@
         copy.wait()
 
 
-def compress_kernel(field_hbm, weight_hbm, out_ref, field_ref, weight_ref, sems):
+def compress_kernel(field_hbm, weight_hbm, coupling_hbm, roster_hbm, out_ref, next_ref, roster_ref, field_ref, weight_ref, sems):
     blocks = out_ref.shape[0]
     half = blocks // 2
     parts = [pl.ds(0, half), pl.ds(half, blocks - half)]
     copies = started(
-        [(field_hbm, field_ref)] + [(weight_hbm.at[part], weight_ref.at[part]) for part in parts], sems
+        [(field_hbm, field_ref)]
+        + [(weight_hbm.at[part], weight_ref.at[part]) for part in parts]
+        + [(roster_hbm, roster_ref), (coupling_hbm.at[0], next_ref)],
+        sems,
     )
     copies[0].wait()
     for k in range(blocks):
@@ -97,6 +100,7 @@
         lanes = pl.ds(128 * k, 128)
         rows = jnp.concatenate([field_ref[0, :, lanes], field_ref[1, :, lanes]], axis=0)
         out_ref[k] = joined(product(rows, weight_ref[k].reshape(128, 128)))
+    finish(copies[3:])
 
 
 def entries(row, count):
@@ -118,9 +122,8 @@
     packed_ref[blocks, 0:8, 0:blocks] = jnp.broadcast_to(row.astype(F32), (8, blocks))
 
 
-def packed_row(packed_ref):
-    blocks = packed_ref.shape[0] - 1
-    return entries(packed_ref[blocks, 0:8, 0:blocks], blocks)
+def packed_row(packed_ref, blocks):
+    return entries(packed_ref[packed_ref.shape[0] - 1, 0:8, 0:blocks], blocks)
 
 
 def prepare_block(k, place, weight_ref, own_out, other_out, packed_ref=None):
@@ -131,36 +134,38 @@
         packed_ref[k] = other_half
 
 
-def first_kernel(own_ref, coupling_hbm, roster_hbm, *refs):
-    ready_out, other_out, back_ref, roster_ref, own_4, other_4, packed_4, weight_1, weight_2, *rest = refs
-    weight_0, weight_4, sems = rest
-    blocks = own_ref.shape[0]
-    copies = started(
-        [(roster_hbm, roster_ref)]
-        + [(coupling_hbm.at[n], out) for n, out in ((0, weight_0), (4, weight_4), (1, weight_1), (2, weight_2))],
-        sems,
-    )
-    copies[0].wait()
-    places = slots(roster_ref[0], blocks, back_ref)
-    put_row(packed_4, roster_ref[4])
-    copies[1].wait()
-    for k, place in enumerate(places):
-        own_half, other_half = halves(weight_0[k].reshape(128, 128))
-        other_out[place] = filled(other_half)
-        ready_out[place] = times(own_ref[k], filled(own_half))
-    copies[2].wait()
-    for k in range(blocks):
-        prepare_block(k, k, weight_4, own_4, other_4, packed_4)
-    finish(copies[3:])
-
-
-def ahead_kernel(level, own_ref, weight_ref, roster_ref, coupling_hbm, *refs):
-    ready_out, other_out, back_ref, weight_3, weight_6, sems = refs
-    copies = started([(coupling_hbm.at[3], weight_3), (coupling_hbm.at[6], weight_6)], sems)
+def start_level(level, own_ref, weight_ref, roster_ref, ready_out, other_out, back_ref):
     for k, place in enumerate(slots(roster_ref[level], own_ref.shape[0], back_ref)):
         own_half, other_half = halves(weight_ref[k].reshape(128, 128))
         other_out[place] = filled(other_half)
         ready_out[place] = times(own_ref[k], filled(own_half))
+
+
+def first_kernel(own_ref, weight_0, roster_ref, coupling_hbm, *refs):
+    ready_out, other_out, back_ref, own_4, other_4, packed_a, packed_b, weight_1, weight_2, weight_4, sems = refs
+    blocks = own_ref.shape[0]
+    half = packed_b.shape[0]
+    copies = started([(coupling_hbm.at[n], out) for n, out in ((4, weight_4), (1, weight_1), (2, weight_2))], sems)
+    start_level(0, own_ref, weight_0, roster_ref, ready_out, other_out, back_ref)
+    packed_a[half, 0:8, 0:blocks] = jnp.broadcast_to(roster_ref[4].astype(F32), (8, blocks))
+    copies[0].wait()
+    for k in range(blocks):
+        own_half, other_half = halves(weight_4[k].reshape(128, 128))
+        own_4[k] = filled(own_half)
+        other_4[k] = filled(other_half)
+        if k < half:
+            packed_a[k] = other_half
+        else:
+            packed_b[k - half] = other_half
+    finish(copies[1:])
+
+
+def ahead_kernel(level, own_ref, weight_ref, roster_ref, weight_2, coupling_hbm, *refs):
+    ready_out, other_out, back_ref, own_2, other_2, back_2, weight_3, weight_6, sems = refs
+    copies = started([(coupling_hbm.at[3], weight_3), (coupling_hbm.at[6], weight_6)], sems)
+    start_level(level, own_ref, weight_ref, roster_ref, ready_out, other_out, back_ref)
+    for k, place in enumerate(slots(roster_ref[level + 1], own_ref.shape[0], back_2)):
+        prepare_block(k, place, weight_2, own_2, other_2)
     finish(copies)
 
 
@@ -185,9 +190,11 @@
             prepare_block(k, k, weights[n], outs[2 * n], outs[2 * n + 1])
 
 
-def unpack_kernel(packed_ref, after_ref, out_ref):
+def unpack_kernel(packed_ref, *rest):
+    out_ref = rest[-1]
     for k in range(out_ref.shape[0]):
-        out_ref[k] = filled(packed_ref[k])
+        half = packed_ref.shape[0] - 1
+        out_ref[k] = filled(packed_ref[k] if k < half else rest[0][k - half])
 
 
 def spread_kernel(weight_ref, after_ref, out_ref):
@@ -219,7 +226,7 @@
 
 def side_kernel(level, roster_ref, packed_ref, corner_ref, away_ref, beside_ref, wide_ref, out_ref, there_ref):
     blocks = out_ref.shape[0]
-    for k, place in enumerate(packed_row(packed_ref)):
+    for k, place in enumerate(packed_row(packed_ref, out_ref.shape[0])):
         there_ref[k] = beside_ref[k] + times(corner_ref[place], away_ref[k])
     for k, place in enumerate(entries(roster_ref[level], blocks)):
         out_ref[k] = times(there_ref[place], wide_ref[k])
@@ -234,7 +241,7 @@
 
 
 def corner_kernel(packed_ref, other_ref, wide_ref, out_ref):
-    for k, place in enumerate(packed_row(packed_ref)):
+    for k, place in enumerate(packed_row(packed_ref, out_ref.shape[0])):
         out_ref[k] = times(other_ref[place], wide_ref[k])
 
 
@@ -358,40 +365,51 @@
         )(*indices, field, core, far, both, dense, after)
 
     part = functools.partial
-    coeffs = run(
+    coeffs, weight_0, names = run(
         compress_kernel,
-        state,
-        in_hbm(field_in, compress),
-        scratch=[VMEM(field_in.shape, F32), VMEM(compress.shape, F32), DMA((3,))],
-        hbm=(0, 1),
+        [state, level_weights, VMEM(roster.shape, jnp.int32)],
+        [*in_hbm(field_in, compress), coupling_hbm, roster_hbm],
+        scratch=[VMEM(field_in.shape, F32), VMEM(compress.shape, F32), DMA((5,))],
+        hbm=(0, 1, 2, 3),
     )
 
     other = flipped(coeffs, top, 0)
-    ready, wide_0, back_0, names, own_4, wide_4, packed_4, weight_1, weight_2 = run(
+    half = blocks // 2
+    ready, wide_0, back_0, own_4, wide_4, packed_4, packed_more, weight_1, weight_2 = run(
         first_kernel,
-        [state, wide, back, VMEM(roster.shape, jnp.int32), wide, wide, packed, level_weights, level_weights],
-        [coeffs, coupling_hbm, roster_hbm],
-        scratch=[level_weights, level_weights, DMA((5,))],
-        hbm=(1, 2),
+        [
+            state,
+            wide,
+            back,
+            wide,
+            wide,
+            VMEM((half + 1, 64, 128), F32),
+            VMEM((blocks - half, 64, 128), F32),
+            level_weights,
+            level_weights,
+        ],
+        [coeffs, weight_0, names, coupling_hbm],
+        scratch=[level_weights, DMA((3,))],
+        hbm=(3,),
     )
     away_4 = flipped(packed_4, top // 4, 0)
-    own_2, wide_2, back_2 = run(part(sorted_kernel, 2), [wide, wide, back], [weight_2, names], [coeffs])
-    coeffs = run(level_kernel, state, [back_0, other, wide_0, ready], [own_2])
+    far = flipped(tied(field_in, wide_4), 0, 2)
+    coeffs = run(level_kernel, state, [back_0, other, wide_0, ready])
 
     other = flipped(coeffs, top // 2, 0)
-    ready, wide_1, back_1, weight_3, weight_6 = run(
+    ready, wide_1, back_1, own_2, wide_2, back_2, weight_3, weight_6 = run(
         part(ahead_kernel, 1),
-        [state, wide, back, level_weights, level_weights],
-        [coeffs, weight_1, names, coupling_hbm],
+        [state, wide, back, wide, wide, back, level_weights, level_weights],
+        [coeffs, weight_1, names, weight_2, coupling_hbm],
         scratch=[DMA((2,))],
-        hbm=(3,),
+        hbm=(4,),
     )
     own_3, wide_3, back_3 = run(part(sorted_kernel, 3), [wide, wide, back], [weight_3, names], [coeffs])
     own_6, wide_6, packed_6 = run(part(packed_kernel, 6), [wide, wide, packed], [weight_6, names], [coeffs])
     coeffs = run(level_kernel, state, [back_1, other, wide_1, ready], [own_3, own_6])
 
     other = flipped(coeffs, top // 4, 0)
-    far = flipped(tied(field_in, coeffs), 0, 2)
+    away_more = flipped(tied(packed_more, coeffs), top // 4, 0)
     away_6 = flipped(tied(packed_6, coeffs), top, 0)
     ready = run(part(own_sorted_kernel, 2), state, [coeffs, own_2, names])
     coeffs = run(level_kernel, state, [back_2, other, wide_2, ready])
@@ -414,7 +432,7 @@
     )
     core = flipped(tied(field_in, coeffs), 0, 1)
     both = flipped(tied(far, coeffs), 0, 1)
-    away = run(unpack_kernel, wide, [away_4], [coeffs])
+    away = run(unpack_kernel, wide, [away_4, away_more], [coeffs])
     side = run(part(side_kernel, 5), state, [names, away_4, corner, away, beside, wide_5], scratch=[state])
     coeffs = run(part(double_kernel, 4), state, [names, other, wide_4, ready, own_5, side], [own_7], scratch=[state])
 

time: 46.9 us -> 52.1 us (1.11)
  waiting for transfers between devices: 6.27 us -> 10.4 us
  starting transfers between devices: 21.9 us -> 23.4 us
    ppermute x15 -> x16, waiting for transfers between devices: 6.27 us -> 10.4 us  [flipped(): return lax.ppermute(value, ('leaf', 'sub'), pairs)]
    ppermute x15 -> x16, starting transfers between devices: 21.9 us -> 23.4 us  [flipped(): return lax.ppermute(value, ('leaf', 'sub'), pairs)]
    pallas_call x23 -> x22, Pallas kernels: 14.3 us -> 14 us  [run(): call(kernel, outs, spaces, [VMEM] * len(outs) if several else VMEM, scratch)]
  transfers between devices with their start and end apart: 15 -> 16, of which waited for: 6 -> 6; matrix products, arithmetic and copies ran while one was open for 0% -> 0% of each run, Pallas kernels for 32% -> 27%
where the time goes in v8:
time: 52.1 us; the launch traced here: 52 us
  starting transfers between devices  23.4 us (45%)
  Pallas kernels  17.6 us (34%)
  waiting for transfers between devices  10.4 us (20%)
  between operations  0.55 us (1%)
    ppermute x16, starting transfers between devices, flipped(): return lax.ppermute(value, ('leaf', 'sub'), pairs)  23.4 us
    pallas_call x22, Pallas kernels, run(): call(kernel, outs, spaces, [VMEM] * len(outs) if several else VMEM, scratch)  14 us
    ppermute x16, waiting for transfers between devices, flipped(): return lax.ppermute(value, ('leaf', 'sub'), pairs)  10.4 us
    pallas_call x2, Pallas kernels, near_piece(): call(functools.partial(near_kernel, begin), VMEM((count, 2 * rhs, 128), F...  2.34 us
    pallas_call x1, Pallas kernels, on_device(): call(part(last_kernel, 7), jax.ShapeDtypeStruct(field_in.shape, F32), [VM...  1.26 us
  transfers between devices with their start and end apart: 16, of which 6 were waited for; matrix products, arithmetic and copies ran while one was open for 0% of the time, Pallas kernels for 27%

profile of v8, /device:TPU:64, one launch (start us, length us, event | category | flops | bytes accessed | tf_op | source)
XLA Modules:
  0.0 52.0 jit_solution(5082209224759558397)
XLA Ops:
  0.0 1.8 %shard_map.100 = (f32[12,16,128]{2,1,0:T(8,128)S(1)}, f32[12,2,64,128]{3,2,1,0:T(8,128)S(1)}, s32[8,1,12]{2,1,0:T(1,128)S(1)}) custom-call(f32[2,16,1536]{2,1,0:T(8,128)} %own_ref.3, f32[12,2,64,128]{3,2,1,0:T(8,128)} %weight_hbm.1, f32[8,12,2,64,128]{4,3,2,1,0:T(8,128)} %coupling_hbm.7, s32[8,1,12]{2,1,0:T(1,128)} %roster_hbm.1), custom_call_target="tpu_custom_call" | custom-call | flops 2000000 | bytes 1048576 | tf_op jit(solution)/shard_map/pallas_call | solution.py:359
  1.8 3.1 %collective-permute-start = (f32[12,16,128]{2,1,0:T(8,128)S(1)}, f32[12,16,128]{2,1,0:T(8,128)S(1)}, u32[]{:S(2)}, u32[]{:S(2)}) collective-permute-start(f32[12,16,128]{2,1,0:T(8,128)S(1)} %get-tuple-element.41.own_ref), channel_id=1, source_target_pairs={{0,128},{1,129},{2,130},{3,131},{4,132},{5,133},{6,134},{7,135},{8... | collective-permute-start | bytes 294920 | tf_op jit(solution)/shard_map/ppermute | solution.py:322
  4.9 2.4 %shard_map.101 = (f32[12,16,128]{2,1,0:T(8,128)S(1)}, bf16[12,256,128]{2,1,0:T(8,128)(2,1)S(1)}, s32[8,128]{1,0:T(8,128)S(1)}, bf16[12,256,128]{2,1,0:T(8,128)(2...) custom-call(f32[12,16,128]{2,1,0:T(8,128)S(1)} %get-tuple-element.41, ...), custom_call_target="tpu_custom_call" | custom-call | flops 2000000 | bytes 1048576 | tf_op jit(solution)/shard_map/pallas_call | solution.py:359
  7.3 0.7 %collective-permute-done.other_ref = f32[12,16,128]{2,1,0:T(8,128)S(1)} collective-permute-done((f32[12,16,128]{2,1,0:T(8,128)S(1)}, f32[12,16,128]{2,1,0:T(8,128)S(1)}, u32[]{:S(2)}, u32[]{:S(2)}) %collective-permute-start) | collective-permute-done | bytes 98336 | tf_op jit(solution)/shard_map/ppermute | solution.py:322
  8.0 0.2 shard_map.102.own_ref.after_ref
  8.3 0.0 copy-start.1
  8.3 1.6 %collective-permute-start.1 = (f32[12,16,128]{2,1,0:T(8,128)S(1)}, f32[12,16,128]{2,1,0:T(8,128)S(1)}, u32[]{:S(2)}, u32[]{:S(2)}) collective-permute-start(f32[12,16,128]{2,1,0:T(8,128)S(1)} %shard_map.102.own_ref.after_ref), channel_id=1, source_target_pairs={{0,64},{1,65},{2,66},{3,67},{4,68},{5,69},{6,70},{7,71},{8,72},{9,... | collective-permute-start | bytes 294920 | tf_op jit(solution)/shard_map/ppermute | solution.py:322
  9.9 2.3 %shard_map.103 = (f32[12,16,128]{2,1,0:T(8,128)S(1)}, bf16[12,256,128]{2,1,0:T(8,128)(2,1)S(1)}, s32[8,128]{1,0:T(8,128)S(1)}, bf16[12,256,128]{2,1,0:T(8,128)(2...) custom-call(f32[12,16,128]{2,1,0:T(8,128)S(1)} %shard_map.102.own_re, ...), custom_call_target="tpu_custom_call" | custom-call | flops 2000000 | bytes 1048576 | tf_op jit(solution)/shard_map/pallas_call | solution.py:359
  12.2 0.5 %shard_map.105 = (bf16[12,256,128]{2,1,0:T(8,128)(2,1)S(1)}, bf16[12,256,128]{2,1,0:T(8,128)(2,1)S(1)}, f32[13,64,128]{2,1,0:T(8,128)S(1)}) custom-call(f32[12,2,64,128]{3,2,1,0:T(8,128)S(1)} %get-tuple-element.55.weight_ref, s32[8,1,12]{2,1,0:T(1,128)S(1)} %get-tuple-element.40.roster_ref, f32[12,16,128]{2,1,0:T(8,128)S(1)} %shard_map.102.own_ref.after_ref), custom_call_target="tpu_custom_call" | custom-call | flops 2000000 | bytes 1048576 | tf_op jit(solution)/shard_map/pallas_call | solution.py:359
  12.7 0.5 %shard_map.104 = (bf16[12,256,128]{2,1,0:T(8,128)(2,1)S(1)}, bf16[12,256,128]{2,1,0:T(8,128)(2,1)S(1)}, s32[8,128]{1,0:T(8,128)S(1)}) custom-call(f32[12,2,64,128]{3,2,1,0:T(8,128)S(1)} %get-tuple-element.48.weight_ref, s32[8,1,12]{2,1,0:T(1,128)S(1)} %get-tuple-element.40.roster_ref, f32[12,16,128]{2,1,0:T(8,128)S(1)} %shard_map.102.own_ref.after_ref), custom_call_target="tpu_custom_call" | custom-call | flops 2000000 | bytes 1048576 | tf_op jit(solution)/shard_map/pallas_call | solution.py:359
  13.3 0.0 collective-permute-done.1.other_ref
  13.3 0.2 shard_map.106.own_ref
  13.5 1.7 %collective-permute-start.2 = (f32[12,16,128]{2,1,0:T(8,128)S(1)}, f32[12,16,128]{2,1,0:T(8,128)S(1)}, u32[]{:S(2)}, u32[]{:S(2)}) collective-permute-start(f32[12,16,128]{2,1,0:T(8,128)S(1)} %shard_map.106.own_ref), channel_id=1, source_target_pairs={{0,32},{1,33},{2,34},{3,35},{4,36},{5,37},{6,38},{7,39},{8,40},{9,... | collective-permute-start | bytes 294920 | tf_op jit(solution)/shard_map/ppermute | solution.py:322
  15.2 2.9 %collective-permute-start.14 = (f32[2,16,1536]{2,1,0:T(8,128)S(1)}, f32[2,16,1536]{2,1,0:T(8,128)S(1)}, u32[]{:S(2)}, u32[]{:S(2)}) collective-permute-start(f32[2,16,1536]{2,1,0:T(8,128)S(1)} %copy-done.1), channel_id=1, source_target_pairs={{0,2},{1,3},{2,0},{3,1},{4,6},{5,7},{6,4},{7,5},{8,10},{9,11},{10,... | collective-permute-start | bytes 589832 | tf_op jit(solution)/shard_map/ppermute | solution.py:322
  18.1 0.1 collective-permute-start.5
  18.2 2.8 %collective-permute-start.10 = (f32[13,64,128]{2,1,0:T(8,128)S(1)}, f32[13,64,128]{2,1,0:T(8,128)S(1)}, u32[]{:S(2)}, u32[]{:S(2)}) collective-permute-start(f32[13,64,128]{2,1,0:T(8,128)S(1)} %get-tuple-element.69), channel_id=1, source_target_pairs={{0,128},{1,129},{2,130},{3,131},{4,132},{5,133},{6,134},{7,135},{8... | collective-permute-start | bytes 1277960 | tf_op jit(solution)/shard_map/ppermute | solution.py:322
  21.0 0.2 shard_map.107.ready_ref
  21.2 0.0 collective-permute-done.2.other_ref
  21.2 0.2 shard_map.108.own_ref
  21.5 0.1 collective-permute-start.3
  21.6 2.0 %collective-permute-start.7 = (f32[6,64,128]{2,1,0:T(8,128)S(1)}, f32[6,64,128]{2,1,0:T(8,128)S(1)}, u32[]{:S(2)}, u32[]{:S(2)}) collective-permute-start(f32[6,64,128]{2,1,0:T(8,128)S(1)} %get-tuple-element.65), channel_id=1, source_target_pairs={{0,32},{1,33},{2,34},{3,35},{4,36},{5,37},{6,38},{7,39},{8,40},{9,... | collective-permute-start | bytes 589832 | tf_op jit(solution)/shard_map/ppermute | solution.py:322
  23.5 0.2 shard_map.109.ready_ref
  23.8 0.0 collective-permute-done.3.other_ref
  23.8 0.2 shard_map.110.own_ref.after_ref.rest_1_
  24.0 0.2 shard_map.111.ready_ref
  24.3 0.0 copy-start.2
  24.3 0.0 copy-start
  24.3 0.0 copy-start.3
  24.3 0.0 copy-start.4
  24.3 0.0 copy-start.5
  24.3 0.0 copy-start.6
  24.3 1.0 %collective-permute-start.8 = (f32[12,16,128]{2,1,0:T(8,128)S(1)}, f32[12,16,128]{2,1,0:T(8,128)S(1)}, u32[]{:S(2)}, u32[]{:S(2)}) collective-permute-start(f32[12,16,128]{2,1,0:T(8,128)S(1)} %shard_map.111.ready_ref), channel_id=1, source_target_pairs={{0,32},{1,33},{2,34},{3,35},{4,36},{5,37},{6,38},{7,39},{8,40},{9,... | collective-permute-start | bytes 294920 | tf_op jit(solution)/shard_map/ppermute | solution.py:322
  25.4 0.5 %collective-permute-done.14.far_ref = f32[2,16,1536]{2,1,0:T(8,128)S(1)} collective-permute-done((f32[2,16,1536]{2,1,0:T(8,128)S(1)}, f32[2,16,1536]{2,1,0:T(8,128)S(1)}, u32[]{:S(2)}, u32[]{:S(2)}) %collective-permute-start.14) | collective-permute-done | bytes 196640 | tf_op jit(solution)/shard_map/ppermute | solution.py:322
  25.9 0.0 collective-permute-start.15
  25.9 2.9 %collective-permute-done.5.packed_ref = f32[7,64,128]{2,1,0:T(8,128)S(1)} collective-permute-done((f32[7,64,128]{2,1,0:T(8,128)S(1)}, f32[7,64,128]{2,1,0:T(8,128)S(1)}, u32[]{:S(2)}, u32[]{:S(2)}) %collective-permute-start.5) | collective-permute-done | bytes 229408 | tf_op jit(solution)/shard_map/ppermute | solution.py:322
  28.9 0.0 collective-permute-start.13
  28.9 3.5 %collective-permute-done.7.rest_0_ = f32[6,64,128]{2,1,0:T(8,128)S(1)} collective-permute-done((f32[6,64,128]{2,1,0:T(8,128)S(1)}, f32[6,64,128]{2,1,0:T(8,128)S(1)}, u32[]{:S(2)}, u32[]{:S(2)}) %collective-permute-start.7) | collective-permute-done | bytes 196640 | tf_op jit(solution)/shard_map/ppermute | solution.py:322
  32.4 1.8 %collective-permute-start.6 = (f32[12,16,128]{2,1,0:T(8,128)S(1)}, f32[12,16,128]{2,1,0:T(8,128)S(1)}, u32[]{:S(2)}, u32[]{:S(2)}) collective-permute-start(f32[12,16,128]{2,1,0:T(8,128)S(1)} %shard_map.110.own_ref.after_ref.rest_1_), channel_id=1, source_target_pairs={{0,34},{1,35},{2,32},{3,33},{4,38},{5,39},{6,36},{7,37},{8,42},{9,... | collective-permute-start | bytes 294920 | tf_op jit(solution)/shard_map/ppermute | solution.py:322
  34.1 0.0 collective-permute-done.8.beside_ref
  34.1 2.1 %collective-permute-start.4 = (f32[12,16,128]{2,1,0:T(8,128)S(1)}, f32[12,16,128]{2,1,0:T(8,128)S(1)}, u32[]{:S(2)}, u32[]{:S(2)}) collective-permute-start(f32[12,16,128]{2,1,0:T(8,128)S(1)} %shard_map.110.own_ref.after_ref.rest_1_), channel_id=1, source_target_pairs={{0,2},{1,3},{2,0},{3,1},{4,6},{5,7},{6,4},{7,5},{8,10},{9,11},{10,... | collective-permute-start | bytes 294920 | tf_op jit(solution)/shard_map/ppermute | solution.py:322
  36.3 2.2 %shard_map.112 = (bf16[12,256,128]{2,1,0:T(8,128)(2,1)S(1)}, bf16[12,256,128]{2,1,0:T(8,128)(2,1)S(1)}, bf16[12,256,128]{2,1,0:T(8,128)(2,1)S(1)}, bf16[12,256,128]{2,1,0:T(8,128)(2,1)S(1)}) custom-call(f32[8,12,2,64,128]{4,3,2,1,0:T(8,128)} %coupling_hbm.7, f32[12,16,128]{2,1,0:T(8,128)S(1)} %shard_map.110.own_ref.after_ref.rest_1_), custom_call_target="tpu_custom_call" | custom-call | flops 2000000 | bytes 1048576 | tf_op jit(solution)/shard_map/pallas_call | solution.py:359
  38.5 0.2 shard_map.113.away_ref
  38.7 0.0 collective-permute-done.6.corner_ref
  38.7 0.5 %shard_map.114.side_ref = f32[12,16,128]{2,1,0:T(8,128)S(1)} custom-call(s32[8,1,12]{2,1,0:T(1,128)S(1)} %get-tuple-element.40.roster_ref, f32[7,64,128]{2,1,0:T(8,128)S(1)} %collective-permute-done.5.packed_ref, f32[12,16,128]{2,1,0:T(8,128)S(1)} %collective-permute-done.6.corner_ref, bf16[12,256,128]{2,1,0:T(8,128)(2,1)S(1)} %shard_map.113.away_ref, ...), custom_call_target="tpu_custom_call" | custom-call | flops 2000000 | bytes 1048576 | tf_op jit(solution)/shard_map/pallas_call | solution.py:359
  39.2 1.0 %collective-permute-done.4.other_ref = f32[12,16,128]{2,1,0:T(8,128)S(1)} collective-permute-done((f32[12,16,128]{2,1,0:T(8,128)S(1)}, f32[12,16,128]{2,1,0:T(8,128)S(1)}, u32[]{:S(2)}, u32[]{:S(2)}) %collective-permute-start.4) | collective-permute-done | bytes 98336 | tf_op jit(solution)/shard_map/ppermute | solution.py:322
  40.2 0.4 shard_map.115.own_ref.rest_0_.after_ref
  40.7 0.8 %collective-permute-start.12 = (f32[12,16,128]{2,1,0:T(8,128)S(1)}, f32[12,16,128]{2,1,0:T(8,128)S(1)}, u32[]{:S(2)}, u32[]{:S(2)}) collective-permute-start(f32[12,16,128]{2,1,0:T(8,128)S(1)} %shard_map.115.own_ref.rest_0_.after_ref), channel_id=1, source_target_pairs={{0,64},{1,65},{2,66},{3,67},{4,68},{5,69},{6,70},{7,71},{8,72},{9,... | collective-permute-start | bytes 294920 | tf_op jit(solution)/shard_map/ppermute | solution.py:322
  41.5 2.6 %collective-permute-start.11 = (f32[12,16,128]{2,1,0:T(8,128)S(1)}, f32[12,16,128]{2,1,0:T(8,128)S(1)}, u32[]{:S(2)}, u32[]{:S(2)}) collective-permute-start(f32[12,16,128]{2,1,0:T(8,128)S(1)} %shard_map.115.own_ref.rest_0_.after_ref), channel_id=1, source_target_pairs={{0,192},{1,193},{2,194},{3,195},{4,196},{5,197},{6,198},{7,199},{8... | collective-permute-start | bytes 294920 | tf_op jit(solution)/shard_map/ppermute | solution.py:322
  44.1 0.2 shard_map.116.ready_ref
  44.3 0.0 collective-permute-done.15.both_ref
  44.3 0.9 %collective-permute-start.9 = (f32[12,16,128]{2,1,0:T(8,128)S(1)}, f32[12,16,128]{2,1,0:T(8,128)S(1)}, u32[]{:S(2)}, u32[]{:S(2)}) collective-permute-start(f32[12,16,128]{2,1,0:T(8,128)S(1)} %shard_map.116.ready_ref), channel_id=1, source_target_pairs={{0,128},{1,129},{2,130},{3,131},{4,132},{5,133},{6,134},{7,135},{8... | collective-permute-start | bytes 294920 | tf_op jit(solution)/shard_map/ppermute | solution.py:322
  45.2 0.1 shard_map.122.expand_ref
  45.3 0.0 collective-permute-done.13.core_ref
  45.4 1.0 %shard_map.119.rest_0_ = f32[4,32,128]{2,1,0:T(8,128)S(1)} custom-call(s32[2,12]{1,0:T(2,128)S(1)} %bitcast.6, s32[2,12]{1,0:T(2,128)S(1)} %bitcast.8, s32[2,12]{1,0:T(2,128)S(1)} %bitcast.10, s32[4,4]{1,0:T(4,128)S(1)} %bitcast.4, f32[2,16,1536]{2,1,0:T(8,128)S(1)} %copy-done.1, f32[2,16,1536]{2,1,0:T(8,128)S(1)} %collective-permute-done.13.core_ref, ...), custom_call_target="tpu_custom_call" | custom-call | flops 2000000 | bytes 1048576 | tf_op jit(solution)/shard_map/pallas_call | solution.py:363
  46.4 0.0 collective-permute-done.12.other_ref
  46.4 0.3 shard_map.120.own_ref
  46.7 0.2 shard_map.121.ready_ref
  47.0 1.3 %shard_map.123.rest_1_ = f32[8,32,128]{2,1,0:T(8,128)S(1)} custom-call(s32[2,12]{1,0:T(2,128)S(1)} %bitcast.7, s32[2,12]{1,0:T(2,128)S(1)} %bitcast.9, s32[2,12]{1,0:T(2,128)S(1)} %bitcast.11, s32[4,4]{1,0:T(4,128)S(1)} %bitcast.5, f32[2,16,1536]{2,1,0:T(8,128)S(1)} %copy-done.1, f32[2,16,1536]{2,1,0:T(8,128)S(1)} %collective-permute-done.13.core_ref, ...), custom_call_target="tpu_custom_call" | custom-call | flops 2000000 | bytes 1048576 | tf_op jit(solution)/shard_map/pallas_call | solution.py:363
  48.4 0.0 collective-permute-done.10.packed_ref
  48.4 0.2 shard_map.117.wide_ref
  48.6 0.0 collective-permute-done.11.other_ref
  48.6 0.3 shard_map.118.corner_ref
  48.9 1.6 %collective-permute-done.9.beside_ref = f32[12,16,128]{2,1,0:T(8,128)S(1)} collective-permute-done((f32[12,16,128]{2,1,0:T(8,128)S(1)}, f32[12,16,128]{2,1,0:T(8,128)S(1)}, u32[]{:S(2)}, u32[]{:S(2)}) %collective-permute-start.9) | collective-permute-done | bytes 98336 | tf_op jit(solution)/shard_map/ppermute | solution.py:322
  50.5 1.3 %shard_map.124 = f32[2,16,1536]{2,1,0:T(8,128)} custom-call(s32[8,1,12]{2,1,0:T(1,128)S(1)} %get-tuple-element.40.roster_ref, f32[12,16,128]{2,1,0:T(8,128)S(1)} %collective-permute-done.9.beside_ref, f32[12,16,128]{2,1,0:T(8,128)S(1)} %shard_map.118.corner_ref, bf16[12,256,128]{2,1,0:T(8,128)(2,1)S(1)} %get-tuple-element.70.wide_ref, ...), custom_call_target="tpu_custom_call" | custom-call | flops 2000000 | bytes 1048576 | tf_op jit(solution)/shard_map/pallas_call | solution.py:449
  (7 shorter events, 0.0 us)
Async XLA Ops:
  1.8 6.2 %collective-permute-start = (f32[12,16,128]{2,1,0:T(8,128)S(1)}, f32[12,16,128]{2,1,0:T(8,128)S(1)}, u32[]{:S(2)}, u32[]{:S(2)}) collective-permute-start(f32[12,16,128]{2,1,0:T(8,128)S(1)} %get-tuple-element.41.own_ref), channel_id=1, source_target_pairs={{0,128},{1,129},{2,130},{3,131},{4,132},{5,133},{6,134},{7,135},{8... | collective-permute-start | bytes 294920 | tf_op jit(solution)/shard_map/ppermute | solution.py:322
  8.3 6.9 %copy-start.1 = (f32[2,16,1536]{2,1,0:T(8,128)S(1)}, f32[2,16,1536]{2,1,0:T(8,128)}, u32[]{:S(2)}) copy-start(f32[2,16,1536]{2,1,0:T(8,128)} %own_ref.3) | copy-start | bytes 589828
  8.3 5.0 %collective-permute-start.1 = (f32[12,16,128]{2,1,0:T(8,128)S(1)}, f32[12,16,128]{2,1,0:T(8,128)S(1)}, u32[]{:S(2)}, u32[]{:S(2)}) collective-permute-start(f32[12,16,128]{2,1,0:T(8,128)S(1)} %shard_map.102.own_ref.after_ref), channel_id=1, source_target_pairs={{0,64},{1,65},{2,66},{3,67},{4,68},{5,69},{6,70},{7,71},{8,72},{9,... | collective-permute-start | bytes 294920 | tf_op jit(solution)/shard_map/ppermute | solution.py:322
  13.5 7.7 %collective-permute-start.2 = (f32[12,16,128]{2,1,0:T(8,128)S(1)}, f32[12,16,128]{2,1,0:T(8,128)S(1)}, u32[]{:S(2)}, u32[]{:S(2)}) collective-permute-start(f32[12,16,128]{2,1,0:T(8,128)S(1)} %shard_map.106.own_ref), channel_id=1, source_target_pairs={{0,32},{1,33},{2,34},{3,35},{4,36},{5,37},{6,38},{7,39},{8,40},{9,... | collective-permute-start | bytes 294920 | tf_op jit(solution)/shard_map/ppermute | solution.py:322
  15.2 10.8 %collective-permute-start.14 = (f32[2,16,1536]{2,1,0:T(8,128)S(1)}, f32[2,16,1536]{2,1,0:T(8,128)S(1)}, u32[]{:S(2)}, u32[]{:S(2)}) collective-permute-start(f32[2,16,1536]{2,1,0:T(8,128)S(1)} %copy-done.1), channel_id=1, source_target_pairs={{0,2},{1,3},{2,0},{3,1},{4,6},{5,7},{6,4},{7,5},{8,10},{9,11},{10,... | collective-permute-start | bytes 589832 | tf_op jit(solution)/shard_map/ppermute | solution.py:322
  18.1 10.8 %collective-permute-start.5 = (f32[7,64,128]{2,1,0:T(8,128)S(1)}, f32[7,64,128]{2,1,0:T(8,128)S(1)}, u32[]{:S(2)}, u32[]{:S(2)}) collective-permute-start(f32[7,64,128]{2,1,0:T(8,128)S(1)} %get-tuple-element.63), channel_id=1, source_target_pairs={{0,32},{1,33},{2,34},{3,35},{4,36},{5,37},{6,38},{7,39},{8,40},{9,... | collective-permute-start | bytes 688136 | tf_op jit(solution)/shard_map/ppermute | solution.py:322
  18.2 30.2 %collective-permute-start.10 = (f32[13,64,128]{2,1,0:T(8,128)S(1)}, f32[13,64,128]{2,1,0:T(8,128)S(1)}, u32[]{:S(2)}, u32[]{:S(2)}) collective-permute-start(f32[13,64,128]{2,1,0:T(8,128)S(1)} %get-tuple-element.69), channel_id=1, source_target_pairs={{0,128},{1,129},{2,130},{3,131},{4,132},{5,133},{6,134},{7,135},{8... | collective-permute-start | bytes 1277960 | tf_op jit(solution)/shard_map/ppermute | solution.py:322
  21.5 2.3 %collective-permute-start.3 = (f32[12,16,128]{2,1,0:T(8,128)S(1)}, f32[12,16,128]{2,1,0:T(8,128)S(1)}, u32[]{:S(2)}, u32[]{:S(2)}) collective-permute-start(f32[12,16,128]{2,1,0:T(8,128)S(1)} %shard_map.108.own_ref), channel_id=1, source_target_pairs={{0,1},{1,0},{2,3},{3,2},{4,5},{5,4},{6,7},{7,6},{8,9},{9,8},{10,11... | collective-permute-start | bytes 294920 | tf_op jit(solution)/shard_map/ppermute | solution.py:322
  21.6 10.8 %collective-permute-start.7 = (f32[6,64,128]{2,1,0:T(8,128)S(1)}, f32[6,64,128]{2,1,0:T(8,128)S(1)}, u32[]{:S(2)}, u32[]{:S(2)}) collective-permute-start(f32[6,64,128]{2,1,0:T(8,128)S(1)} %get-tuple-element.65), channel_id=1, source_target_pairs={{0,32},{1,33},{2,34},{3,35},{4,36},{5,37},{6,38},{7,39},{8,40},{9,... | collective-permute-start | bytes 589832 | tf_op jit(solution)/shard_map/ppermute | solution.py:322
  24.3 20.9 %copy-start.2 = (f32[12,2,64,128]{3,2,1,0:T(8,128)S(1)}, f32[12,2,64,128]{3,2,1,0:T(8,128)}, u32[]{:S(2)}) copy-start(f32[12,2,64,128]{3,2,1,0:T(8,128)} %weight_ref.4) | copy-start | bytes 2359300
  24.3 21.0 %copy-start = (f32[12,2,2,128,128]{4,3,2,1,0:T(8,128)S(1)}, f32[12,2,2,128,128]{4,3,2,1,0:T(8,128)}, u32[]{:S(2)}) copy-start(f32[12,2,2,128,128]{4,3,2,1,0:T(8,128)} %weight_ref.5) | copy-start | bytes 9437188
  24.3 21.0 %copy-start.3 = (s32[1,4,4]{2,1,0:T(4,128)S(1)}, s32[1,4,4]{2,1,0:T(4,128)}, u32[]{:S(2)}) copy-start(s32[1,4,4]{2,1,0:T(4,128)} %param.19) | copy-start | bytes 196
  24.3 21.0 %copy-start.4 = (s32[12,2]{0,1:T(2,128)S(1)}, s32[12,2]{0,1:T(2,128)}, u32[]{:S(2)}) copy-start(s32[12,2]{0,1:T(2,128)} %param.16) | copy-start | bytes 292
  24.3 21.0 %copy-start.5 = (s32[12,2]{0,1:T(2,128)S(1)}, s32[12,2]{0,1:T(2,128)}, u32[]{:S(2)}) copy-start(s32[12,2]{0,1:T(2,128)} %param.17) | copy-start | bytes 292
  24.3 21.0 %copy-start.6 = (s32[12,2]{0,1:T(2,128)S(1)}, s32[12,2]{0,1:T(2,128)}, u32[]{:S(2)}) copy-start(s32[12,2]{0,1:T(2,128)} %param.18) | copy-start | bytes 292
  24.3 9.8 %collective-permute-start.8 = (f32[12,16,128]{2,1,0:T(8,128)S(1)}, f32[12,16,128]{2,1,0:T(8,128)S(1)}, u32[]{:S(2)}, u32[]{:S(2)}) collective-permute-start(f32[12,16,128]{2,1,0:T(8,128)S(1)} %shard_map.111.ready_ref), channel_id=1, source_target_pairs={{0,32},{1,33},{2,34},{3,35},{4,36},{5,37},{6,38},{7,39},{8,40},{9,... | collective-permute-start | bytes 294920 | tf_op jit(solution)/shard_map/ppermute | solution.py:322
  25.9 18.4 %collective-permute-start.15 = (f32[2,16,1536]{2,1,0:T(8,128)S(1)}, f32[2,16,1536]{2,1,0:T(8,128)S(1)}, u32[]{:S(2)}, u32[]{:S(2)}) collective-permute-start(f32[2,16,1536]{2,1,0:T(8,128)S(1)} %collective-permute-done.14.far_ref), channel_id=1, source_target_pairs={{0,1},{1,0},{2,3},{3,2},{4,5},{5,4},{6,7},{7,6},{8,9},{9,8},{10,11... | collective-permute-start | bytes 589832 | tf_op jit(solution)/shard_map/ppermute | solution.py:322
  28.9 16.4 %collective-permute-start.13 = (f32[2,16,1536]{2,1,0:T(8,128)S(1)}, f32[2,16,1536]{2,1,0:T(8,128)S(1)}, u32[]{:S(2)}, u32[]{:S(2)}) collective-permute-start(f32[2,16,1536]{2,1,0:T(8,128)S(1)} %copy-done.1), channel_id=1, source_target_pairs={{0,1},{1,0},{2,3},{3,2},{4,5},{5,4},{6,7},{7,6},{8,9},{9,8},{10,11... | collective-permute-start | bytes 589832 | tf_op jit(solution)/shard_map/ppermute | solution.py:322
  32.4 6.3 %collective-permute-start.6 = (f32[12,16,128]{2,1,0:T(8,128)S(1)}, f32[12,16,128]{2,1,0:T(8,128)S(1)}, u32[]{:S(2)}, u32[]{:S(2)}) collective-permute-start(f32[12,16,128]{2,1,0:T(8,128)S(1)} %shard_map.110.own_ref.after_ref.rest_1_), channel_id=1, source_target_pairs={{0,34},{1,35},{2,32},{3,33},{4,38},{5,39},{6,36},{7,37},{8,42},{9,... | collective-permute-start | bytes 294920 | tf_op jit(solution)/shard_map/ppermute | solution.py:322
  34.1 6.1 %collective-permute-start.4 = (f32[12,16,128]{2,1,0:T(8,128)S(1)}, f32[12,16,128]{2,1,0:T(8,128)S(1)}, u32[]{:S(2)}, u32[]{:S(2)}) collective-permute-start(f32[12,16,128]{2,1,0:T(8,128)S(1)} %shard_map.110.own_ref.after_ref.rest_1_), channel_id=1, source_target_pairs={{0,2},{1,3},{2,0},{3,1},{4,6},{5,7},{6,4},{7,5},{8,10},{9,11},{10,... | collective-permute-start | bytes 294920 | tf_op jit(solution)/shard_map/ppermute | solution.py:322
  40.7 5.7 %collective-permute-start.12 = (f32[12,16,128]{2,1,0:T(8,128)S(1)}, f32[12,16,128]{2,1,0:T(8,128)S(1)}, u32[]{:S(2)}, u32[]{:S(2)}) collective-permute-start(f32[12,16,128]{2,1,0:T(8,128)S(1)} %shard_map.115.own_ref.rest_0_.after_ref), channel_id=1, source_target_pairs={{0,64},{1,65},{2,66},{3,67},{4,68},{5,69},{6,70},{7,71},{8,72},{9,... | collective-permute-start | bytes 294920 | tf_op jit(solution)/shard_map/ppermute | solution.py:322
  41.5 7.1 %collective-permute-start.11 = (f32[12,16,128]{2,1,0:T(8,128)S(1)}, f32[12,16,128]{2,1,0:T(8,128)S(1)}, u32[]{:S(2)}, u32[]{:S(2)}) collective-permute-start(f32[12,16,128]{2,1,0:T(8,128)S(1)} %shard_map.115.own_ref.rest_0_.after_ref), channel_id=1, source_target_pairs={{0,192},{1,193},{2,194},{3,195},{4,196},{5,197},{6,198},{7,199},{8... | collective-permute-start | bytes 294920 | tf_op jit(solution)/shard_map/ppermute | solution.py:322
  44.3 6.2 %collective-permute-start.9 = (f32[12,16,128]{2,1,0:T(8,128)S(1)}, f32[12,16,128]{2,1,0:T(8,128)S(1)}, u32[]{:S(2)}, u32[]{:S(2)}) collective-permute-start(f32[12,16,128]{2,1,0:T(8,128)S(1)} %shard_map.116.ready_ref), channel_id=1, source_target_pairs={{0,128},{1,129},{2,130},{3,131},{4,132},{5,133},{6,134},{7,135},{8... | collective-permute-start | bytes 294920 | tf_op jit(solution)/shard_map/ppermute | solution.py:322

commit v9 on v8

--- a/solution.py
+++ b/solution.py
@@ -180,14 +180,10 @@
         prepare_block(k, k, weight_ref, own_out, other_out, packed_ref)
 
 
-def fetch_kernel(levels, coupling_hbm, after_ref, *refs):
-    count = len(levels)
-    outs, weights, sems = refs[: 2 * count], refs[2 * count : -1], refs[-1]
-    copies = started([(coupling_hbm.at[level], out) for level, out in zip(levels, weights)], sems)
-    for n in range(count):
-        copies[n].wait()
-        for k in range(weights[n].shape[0]):
-            prepare_block(k, k, weights[n], outs[2 * n], outs[2 * n + 1])
+def fetch_kernel(levels, coupling_ref, after_ref, *outs):
+    for n, level in enumerate(levels):
+        for k in range(coupling_ref.shape[1]):
+            prepare_block(k, k, coupling_ref.at[level], outs[2 * n], outs[2 * n + 1])
 
 
 def unpack_kernel(packed_ref, *rest):
@@ -202,7 +198,8 @@
         out_ref[k] = jnp.concatenate(split(weight_ref[k].reshape(128, 128)), axis=0)
 
 
-def own_kernel(own_ref, wide_ref, out_ref):
+def own_kernel(own_ref, wide_ref, *rest):
+    out_ref = rest[-1]
     for k in range(out_ref.shape[0]):
         out_ref[k] = times(own_ref[k], wide_ref[k])
 
@@ -393,7 +390,6 @@
         hbm=(3,),
     )
     away_4 = flipped(packed_4, top // 4, 0)
-    far = flipped(tied(field_in, wide_4), 0, 2)
     coeffs = run(level_kernel, state, [back_0, other, wide_0, ready])
 
     other = flipped(coeffs, top // 2, 0)
@@ -423,15 +419,9 @@
     beside = flipped(ready, top // 4, 0)
     other = flipped(coeffs, 0, 2)
     own_5, wide_5, own_7, wide_7 = run(
-        part(fetch_kernel, (5, 7)),
-        [wide] * 4,
-        [coupling_hbm],
-        [coeffs],
-        scratch=[level_weights, level_weights, DMA((2,))],
-        hbm=(0,),
-    )
-    core = flipped(tied(field_in, coeffs), 0, 1)
-    both = flipped(tied(far, coeffs), 0, 1)
+        part(fetch_kernel, (5, 7)), [wide] * 4, [pltpu.with_memory_space_constraint(coupling, VMEM)], [coeffs]
+    )
+    far = flipped(tied(field_in, coeffs), 0, 2)
     away = run(unpack_kernel, wide, [away_4, away_more], [coeffs])
     side = run(part(side_kernel, 5), state, [names, away_4, corner, away, beside, wide_5], scratch=[state])
     coeffs = run(part(double_kernel, 4), state, [names, other, wide_4, ready, own_5, side], [own_7], scratch=[state])
@@ -442,9 +432,11 @@
     beside = flipped(ready, top, 0)
     last = run(spread_kernel, wide, [expanding], [coeffs])
     away = run(unpack_kernel, wide, [away_6], [coeffs])
-    pieces = [near_piece(n, coeffs) for n in range(len(NEAR_PARTS))]
-    here = run(part(plain_kernel, 6), state, [names, other, wide_6, ready], [pieces[0]])
-    ready = run(own_kernel, state, [here, own_7])
+    core = flipped(tied(field_in, coeffs), 0, 1)
+    both = flipped(tied(far, coeffs), 0, 1)
+    here = run(part(plain_kernel, 6), state, [names, other, wide_6, ready], [last])
+    ready = run(own_kernel, state, [here, own_7], [away])
+    pieces = [near_piece(n, ready) for n in range(len(NEAR_PARTS))]
     corner = run(corner_kernel, state, [away_6, corner, away])
     return call(
         part(last_kernel, 7),

time: 52.1 us -> 50.9 us (0.977)
  waiting for transfers between devices: 10.4 us -> 8.2 us
  starting transfers between devices: 23.4 us -> 25.3 us
  Pallas kernels: 17.6 us -> 16.6 us
    ppermute x16, waiting for transfers between devices: 10.4 us -> 8.2 us  [flipped(): return lax.ppermute(value, ('leaf', 'sub'), pairs)]
    ppermute x16, starting transfers between devices: 23.4 us -> 25.3 us  [flipped(): return lax.ppermute(value, ('leaf', 'sub'), pairs)]
    pallas_call x22, Pallas kernels: 14 us -> 13 us  [run(): call(kernel, outs, spaces, [VMEM] * len(outs) if several else VMEM, scratch)]
  transfers between devices with their start and end apart: 16 -> 16, of which waited for: 6 -> 6; matrix products, arithmetic and copies ran while one was open for 0% -> 0% of each run, Pallas kernels for 27% -> 26%
where the time goes in v9:
time: 50.9 us; the launch traced here: 50.8 us
  starting transfers between devices  25.3 us (50%)
  Pallas kernels  16.6 us (33%)
  waiting for transfers between devices  8.2 us (16%)
  between operations  0.56 us (1%)
    ppermute x16, starting transfers between devices, flipped(): return lax.ppermute(value, ('leaf', 'sub'), pairs)  25.3 us
    pallas_call x22, Pallas kernels, run(): call(kernel, outs, spaces, [VMEM] * len(outs) if several else VMEM, scratch)  13 us
    ppermute x16, waiting for transfers between devices, flipped(): return lax.ppermute(value, ('leaf', 'sub'), pairs)  8.2 us
    pallas_call x2, Pallas kernels, near_piece(): call(functools.partial(near_kernel, begin), VMEM((count, 2 * rhs, 128), F...  2.35 us
    pallas_call x1, Pallas kernels, on_device(): call(part(last_kernel, 7), jax.ShapeDtypeStruct(field_in.shape, F32), [VM...  1.26 us
  transfers between devices with their start and end apart: 16, of which 6 were waited for; matrix products, arithmetic and copies ran while one was open for 0% of the time, Pallas kernels for 26%

profile of v9, /device:TPU:64, one launch (start us, length us, event | category | flops | bytes accessed | tf_op | source)
XLA Modules:
  0.0 50.8 jit_solution(1225254384663268546)
XLA Ops:
  0.0 1.8 %shard_map.100 = (f32[12,16,128]{2,1,0:T(8,128)S(1)}, f32[12,2,64,128]{3,2,1,0:T(8,128)S(1)}, s32[8,1,12]{2,1,0:T(1,128)S(1)}) custom-call(f32[2,16,1536]{2,1,0:T(8,128)} %own_ref.3, f32[12,2,64,128]{3,2,1,0:T(8,128)} %weight_hbm.1, f32[8,12,2,64,128]{4,3,2,1,0:T(8,128)} %coupling_ref.1, s32[8,1,12]{2,1,0:T(1,128)} %roster_hbm.1), custom_call_target="tpu_custom_call" | custom-call | flops 2000000 | bytes 1048576 | tf_op jit(solution)/shard_map/pallas_call | solution.py:356
  1.8 3.1 %collective-permute-start = (f32[12,16,128]{2,1,0:T(8,128)S(1)}, f32[12,16,128]{2,1,0:T(8,128)S(1)}, u32[]{:S(2)}, u32[]{:S(2)}) collective-permute-start(f32[12,16,128]{2,1,0:T(8,128)S(1)} %get-tuple-element.41.own_ref), channel_id=1, source_target_pairs={{0,128},{1,129},{2,130},{3,131},{4,132},{5,133},{6,134},{7,135},{8... | collective-permute-start | bytes 294920 | tf_op jit(solution)/shard_map/ppermute | solution.py:319
  4.9 2.4 %shard_map.101 = (f32[12,16,128]{2,1,0:T(8,128)S(1)}, bf16[12,256,128]{2,1,0:T(8,128)(2,1)S(1)}, s32[8,128]{1,0:T(8,128)S(1)}, bf16[12,256,128]{2,1,0:T(8,128)(2...) custom-call(f32[12,16,128]{2,1,0:T(8,128)S(1)} %get-tuple-element.41, ...), custom_call_target="tpu_custom_call" | custom-call | flops 2000000 | bytes 1048576 | tf_op jit(solution)/shard_map/pallas_call | solution.py:356
  7.3 0.7 %collective-permute-done.other_ref = f32[12,16,128]{2,1,0:T(8,128)S(1)} collective-permute-done((f32[12,16,128]{2,1,0:T(8,128)S(1)}, f32[12,16,128]{2,1,0:T(8,128)S(1)}, u32[]{:S(2)}, u32[]{:S(2)}) %collective-permute-start) | collective-permute-done | bytes 98336 | tf_op jit(solution)/shard_map/ppermute | solution.py:319
  8.0 0.2 shard_map.102.own_ref.after_ref
  8.3 1.6 %collective-permute-start.1 = (f32[12,16,128]{2,1,0:T(8,128)S(1)}, f32[12,16,128]{2,1,0:T(8,128)S(1)}, u32[]{:S(2)}, u32[]{:S(2)}) collective-permute-start(f32[12,16,128]{2,1,0:T(8,128)S(1)} %shard_map.102.own_ref.after_ref), channel_id=1, source_target_pairs={{0,64},{1,65},{2,66},{3,67},{4,68},{5,69},{6,70},{7,71},{8,72},{9,... | collective-permute-start | bytes 294920 | tf_op jit(solution)/shard_map/ppermute | solution.py:319
  9.9 2.6 %shard_map.103 = (f32[12,16,128]{2,1,0:T(8,128)S(1)}, bf16[12,256,128]{2,1,0:T(8,128)(2,1)S(1)}, s32[8,128]{1,0:T(8,128)S(1)}, bf16[12,256,128]{2,1,0:T(8,128)(2...) custom-call(f32[12,16,128]{2,1,0:T(8,128)S(1)} %shard_map.102.own_re, ...), custom_call_target="tpu_custom_call" | custom-call | flops 2000000 | bytes 1048576 | tf_op jit(solution)/shard_map/pallas_call | solution.py:356
  12.5 0.0 copy-start.1
  12.5 0.0 slice-start.1
  12.5 0.5 %shard_map.105 = (bf16[12,256,128]{2,1,0:T(8,128)(2,1)S(1)}, bf16[12,256,128]{2,1,0:T(8,128)(2,1)S(1)}, f32[13,64,128]{2,1,0:T(8,128)S(1)}) custom-call(f32[12,2,64,128]{3,2,1,0:T(8,128)S(1)} %get-tuple-element.55.weight_ref, s32[8,1,12]{2,1,0:T(1,128)S(1)} %get-tuple-element.40.roster_ref, f32[12,16,128]{2,1,0:T(8,128)S(1)} %shard_map.102.own_ref.after_ref), custom_call_target="tpu_custom_call" | custom-call | flops 2000000 | bytes 1048576 | tf_op jit(solution)/shard_map/pallas_call | solution.py:356
  13.1 0.5 %shard_map.104 = (bf16[12,256,128]{2,1,0:T(8,128)(2,1)S(1)}, bf16[12,256,128]{2,1,0:T(8,128)(2,1)S(1)}, s32[8,128]{1,0:T(8,128)S(1)}) custom-call(f32[12,2,64,128]{3,2,1,0:T(8,128)S(1)} %get-tuple-element.48.weight_ref, s32[8,1,12]{2,1,0:T(1,128)S(1)} %get-tuple-element.40.roster_ref, f32[12,16,128]{2,1,0:T(8,128)S(1)} %shard_map.102.own_ref.after_ref), custom_call_target="tpu_custom_call" | custom-call | flops 2000000 | bytes 1048576 | tf_op jit(solution)/shard_map/pallas_call | solution.py:356
  13.6 0.0 collective-permute-done.1.other_ref
  13.6 0.2 shard_map.106.own_ref
  13.9 1.7 %collective-permute-start.2 = (f32[12,16,128]{2,1,0:T(8,128)S(1)}, f32[12,16,128]{2,1,0:T(8,128)S(1)}, u32[]{:S(2)}, u32[]{:S(2)}) collective-permute-start(f32[12,16,128]{2,1,0:T(8,128)S(1)} %shard_map.106.own_ref), channel_id=1, source_target_pairs={{0,32},{1,33},{2,34},{3,35},{4,36},{5,37},{6,38},{7,39},{8,40},{9,... | collective-permute-start | bytes 294920 | tf_op jit(solution)/shard_map/ppermute | solution.py:319
  15.5 0.5 collective-permute-start.5
  16.0 1.6 %collective-permute-start.7 = (f32[6,64,128]{2,1,0:T(8,128)S(1)}, f32[6,64,128]{2,1,0:T(8,128)S(1)}, u32[]{:S(2)}, u32[]{:S(2)}) collective-permute-start(f32[6,64,128]{2,1,0:T(8,128)S(1)} %get-tuple-element.65), channel_id=1, source_target_pairs={{0,32},{1,33},{2,34},{3,35},{4,36},{5,37},{6,38},{7,39},{8,40},{9,... | collective-permute-start | bytes 589832 | tf_op jit(solution)/shard_map/ppermute | solution.py:319
  17.6 0.2 shard_map.107.ready_ref
  17.8 1.8 %collective-permute-done.2.other_ref = f32[12,16,128]{2,1,0:T(8,128)S(1)} collective-permute-done((f32[12,16,128]{2,1,0:T(8,128)S(1)}, f32[12,16,128]{2,1,0:T(8,128)S(1)}, u32[]{:S(2)}, u32[]{:S(2)}) %collective-permute-start.2) | collective-permute-done | bytes 98336 | tf_op jit(solution)/shard_map/ppermute | solution.py:319
  19.6 0.2 shard_map.108.own_ref
  19.9 0.1 collective-permute-start.3
  20.0 2.8 %collective-permute-start.10 = (f32[13,64,128]{2,1,0:T(8,128)S(1)}, f32[13,64,128]{2,1,0:T(8,128)S(1)}, u32[]{:S(2)}, u32[]{:S(2)}) collective-permute-start(f32[13,64,128]{2,1,0:T(8,128)S(1)} %get-tuple-element.69), channel_id=1, source_target_pairs={{0,128},{1,129},{2,130},{3,131},{4,132},{5,133},{6,134},{7,135},{8... | collective-permute-start | bytes 1277960 | tf_op jit(solution)/shard_map/ppermute | solution.py:319
  22.8 0.2 shard_map.109.ready_ref
  23.0 0.0 collective-permute-done.3.other_ref
  23.0 0.2 shard_map.110.own_ref.after_ref.rest_1_
  23.3 3.3 %collective-permute-start.14 = (f32[2,16,1536]{2,1,0:T(8,128)S(1)}, f32[2,16,1536]{2,1,0:T(8,128)S(1)}, u32[]{:S(2)}, u32[]{:S(2)}) collective-permute-start(f32[2,16,1536]{2,1,0:T(8,128)S(1)} %copy-done.1), channel_id=1, source_target_pairs={{0,2},{1,3},{2,0},{3,1},{4,6},{5,7},{6,4},{7,5},{8,10},{9,11},{10,... | collective-permute-start | bytes 589832 | tf_op jit(solution)/shard_map/ppermute | solution.py:319
  26.6 0.2 shard_map.111.ready_ref
  26.8 0.0 copy-start.2
  26.8 0.8 %collective-permute-start.8 = (f32[12,16,128]{2,1,0:T(8,128)S(1)}, f32[12,16,128]{2,1,0:T(8,128)S(1)}, u32[]{:S(2)}, u32[]{:S(2)}) collective-permute-start(f32[12,16,128]{2,1,0:T(8,128)S(1)} %shard_map.111.ready_ref), channel_id=1, source_target_pairs={{0,32},{1,33},{2,34},{3,35},{4,36},{5,37},{6,38},{7,39},{8,40},{9,... | collective-permute-start | bytes 294920 | tf_op jit(solution)/shard_map/ppermute | solution.py:319
  27.6 0.0 collective-permute-done.5.packed_ref
  27.6 0.5 collective-permute-start.6
  28.1 0.0 collective-permute-done.7.rest_0_
  28.1 2.9 %collective-permute-start.4 = (f32[12,16,128]{2,1,0:T(8,128)S(1)}, f32[12,16,128]{2,1,0:T(8,128)S(1)}, u32[]{:S(2)}, u32[]{:S(2)}) collective-permute-start(f32[12,16,128]{2,1,0:T(8,128)S(1)} %shard_map.110.own_ref.after_ref.rest_1_), channel_id=1, source_target_pairs={{0,2},{1,3},{2,0},{3,1},{4,6},{5,7},{6,4},{7,5},{8,10},{9,11},{10,... | collective-permute-start | bytes 294920 | tf_op jit(solution)/shard_map/ppermute | solution.py:319
  31.0 0.9 %shard_map.112 = (bf16[12,256,128]{2,1,0:T(8,128)(2,1)S(1)}, bf16[12,256,128]{2,1,0:T(8,128)(2,1)S(1)}, bf16[12,256,128]{2,1,0:T(8,128)(2,1)S(1)}, bf16[12,256,128]{2,1,0:T(8,128)(2,1)S(1)}) custom-call(f32[8,12,2,64,128]{4,3,2,1,0:T(8,128)S(1)} %bitcast.5, f32[12,16,128]{2,1,0:T(8,128)S(1)} %shard_map.110.own_ref.after_ref.rest_1_), custom_call_target="tpu_custom_call" | custom-call | flops 2000000 | bytes 1048576 | tf_op jit(solution)/shard_map/pallas_call | solution.py:356
  32.0 0.2 shard_map.113.away_ref
  32.1 3.0 %collective-permute-done.8.beside_ref = f32[12,16,128]{2,1,0:T(8,128)S(1)} collective-permute-done((f32[12,16,128]{2,1,0:T(8,128)S(1)}, f32[12,16,128]{2,1,0:T(8,128)S(1)}, u32[]{:S(2)}, u32[]{:S(2)}) %collective-permute-start.8) | collective-permute-done | bytes 98336 | tf_op jit(solution)/shard_map/ppermute | solution.py:319
  35.1 0.9 %collective-permute-done.6.corner_ref = f32[12,16,128]{2,1,0:T(8,128)S(1)} collective-permute-done((f32[12,16,128]{2,1,0:T(8,128)S(1)}, f32[12,16,128]{2,1,0:T(8,128)S(1)}, u32[]{:S(2)}, u32[]{:S(2)}) %collective-permute-start.6) | collective-permute-done | bytes 98336 | tf_op jit(solution)/shard_map/ppermute | solution.py:319
  36.0 0.5 %shard_map.114.side_ref = f32[12,16,128]{2,1,0:T(8,128)S(1)} custom-call(s32[8,1,12]{2,1,0:T(1,128)S(1)} %get-tuple-element.40.roster_ref, f32[7,64,128]{2,1,0:T(8,128)S(1)} %collective-permute-done.5.packed_ref, f32[12,16,128]{2,1,0:T(8,128)S(1)} %collective-permute-done.6.corner_ref, bf16[12,256,128]{2,1,0:T(8,128)(2,1)S(1)} %shard_map.113.away_ref, ...), custom_call_target="tpu_custom_call" | custom-call | flops 2000000 | bytes 1048576 | tf_op jit(solution)/shard_map/pallas_call | solution.py:356
  36.6 0.0 copy-start
  36.6 0.0 copy-start.3
  36.6 0.0 copy-start.4
  36.6 0.0 copy-start.5
  36.6 0.0 copy-start.6
  36.6 0.5 collective-permute-done.4.other_ref
  37.1 0.4 shard_map.115.own_ref.rest_0_.after_ref
  37.5 0.1 collective-permute-start.13
  37.6 0.0 collective-permute-done.14.far_ref
  37.6 0.5 collective-permute-start.15
  38.1 0.7 %collective-permute-start.12 = (f32[12,16,128]{2,1,0:T(8,128)S(1)}, f32[12,16,128]{2,1,0:T(8,128)S(1)}, u32[]{:S(2)}, u32[]{:S(2)}) collective-permute-start(f32[12,16,128]{2,1,0:T(8,128)S(1)} %shard_map.115.own_ref.rest_0_.after_ref), channel_id=1, source_target_pairs={{0,64},{1,65},{2,66},{3,67},{4,68},{5,69},{6,70},{7,71},{8,72},{9,... | collective-permute-start | bytes 294920 | tf_op jit(solution)/shard_map/ppermute | solution.py:319
  38.8 2.6 %collective-permute-start.11 = (f32[12,16,128]{2,1,0:T(8,128)S(1)}, f32[12,16,128]{2,1,0:T(8,128)S(1)}, u32[]{:S(2)}, u32[]{:S(2)}) collective-permute-start(f32[12,16,128]{2,1,0:T(8,128)S(1)} %shard_map.115.own_ref.rest_0_.after_ref), channel_id=1, source_target_pairs={{0,192},{1,193},{2,194},{3,195},{4,196},{5,197},{6,198},{7,199},{8... | collective-permute-start | bytes 294920 | tf_op jit(solution)/shard_map/ppermute | solution.py:319
  41.4 0.2 shard_map.116.ready_ref
  41.7 1.3 %collective-permute-done.12.other_ref = f32[12,16,128]{2,1,0:T(8,128)S(1)} collective-permute-done((f32[12,16,128]{2,1,0:T(8,128)S(1)}, f32[12,16,128]{2,1,0:T(8,128)S(1)}, u32[]{:S(2)}, u32[]{:S(2)}) %collective-permute-start.12) | collective-permute-done | bytes 98336 | tf_op jit(solution)/shard_map/ppermute | solution.py:319
  42.9 2.7 %collective-permute-start.9 = (f32[12,16,128]{2,1,0:T(8,128)S(1)}, f32[12,16,128]{2,1,0:T(8,128)S(1)}, u32[]{:S(2)}, u32[]{:S(2)}) collective-permute-start(f32[12,16,128]{2,1,0:T(8,128)S(1)} %shard_map.116.ready_ref), channel_id=1, source_target_pairs={{0,128},{1,129},{2,130},{3,131},{4,132},{5,133},{6,134},{7,135},{8... | collective-permute-start | bytes 294920 | tf_op jit(solution)/shard_map/ppermute | solution.py:319
  45.7 0.1 shard_map.119.rest_0_.expand_ref
  45.7 0.3 shard_map.120.own_ref
  46.1 0.0 collective-permute-done.10.packed_ref
  46.1 0.2 shard_map.117.wide_ref.rest_0_
  46.3 0.2 shard_map.121.rest_0_.ready_ref
  46.5 0.3 shard_map.118.corner_ref
  46.8 0.0 collective-permute-done.13.core_ref
  46.8 0.0 collective-permute-done.15.both_ref
  46.9 1.3 %shard_map.123.rest_1_ = f32[8,32,128]{2,1,0:T(8,128)S(1)} custom-call(s32[2,12]{1,0:T(2,128)S(1)} %bitcast.8, s32[2,12]{1,0:T(2,128)S(1)} %bitcast.10, s32[2,12]{1,0:T(2,128)S(1)} %bitcast.12, s32[4,4]{1,0:T(4,128)S(1)} %bitcast.6, f32[2,16,1536]{2,1,0:T(8,128)S(1)} %copy-done.1, f32[2,16,1536]{2,1,0:T(8,128)S(1)} %collective-permute-done.13.core_ref, ...), custom_call_target="tpu_custom_call" | custom-call | flops 2000000 | bytes 1048576 | tf_op jit(solution)/shard_map/pallas_call | solution.py:360
  48.3 1.0 %shard_map.122.rest_0_ = f32[4,32,128]{2,1,0:T(8,128)S(1)} custom-call(s32[2,12]{1,0:T(2,128)S(1)} %bitcast.9, s32[2,12]{1,0:T(2,128)S(1)} %bitcast.11, s32[2,12]{1,0:T(2,128)S(1)} %bitcast.13, s32[4,4]{1,0:T(4,128)S(1)} %bitcast.7, f32[2,16,1536]{2,1,0:T(8,128)S(1)} %copy-done.1, f32[2,16,1536]{2,1,0:T(8,128)S(1)} %collective-permute-done.13.core_ref, ...), custom_call_target="tpu_custom_call" | custom-call | flops 2000000 | bytes 1048576 | tf_op jit(solution)/shard_map/pallas_call | solution.py:360
  49.3 0.0 collective-permute-done.9.beside_ref
  49.4 1.3 %shard_map.124 = f32[2,16,1536]{2,1,0:T(8,128)} custom-call(s32[8,1,12]{2,1,0:T(1,128)S(1)} %get-tuple-element.40.roster_ref, f32[12,16,128]{2,1,0:T(8,128)S(1)} %collective-permute-done.9.beside_ref, f32[12,16,128]{2,1,0:T(8,128)S(1)} %shard_map.118.corner_ref, bf16[12,256,128]{2,1,0:T(8,128)(2,1)S(1)} %get-tuple-element.70.wide_ref, ...), custom_call_target="tpu_custom_call" | custom-call | flops 2000000 | bytes 1048576 | tf_op jit(solution)/shard_map/pallas_call | solution.py:441
  (12 shorter events, 0.0 us)
Async XLA Ops:
  1.8 6.2 %collective-permute-start = (f32[12,16,128]{2,1,0:T(8,128)S(1)}, f32[12,16,128]{2,1,0:T(8,128)S(1)}, u32[]{:S(2)}, u32[]{:S(2)}) collective-permute-start(f32[12,16,128]{2,1,0:T(8,128)S(1)} %get-tuple-element.41.own_ref), channel_id=1, source_target_pairs={{0,128},{1,129},{2,130},{3,131},{4,132},{5,133},{6,134},{7,135},{8... | collective-permute-start | bytes 294920 | tf_op jit(solution)/shard_map/ppermute | solution.py:319
  8.3 5.4 %collective-permute-start.1 = (f32[12,16,128]{2,1,0:T(8,128)S(1)}, f32[12,16,128]{2,1,0:T(8,128)S(1)}, u32[]{:S(2)}, u32[]{:S(2)}) collective-permute-start(f32[12,16,128]{2,1,0:T(8,128)S(1)} %shard_map.102.own_ref.after_ref), channel_id=1, source_target_pairs={{0,64},{1,65},{2,66},{3,67},{4,68},{5,69},{6,70},{7,71},{8,72},{9,... | collective-permute-start | bytes 294920 | tf_op jit(solution)/shard_map/ppermute | solution.py:319
  9.9 21.2 %slice-start = ((s8[6291456]{0:T(1024)(128)(4,1)}), s8[4194304]{0:T(1024)(128)(4,1)S(1)}, s32[]{:S(2)}) async-start(s8[6291456]{0:T(1024)(128)(4,1)} %bitcast.4), calls=%async_computation | async-start | bytes 8388608
  12.5 10.8 %copy-start.1 = (f32[2,16,1536]{2,1,0:T(8,128)S(1)}, f32[2,16,1536]{2,1,0:T(8,128)}, u32[]{:S(2)}) copy-start(f32[2,16,1536]{2,1,0:T(8,128)} %own_ref.3) | copy-start | bytes 589828
  12.5 18.5 %slice-start.1 = ((s8[6291456]{0:T(1024)(128)(4,1)}), s8[2097152]{0:T(1024)(128)(4,1)S(1)}, s32[]{:S(2)}) async-start(s8[6291456]{0:T(1024)(128)(4,1)} %bitcast.4), calls=%async_computation.1 | async-start | bytes 4194304
  13.9 5.8 %collective-permute-start.2 = (f32[12,16,128]{2,1,0:T(8,128)S(1)}, f32[12,16,128]{2,1,0:T(8,128)S(1)}, u32[]{:S(2)}, u32[]{:S(2)}) collective-permute-start(f32[12,16,128]{2,1,0:T(8,128)S(1)} %shard_map.106.own_ref), channel_id=1, source_target_pairs={{0,32},{1,33},{2,34},{3,35},{4,36},{5,37},{6,38},{7,39},{8,40},{9,... | collective-permute-start | bytes 294920 | tf_op jit(solution)/shard_map/ppermute | solution.py:319
  15.5 12.1 %collective-permute-start.5 = (f32[7,64,128]{2,1,0:T(8,128)S(1)}, f32[7,64,128]{2,1,0:T(8,128)S(1)}, u32[]{:S(2)}, u32[]{:S(2)}) collective-permute-start(f32[7,64,128]{2,1,0:T(8,128)S(1)} %get-tuple-element.63), channel_id=1, source_target_pairs={{0,32},{1,33},{2,34},{3,35},{4,36},{5,37},{6,38},{7,39},{8,40},{9,... | collective-permute-start | bytes 688136 | tf_op jit(solution)/shard_map/ppermute | solution.py:319
  16.0 12.1 %collective-permute-start.7 = (f32[6,64,128]{2,1,0:T(8,128)S(1)}, f32[6,64,128]{2,1,0:T(8,128)S(1)}, u32[]{:S(2)}, u32[]{:S(2)}) collective-permute-start(f32[6,64,128]{2,1,0:T(8,128)S(1)} %get-tuple-element.65), channel_id=1, source_target_pairs={{0,32},{1,33},{2,34},{3,35},{4,36},{5,37},{6,38},{7,39},{8,40},{9,... | collective-permute-start | bytes 589832 | tf_op jit(solution)/shard_map/ppermute | solution.py:319
  19.9 3.2 %collective-permute-start.3 = (f32[12,16,128]{2,1,0:T(8,128)S(1)}, f32[12,16,128]{2,1,0:T(8,128)S(1)}, u32[]{:S(2)}, u32[]{:S(2)}) collective-permute-start(f32[12,16,128]{2,1,0:T(8,128)S(1)} %shard_map.108.own_ref), channel_id=1, source_target_pairs={{0,1},{1,0},{2,3},{3,2},{4,5},{5,4},{6,7},{7,6},{8,9},{9,8},{10,11... | collective-permute-start | bytes 294920 | tf_op jit(solution)/shard_map/ppermute | solution.py:319
  20.0 26.1 %collective-permute-start.10 = (f32[13,64,128]{2,1,0:T(8,128)S(1)}, f32[13,64,128]{2,1,0:T(8,128)S(1)}, u32[]{:S(2)}, u32[]{:S(2)}) collective-permute-start(f32[13,64,128]{2,1,0:T(8,128)S(1)} %get-tuple-element.69), channel_id=1, source_target_pairs={{0,128},{1,129},{2,130},{3,131},{4,132},{5,133},{6,134},{7,135},{8... | collective-permute-start | bytes 1277960 | tf_op jit(solution)/shard_map/ppermute | solution.py:319
  23.3 14.3 %collective-permute-start.14 = (f32[2,16,1536]{2,1,0:T(8,128)S(1)}, f32[2,16,1536]{2,1,0:T(8,128)S(1)}, u32[]{:S(2)}, u32[]{:S(2)}) collective-permute-start(f32[2,16,1536]{2,1,0:T(8,128)S(1)} %copy-done.1), channel_id=1, source_target_pairs={{0,2},{1,3},{2,0},{3,1},{4,6},{5,7},{6,4},{7,5},{8,10},{9,11},{10,... | collective-permute-start | bytes 589832 | tf_op jit(solution)/shard_map/ppermute | solution.py:319
  26.8 18.9 %copy-start.2 = (f32[12,2,64,128]{3,2,1,0:T(8,128)S(1)}, f32[12,2,64,128]{3,2,1,0:T(8,128)}, u32[]{:S(2)}) copy-start(f32[12,2,64,128]{3,2,1,0:T(8,128)} %weight_ref.3) | copy-start | bytes 2359300
  26.8 8.3 %collective-permute-start.8 = (f32[12,16,128]{2,1,0:T(8,128)S(1)}, f32[12,16,128]{2,1,0:T(8,128)S(1)}, u32[]{:S(2)}, u32[]{:S(2)}) collective-permute-start(f32[12,16,128]{2,1,0:T(8,128)S(1)} %shard_map.111.ready_ref), channel_id=1, source_target_pairs={{0,32},{1,33},{2,34},{3,35},{4,36},{5,37},{6,38},{7,39},{8,40},{9,... | collective-permute-start | bytes 294920 | tf_op jit(solution)/shard_map/ppermute | solution.py:319
  27.6 8.4 %collective-permute-start.6 = (f32[12,16,128]{2,1,0:T(8,128)S(1)}, f32[12,16,128]{2,1,0:T(8,128)S(1)}, u32[]{:S(2)}, u32[]{:S(2)}) collective-permute-start(f32[12,16,128]{2,1,0:T(8,128)S(1)} %shard_map.110.own_ref.after_ref.rest_1_), channel_id=1, source_target_pairs={{0,34},{1,35},{2,32},{3,33},{4,38},{5,39},{6,36},{7,37},{8,42},{9,... | collective-permute-start | bytes 294920 | tf_op jit(solution)/shard_map/ppermute | solution.py:319
  28.1 9.0 %collective-permute-start.4 = (f32[12,16,128]{2,1,0:T(8,128)S(1)}, f32[12,16,128]{2,1,0:T(8,128)S(1)}, u32[]{:S(2)}, u32[]{:S(2)}) collective-permute-start(f32[12,16,128]{2,1,0:T(8,128)S(1)} %shard_map.110.own_ref.after_ref.rest_1_), channel_id=1, source_target_pairs={{0,2},{1,3},{2,0},{3,1},{4,6},{5,7},{6,4},{7,5},{8,10},{9,11},{10,... | collective-permute-start | bytes 294920 | tf_op jit(solution)/shard_map/ppermute | solution.py:319
  36.6 10.3 %copy-start = (f32[12,2,2,128,128]{4,3,2,1,0:T(8,128)S(1)}, f32[12,2,2,128,128]{4,3,2,1,0:T(8,128)}, u32[]{:S(2)}) copy-start(f32[12,2,2,128,128]{4,3,2,1,0:T(8,128)} %weight_ref.5) | copy-start | bytes 9437188
  36.6 10.3 %copy-start.3 = (s32[1,4,4]{2,1,0:T(4,128)S(1)}, s32[1,4,4]{2,1,0:T(4,128)}, u32[]{:S(2)}) copy-start(s32[1,4,4]{2,1,0:T(4,128)} %param.19) | copy-start | bytes 196
  36.6 10.3 %copy-start.4 = (s32[12,2]{0,1:T(2,128)S(1)}, s32[12,2]{0,1:T(2,128)}, u32[]{:S(2)}) copy-start(s32[12,2]{0,1:T(2,128)} %param.16) | copy-start | bytes 292
  36.6 10.3 %copy-start.5 = (s32[12,2]{0,1:T(2,128)S(1)}, s32[12,2]{0,1:T(2,128)}, u32[]{:S(2)}) copy-start(s32[12,2]{0,1:T(2,128)} %param.17) | copy-start | bytes 292
  36.6 10.3 %copy-start.6 = (s32[12,2]{0,1:T(2,128)S(1)}, s32[12,2]{0,1:T(2,128)}, u32[]{:S(2)}) copy-start(s32[12,2]{0,1:T(2,128)} %param.18) | copy-start | bytes 292
  37.5 9.3 %collective-permute-start.13 = (f32[2,16,1536]{2,1,0:T(8,128)S(1)}, f32[2,16,1536]{2,1,0:T(8,128)S(1)}, u32[]{:S(2)}, u32[]{:S(2)}) collective-permute-start(f32[2,16,1536]{2,1,0:T(8,128)S(1)} %copy-done.1), channel_id=1, source_target_pairs={{0,1},{1,0},{2,3},{3,2},{4,5},{5,4},{6,7},{7,6},{8,9},{9,8},{10,11... | collective-permute-start | bytes 589832 | tf_op jit(solution)/shard_map/ppermute | solution.py:319
  37.6 9.2 %collective-permute-start.15 = (f32[2,16,1536]{2,1,0:T(8,128)S(1)}, f32[2,16,1536]{2,1,0:T(8,128)S(1)}, u32[]{:S(2)}, u32[]{:S(2)}) collective-permute-start(f32[2,16,1536]{2,1,0:T(8,128)S(1)} %collective-permute-done.14.far_ref), channel_id=1, source_target_pairs={{0,1},{1,0},{2,3},{3,2},{4,5},{5,4},{6,7},{7,6},{8,9},{9,8},{10,11... | collective-permute-start | bytes 589832 | tf_op jit(solution)/shard_map/ppermute | solution.py:319
  38.1 4.8 %collective-permute-start.12 = (f32[12,16,128]{2,1,0:T(8,128)S(1)}, f32[12,16,128]{2,1,0:T(8,128)S(1)}, u32[]{:S(2)}, u32[]{:S(2)}) collective-permute-start(f32[12,16,128]{2,1,0:T(8,128)S(1)} %shard_map.115.own_ref.rest_0_.after_ref), channel_id=1, source_target_pairs={{0,64},{1,65},{2,66},{3,67},{4,68},{5,69},{6,70},{7,71},{8,72},{9,... | collective-permute-start | bytes 294920 | tf_op jit(solution)/shard_map/ppermute | solution.py:319
  38.8 7.7 %collective-permute-start.11 = (f32[12,16,128]{2,1,0:T(8,128)S(1)}, f32[12,16,128]{2,1,0:T(8,128)S(1)}, u32[]{:S(2)}, u32[]{:S(2)}) collective-permute-start(f32[12,16,128]{2,1,0:T(8,128)S(1)} %shard_map.115.own_ref.rest_0_.after_ref), channel_id=1, source_target_pairs={{0,192},{1,193},{2,194},{3,195},{4,196},{5,197},{6,198},{7,199},{8... | collective-permute-start | bytes 294920 | tf_op jit(solution)/shard_map/ppermute | solution.py:319
  42.9 6.4 %collective-permute-start.9 = (f32[12,16,128]{2,1,0:T(8,128)S(1)}, f32[12,16,128]{2,1,0:T(8,128)S(1)}, u32[]{:S(2)}, u32[]{:S(2)}) collective-permute-start(f32[12,16,128]{2,1,0:T(8,128)S(1)} %shard_map.116.ready_ref), channel_id=1, source_target_pairs={{0,128},{1,129},{2,130},{3,131},{4,132},{5,133},{6,134},{7,135},{8... | collective-permute-start | bytes 294920 | tf_op jit(solution)/shard_map/ppermute | solution.py:319

commit v10 on v9

--- a/solution.py
+++ b/solution.py
@@ -142,22 +142,14 @@
 
 
 def first_kernel(own_ref, weight_0, roster_ref, coupling_hbm, *refs):
-    ready_out, other_out, back_ref, own_4, other_4, packed_a, packed_b, weight_1, weight_2, weight_4, sems = refs
-    blocks = own_ref.shape[0]
-    half = packed_b.shape[0]
-    copies = started([(coupling_hbm.at[n], out) for n, out in ((4, weight_4), (1, weight_1), (2, weight_2))], sems)
+    ready_out, other_out, back_ref, weight_1, weight_2, sems = refs
+    copies = started([(coupling_hbm.at[n], out) for n, out in ((1, weight_1), (2, weight_2))], sems)
     start_level(0, own_ref, weight_0, roster_ref, ready_out, other_out, back_ref)
-    packed_a[half, 0:8, 0:blocks] = jnp.broadcast_to(roster_ref[4].astype(F32), (8, blocks))
-    copies[0].wait()
-    for k in range(blocks):
-        own_half, other_half = halves(weight_4[k].reshape(128, 128))
-        own_4[k] = filled(own_half)
-        other_4[k] = filled(other_half)
-        if k < half:
-            packed_a[k] = other_half
-        else:
-            packed_b[k - half] = other_half
-    finish(copies[1:])
+    finish(copies)
+
+
+def middle_kernel(level, own_ref, coupling_ref, roster_ref, *outs):
+    start_level(level, own_ref, coupling_ref.at[level], roster_ref, *outs)
 
 
 def ahead_kernel(level, own_ref, weight_ref, roster_ref, weight_2, coupling_hbm, *refs):
@@ -180,17 +172,16 @@
         prepare_block(k, k, weight_ref, own_out, other_out, packed_ref)
 
 
-def fetch_kernel(levels, coupling_ref, after_ref, *outs):
-    for n, level in enumerate(levels):
-        for k in range(coupling_ref.shape[1]):
-            prepare_block(k, k, coupling_ref.at[level], outs[2 * n], outs[2 * n + 1])
-
-
-def unpack_kernel(packed_ref, *rest):
-    out_ref = rest[-1]
+def fetch_kernel(coupling_ref, roster_ref, after_ref, own_5, other_5, back_5, own_7, other_7):
+    for k, place in enumerate(slots(roster_ref[5], coupling_ref.shape[1], back_5)):
+        prepare_block(k, place, coupling_ref.at[5], own_5, other_5)
+    for k in range(coupling_ref.shape[1]):
+        prepare_block(k, k, coupling_ref.at[7], own_7, other_7)
+
+
+def unpack_kernel(packed_ref, after_ref, out_ref):
     for k in range(out_ref.shape[0]):
-        half = packed_ref.shape[0] - 1
-        out_ref[k] = filled(packed_ref[k] if k < half else rest[0][k - half])
+        out_ref[k] = filled(packed_ref[k])
 
 
 def spread_kernel(weight_ref, after_ref, out_ref):
@@ -219,22 +210,6 @@
     out_ref = rest[-1]
     for k, place in enumerate(entries(roster_ref[level], out_ref.shape[0])):
         out_ref[k] = ready_ref[k] + times(other_ref[place], wide_ref[k])
-
-
-def side_kernel(level, roster_ref, packed_ref, corner_ref, away_ref, beside_ref, wide_ref, out_ref, there_ref):
-    blocks = out_ref.shape[0]
-    for k, place in enumerate(packed_row(packed_ref, out_ref.shape[0])):
-        there_ref[k] = beside_ref[k] + times(corner_ref[place], away_ref[k])
-    for k, place in enumerate(entries(roster_ref[level], blocks)):
-        out_ref[k] = times(there_ref[place], wide_ref[k])
-
-
-def double_kernel(level, roster_ref, other_ref, wide_ref, ready_ref, next_ref, side_ref, *rest):
-    out_ref, here_ref = rest[-2:]
-    for k, place in enumerate(entries(roster_ref[level], out_ref.shape[0])):
-        here_ref[k] = ready_ref[k] + times(other_ref[place], wide_ref[k])
-    for k in range(out_ref.shape[0]):
-        out_ref[k] = side_ref[k] + times(here_ref[k], next_ref[k])
 
 
 def corner_kernel(packed_ref, other_ref, wide_ref, out_ref):
@@ -371,25 +346,14 @@
     )
 
     other = flipped(coeffs, top, 0)
-    half = blocks // 2
-    ready, wide_0, back_0, own_4, wide_4, packed_4, packed_more, weight_1, weight_2 = run(
+    far = flipped(tied(field_in, coeffs), 0, 2)
+    ready, wide_0, back_0, weight_1, weight_2 = run(
         first_kernel,
-        [
-            state,
-            wide,
-            back,
-            wide,
-            wide,
-            VMEM((half + 1, 64, 128), F32),
-            VMEM((blocks - half, 64, 128), F32),
-            level_weights,
-            level_weights,
-        ],
+        [state, wide, back, level_weights, level_weights],
         [coeffs, weight_0, names, coupling_hbm],
-        scratch=[level_weights, DMA((3,))],
+        scratch=[DMA((2,))],
         hbm=(3,),
     )
-    away_4 = flipped(packed_4, top // 4, 0)
     coeffs = run(level_kernel, state, [back_0, other, wide_0, ready])
 
     other = flipped(coeffs, top // 2, 0)
@@ -400,31 +364,33 @@
         scratch=[DMA((2,))],
         hbm=(4,),
     )
-    own_3, wide_3, back_3 = run(part(sorted_kernel, 3), [wide, wide, back], [weight_3, names], [coeffs])
     own_6, wide_6, packed_6 = run(part(packed_kernel, 6), [wide, wide, packed], [weight_6, names], [coeffs])
-    coeffs = run(level_kernel, state, [back_1, other, wide_1, ready], [own_3, own_6])
+    coeffs = run(level_kernel, state, [back_1, other, wide_1, ready], [own_6])
 
     other = flipped(coeffs, top // 4, 0)
-    away_more = flipped(tied(packed_more, coeffs), top // 4, 0)
     away_6 = flipped(tied(packed_6, coeffs), top, 0)
     ready = run(part(own_sorted_kernel, 2), state, [coeffs, own_2, names])
-    coeffs = run(level_kernel, state, [back_2, other, wide_2, ready])
+    own_3, wide_3, back_3 = run(part(sorted_kernel, 3), [wide, wide, back], [weight_3, names], [coeffs])
+    coeffs = run(level_kernel, state, [back_2, other, wide_2, ready], [own_3])
 
     other = flipped(coeffs, 0, 1)
     ready = run(part(own_sorted_kernel, 3), state, [coeffs, own_3, names])
     coeffs = run(level_kernel, state, [back_3, other, wide_3, ready])
 
-    corner = flipped(coeffs, top // 4, 2)
-    ready = run(own_kernel, state, [coeffs, own_4])
-    beside = flipped(ready, top // 4, 0)
     other = flipped(coeffs, 0, 2)
-    own_5, wide_5, own_7, wide_7 = run(
-        part(fetch_kernel, (5, 7)), [wide] * 4, [pltpu.with_memory_space_constraint(coupling, VMEM)], [coeffs]
-    )
-    far = flipped(tied(field_in, coeffs), 0, 2)
-    away = run(unpack_kernel, wide, [away_4, away_more], [coeffs])
-    side = run(part(side_kernel, 5), state, [names, away_4, corner, away, beside, wide_5], scratch=[state])
-    coeffs = run(part(double_kernel, 4), state, [names, other, wide_4, ready, own_5, side], [own_7], scratch=[state])
+    core = flipped(tied(field_in, coeffs), 0, 1)
+    both = flipped(tied(far, coeffs), 0, 1)
+    everything = pltpu.with_memory_space_constraint(coupling, VMEM)
+    ready, wide_4, back_4 = run(part(middle_kernel, 4), [state, wide, back], [coeffs, everything, names])
+    own_5, wide_5, back_5, own_7, wide_7 = run(
+        fetch_kernel, [wide, wide, back, wide, wide], [everything, names], [coeffs]
+    )
+    coeffs = run(level_kernel, state, [back_4, other, wide_4, ready], [own_7])
+
+    other = flipped(coeffs, top // 4, 0)
+    ready = run(part(own_sorted_kernel, 5), state, [coeffs, own_5, names])
+    pieces = [near_piece(n, coeffs) for n in range(len(NEAR_PARTS))]
+    coeffs = run(level_kernel, state, [back_5, other, wide_5, ready], pieces)
 
     other = flipped(coeffs, top // 2, 0)
     ready = run(own_kernel, state, [coeffs, own_6])
@@ -432,11 +398,8 @@
     beside = flipped(ready, top, 0)
     last = run(spread_kernel, wide, [expanding], [coeffs])
     away = run(unpack_kernel, wide, [away_6], [coeffs])
-    core = flipped(tied(field_in, coeffs), 0, 1)
-    both = flipped(tied(far, coeffs), 0, 1)
     here = run(part(plain_kernel, 6), state, [names, other, wide_6, ready], [last])
     ready = run(own_kernel, state, [here, own_7], [away])
-    pieces = [near_piece(n, ready) for n in range(len(NEAR_PARTS))]
     corner = run(corner_kernel, state, [away_6, corner, away])
     return call(
         part(last_kernel, 7),

time: 50.9 us -> 46.6 us (0.916)
  starting transfers between devices: 25.3 us -> 19.2 us
  waiting for transfers between devices: 8.2 us -> 10.3 us
    ppermute x16 -> x13, starting transfers between devices: 25.3 us -> 19.2 us  [flipped(): return lax.ppermute(value, ('leaf', 'sub'), pairs)]
    ppermute x16 -> x13, waiting for transfers between devices: 8.2 us -> 10.3 us  [flipped(): return lax.ppermute(value, ('leaf', 'sub'), pairs)]
  transfers between devices with their start and end apart: 16 -> 13, of which waited for: 6 -> 7; matrix products, arithmetic and copies ran while one was open for 0% -> 0% of each run, Pallas kernels for 26% -> 28%
where the time goes in v10:
time: 46.6 us; the launch traced here: 46.5 us
  starting transfers between devices  19.2 us (41%)
  Pallas kernels  16.4 us (35%)
  waiting for transfers between devices  10.3 us (22%)
  between operations  0.52 us (1%)
    ppermute x13, starting transfers between devices, flipped(): return lax.ppermute(value, ('leaf', 'sub'), pairs)  19.2 us
    pallas_call x22, Pallas kernels, run(): call(kernel, outs, spaces, [VMEM] * len(outs) if several else VMEM, scratch)  12.8 us
    ppermute x13, waiting for transfers between devices, flipped(): return lax.ppermute(value, ('leaf', 'sub'), pairs)  10.3 us
    pallas_call x2, Pallas kernels, near_piece(): call(functools.partial(near_kernel, begin), VMEM((count, 2 * rhs, 128), F...  2.35 us
    pallas_call x1, Pallas kernels, on_device(): call(part(last_kernel, 7), jax.ShapeDtypeStruct(field_in.shape, F32), [VM...  1.27 us
  transfers between devices with their start and end apart: 13, of which 7 were waited for; matrix products, arithmetic and copies ran while one was open for 0% of the time, Pallas kernels for 28%

profile of v10, /device:TPU:64, one launch (start us, length us, event | category | flops | bytes accessed | tf_op | source)
XLA Modules:
  0.0 46.5 jit_solution(9872054747442026945)
XLA Ops:
  0.0 1.8 %shard_map.100 = (f32[12,16,128]{2,1,0:T(8,128)S(1)}, f32[12,2,64,128]{3,2,1,0:T(8,128)S(1)}, s32[8,1,12]{2,1,0:T(1,128)S(1)}) custom-call(f32[2,16,1536]{2,1,0:T(8,128)} %own_ref.3, f32[12,2,64,128]{3,2,1,0:T(8,128)} %weight_hbm.1, f32[8,12,2,64,128]{4,3,2,1,0:T(8,128)} %coupling_ref.3, s32[8,1,12]{2,1,0:T(1,128)} %roster_hbm.1), custom_call_target="tpu_custom_call" | custom-call | flops 2000000 | bytes 1048576 | tf_op jit(solution)/shard_map/pallas_call | solution.py:331
  1.8 3.1 %collective-permute-start = (f32[12,16,128]{2,1,0:T(8,128)S(1)}, f32[12,16,128]{2,1,0:T(8,128)S(1)}, u32[]{:S(2)}, u32[]{:S(2)}) collective-permute-start(f32[12,16,128]{2,1,0:T(8,128)S(1)} %get-tuple-element.40.own_ref), channel_id=1, source_target_pairs={{0,128},{1,129},{2,130},{3,131},{4,132},{5,133},{6,134},{7,135},{8... | collective-permute-start | bytes 294920 | tf_op jit(solution)/shard_map/ppermute | solution.py:294
  4.9 2.0 %shard_map.101 = (f32[12,16,128]{2,1,0:T(8,128)S(1)}, bf16[12,256,128]{2,1,0:T(8,128)(2,1)S(1)}, s32[8,128]{1,0:T(8,128)S(1)}, f32[12,2,64,128]{3,2,1,0:T(8,128)S(1)}, f32[12,2,64,128]{3,2,1,0:T(8,128)S(1)}) custom-call(f32[12,16,128]{2,1,0:T(8,128)S(1)} %get-tuple-element.40.own_ref, f32[12,2,64,128]{3,2,1,0:T(8,128)S(1)} %get-tuple-element.41.weight_0, ...), custom_call_target="tpu_custom_call" | custom-call | flops 2000000 | bytes 1048576 | tf_op jit(solution)/shard_map/pallas_call | solution.py:331
  7.0 0.0 copy-start.1
  7.0 1.1 %collective-permute-done.other_ref = f32[12,16,128]{2,1,0:T(8,128)S(1)} collective-permute-done((f32[12,16,128]{2,1,0:T(8,128)S(1)}, f32[12,16,128]{2,1,0:T(8,128)S(1)}, u32[]{:S(2)}, u32[]{:S(2)}) %collective-permute-start) | collective-permute-done | bytes 98336 | tf_op jit(solution)/shard_map/ppermute | solution.py:294
  8.0 0.2 shard_map.102.own_ref.after_ref
  8.3 1.6 %collective-permute-start.1 = (f32[12,16,128]{2,1,0:T(8,128)S(1)}, f32[12,16,128]{2,1,0:T(8,128)S(1)}, u32[]{:S(2)}, u32[]{:S(2)}) collective-permute-start(f32[12,16,128]{2,1,0:T(8,128)S(1)} %shard_map.102.own_ref.after_ref), channel_id=1, source_target_pairs={{0,64},{1,65},{2,66},{3,67},{4,68},{5,69},{6,70},{7,71},{8,72},{9,... | collective-permute-start | bytes 294920 | tf_op jit(solution)/shard_map/ppermute | solution.py:294
  9.9 2.6 %shard_map.103 = (f32[12,16,128]{2,1,0:T(8,128)S(1)}, bf16[12,256,128]{2,1,0:T(8,128)(2,1)S(1)}, s32[8,128]{1,0:T(8,128)S(1)}, bf16[12,256,128]{2,1,0:T(8,128)(2...) custom-call(f32[12,16,128]{2,1,0:T(8,128)S(1)} %shard_map.102.own_re, ...), custom_call_target="tpu_custom_call" | custom-call | flops 2000000 | bytes 1048576 | tf_op jit(solution)/shard_map/pallas_call | solution.py:331
  12.5 0.0 slice-start.1
  12.5 0.5 %shard_map.104 = (bf16[12,256,128]{2,1,0:T(8,128)(2,1)S(1)}, bf16[12,256,128]{2,1,0:T(8,128)(2,1)S(1)}, f32[13,64,128]{2,1,0:T(8,128)S(1)}) custom-call(f32[12,2,64,128]{3,2,1,0:T(8,128)S(1)} %get-tuple-element.51.weight_ref, s32[8,1,12]{2,1,0:T(1,128)S(1)} %get-tuple-element.39.roster_ref, f32[12,16,128]{2,1,0:T(8,128)S(1)} %shard_map.102.own_ref.after_ref), custom_call_target="tpu_custom_call" | custom-call | flops 2000000 | bytes 1048576 | tf_op jit(solution)/shard_map/pallas_call | solution.py:331
  13.1 0.0 collective-permute-done.1.other_ref
  13.1 0.2 shard_map.105.after_ref.own_ref
  13.3 1.7 %collective-permute-start.2 = (f32[12,16,128]{2,1,0:T(8,128)S(1)}, f32[12,16,128]{2,1,0:T(8,128)S(1)}, u32[]{:S(2)}, u32[]{:S(2)}) collective-permute-start(f32[12,16,128]{2,1,0:T(8,128)S(1)} %shard_map.105.after_ref.own_ref), channel_id=1, source_target_pairs={{0,32},{1,33},{2,34},{3,35},{4,36},{5,37},{6,38},{7,39},{8,40},{9,... | collective-permute-start | bytes 294920 | tf_op jit(solution)/shard_map/ppermute | solution.py:294
  15.0 0.0 copy-done.1
  15.0 2.9 %collective-permute-start.7 = (f32[2,16,1536]{2,1,0:T(8,128)S(1)}, f32[2,16,1536]{2,1,0:T(8,128)S(1)}, u32[]{:S(2)}, u32[]{:S(2)}) collective-permute-start(f32[2,16,1536]{2,1,0:T(8,128)S(1)} %copy-done.1), channel_id=1, source_target_pairs={{0,2},{1,3},{2,0},{3,1},{4,6},{5,7},{6,4},{7,5},{8,10},{9,11},{10,... | collective-permute-start | bytes 589832 | tf_op jit(solution)/shard_map/ppermute | solution.py:294
  17.9 2.9 %collective-permute-start.10 = (f32[13,64,128]{2,1,0:T(8,128)S(1)}, f32[13,64,128]{2,1,0:T(8,128)S(1)}, u32[]{:S(2)}, u32[]{:S(2)}) collective-permute-start(f32[13,64,128]{2,1,0:T(8,128)S(1)} %get-tuple-element.70), channel_id=1, source_target_pairs={{0,128},{1,129},{2,130},{3,131},{4,132},{5,133},{6,134},{7,135},{8... | collective-permute-start | bytes 1277960 | tf_op jit(solution)/shard_map/ppermute | solution.py:294
  20.8 0.2 shard_map.107.ready_ref
  21.1 0.5 %shard_map.106 = (bf16[12,256,128]{2,1,0:T(8,128)(2,1)S(1)}, bf16[12,256,128]{2,1,0:T(8,128)(2,1)S(1)}, s32[8,128]{1,0:T(8,128)S(1)}) custom-call(f32[12,2,64,128]{3,2,1,0:T(8,128)S(1)} %get-tuple-element.47.weight_ref, s32[8,1,12]{2,1,0:T(1,128)S(1)} %get-tuple-element.39.roster_ref, f32[12,16,128]{2,1,0:T(8,128)S(1)} %shard_map.105.after_ref.own_ref), custom_call_target="tpu_custom_call" | custom-call | flops 2000000 | bytes 1048576 | tf_op jit(solution)/shard_map/pallas_call | solution.py:331
  21.6 0.0 collective-permute-done.2.other_ref
  21.6 0.2 shard_map.108.own_ref
  21.9 0.1 collective-permute-start.3
  22.0 0.2 shard_map.109.ready_ref
  22.2 1.0 %collective-permute-done.3.other_ref = f32[12,16,128]{2,1,0:T(8,128)S(1)} collective-permute-done((f32[12,16,128]{2,1,0:T(8,128)S(1)}, f32[12,16,128]{2,1,0:T(8,128)S(1)}, u32[]{:S(2)}, u32[]{:S(2)}) %collective-permute-start.3) | collective-permute-done | bytes 98336 | tf_op jit(solution)/shard_map/ppermute | solution.py:294
  23.3 0.2 shard_map.110.after_ref.own_ref
  23.5 0.0 copy-start
  23.5 0.0 copy-start.3
  23.5 0.0 copy-start.4
  23.5 0.0 copy-start.5
  23.5 0.0 copy-start.6
  23.6 0.0 collective-permute-done.7.far_ref
  23.6 0.2 collective-permute-start.8
  23.8 0.4 collective-permute-start.6
  24.2 1.7 %collective-permute-start.4 = (f32[12,16,128]{2,1,0:T(8,128)S(1)}, f32[12,16,128]{2,1,0:T(8,128)S(1)}, u32[]{:S(2)}, u32[]{:S(2)}) collective-permute-start(f32[12,16,128]{2,1,0:T(8,128)S(1)} %shard_map.110.after_ref.own_ref), channel_id=1, source_target_pairs={{0,2},{1,3},{2,0},{3,1},{4,6},{5,7},{6,4},{7,5},{8,10},{9,11},{10,... | collective-permute-start | bytes 294920 | tf_op jit(solution)/shard_map/ppermute | solution.py:294
  25.8 0.0 slice-done
  25.8 0.0 slice-done.1
  25.8 1.0 %shard_map.111 = (bf16[12,256,128]{2,1,0:T(8,128)(2,1)S(1)}, bf16[12,256,128]{2,1,0:T(8,128)(2,1)S(1)}, s32[8,128]{1,0:T(8,128)S(1)}, bf16[12,256,128]{2,1,0:T(8,128)(2,1)S(1)}, bf16[12,256,128]{2,1,0:T(8,128)(2,1)S(1)}) custom-call(f32[8,12,2,64,128]{4,3,2,1,0:T(8,128)S(1)} %bitcast.5, s32[8,1,12]{2,1,0:T(1,128)S(1)} %get-tuple-element.39.roster_ref, ...), custom_call_target="tpu_custom_call" | custom-call | flops 2000000 | bytes 1048576 | tf_op jit(solution)/shard_map/pallas_call | solution.py:331
  26.8 0.8 %shard_map.112 = (f32[12,16,128]{2,1,0:T(8,128)S(1)}, bf16[12,256,128]{2,1,0:T(8,128)(2,1)S(1)}, s32[8,128]{1,0:T(8,128)S(1)}) custom-call(f32[12,16,128]{2,1,0:T(8,128)S(1)} %shard_map.110.after_ref.own_ref, f32[8,12,2,64,128]{4,3,2,1,0:T(8,128)S(1)} %bitcast.5, s32[8,1,12]{2,1,0:T(1,128)S(1)} %get-tuple-element.39.roster_ref), custom_call_target="tpu_custom_call" | custom-call | flops 2000000 | bytes 1048576 | tf_op jit(solution)/shard_map/pallas_call | solution.py:331
  27.6 3.0 %collective-permute-done.4.other_ref = f32[12,16,128]{2,1,0:T(8,128)S(1)} collective-permute-done((f32[12,16,128]{2,1,0:T(8,128)S(1)}, f32[12,16,128]{2,1,0:T(8,128)S(1)}, u32[]{:S(2)}, u32[]{:S(2)}) %collective-permute-start.4) | collective-permute-done | bytes 98336 | tf_op jit(solution)/shard_map/ppermute | solution.py:294
  30.5 0.2 shard_map.113.own_ref.rest_0_
  30.8 0.4 collective-permute-start.5
  31.2 0.2 shard_map.114.ready_ref
  31.4 0.0 collective-permute-done.8.both_ref
  31.4 0.0 collective-permute-done.6.core_ref
  31.4 0.0 copy-done
  31.4 0.0 copy-done.3
  31.5 0.0 copy-done.4
  31.5 1.3 %shard_map.116.rest_1_ = f32[8,32,128]{2,1,0:T(8,128)S(1)} custom-call(s32[2,12]{1,0:T(2,128)S(1)} %bitcast.8, s32[2,12]{1,0:T(2,128)S(1)} %bitcast.10, s32[2,12]{1,0:T(2,128)S(1)} %bitcast.12, s32[4,4]{1,0:T(4,128)S(1)} %bitcast.6, f32[2,16,1536]{2,1,0:T(8,128)S(1)} %copy-done.1, f32[2,16,1536]{2,1,0:T(8,128)S(1)} %collective-permute-done.6.core_ref, ...), custom_call_target="tpu_custom_call" | custom-call | flops 2000000 | bytes 1048576 | tf_op jit(solution)/shard_map/pallas_call | solution.py:335
  32.9 1.0 %shard_map.115.rest_0_ = f32[4,32,128]{2,1,0:T(8,128)S(1)} custom-call(s32[2,12]{1,0:T(2,128)S(1)} %bitcast.9, s32[2,12]{1,0:T(2,128)S(1)} %bitcast.11, s32[2,12]{1,0:T(2,128)S(1)} %bitcast.13, s32[4,4]{1,0:T(4,128)S(1)} %bitcast.7, f32[2,16,1536]{2,1,0:T(8,128)S(1)} %copy-done.1, f32[2,16,1536]{2,1,0:T(8,128)S(1)} %collective-permute-done.6.core_ref, ...), custom_call_target="tpu_custom_call" | custom-call | flops 2000000 | bytes 1048576 | tf_op jit(solution)/shard_map/pallas_call | solution.py:335
  33.9 1.7 %collective-permute-done.5.other_ref = f32[12,16,128]{2,1,0:T(8,128)S(1)} collective-permute-done((f32[12,16,128]{2,1,0:T(8,128)S(1)}, f32[12,16,128]{2,1,0:T(8,128)S(1)}, u32[]{:S(2)}, u32[]{:S(2)}) %collective-permute-start.5) | collective-permute-done | bytes 98336 | tf_op jit(solution)/shard_map/ppermute | solution.py:294
  35.6 0.2 shard_map.117.own_ref.after_ref
  35.9 0.7 %collective-permute-start.12 = (f32[12,16,128]{2,1,0:T(8,128)S(1)}, f32[12,16,128]{2,1,0:T(8,128)S(1)}, u32[]{:S(2)}, u32[]{:S(2)}) collective-permute-start(f32[12,16,128]{2,1,0:T(8,128)S(1)} %shard_map.117.own_ref.after_ref), channel_id=1, source_target_pairs={{0,64},{1,65},{2,66},{3,67},{4,68},{5,69},{6,70},{7,71},{8,72},{9,... | collective-permute-start | bytes 294920 | tf_op jit(solution)/shard_map/ppermute | solution.py:294
  36.6 2.1 %collective-permute-start.11 = (f32[12,16,128]{2,1,0:T(8,128)S(1)}, f32[12,16,128]{2,1,0:T(8,128)S(1)}, u32[]{:S(2)}, u32[]{:S(2)}) collective-permute-start(f32[12,16,128]{2,1,0:T(8,128)S(1)} %shard_map.117.own_ref.after_ref), channel_id=1, source_target_pairs={{0,192},{1,193},{2,194},{3,195},{4,196},{5,197},{6,198},{7,199},{8... | collective-permute-start | bytes 294920 | tf_op jit(solution)/shard_map/ppermute | solution.py:294
  38.6 0.2 shard_map.118.ready_ref
  38.9 1.5 %collective-permute-start.9 = (f32[12,16,128]{2,1,0:T(8,128)S(1)}, f32[12,16,128]{2,1,0:T(8,128)S(1)}, u32[]{:S(2)}, u32[]{:S(2)}) collective-permute-start(f32[12,16,128]{2,1,0:T(8,128)S(1)} %shard_map.118.ready_ref), channel_id=1, source_target_pairs={{0,128},{1,129},{2,130},{3,131},{4,132},{5,133},{6,134},{7,135},{8... | collective-permute-start | bytes 294920 | tf_op jit(solution)/shard_map/ppermute | solution.py:294
  40.4 0.1 shard_map.121.rest_0_.expand_ref
  40.5 0.0 collective-permute-done.10.packed_ref
  40.5 0.2 shard_map.119.wide_ref.rest_0_
  40.7 0.6 %collective-permute-done.12.other_ref = f32[12,16,128]{2,1,0:T(8,128)S(1)} collective-permute-done((f32[12,16,128]{2,1,0:T(8,128)S(1)}, f32[12,16,128]{2,1,0:T(8,128)S(1)}, u32[]{:S(2)}, u32[]{:S(2)}) %collective-permute-start.12) | collective-permute-done | bytes 98336 | tf_op jit(solution)/shard_map/ppermute | solution.py:294
  41.3 0.3 shard_map.122.own_ref
  41.6 0.2 shard_map.123.ready_ref
  41.8 1.2 %collective-permute-done.11.other_ref = f32[12,16,128]{2,1,0:T(8,128)S(1)} collective-permute-done((f32[12,16,128]{2,1,0:T(8,128)S(1)}, f32[12,16,128]{2,1,0:T(8,128)S(1)}, u32[]{:S(2)}, u32[]{:S(2)}) %collective-permute-start.11) | collective-permute-done | bytes 98336 | tf_op jit(solution)/shard_map/ppermute | solution.py:294
  43.0 0.3 shard_map.120.corner_ref
  43.3 1.7 %collective-permute-done.9.beside_ref = f32[12,16,128]{2,1,0:T(8,128)S(1)} collective-permute-done((f32[12,16,128]{2,1,0:T(8,128)S(1)}, f32[12,16,128]{2,1,0:T(8,128)S(1)}, u32[]{:S(2)}, u32[]{:S(2)}) %collective-permute-start.9) | collective-permute-done | bytes 98336 | tf_op jit(solution)/shard_map/ppermute | solution.py:294
  45.1 1.3 %shard_map.124 = f32[2,16,1536]{2,1,0:T(8,128)} custom-call(s32[8,1,12]{2,1,0:T(1,128)S(1)} %get-tuple-element.39.roster_ref, f32[12,16,128]{2,1,0:T(8,128)S(1)} %collective-permute-done.9.beside_ref, f32[12,16,128]{2,1,0:T(8,128)S(1)} %shard_map.120.corner_ref, bf16[12,256,128]{2,1,0:T(8,128)(2,1)S(1)} %get-tuple-element.71.wide_ref, ...), custom_call_target="tpu_custom_call" | custom-call | flops 2000000 | bytes 1048576 | tf_op jit(solution)/shard_map/pallas_call | solution.py:404
  (6 shorter events, 0.0 us)
Async XLA Ops:
  1.8 6.2 %collective-permute-start = (f32[12,16,128]{2,1,0:T(8,128)S(1)}, f32[12,16,128]{2,1,0:T(8,128)S(1)}, u32[]{:S(2)}, u32[]{:S(2)}) collective-permute-start(f32[12,16,128]{2,1,0:T(8,128)S(1)} %get-tuple-element.40.own_ref), channel_id=1, source_target_pairs={{0,128},{1,129},{2,130},{3,131},{4,132},{5,133},{6,134},{7,135},{8... | collective-permute-start | bytes 294920 | tf_op jit(solution)/shard_map/ppermute | solution.py:294
  7.0 8.0 %copy-start.1 = (f32[2,16,1536]{2,1,0:T(8,128)S(1)}, f32[2,16,1536]{2,1,0:T(8,128)}, u32[]{:S(2)}) copy-start(f32[2,16,1536]{2,1,0:T(8,128)} %own_ref.3) | copy-start | bytes 589828
  8.3 4.8 %collective-permute-start.1 = (f32[12,16,128]{2,1,0:T(8,128)S(1)}, f32[12,16,128]{2,1,0:T(8,128)S(1)}, u32[]{:S(2)}, u32[]{:S(2)}) collective-permute-start(f32[12,16,128]{2,1,0:T(8,128)S(1)} %shard_map.102.own_ref.after_ref), channel_id=1, source_target_pairs={{0,64},{1,65},{2,66},{3,67},{4,68},{5,69},{6,70},{7,71},{8,72},{9,... | collective-permute-start | bytes 294920 | tf_op jit(solution)/shard_map/ppermute | solution.py:294
  9.9 16.0 %slice-start = ((s8[6291456]{0:T(1024)(128)(4,1)}), s8[4194304]{0:T(1024)(128)(4,1)S(1)}, s32[]{:S(2)}) async-start(s8[6291456]{0:T(1024)(128)(4,1)} %bitcast.4), calls=%async_computation | async-start | bytes 8388608
  12.5 13.3 %slice-start.1 = ((s8[6291456]{0:T(1024)(128)(4,1)}), s8[2097152]{0:T(1024)(128)(4,1)S(1)}, s32[]{:S(2)}) async-start(s8[6291456]{0:T(1024)(128)(4,1)} %bitcast.4), calls=%async_computation.1 | async-start | bytes 4194304
  13.3 8.3 %collective-permute-start.2 = (f32[12,16,128]{2,1,0:T(8,128)S(1)}, f32[12,16,128]{2,1,0:T(8,128)S(1)}, u32[]{:S(2)}, u32[]{:S(2)}) collective-permute-start(f32[12,16,128]{2,1,0:T(8,128)S(1)} %shard_map.105.after_ref.own_ref), channel_id=1, source_target_pairs={{0,32},{1,33},{2,34},{3,35},{4,36},{5,37},{6,38},{7,39},{8,40},{9,... | collective-permute-start | bytes 294920 | tf_op jit(solution)/shard_map/ppermute | solution.py:294
  15.0 8.6 %collective-permute-start.7 = (f32[2,16,1536]{2,1,0:T(8,128)S(1)}, f32[2,16,1536]{2,1,0:T(8,128)S(1)}, u32[]{:S(2)}, u32[]{:S(2)}) collective-permute-start(f32[2,16,1536]{2,1,0:T(8,128)S(1)} %copy-done.1), channel_id=1, source_target_pairs={{0,2},{1,3},{2,0},{3,1},{4,6},{5,7},{6,4},{7,5},{8,10},{9,11},{10,... | collective-permute-start | bytes 589832 | tf_op jit(solution)/shard_map/ppermute | solution.py:294
  17.9 22.6 %collective-permute-start.10 = (f32[13,64,128]{2,1,0:T(8,128)S(1)}, f32[13,64,128]{2,1,0:T(8,128)S(1)}, u32[]{:S(2)}, u32[]{:S(2)}) collective-permute-start(f32[13,64,128]{2,1,0:T(8,128)S(1)} %get-tuple-element.70), channel_id=1, source_target_pairs={{0,128},{1,129},{2,130},{3,131},{4,132},{5,133},{6,134},{7,135},{8... | collective-permute-start | bytes 1277960 | tf_op jit(solution)/shard_map/ppermute | solution.py:294
  21.9 1.4 %collective-permute-start.3 = (f32[12,16,128]{2,1,0:T(8,128)S(1)}, f32[12,16,128]{2,1,0:T(8,128)S(1)}, u32[]{:S(2)}, u32[]{:S(2)}) collective-permute-start(f32[12,16,128]{2,1,0:T(8,128)S(1)} %shard_map.108.own_ref), channel_id=1, source_target_pairs={{0,1},{1,0},{2,3},{3,2},{4,5},{5,4},{6,7},{7,6},{8,9},{9,8},{10,11... | collective-permute-start | bytes 294920 | tf_op jit(solution)/shard_map/ppermute | solution.py:294
  23.5 7.9 %copy-start = (f32[12,2,2,128,128]{4,3,2,1,0:T(8,128)S(1)}, f32[12,2,2,128,128]{4,3,2,1,0:T(8,128)}, u32[]{:S(2)}) copy-start(f32[12,2,2,128,128]{4,3,2,1,0:T(8,128)} %weight_ref.4) | copy-start | bytes 9437188
  23.5 7.9 %copy-start.3 = (s32[1,4,4]{2,1,0:T(4,128)S(1)}, s32[1,4,4]{2,1,0:T(4,128)}, u32[]{:S(2)}) copy-start(s32[1,4,4]{2,1,0:T(4,128)} %param.19) | copy-start | bytes 196
  23.5 7.9 %copy-start.4 = (s32[12,2]{0,1:T(2,128)S(1)}, s32[12,2]{0,1:T(2,128)}, u32[]{:S(2)}) copy-start(s32[12,2]{0,1:T(2,128)} %param.16) | copy-start | bytes 292
  23.5 7.9 %copy-start.5 = (s32[12,2]{0,1:T(2,128)S(1)}, s32[12,2]{0,1:T(2,128)}, u32[]{:S(2)}) copy-start(s32[12,2]{0,1:T(2,128)} %param.17) | copy-start | bytes 292
  23.5 7.9 %copy-start.6 = (s32[12,2]{0,1:T(2,128)S(1)}, s32[12,2]{0,1:T(2,128)}, u32[]{:S(2)}) copy-start(s32[12,2]{0,1:T(2,128)} %param.18) | copy-start | bytes 292
  23.6 7.8 %collective-permute-start.8 = (f32[2,16,1536]{2,1,0:T(8,128)S(1)}, f32[2,16,1536]{2,1,0:T(8,128)S(1)}, u32[]{:S(2)}, u32[]{:S(2)}) collective-permute-start(f32[2,16,1536]{2,1,0:T(8,128)S(1)} %collective-permute-done.7.far_ref), channel_id=1, source_target_pairs={{0,1},{1,0},{2,3},{3,2},{4,5},{5,4},{6,7},{7,6},{8,9},{9,8},{10,11... | collective-permute-start | bytes 589832 | tf_op jit(solution)/shard_map/ppermute | solution.py:294
  23.8 7.6 %collective-permute-start.6 = (f32[2,16,1536]{2,1,0:T(8,128)S(1)}, f32[2,16,1536]{2,1,0:T(8,128)S(1)}, u32[]{:S(2)}, u32[]{:S(2)}) collective-permute-start(f32[2,16,1536]{2,1,0:T(8,128)S(1)} %copy-done.1), channel_id=1, source_target_pairs={{0,1},{1,0},{2,3},{3,2},{4,5},{5,4},{6,7},{7,6},{8,9},{9,8},{10,11... | collective-permute-start | bytes 589832 | tf_op jit(solution)/shard_map/ppermute | solution.py:294
  24.2 6.4 %collective-permute-start.4 = (f32[12,16,128]{2,1,0:T(8,128)S(1)}, f32[12,16,128]{2,1,0:T(8,128)S(1)}, u32[]{:S(2)}, u32[]{:S(2)}) collective-permute-start(f32[12,16,128]{2,1,0:T(8,128)S(1)} %shard_map.110.after_ref.own_ref), channel_id=1, source_target_pairs={{0,2},{1,3},{2,0},{3,1},{4,6},{5,7},{6,4},{7,5},{8,10},{9,11},{10,... | collective-permute-start | bytes 294920 | tf_op jit(solution)/shard_map/ppermute | solution.py:294
  30.5 9.9 %copy-start.2 = (f32[12,2,64,128]{3,2,1,0:T(8,128)S(1)}, f32[12,2,64,128]{3,2,1,0:T(8,128)}, u32[]{:S(2)}) copy-start(f32[12,2,64,128]{3,2,1,0:T(8,128)} %weight_ref.5) | copy-start | bytes 2359300
  30.8 4.9 %collective-permute-start.5 = (f32[12,16,128]{2,1,0:T(8,128)S(1)}, f32[12,16,128]{2,1,0:T(8,128)S(1)}, u32[]{:S(2)}, u32[]{:S(2)}) collective-permute-start(f32[12,16,128]{2,1,0:T(8,128)S(1)} %shard_map.113.own_ref.rest_0_), channel_id=1, source_target_pairs={{0,32},{1,33},{2,34},{3,35},{4,36},{5,37},{6,38},{7,39},{8,40},{9,... | collective-permute-start | bytes 294920 | tf_op jit(solution)/shard_map/ppermute | solution.py:294
  35.9 5.4 %collective-permute-start.12 = (f32[12,16,128]{2,1,0:T(8,128)S(1)}, f32[12,16,128]{2,1,0:T(8,128)S(1)}, u32[]{:S(2)}, u32[]{:S(2)}) collective-permute-start(f32[12,16,128]{2,1,0:T(8,128)S(1)} %shard_map.117.own_ref.after_ref), channel_id=1, source_target_pairs={{0,64},{1,65},{2,66},{3,67},{4,68},{5,69},{6,70},{7,71},{8,72},{9,... | collective-permute-start | bytes 294920 | tf_op jit(solution)/shard_map/ppermute | solution.py:294
  36.6 6.5 %collective-permute-start.11 = (f32[12,16,128]{2,1,0:T(8,128)S(1)}, f32[12,16,128]{2,1,0:T(8,128)S(1)}, u32[]{:S(2)}, u32[]{:S(2)}) collective-permute-start(f32[12,16,128]{2,1,0:T(8,128)S(1)} %shard_map.117.own_ref.after_ref), channel_id=1, source_target_pairs={{0,192},{1,193},{2,194},{3,195},{4,196},{5,197},{6,198},{7,199},{8... | collective-permute-start | bytes 294920 | tf_op jit(solution)/shard_map/ppermute | solution.py:294
  38.9 6.2 %collective-permute-start.9 = (f32[12,16,128]{2,1,0:T(8,128)S(1)}, f32[12,16,128]{2,1,0:T(8,128)S(1)}, u32[]{:S(2)}, u32[]{:S(2)}) collective-permute-start(f32[12,16,128]{2,1,0:T(8,128)S(1)} %shard_map.118.ready_ref), channel_id=1, source_target_pairs={{0,128},{1,129},{2,130},{3,131},{4,132},{5,133},{6,134},{7,135},{8... | collective-permute-start | bytes 294920 | tf_op jit(solution)/shard_map/ppermute | solution.py:294

commit v11 on v9

--- a/solution.py
+++ b/solution.py
@@ -90,7 +90,7 @@
     copies = started(
         [(field_hbm, field_ref)]
         + [(weight_hbm.at[part], weight_ref.at[part]) for part in parts]
-        + [(roster_hbm, roster_ref), (coupling_hbm.at[0], next_ref)],
+        + [(roster_hbm, roster_ref), (coupling_hbm.at[4], next_ref)],
         sems,
     )
     copies[0].wait()
@@ -141,22 +141,19 @@
         ready_out[place] = times(own_ref[k], filled(own_half))
 
 
-def first_kernel(own_ref, weight_0, roster_ref, coupling_hbm, *refs):
-    ready_out, other_out, back_ref, own_4, other_4, packed_a, packed_b, weight_1, weight_2, weight_4, sems = refs
-    blocks = own_ref.shape[0]
-    half = packed_b.shape[0]
-    copies = started([(coupling_hbm.at[n], out) for n, out in ((4, weight_4), (1, weight_1), (2, weight_2))], sems)
+def pack_kernel(level, weight_ref, roster_ref, out_ref):
+    put_row(out_ref, roster_ref[level])
+    for k in range(weight_ref.shape[0]):
+        out_ref[k] = halves(weight_ref[k].reshape(128, 128))[1]
+
+
+def first_kernel(own_ref, weight_4, roster_ref, coupling_hbm, *refs):
+    ready_out, other_out, back_ref, own_4, other_4, weight_1, weight_2, weight_0, sems = refs
+    copies = started([(coupling_hbm.at[n], out) for n, out in enumerate((weight_0, weight_1, weight_2))], sems)
+    for k in range(own_ref.shape[0]):
+        prepare_block(k, k, weight_4, own_4, other_4)
+    copies[0].wait()
     start_level(0, own_ref, weight_0, roster_ref, ready_out, other_out, back_ref)
-    packed_a[half, 0:8, 0:blocks] = jnp.broadcast_to(roster_ref[4].astype(F32), (8, blocks))
-    copies[0].wait()
-    for k in range(blocks):
-        own_half, other_half = halves(weight_4[k].reshape(128, 128))
-        own_4[k] = filled(own_half)
-        other_4[k] = filled(other_half)
-        if k < half:
-            packed_a[k] = other_half
-        else:
-            packed_b[k - half] = other_half
     finish(copies[1:])
 
 
@@ -186,11 +183,9 @@
             prepare_block(k, k, coupling_ref.at[level], outs[2 * n], outs[2 * n + 1])
 
 
-def unpack_kernel(packed_ref, *rest):
-    out_ref = rest[-1]
+def unpack_kernel(packed_ref, after_ref, out_ref):
     for k in range(out_ref.shape[0]):
-        half = packed_ref.shape[0] - 1
-        out_ref[k] = filled(packed_ref[k] if k < half else rest[0][k - half])
+        out_ref[k] = filled(packed_ref[k])
 
 
 def spread_kernel(weight_ref, after_ref, out_ref):
@@ -362,7 +357,7 @@
         )(*indices, field, core, far, both, dense, after)
 
     part = functools.partial
-    coeffs, weight_0, names = run(
+    coeffs, weight_4, names = run(
         compress_kernel,
         [state, level_weights, VMEM(roster.shape, jnp.int32)],
         [*in_hbm(field_in, compress), coupling_hbm, roster_hbm],
@@ -371,25 +366,15 @@
     )
 
     other = flipped(coeffs, top, 0)
-    half = blocks // 2
-    ready, wide_0, back_0, own_4, wide_4, packed_4, packed_more, weight_1, weight_2 = run(
+    packed_4 = run(part(pack_kernel, 4), packed, [weight_4, names])
+    away_4 = flipped(packed_4, top // 4, 0)
+    ready, wide_0, back_0, own_4, wide_4, weight_1, weight_2 = run(
         first_kernel,
-        [
-            state,
-            wide,
-            back,
-            wide,
-            wide,
-            VMEM((half + 1, 64, 128), F32),
-            VMEM((blocks - half, 64, 128), F32),
-            level_weights,
-            level_weights,
-        ],
-        [coeffs, weight_0, names, coupling_hbm],
+        [state, wide, back, wide, wide, level_weights, level_weights],
+        [coeffs, weight_4, names, coupling_hbm],
         scratch=[level_weights, DMA((3,))],
         hbm=(3,),
     )
-    away_4 = flipped(packed_4, top // 4, 0)
     coeffs = run(level_kernel, state, [back_0, other, wide_0, ready])
 
     other = flipped(coeffs, top // 2, 0)
@@ -405,7 +390,7 @@
     coeffs = run(level_kernel, state, [back_1, other, wide_1, ready], [own_3, own_6])
 
     other = flipped(coeffs, top // 4, 0)
-    away_more = flipped(tied(packed_more, coeffs), top // 4, 0)
+    far = flipped(tied(field_in, coeffs), 0, 2)
     away_6 = flipped(tied(packed_6, coeffs), top, 0)
     ready = run(part(own_sorted_kernel, 2), state, [coeffs, own_2, names])
     coeffs = run(level_kernel, state, [back_2, other, wide_2, ready])
@@ -421,8 +406,9 @@
     own_5, wide_5, own_7, wide_7 = run(
         part(fetch_kernel, (5, 7)), [wide] * 4, [pltpu.with_memory_space_constraint(coupling, VMEM)], [coeffs]
     )
-    far = flipped(tied(field_in, coeffs), 0, 2)
-    away = run(unpack_kernel, wide, [away_4, away_more], [coeffs])
+    core = flipped(tied(field_in, coeffs), 0, 1)
+    both = flipped(tied(far, coeffs), 0, 1)
+    away = run(unpack_kernel, wide, [away_4], [coeffs])
     side = run(part(side_kernel, 5), state, [names, away_4, corner, away, beside, wide_5], scratch=[state])
     coeffs = run(part(double_kernel, 4), state, [names, other, wide_4, ready, own_5, side], [own_7], scratch=[state])
 
@@ -432,11 +418,10 @@
     beside = flipped(ready, top, 0)
     last = run(spread_kernel, wide, [expanding], [coeffs])
     away = run(unpack_kernel, wide, [away_6], [coeffs])
-    core = flipped(tied(field_in, coeffs), 0, 1)
-    both = flipped(tied(far, coeffs), 0, 1)
-    here = run(part(plain_kernel, 6), state, [names, other, wide_6, ready], [last])
+    pieces = [near_piece(0, coeffs)]
+    here = run(part(plain_kernel, 6), state, [names, other, wide_6, ready], [last, pieces[0]])
     ready = run(own_kernel, state, [here, own_7], [away])
-    pieces = [near_piece(n, ready) for n in range(len(NEAR_PARTS))]
+    pieces.append(near_piece(1, ready))
     corner = run(corner_kernel, state, [away_6, corner, away])
     return call(
         part(last_kernel, 7),

time: 50.9 us -> 49.7 us (0.976)
  starting transfers between devices: 25.3 us -> 20.7 us
  waiting for transfers between devices: 8.2 us -> 11.3 us
    ppermute x16 -> x15, starting transfers between devices: 25.3 us -> 20.7 us  [flipped(): return lax.ppermute(value, ('leaf', 'sub'), pairs)]
    ppermute x16 -> x15, waiting for transfers between devices: 8.2 us -> 11.3 us  [flipped(): return lax.ppermute(value, ('leaf', 'sub'), pairs)]
    pallas_call x22 -> x23, Pallas kernels: 13 us -> 13.3 us  [run(): call(kernel, outs, spaces, [VMEM] * len(outs) if several else VMEM, scratch)]
  transfers between devices with their start and end apart: 16 -> 15, of which waited for: 6 -> 7; matrix products, arithmetic and copies ran while one was open for 0% -> 0% of each run, Pallas kernels for 26% -> 28%
where the time goes in v11:
time: 49.7 us; the launch traced here: 49.5 us
  starting transfers between devices  20.7 us (42%)
  Pallas kernels  16.9 us (34%)
  waiting for transfers between devices  11.3 us (23%)
  between operations  0.54 us (1%)
    ppermute x15, starting transfers between devices, flipped(): return lax.ppermute(value, ('leaf', 'sub'), pairs)  20.7 us
    pallas_call x23, Pallas kernels, run(): call(kernel, outs, spaces, [VMEM] * len(outs) if several else VMEM, scratch)  13.3 us
    ppermute x15, waiting for transfers between devices, flipped(): return lax.ppermute(value, ('leaf', 'sub'), pairs)  11.3 us
    pallas_call x2, Pallas kernels, near_piece(): call(functools.partial(near_kernel, begin), VMEM((count, 2 * rhs, 128), F...  2.33 us
    pallas_call x1, Pallas kernels, on_device(): call(part(last_kernel, 7), jax.ShapeDtypeStruct(field_in.shape, F32), [VM...  1.26 us
  transfers between devices with their start and end apart: 15, of which 7 were waited for; matrix products, arithmetic and copies ran while one was open for 0% of the time, Pallas kernels for 28%

profile of v11, /device:TPU:64, one launch (start us, length us, event | category | flops | bytes accessed | tf_op | source)
XLA Modules:
  0.0 49.5 jit_solution(2812029862826563939)
XLA Ops:
  0.0 1.8 %shard_map.100 = (f32[12,16,128]{2,1,0:T(8,128)S(1)}, f32[12,2,64,128]{3,2,1,0:T(8,128)S(1)}, s32[8,1,12]{2,1,0:T(1,128)S(1)}) custom-call(f32[2,16,1536]{2,1,0:T(8,128)} %own_ref.3, f32[12,2,64,128]{3,2,1,0:T(8,128)} %weight_hbm.1, f32[8,12,2,64,128]{4,3,2,1,0:T(8,128)} %coupling_ref.1, s32[8,1,12]{2,1,0:T(1,128)} %roster_hbm.1), custom_call_target="tpu_custom_call" | custom-call | flops 2000000 | bytes 1048576 | tf_op jit(solution)/shard_map/pallas_call | solution.py:351
  1.8 3.1 %collective-permute-start = (f32[12,16,128]{2,1,0:T(8,128)S(1)}, f32[12,16,128]{2,1,0:T(8,128)S(1)}, u32[]{:S(2)}, u32[]{:S(2)}) collective-permute-start(f32[12,16,128]{2,1,0:T(8,128)S(1)} %get-tuple-element.38.own_ref), channel_id=1, source_target_pairs={{0,128},{1,129},{2,130},{3,131},{4,132},{5,133},{6,134},{7,135},{8... | collective-permute-start | bytes 294920 | tf_op jit(solution)/shard_map/ppermute | solution.py:314
  4.9 0.3 shard_map.113
  5.2 1.7 %collective-permute-start.5 = (f32[13,64,128]{2,1,0:T(8,128)S(1)}, f32[13,64,128]{2,1,0:T(8,128)S(1)}, u32[]{:S(2)}, u32[]{:S(2)}) collective-permute-start(f32[13,64,128]{2,1,0:T(8,128)S(1)} %shard_map.113), channel_id=1, source_target_pairs={{0,32},{1,33},{2,34},{3,35},{4,36},{5,37},{6,38},{7,39},{8,40},{9,... | collective-permute-start | bytes 1277960 | tf_op jit(solution)/shard_map/ppermute | solution.py:314
  6.9 2.3 %shard_map.101 = (f32[12,16,128]{2,1,0:T(8,128)S(1)}, bf16[12,256,128]{2,1,0:T(8,128)(2,1)S(1)}, s32[8,128]{1,0:T(8,128)S(1)}, bf16[12,256,128]{2,1,0:T(8,128)(2...) custom-call(f32[12,16,128]{2,1,0:T(8,128)S(1)} %get-tuple-element.38.own_, ...), custom_call_target="tpu_custom_call" | custom-call | flops 2000000 | bytes 1048576 | tf_op jit(solution)/shard_map/pallas_call | solution.py:351
  9.2 0.0 collective-permute-done.other_ref
  9.2 0.2 shard_map.102.own_ref.after_ref
  9.4 0.7 %collective-permute-start.1 = (f32[12,16,128]{2,1,0:T(8,128)S(1)}, f32[12,16,128]{2,1,0:T(8,128)S(1)}, u32[]{:S(2)}, u32[]{:S(2)}) collective-permute-start(f32[12,16,128]{2,1,0:T(8,128)S(1)} %shard_map.102.own_ref.after_ref), channel_id=1, source_target_pairs={{0,64},{1,65},{2,66},{3,67},{4,68},{5,69},{6,70},{7,71},{8,72},{9,... | collective-permute-start | bytes 294920 | tf_op jit(solution)/shard_map/ppermute | solution.py:314
  10.1 2.7 %shard_map.103 = (f32[12,16,128]{2,1,0:T(8,128)S(1)}, bf16[12,256,128]{2,1,0:T(8,128)(2,1)S(1)}, s32[8,128]{1,0:T(8,128)S(1)}, bf16[12,256,128]{2,1,0:T(8,128)(2...) custom-call(f32[12,16,128]{2,1,0:T(8,128)S(1)} %shard_map.102.own_re, ...), custom_call_target="tpu_custom_call" | custom-call | flops 2000000 | bytes 1048576 | tf_op jit(solution)/shard_map/pallas_call | solution.py:351
  12.9 0.0 slice-start.1
  12.9 0.5 %shard_map.104 = (bf16[12,256,128]{2,1,0:T(8,128)(2,1)S(1)}, bf16[12,256,128]{2,1,0:T(8,128)(2,1)S(1)}, s32[8,128]{1,0:T(8,128)S(1)}) custom-call(f32[12,2,64,128]{3,2,1,0:T(8,128)S(1)} %get-tuple-element.45.weight_ref, s32[8,1,12]{2,1,0:T(1,128)S(1)} %get-tuple-element.37.roster_ref, f32[12,16,128]{2,1,0:T(8,128)S(1)} %shard_map.102.own_ref.after_ref), custom_call_target="tpu_custom_call" | custom-call | flops 2000000 | bytes 1048576 | tf_op jit(solution)/shard_map/pallas_call | solution.py:351
  13.4 0.5 %shard_map.105 = (bf16[12,256,128]{2,1,0:T(8,128)(2,1)S(1)}, bf16[12,256,128]{2,1,0:T(8,128)(2,1)S(1)}, f32[13,64,128]{2,1,0:T(8,128)S(1)}) custom-call(f32[12,2,64,128]{3,2,1,0:T(8,128)S(1)} %get-tuple-element.52.weight_ref, s32[8,1,12]{2,1,0:T(1,128)S(1)} %get-tuple-element.37.roster_ref, f32[12,16,128]{2,1,0:T(8,128)S(1)} %shard_map.102.own_ref.after_ref), custom_call_target="tpu_custom_call" | custom-call | flops 2000000 | bytes 1048576 | tf_op jit(solution)/shard_map/pallas_call | solution.py:351
  14.0 0.2 collective-permute-done.1.other_ref
  14.1 0.2 shard_map.106.own_ref
  14.4 1.2 %collective-permute-start.2 = (f32[12,16,128]{2,1,0:T(8,128)S(1)}, f32[12,16,128]{2,1,0:T(8,128)S(1)}, u32[]{:S(2)}, u32[]{:S(2)}) collective-permute-start(f32[12,16,128]{2,1,0:T(8,128)S(1)} %shard_map.106.own_ref), channel_id=1, source_target_pairs={{0,32},{1,33},{2,34},{3,35},{4,36},{5,37},{6,38},{7,39},{8,40},{9,... | collective-permute-start | bytes 294920 | tf_op jit(solution)/shard_map/ppermute | solution.py:314
  15.6 2.7 %collective-permute-start.9 = (f32[13,64,128]{2,1,0:T(8,128)S(1)}, f32[13,64,128]{2,1,0:T(8,128)S(1)}, u32[]{:S(2)}, u32[]{:S(2)}) collective-permute-start(f32[13,64,128]{2,1,0:T(8,128)S(1)} %get-tuple-element.63), channel_id=1, source_target_pairs={{0,128},{1,129},{2,130},{3,131},{4,132},{5,133},{6,134},{7,135},{8... | collective-permute-start | bytes 1277960 | tf_op jit(solution)/shard_map/ppermute | solution.py:314
  18.4 0.2 shard_map.107.ready_ref
  18.6 0.5 collective-permute-done.2.other_ref
  19.1 0.2 shard_map.108.own_ref
  19.3 0.1 collective-permute-start.3
  19.4 3.0 %collective-permute-start.13 = (f32[2,16,1536]{2,1,0:T(8,128)S(1)}, f32[2,16,1536]{2,1,0:T(8,128)S(1)}, u32[]{:S(2)}, u32[]{:S(2)}) collective-permute-start(f32[2,16,1536]{2,1,0:T(8,128)S(1)} %copy-done.1), channel_id=1, source_target_pairs={{0,2},{1,3},{2,0},{3,1},{4,6},{5,7},{6,4},{7,5},{8,10},{9,11},{10,... | collective-permute-start | bytes 589832 | tf_op jit(solution)/shard_map/ppermute | solution.py:314
  22.4 0.2 shard_map.109.ready_ref
  22.7 0.0 collective-permute-done.3.other_ref
  22.7 0.2 shard_map.110.own_ref.after_ref
  22.9 0.2 shard_map.111.ready_ref
  23.2 0.0 copy-start.2
  23.2 0.0 copy-start
  23.2 0.0 copy-start.3
  23.2 0.0 copy-start.4
  23.2 0.0 copy-start.5
  23.2 0.0 copy-start.6
  23.2 0.7 %collective-permute-start.7 = (f32[12,16,128]{2,1,0:T(8,128)S(1)}, f32[12,16,128]{2,1,0:T(8,128)S(1)}, u32[]{:S(2)}, u32[]{:S(2)}) collective-permute-start(f32[12,16,128]{2,1,0:T(8,128)S(1)} %shard_map.111.ready_ref), channel_id=1, source_target_pairs={{0,32},{1,33},{2,34},{3,35},{4,36},{5,37},{6,38},{7,39},{8,40},{9,... | collective-permute-start | bytes 294920 | tf_op jit(solution)/shard_map/ppermute | solution.py:314
  23.9 0.0 collective-permute-start.12
  23.9 4.9 %collective-permute-done.13.far_ref = f32[2,16,1536]{2,1,0:T(8,128)S(1)} collective-permute-done((f32[2,16,1536]{2,1,0:T(8,128)S(1)}, f32[2,16,1536]{2,1,0:T(8,128)S(1)}, u32[]{:S(2)}, u32[]{:S(2)}) %collective-permute-start.13) | collective-permute-done | bytes 196640 | tf_op jit(solution)/shard_map/ppermute | solution.py:314
  28.8 0.0 collective-permute-start.14
  28.8 0.0 collective-permute-done.5.packed_ref
  28.8 2.6 %collective-permute-start.6 = (f32[12,16,128]{2,1,0:T(8,128)S(1)}, f32[12,16,128]{2,1,0:T(8,128)S(1)}, u32[]{:S(2)}, u32[]{:S(2)}) collective-permute-start(f32[12,16,128]{2,1,0:T(8,128)S(1)} %shard_map.110.own_ref.after_ref), channel_id=1, source_target_pairs={{0,34},{1,35},{2,32},{3,33},{4,38},{5,39},{6,36},{7,37},{8,42},{9,... | collective-permute-start | bytes 294920 | tf_op jit(solution)/shard_map/ppermute | solution.py:314
  31.4 0.0 collective-permute-done.7.beside_ref
  31.4 0.7 %collective-permute-start.4 = (f32[12,16,128]{2,1,0:T(8,128)S(1)}, f32[12,16,128]{2,1,0:T(8,128)S(1)}, u32[]{:S(2)}, u32[]{:S(2)}) collective-permute-start(f32[12,16,128]{2,1,0:T(8,128)S(1)} %shard_map.110.own_ref.after_ref), channel_id=1, source_target_pairs={{0,2},{1,3},{2,0},{3,1},{4,6},{5,7},{6,4},{7,5},{8,10},{9,11},{10,... | collective-permute-start | bytes 294920 | tf_op jit(solution)/shard_map/ppermute | solution.py:314
  32.1 0.0 slice-done
  32.1 0.9 %shard_map.112 = (bf16[12,256,128]{2,1,0:T(8,128)(2,1)S(1)}, bf16[12,256,128]{2,1,0:T(8,128)(2,1)S(1)}, bf16[12,256,128]{2,1,0:T(8,128)(2,1)S(1)}, bf16[12,256,128]{2,1,0:T(8,128)(2,1)S(1)}) custom-call(f32[8,12,2,64,128]{4,3,2,1,0:T(8,128)S(1)} %bitcast.5, f32[12,16,128]{2,1,0:T(8,128)S(1)} %shard_map.110.own_ref.after_ref), custom_call_target="tpu_custom_call" | custom-call | flops 2000000 | bytes 1048576 | tf_op jit(solution)/shard_map/pallas_call | solution.py:351
  33.1 0.2 shard_map.114.away_ref
  33.2 3.0 %collective-permute-done.6.corner_ref = f32[12,16,128]{2,1,0:T(8,128)S(1)} collective-permute-done((f32[12,16,128]{2,1,0:T(8,128)S(1)}, f32[12,16,128]{2,1,0:T(8,128)S(1)}, u32[]{:S(2)}, u32[]{:S(2)}) %collective-permute-start.6) | collective-permute-done | bytes 98336 | tf_op jit(solution)/shard_map/ppermute | solution.py:314
  36.2 0.5 %shard_map.115.side_ref = f32[12,16,128]{2,1,0:T(8,128)S(1)} custom-call(s32[8,1,12]{2,1,0:T(1,128)S(1)} %get-tuple-element.37.roster_ref, f32[13,64,128]{2,1,0:T(8,128)S(1)} %collective-permute-done.5.packed_ref, f32[12,16,128]{2,1,0:T(8,128)S(1)} %collective-permute-done.6.corner_ref, bf16[12,256,128]{2,1,0:T(8,128)(2,1)S(1)} %shard_map.114.away_ref, ...), custom_call_target="tpu_custom_call" | custom-call | flops 2000000 | bytes 1048576 | tf_op jit(solution)/shard_map/pallas_call | solution.py:351
  36.8 1.1 %collective-permute-done.4.other_ref = f32[12,16,128]{2,1,0:T(8,128)S(1)} collective-permute-done((f32[12,16,128]{2,1,0:T(8,128)S(1)}, f32[12,16,128]{2,1,0:T(8,128)S(1)}, u32[]{:S(2)}, u32[]{:S(2)}) %collective-permute-start.4) | collective-permute-done | bytes 98336 | tf_op jit(solution)/shard_map/ppermute | solution.py:314
  37.8 0.4 shard_map.116.own_ref.after_ref.rest_0_
  38.3 0.9 %collective-permute-start.11 = (f32[12,16,128]{2,1,0:T(8,128)S(1)}, f32[12,16,128]{2,1,0:T(8,128)S(1)}, u32[]{:S(2)}, u32[]{:S(2)}) collective-permute-start(f32[12,16,128]{2,1,0:T(8,128)S(1)} %shard_map.116.own_ref.after_ref.rest_0_), channel_id=1, source_target_pairs={{0,64},{1,65},{2,66},{3,67},{4,68},{5,69},{6,70},{7,71},{8,72},{9,... | collective-permute-start | bytes 294920 | tf_op jit(solution)/shard_map/ppermute | solution.py:314
  39.2 2.4 %collective-permute-start.10 = (f32[12,16,128]{2,1,0:T(8,128)S(1)}, f32[12,16,128]{2,1,0:T(8,128)S(1)}, u32[]{:S(2)}, u32[]{:S(2)}) collective-permute-start(f32[12,16,128]{2,1,0:T(8,128)S(1)} %shard_map.116.own_ref.after_ref.rest_0_), channel_id=1, source_target_pairs={{0,192},{1,193},{2,194},{3,195},{4,196},{5,197},{6,198},{7,199},{8... | collective-permute-start | bytes 294920 | tf_op jit(solution)/shard_map/ppermute | solution.py:314
  41.7 0.2 shard_map.117.ready_ref
  41.9 0.0 collective-permute-done.12.core_ref
  41.9 0.9 %collective-permute-start.8 = (f32[12,16,128]{2,1,0:T(8,128)S(1)}, f32[12,16,128]{2,1,0:T(8,128)S(1)}, u32[]{:S(2)}, u32[]{:S(2)}) collective-permute-start(f32[12,16,128]{2,1,0:T(8,128)S(1)} %shard_map.117.ready_ref), channel_id=1, source_target_pairs={{0,128},{1,129},{2,130},{3,131},{4,132},{5,133},{6,134},{7,135},{8... | collective-permute-start | bytes 294920 | tf_op jit(solution)/shard_map/ppermute | solution.py:314
  42.8 0.1 shard_map.120.rest_0_.expand_ref
  42.9 0.0 collective-permute-done.14.both_ref
  43.0 1.0 %shard_map.121.rest_1_.rest_0_ = f32[4,32,128]{2,1,0:T(8,128)S(1)} custom-call(s32[2,12]{1,0:T(2,128)S(1)} %bitcast.8, s32[2,12]{1,0:T(2,128)S(1)} %bitcast.10, s32[2,12]{1,0:T(2,128)S(1)} %bitcast.12, s32[4,4]{1,0:T(4,128)S(1)} %bitcast.6, f32[2,16,1536]{2,1,0:T(8,128)S(1)} %copy-done.1, f32[2,16,1536]{2,1,0:T(8,128)S(1)} %collective-permute-done.12.core_ref, ...), custom_call_target="tpu_custom_call" | custom-call | flops 2000000 | bytes 1048576 | tf_op jit(solution)/shard_map/pallas_call | solution.py:355
  44.0 0.0 collective-permute-done.11.other_ref
  44.0 0.3 shard_map.122.own_ref
  44.3 0.0 collective-permute-done.9.packed_ref
  44.4 0.2 shard_map.118.wide_ref.rest_0_
  44.5 0.2 shard_map.123.rest_0_.ready_ref
  44.8 1.3 %collective-permute-done.10.other_ref = f32[12,16,128]{2,1,0:T(8,128)S(1)} collective-permute-done((f32[12,16,128]{2,1,0:T(8,128)S(1)}, f32[12,16,128]{2,1,0:T(8,128)S(1)}, u32[]{:S(2)}, u32[]{:S(2)}) %collective-permute-start.10) | collective-permute-done | bytes 98336 | tf_op jit(solution)/shard_map/ppermute | solution.py:314
  46.1 0.3 shard_map.119.corner_ref
  46.4 1.3 %shard_map.124.rest_1_ = f32[8,32,128]{2,1,0:T(8,128)S(1)} custom-call(s32[2,12]{1,0:T(2,128)S(1)} %bitcast.9, s32[2,12]{1,0:T(2,128)S(1)} %bitcast.11, s32[2,12]{1,0:T(2,128)S(1)} %bitcast.13, s32[4,4]{1,0:T(4,128)S(1)} %bitcast.7, f32[2,16,1536]{2,1,0:T(8,128)S(1)} %copy-done.1, f32[2,16,1536]{2,1,0:T(8,128)S(1)} %collective-permute-done.12.core_ref, ...), custom_call_target="tpu_custom_call" | custom-call | flops 2000000 | bytes 1048576 | tf_op jit(solution)/shard_map/pallas_call | solution.py:355
  47.8 0.3 collective-permute-done.8.beside_ref
  48.1 1.3 %shard_map.125 = f32[2,16,1536]{2,1,0:T(8,128)} custom-call(s32[8,1,12]{2,1,0:T(1,128)S(1)} %get-tuple-element.37.roster_ref, f32[12,16,128]{2,1,0:T(8,128)S(1)} %collective-permute-done.8.beside_ref, f32[12,16,128]{2,1,0:T(8,128)S(1)} %shard_map.119.corner_ref, bf16[12,256,128]{2,1,0:T(8,128)(2,1)S(1)} %get-tuple-element.64.wide_ref, ...), custom_call_target="tpu_custom_call" | custom-call | flops 2000000 | bytes 1048576 | tf_op jit(solution)/shard_map/pallas_call | solution.py:426
  (11 shorter events, 0.0 us)
Async XLA Ops:
  1.8 7.4 %collective-permute-start = (f32[12,16,128]{2,1,0:T(8,128)S(1)}, f32[12,16,128]{2,1,0:T(8,128)S(1)}, u32[]{:S(2)}, u32[]{:S(2)}) collective-permute-start(f32[12,16,128]{2,1,0:T(8,128)S(1)} %get-tuple-element.38.own_ref), channel_id=1, source_target_pairs={{0,128},{1,129},{2,130},{3,131},{4,132},{5,133},{6,134},{7,135},{8... | collective-permute-start | bytes 294920 | tf_op jit(solution)/shard_map/ppermute | solution.py:314
  5.2 23.6 %collective-permute-start.5 = (f32[13,64,128]{2,1,0:T(8,128)S(1)}, f32[13,64,128]{2,1,0:T(8,128)S(1)}, u32[]{:S(2)}, u32[]{:S(2)}) collective-permute-start(f32[13,64,128]{2,1,0:T(8,128)S(1)} %shard_map.113), channel_id=1, source_target_pairs={{0,32},{1,33},{2,34},{3,35},{4,36},{5,37},{6,38},{7,39},{8,40},{9,... | collective-permute-start | bytes 1277960 | tf_op jit(solution)/shard_map/ppermute | solution.py:314
  9.4 4.7 %collective-permute-start.1 = (f32[12,16,128]{2,1,0:T(8,128)S(1)}, f32[12,16,128]{2,1,0:T(8,128)S(1)}, u32[]{:S(2)}, u32[]{:S(2)}) collective-permute-start(f32[12,16,128]{2,1,0:T(8,128)S(1)} %shard_map.102.own_ref.after_ref), channel_id=1, source_target_pairs={{0,64},{1,65},{2,66},{3,67},{4,68},{5,69},{6,70},{7,71},{8,72},{9,... | collective-permute-start | bytes 294920 | tf_op jit(solution)/shard_map/ppermute | solution.py:314
  10.1 9.3 %copy-start.1 = (f32[2,16,1536]{2,1,0:T(8,128)S(1)}, f32[2,16,1536]{2,1,0:T(8,128)}, u32[]{:S(2)}) copy-start(f32[2,16,1536]{2,1,0:T(8,128)} %own_ref.3) | copy-start | bytes 589828
  10.1 22.0 %slice-start = ((s8[6291456]{0:T(1024)(128)(4,1)}), s8[4194304]{0:T(1024)(128)(4,1)S(1)}, s32[]{:S(2)}) async-start(s8[6291456]{0:T(1024)(128)(4,1)} %bitcast.4), calls=%async_computation | async-start | bytes 8388608
  12.9 19.3 %slice-start.1 = ((s8[6291456]{0:T(1024)(128)(4,1)}), s8[2097152]{0:T(1024)(128)(4,1)S(1)}, s32[]{:S(2)}) async-start(s8[6291456]{0:T(1024)(128)(4,1)} %bitcast.4), calls=%async_computation.1 | async-start | bytes 4194304
  14.4 4.7 %collective-permute-start.2 = (f32[12,16,128]{2,1,0:T(8,128)S(1)}, f32[12,16,128]{2,1,0:T(8,128)S(1)}, u32[]{:S(2)}, u32[]{:S(2)}) collective-permute-start(f32[12,16,128]{2,1,0:T(8,128)S(1)} %shard_map.106.own_ref), channel_id=1, source_target_pairs={{0,32},{1,33},{2,34},{3,35},{4,36},{5,37},{6,38},{7,39},{8,40},{9,... | collective-permute-start | bytes 294920 | tf_op jit(solution)/shard_map/ppermute | solution.py:314
  15.6 28.7 %collective-permute-start.9 = (f32[13,64,128]{2,1,0:T(8,128)S(1)}, f32[13,64,128]{2,1,0:T(8,128)S(1)}, u32[]{:S(2)}, u32[]{:S(2)}) collective-permute-start(f32[13,64,128]{2,1,0:T(8,128)S(1)} %get-tuple-element.63), channel_id=1, source_target_pairs={{0,128},{1,129},{2,130},{3,131},{4,132},{5,133},{6,134},{7,135},{8... | collective-permute-start | bytes 1277960 | tf_op jit(solution)/shard_map/ppermute | solution.py:314
  19.3 3.3 %collective-permute-start.3 = (f32[12,16,128]{2,1,0:T(8,128)S(1)}, f32[12,16,128]{2,1,0:T(8,128)S(1)}, u32[]{:S(2)}, u32[]{:S(2)}) collective-permute-start(f32[12,16,128]{2,1,0:T(8,128)S(1)} %shard_map.108.own_ref), channel_id=1, source_target_pairs={{0,1},{1,0},{2,3},{3,2},{4,5},{5,4},{6,7},{7,6},{8,9},{9,8},{10,11... | collective-permute-start | bytes 294920 | tf_op jit(solution)/shard_map/ppermute | solution.py:314
  19.4 9.4 %collective-permute-start.13 = (f32[2,16,1536]{2,1,0:T(8,128)S(1)}, f32[2,16,1536]{2,1,0:T(8,128)S(1)}, u32[]{:S(2)}, u32[]{:S(2)}) collective-permute-start(f32[2,16,1536]{2,1,0:T(8,128)S(1)} %copy-done.1), channel_id=1, source_target_pairs={{0,2},{1,3},{2,0},{3,1},{4,6},{5,7},{6,4},{7,5},{8,10},{9,11},{10,... | collective-permute-start | bytes 589832 | tf_op jit(solution)/shard_map/ppermute | solution.py:314
  23.2 19.7 %copy-start.2 = (f32[12,2,64,128]{3,2,1,0:T(8,128)S(1)}, f32[12,2,64,128]{3,2,1,0:T(8,128)}, u32[]{:S(2)}) copy-start(f32[12,2,64,128]{3,2,1,0:T(8,128)} %weight_ref.3) | copy-start | bytes 2359300
  23.2 19.7 %copy-start = (f32[12,2,2,128,128]{4,3,2,1,0:T(8,128)S(1)}, f32[12,2,2,128,128]{4,3,2,1,0:T(8,128)}, u32[]{:S(2)}) copy-start(f32[12,2,2,128,128]{4,3,2,1,0:T(8,128)} %weight_ref.5) | copy-start | bytes 9437188
  23.2 19.7 %copy-start.3 = (s32[1,4,4]{2,1,0:T(4,128)S(1)}, s32[1,4,4]{2,1,0:T(4,128)}, u32[]{:S(2)}) copy-start(s32[1,4,4]{2,1,0:T(4,128)} %param.19) | copy-start | bytes 196
  23.2 19.7 %copy-start.4 = (s32[12,2]{0,1:T(2,128)S(1)}, s32[12,2]{0,1:T(2,128)}, u32[]{:S(2)}) copy-start(s32[12,2]{0,1:T(2,128)} %param.16) | copy-start | bytes 292
  23.2 19.7 %copy-start.5 = (s32[12,2]{0,1:T(2,128)S(1)}, s32[12,2]{0,1:T(2,128)}, u32[]{:S(2)}) copy-start(s32[12,2]{0,1:T(2,128)} %param.17) | copy-start | bytes 292
  23.2 19.7 %copy-start.6 = (s32[12,2]{0,1:T(2,128)S(1)}, s32[12,2]{0,1:T(2,128)}, u32[]{:S(2)}) copy-start(s32[12,2]{0,1:T(2,128)} %param.18) | copy-start | bytes 292
  23.2 8.2 %collective-permute-start.7 = (f32[12,16,128]{2,1,0:T(8,128)S(1)}, f32[12,16,128]{2,1,0:T(8,128)S(1)}, u32[]{:S(2)}, u32[]{:S(2)}) collective-permute-start(f32[12,16,128]{2,1,0:T(8,128)S(1)} %shard_map.111.ready_ref), channel_id=1, source_target_pairs={{0,32},{1,33},{2,34},{3,35},{4,36},{5,37},{6,38},{7,39},{8,40},{9,... | collective-permute-start | bytes 294920 | tf_op jit(solution)/shard_map/ppermute | solution.py:314
  23.9 18.0 %collective-permute-start.12 = (f32[2,16,1536]{2,1,0:T(8,128)S(1)}, f32[2,16,1536]{2,1,0:T(8,128)S(1)}, u32[]{:S(2)}, u32[]{:S(2)}) collective-permute-start(f32[2,16,1536]{2,1,0:T(8,128)S(1)} %copy-done.1), channel_id=1, source_target_pairs={{0,1},{1,0},{2,3},{3,2},{4,5},{5,4},{6,7},{7,6},{8,9},{9,8},{10,11... | collective-permute-start | bytes 589832 | tf_op jit(solution)/shard_map/ppermute | solution.py:314
  28.8 14.1 %collective-permute-start.14 = (f32[2,16,1536]{2,1,0:T(8,128)S(1)}, f32[2,16,1536]{2,1,0:T(8,128)S(1)}, u32[]{:S(2)}, u32[]{:S(2)}) collective-permute-start(f32[2,16,1536]{2,1,0:T(8,128)S(1)} %collective-permute-done.13.far_ref), channel_id=1, source_target_pairs={{0,1},{1,0},{2,3},{3,2},{4,5},{5,4},{6,7},{7,6},{8,9},{9,8},{10,11... | collective-permute-start | bytes 589832 | tf_op jit(solution)/shard_map/ppermute | solution.py:314
  28.8 7.4 %collective-permute-start.6 = (f32[12,16,128]{2,1,0:T(8,128)S(1)}, f32[12,16,128]{2,1,0:T(8,128)S(1)}, u32[]{:S(2)}, u32[]{:S(2)}) collective-permute-start(f32[12,16,128]{2,1,0:T(8,128)S(1)} %shard_map.110.own_ref.after_ref), channel_id=1, source_target_pairs={{0,34},{1,35},{2,32},{3,33},{4,38},{5,39},{6,36},{7,37},{8,42},{9,... | collective-permute-start | bytes 294920 | tf_op jit(solution)/shard_map/ppermute | solution.py:314
  31.4 6.4 %collective-permute-start.4 = (f32[12,16,128]{2,1,0:T(8,128)S(1)}, f32[12,16,128]{2,1,0:T(8,128)S(1)}, u32[]{:S(2)}, u32[]{:S(2)}) collective-permute-start(f32[12,16,128]{2,1,0:T(8,128)S(1)} %shard_map.110.own_ref.after_ref), channel_id=1, source_target_pairs={{0,2},{1,3},{2,0},{3,1},{4,6},{5,7},{6,4},{7,5},{8,10},{9,11},{10,... | collective-permute-start | bytes 294920 | tf_op jit(solution)/shard_map/ppermute | solution.py:314
  38.3 5.7 %collective-permute-start.11 = (f32[12,16,128]{2,1,0:T(8,128)S(1)}, f32[12,16,128]{2,1,0:T(8,128)S(1)}, u32[]{:S(2)}, u32[]{:S(2)}) collective-permute-start(f32[12,16,128]{2,1,0:T(8,128)S(1)} %shard_map.116.own_ref.after_ref.rest_0_), channel_id=1, source_target_pairs={{0,64},{1,65},{2,66},{3,67},{4,68},{5,69},{6,70},{7,71},{8,72},{9,... | collective-permute-start | bytes 294920 | tf_op jit(solution)/shard_map/ppermute | solution.py:314
  39.2 6.9 %collective-permute-start.10 = (f32[12,16,128]{2,1,0:T(8,128)S(1)}, f32[12,16,128]{2,1,0:T(8,128)S(1)}, u32[]{:S(2)}, u32[]{:S(2)}) collective-permute-start(f32[12,16,128]{2,1,0:T(8,128)S(1)} %shard_map.116.own_ref.after_ref.rest_0_), channel_id=1, source_target_pairs={{0,192},{1,193},{2,194},{3,195},{4,196},{5,197},{6,198},{7,199},{8... | collective-permute-start | bytes 294920 | tf_op jit(solution)/shard_map/ppermute | solution.py:314
  41.9 6.2 %collective-permute-start.8 = (f32[12,16,128]{2,1,0:T(8,128)S(1)}, f32[12,16,128]{2,1,0:T(8,128)S(1)}, u32[]{:S(2)}, u32[]{:S(2)}) collective-permute-start(f32[12,16,128]{2,1,0:T(8,128)S(1)} %shard_map.117.ready_ref), channel_id=1, source_target_pairs={{0,128},{1,129},{2,130},{3,131},{4,132},{5,133},{6,134},{7,135},{8... | collective-permute-start | bytes 294920 | tf_op jit(solution)/shard_map/ppermute | solution.py:314

commit v12 on v11

--- a/solution.py
+++ b/solution.py
@@ -148,8 +148,9 @@
 
 
 def first_kernel(own_ref, weight_4, roster_ref, coupling_hbm, *refs):
-    ready_out, other_out, back_ref, own_4, other_4, weight_1, weight_2, weight_0, sems = refs
-    copies = started([(coupling_hbm.at[n], out) for n, out in enumerate((weight_0, weight_1, weight_2))], sems)
+    ready_out, other_out, back_ref, own_4, other_4, *outs, weight_0, sems = refs
+    pairs = zip((0, 1, 2, 6, 3), [weight_0] + outs)
+    copies = started([(coupling_hbm.at[n], out) for n, out in pairs], sems)
     for k in range(own_ref.shape[0]):
         prepare_block(k, k, weight_4, own_4, other_4)
     copies[0].wait()
@@ -157,13 +158,11 @@
     finish(copies[1:])
 
 
-def ahead_kernel(level, own_ref, weight_ref, roster_ref, weight_2, coupling_hbm, *refs):
-    ready_out, other_out, back_ref, own_2, other_2, back_2, weight_3, weight_6, sems = refs
-    copies = started([(coupling_hbm.at[3], weight_3), (coupling_hbm.at[6], weight_6)], sems)
+def ahead_kernel(level, own_ref, weight_ref, roster_ref, weight_2, *refs):
+    ready_out, other_out, back_ref, own_2, other_2, back_2 = refs
     start_level(level, own_ref, weight_ref, roster_ref, ready_out, other_out, back_ref)
     for k, place in enumerate(slots(roster_ref[level + 1], own_ref.shape[0], back_2)):
         prepare_block(k, place, weight_2, own_2, other_2)
-    finish(copies)
 
 
 def sorted_kernel(level, weight_ref, roster_ref, after_ref, own_out, other_out, back_ref):
@@ -177,10 +176,14 @@
         prepare_block(k, k, weight_ref, own_out, other_out, packed_ref)
 
 
-def fetch_kernel(levels, coupling_ref, after_ref, *outs):
-    for n, level in enumerate(levels):
-        for k in range(coupling_ref.shape[1]):
-            prepare_block(k, k, coupling_ref.at[level], outs[2 * n], outs[2 * n + 1])
+def fetch_kernel(levels, coupling_hbm, after_ref, *refs):
+    count = len(levels)
+    outs, weights, sems = refs[: 2 * count], refs[2 * count : -1], refs[-1]
+    copies = started([(coupling_hbm.at[level], out) for level, out in zip(levels, weights)], sems)
+    for n in range(count):
+        copies[n].wait()
+        for k in range(weights[n].shape[0]):
+            prepare_block(k, k, weights[n], outs[2 * n], outs[2 * n + 1])
 
 
 def unpack_kernel(packed_ref, after_ref, out_ref):
@@ -368,32 +371,28 @@
     other = flipped(coeffs, top, 0)
     packed_4 = run(part(pack_kernel, 4), packed, [weight_4, names])
     away_4 = flipped(packed_4, top // 4, 0)
-    ready, wide_0, back_0, own_4, wide_4, weight_1, weight_2 = run(
+    ready, wide_0, back_0, own_4, wide_4, weight_1, weight_2, weight_6, weight_3 = run(
         first_kernel,
-        [state, wide, back, wide, wide, level_weights, level_weights],
+        [state, wide, back, wide, wide] + [level_weights] * 4,
         [coeffs, weight_4, names, coupling_hbm],
-        scratch=[level_weights, DMA((3,))],
+        scratch=[level_weights, DMA((5,))],
         hbm=(3,),
     )
     coeffs = run(level_kernel, state, [back_0, other, wide_0, ready])
 
     other = flipped(coeffs, top // 2, 0)
-    ready, wide_1, back_1, own_2, wide_2, back_2, weight_3, weight_6 = run(
-        part(ahead_kernel, 1),
-        [state, wide, back, wide, wide, back, level_weights, level_weights],
-        [coeffs, weight_1, names, weight_2, coupling_hbm],
-        scratch=[DMA((2,))],
-        hbm=(4,),
-    )
-    own_3, wide_3, back_3 = run(part(sorted_kernel, 3), [wide, wide, back], [weight_3, names], [coeffs])
-    own_6, wide_6, packed_6 = run(part(packed_kernel, 6), [wide, wide, packed], [weight_6, names], [coeffs])
-    coeffs = run(level_kernel, state, [back_1, other, wide_1, ready], [own_3, own_6])
+    ready, wide_1, back_1, own_2, wide_2, back_2 = run(
+        part(ahead_kernel, 1), [state, wide, back, wide, wide, back], [coeffs, weight_1, names, weight_2]
+    )
+    own_6, wide_6, packed_6 = run(part(packed_kernel, 6), [wide, wide, packed], [weight_6, names], [ready])
+    away_6 = flipped(tied(packed_6, coeffs), top, 0)
+    coeffs = run(level_kernel, state, [back_1, other, wide_1, ready], [own_6])
 
     other = flipped(coeffs, top // 4, 0)
     far = flipped(tied(field_in, coeffs), 0, 2)
-    away_6 = flipped(tied(packed_6, coeffs), top, 0)
     ready = run(part(own_sorted_kernel, 2), state, [coeffs, own_2, names])
-    coeffs = run(level_kernel, state, [back_2, other, wide_2, ready])
+    own_3, wide_3, back_3 = run(part(sorted_kernel, 3), [wide, wide, back], [weight_3, names], [coeffs])
+    coeffs = run(level_kernel, state, [back_2, other, wide_2, ready], [own_3])
 
     other = flipped(coeffs, 0, 1)
     ready = run(part(own_sorted_kernel, 3), state, [coeffs, own_3, names])
@@ -404,7 +403,12 @@
     beside = flipped(ready, top // 4, 0)
     other = flipped(coeffs, 0, 2)
     own_5, wide_5, own_7, wide_7 = run(
-        part(fetch_kernel, (5, 7)), [wide] * 4, [pltpu.with_memory_space_constraint(coupling, VMEM)], [coeffs]
+        part(fetch_kernel, (5, 7)),
+        [wide] * 4,
+        [coupling_hbm],
+        [coeffs],
+        scratch=[level_weights, level_weights, DMA((2,))],
+        hbm=(0,),
     )
     core = flipped(tied(field_in, coeffs), 0, 1)
     both = flipped(tied(far, coeffs), 0, 1)

time: 49.7 us -> 45.1 us (0.907)
  waiting for transfers between devices: 11.3 us -> 6.38 us
  starting transfers between devices: 20.7 us -> 21.5 us
    ppermute x15, waiting for transfers between devices: 11.3 us -> 6.38 us  [flipped(): return lax.ppermute(value, ('leaf', 'sub'), pairs)]
    ppermute x15, starting transfers between devices: 20.7 us -> 21.5 us  [flipped(): return lax.ppermute(value, ('leaf', 'sub'), pairs)]
  transfers between devices with their start and end apart: 15 -> 15, of which waited for: 7 -> 7; matrix products, arithmetic and copies ran while one was open for 0% -> 0% of each run, Pallas kernels for 28% -> 30%
where the time goes in v12:
time: 45.1 us; the launch traced here: 44.9 us
  starting transfers between devices  21.5 us (48%)
  Pallas kernels  16.5 us (37%)
  waiting for transfers between devices  6.38 us (14%)
  between operations  0.53 us (1%)
    ppermute x15, starting transfers between devices, flipped(): return lax.ppermute(value, ('leaf', 'sub'), pairs)  21.5 us
    pallas_call x23, Pallas kernels, run(): call(kernel, outs, spaces, [VMEM] * len(outs) if several else VMEM, scratch)  12.9 us
    ppermute x15, waiting for transfers between devices, flipped(): return lax.ppermute(value, ('leaf', 'sub'), pairs)  6.38 us
    pallas_call x2, Pallas kernels, near_piece(): call(functools.partial(near_kernel, begin), VMEM((count, 2 * rhs, 128), F...  2.34 us
    pallas_call x1, Pallas kernels, on_device(): call(part(last_kernel, 7), jax.ShapeDtypeStruct(field_in.shape, F32), [VM...  1.26 us
  transfers between devices with their start and end apart: 15, of which 7 were waited for; matrix products, arithmetic and copies ran while one was open for 0% of the time, Pallas kernels for 30%

profile of v12, /device:TPU:64, one launch (start us, length us, event | category | flops | bytes accessed | tf_op | source)
XLA Modules:
  0.0 44.9 jit_solution(15375229128304134177)
XLA Ops:
  0.0 1.8 %shard_map.100 = (f32[12,16,128]{2,1,0:T(8,128)S(1)}, f32[12,2,64,128]{3,2,1,0:T(8,128)S(1)}, s32[8,1,12]{2,1,0:T(1,128)S(1)}) custom-call(f32[2,16,1536]{2,1,0:T(8,128)} %own_ref.3, f32[12,2,64,128]{3,2,1,0:T(8,128)} %weight_hbm.1, f32[8,12,2,64,128]{4,3,2,1,0:T(8,128)} %coupling_hbm.5, s32[8,1,12]{2,1,0:T(1,128)} %roster_hbm.1), custom_call_target="tpu_custom_call" | custom-call | flops 2000000 | bytes 1048576 | tf_op jit(solution)/shard_map/pallas_call | solution.py:354
  1.8 3.1 %collective-permute-start = (f32[12,16,128]{2,1,0:T(8,128)S(1)}, f32[12,16,128]{2,1,0:T(8,128)S(1)}, u32[]{:S(2)}, u32[]{:S(2)}) collective-permute-start(f32[12,16,128]{2,1,0:T(8,128)S(1)} %get-tuple-element.38.own_ref), channel_id=1, source_target_pairs={{0,128},{1,129},{2,130},{3,131},{4,132},{5,133},{6,134},{7,135},{8... | collective-permute-start | bytes 294920 | tf_op jit(solution)/shard_map/ppermute | solution.py:317
  4.9 0.3 shard_map.113
  5.2 0.0 copy-start.1
  5.2 1.7 %collective-permute-start.5 = (f32[13,64,128]{2,1,0:T(8,128)S(1)}, f32[13,64,128]{2,1,0:T(8,128)S(1)}, u32[]{:S(2)}, u32[]{:S(2)}) collective-permute-start(f32[13,64,128]{2,1,0:T(8,128)S(1)} %shard_map.113), channel_id=1, source_target_pairs={{0,32},{1,33},{2,34},{3,35},{4,36},{5,37},{6,38},{7,39},{8,40},{9,... | collective-permute-start | bytes 1277960 | tf_op jit(solution)/shard_map/ppermute | solution.py:317
  6.9 2.3 %shard_map.101 = (f32[12,16,128]{2,1,0:T(8,128)S(1)}, bf16[12,256,128]{2,1,0:T(8,128)(2,1)S(1)}, s32[8,128]{1,0:T(8,128)S(1)}, bf16[12,256,128]{2,1,0:T(8,128)(2...) custom-call(f32[12,16,128]{2,1,0:T(8,128)S(1)} %get-tuple-element.38, ...), custom_call_target="tpu_custom_call" | custom-call | flops 2000000 | bytes 1048576 | tf_op jit(solution)/shard_map/pallas_call | solution.py:354
  9.2 0.0 collective-permute-done.other_ref
  9.2 0.2 shard_map.102.own_ref
  9.4 0.7 %collective-permute-start.1 = (f32[12,16,128]{2,1,0:T(8,128)S(1)}, f32[12,16,128]{2,1,0:T(8,128)S(1)}, u32[]{:S(2)}, u32[]{:S(2)}) collective-permute-start(f32[12,16,128]{2,1,0:T(8,128)S(1)} %shard_map.102.own_ref), channel_id=1, source_target_pairs={{0,64},{1,65},{2,66},{3,67},{4,68},{5,69},{6,70},{7,71},{8,72},{9,... | collective-permute-start | bytes 294920 | tf_op jit(solution)/shard_map/ppermute | solution.py:317
  10.1 1.0 %shard_map.103 = (f32[12,16,128]{2,1,0:T(8,128)S(1)}, bf16[12,256,128]{2,1,0:T(8,128)(2,1)S(1)}, s32[8,128]{1,0:T(8,128)S(1)}, bf16[12,256,128]{2,1,0:T(8,128)(2...) custom-call(f32[12,16,128]{2,1,0:T(8,128)S(1)} %shard_map.102.own_ref, ...), custom_call_target="tpu_custom_call" | custom-call | flops 2000000 | bytes 1048576 | tf_op jit(solution)/shard_map/pallas_call | solution.py:354
  11.1 0.5 %shard_map.104 = (bf16[12,256,128]{2,1,0:T(8,128)(2,1)S(1)}, bf16[12,256,128]{2,1,0:T(8,128)(2,1)S(1)}, f32[13,64,128]{2,1,0:T(8,128)S(1)}) custom-call(f32[12,2,64,128]{3,2,1,0:T(8,128)S(1)} %get-tuple-element.49.weight_ref, s32[8,1,12]{2,1,0:T(1,128)S(1)} %get-tuple-element.37.roster_ref, f32[12,16,128]{2,1,0:T(8,128)S(1)} %get-tuple-element.48.after_ref.ready_ref), custom_call_target="tpu_custom_call" | custom-call | flops 2000000 | bytes 1048576 | tf_op jit(solution)/shard_map/pallas_call | solution.py:354
  11.7 2.5 %collective-permute-start.9 = (f32[13,64,128]{2,1,0:T(8,128)S(1)}, f32[13,64,128]{2,1,0:T(8,128)S(1)}, u32[]{:S(2)}, u32[]{:S(2)}) collective-permute-start(f32[13,64,128]{2,1,0:T(8,128)S(1)} %get-tuple-element.63), channel_id=1, source_target_pairs={{0,128},{1,129},{2,130},{3,131},{4,132},{5,133},{6,134},{7,135},{8... | collective-permute-start | bytes 1277960 | tf_op jit(solution)/shard_map/ppermute | solution.py:317
  14.2 0.6 %collective-permute-done.1.other_ref = f32[12,16,128]{2,1,0:T(8,128)S(1)} collective-permute-done((f32[12,16,128]{2,1,0:T(8,128)S(1)}, f32[12,16,128]{2,1,0:T(8,128)S(1)}, u32[]{:S(2)}, u32[]{:S(2)}) %collective-permute-start.1) | collective-permute-done | bytes 98336 | tf_op jit(solution)/shard_map/ppermute | solution.py:317
  14.9 0.2 shard_map.105.after_ref.own_ref
  15.1 1.0 %collective-permute-start.2 = (f32[12,16,128]{2,1,0:T(8,128)S(1)}, f32[12,16,128]{2,1,0:T(8,128)S(1)}, u32[]{:S(2)}, u32[]{:S(2)}) collective-permute-start(f32[12,16,128]{2,1,0:T(8,128)S(1)} %shard_map.105.after_ref.own_ref), channel_id=1, source_target_pairs={{0,32},{1,33},{2,34},{3,35},{4,36},{5,37},{6,38},{7,39},{8,40},{9,... | collective-permute-start | bytes 294920 | tf_op jit(solution)/shard_map/ppermute | solution.py:317
  16.1 0.0 copy-done.1
  16.1 2.9 %collective-permute-start.13 = (f32[2,16,1536]{2,1,0:T(8,128)S(1)}, f32[2,16,1536]{2,1,0:T(8,128)S(1)}, u32[]{:S(2)}, u32[]{:S(2)}) collective-permute-start(f32[2,16,1536]{2,1,0:T(8,128)S(1)} %copy-done.1), channel_id=1, source_target_pairs={{0,2},{1,3},{2,0},{3,1},{4,6},{5,7},{6,4},{7,5},{8,10},{9,11},{10,... | collective-permute-start | bytes 589832 | tf_op jit(solution)/shard_map/ppermute | solution.py:317
  19.0 0.2 shard_map.107.ready_ref
  19.3 0.5 %shard_map.106 = (bf16[12,256,128]{2,1,0:T(8,128)(2,1)S(1)}, bf16[12,256,128]{2,1,0:T(8,128)(2,1)S(1)}, s32[8,128]{1,0:T(8,128)S(1)}) custom-call(f32[12,2,64,128]{3,2,1,0:T(8,128)S(1)} %get-tuple-element.40.weight_ref, s32[8,1,12]{2,1,0:T(1,128)S(1)} %get-tuple-element.37.roster_ref, f32[12,16,128]{2,1,0:T(8,128)S(1)} %shard_map.105.after_ref.own_ref), custom_call_target="tpu_custom_call" | custom-call | flops 2000000 | bytes 1048576 | tf_op jit(solution)/shard_map/pallas_call | solution.py:354
  19.8 1.0 %collective-permute-done.2.other_ref = f32[12,16,128]{2,1,0:T(8,128)S(1)} collective-permute-done((f32[12,16,128]{2,1,0:T(8,128)S(1)}, f32[12,16,128]{2,1,0:T(8,128)S(1)}, u32[]{:S(2)}, u32[]{:S(2)}) %collective-permute-start.2) | collective-permute-done | bytes 98336 | tf_op jit(solution)/shard_map/ppermute | solution.py:317
  20.8 0.2 shard_map.108.own_ref
  21.0 0.1 collective-permute-start.3
  21.1 0.2 shard_map.109.ready_ref
  21.4 1.0 %collective-permute-done.3.other_ref = f32[12,16,128]{2,1,0:T(8,128)S(1)} collective-permute-done((f32[12,16,128]{2,1,0:T(8,128)S(1)}, f32[12,16,128]{2,1,0:T(8,128)S(1)}, u32[]{:S(2)}, u32[]{:S(2)}) %collective-permute-start.3) | collective-permute-done | bytes 98336 | tf_op jit(solution)/shard_map/ppermute | solution.py:317
  22.4 0.2 shard_map.110.own_ref.after_ref
  22.7 0.2 shard_map.111.ready_ref
  22.9 0.0 copy-start.2
  22.9 1.1 %collective-permute-start.7 = (f32[12,16,128]{2,1,0:T(8,128)S(1)}, f32[12,16,128]{2,1,0:T(8,128)S(1)}, u32[]{:S(2)}, u32[]{:S(2)}) collective-permute-start(f32[12,16,128]{2,1,0:T(8,128)S(1)} %shard_map.111.ready_ref), channel_id=1, source_target_pairs={{0,32},{1,33},{2,34},{3,35},{4,36},{5,37},{6,38},{7,39},{8,40},{9,... | collective-permute-start | bytes 294920 | tf_op jit(solution)/shard_map/ppermute | solution.py:317
  24.0 1.3 %collective-permute-done.13.far_ref = f32[2,16,1536]{2,1,0:T(8,128)S(1)} collective-permute-done((f32[2,16,1536]{2,1,0:T(8,128)S(1)}, f32[2,16,1536]{2,1,0:T(8,128)S(1)}, u32[]{:S(2)}, u32[]{:S(2)}) %collective-permute-start.13) | collective-permute-done | bytes 196640 | tf_op jit(solution)/shard_map/ppermute | solution.py:317
  25.3 0.0 collective-permute-start.12
  25.4 0.5 %collective-permute-start.14 = (f32[2,16,1536]{2,1,0:T(8,128)S(1)}, f32[2,16,1536]{2,1,0:T(8,128)S(1)}, u32[]{:S(2)}, u32[]{:S(2)}) collective-permute-start(f32[2,16,1536]{2,1,0:T(8,128)S(1)} %collective-permute-done.13.far_ref), channel_id=1, source_target_pairs={{0,1},{1,0},{2,3},{3,2},{4,5},{5,4},{6,7},{7,6},{8,9},{9,8},{10,11... | collective-permute-start | bytes 589832 | tf_op jit(solution)/shard_map/ppermute | solution.py:317
  25.9 0.0 collective-permute-done.5.packed_ref
  25.9 0.9 %collective-permute-start.6 = (f32[12,16,128]{2,1,0:T(8,128)S(1)}, f32[12,16,128]{2,1,0:T(8,128)S(1)}, u32[]{:S(2)}, u32[]{:S(2)}) collective-permute-start(f32[12,16,128]{2,1,0:T(8,128)S(1)} %shard_map.110.own_ref.after_ref), channel_id=1, source_target_pairs={{0,34},{1,35},{2,32},{3,33},{4,38},{5,39},{6,36},{7,37},{8,42},{9,... | collective-permute-start | bytes 294920 | tf_op jit(solution)/shard_map/ppermute | solution.py:317
  26.8 1.1 %collective-permute-done.7.beside_ref = f32[12,16,128]{2,1,0:T(8,128)S(1)} collective-permute-done((f32[12,16,128]{2,1,0:T(8,128)S(1)}, f32[12,16,128]{2,1,0:T(8,128)S(1)}, u32[]{:S(2)}, u32[]{:S(2)}) %collective-permute-start.7) | collective-permute-done | bytes 98336 | tf_op jit(solution)/shard_map/ppermute | solution.py:317
  27.9 2.7 %collective-permute-start.4 = (f32[12,16,128]{2,1,0:T(8,128)S(1)}, f32[12,16,128]{2,1,0:T(8,128)S(1)}, u32[]{:S(2)}, u32[]{:S(2)}) collective-permute-start(f32[12,16,128]{2,1,0:T(8,128)S(1)} %shard_map.110.own_ref.after_ref), channel_id=1, source_target_pairs={{0,2},{1,3},{2,0},{3,1},{4,6},{5,7},{6,4},{7,5},{8,10},{9,11},{10,... | collective-permute-start | bytes 294920 | tf_op jit(solution)/shard_map/ppermute | solution.py:317
  30.6 2.2 %shard_map.112 = (bf16[12,256,128]{2,1,0:T(8,128)(2,1)S(1)}, bf16[12,256,128]{2,1,0:T(8,128)(2,1)S(1)}, bf16[12,256,128]{2,1,0:T(8,128)(2,1)S(1)}, bf16[12,256,128]{2,1,0:T(8,128)(2,1)S(1)}) custom-call(f32[8,12,2,64,128]{4,3,2,1,0:T(8,128)} %coupling_hbm.5, f32[12,16,128]{2,1,0:T(8,128)S(1)} %shard_map.110.own_ref.after_ref), custom_call_target="tpu_custom_call" | custom-call | flops 2000000 | bytes 1048576 | tf_op jit(solution)/shard_map/pallas_call | solution.py:354
  32.8 0.0 copy-start
  32.8 0.0 copy-start.3
  32.8 0.0 copy-start.4
  32.8 0.0 copy-start.5
  32.8 0.0 copy-start.6
  32.8 0.2 shard_map.114.away_ref
  33.0 0.0 collective-permute-done.6.corner_ref
  33.0 0.5 %shard_map.115.side_ref = f32[12,16,128]{2,1,0:T(8,128)S(1)} custom-call(s32[8,1,12]{2,1,0:T(1,128)S(1)} %get-tuple-element.37.roster_ref, f32[13,64,128]{2,1,0:T(8,128)S(1)} %collective-permute-done.5.packed_ref, f32[12,16,128]{2,1,0:T(8,128)S(1)} %collective-permute-done.6.corner_ref, bf16[12,256,128]{2,1,0:T(8,128)(2,1)S(1)} %shard_map.114.away_ref, ...), custom_call_target="tpu_custom_call" | custom-call | flops 2000000 | bytes 1048576 | tf_op jit(solution)/shard_map/pallas_call | solution.py:354
  33.6 0.4 collective-permute-done.4.other_ref
  34.0 0.4 shard_map.116.own_ref.after_ref.rest_0_
  34.4 1.1 %collective-permute-start.11 = (f32[12,16,128]{2,1,0:T(8,128)S(1)}, f32[12,16,128]{2,1,0:T(8,128)S(1)}, u32[]{:S(2)}, u32[]{:S(2)}) collective-permute-start(f32[12,16,128]{2,1,0:T(8,128)S(1)} %shard_map.116.own_ref.after_ref.rest_0_), channel_id=1, source_target_pairs={{0,64},{1,65},{2,66},{3,67},{4,68},{5,69},{6,70},{7,71},{8,72},{9,... | collective-permute-start | bytes 294920 | tf_op jit(solution)/shard_map/ppermute | solution.py:317
  35.6 0.8 %collective-permute-start.10 = (f32[12,16,128]{2,1,0:T(8,128)S(1)}, f32[12,16,128]{2,1,0:T(8,128)S(1)}, u32[]{:S(2)}, u32[]{:S(2)}) collective-permute-start(f32[12,16,128]{2,1,0:T(8,128)S(1)} %shard_map.116.own_ref.after_ref.rest_0_), channel_id=1, source_target_pairs={{0,192},{1,193},{2,194},{3,195},{4,196},{5,197},{6,198},{7,199},{8... | collective-permute-start | bytes 294920 | tf_op jit(solution)/shard_map/ppermute | solution.py:317
  36.3 0.2 shard_map.117.ready_ref
  36.6 0.0 collective-permute-done.9.packed_ref
  36.6 2.4 %collective-permute-start.8 = (f32[12,16,128]{2,1,0:T(8,128)S(1)}, f32[12,16,128]{2,1,0:T(8,128)S(1)}, u32[]{:S(2)}, u32[]{:S(2)}) collective-permute-start(f32[12,16,128]{2,1,0:T(8,128)S(1)} %shard_map.117.ready_ref), channel_id=1, source_target_pairs={{0,128},{1,129},{2,130},{3,131},{4,132},{5,133},{6,134},{7,135},{8... | collective-permute-start | bytes 294920 | tf_op jit(solution)/shard_map/ppermute | solution.py:317
  39.0 0.1 shard_map.120.rest_0_.expand_ref
  39.0 0.2 shard_map.118.wide_ref.rest_0_
  39.2 0.0 collective-permute-done.12.core_ref
  39.2 0.0 collective-permute-done.14.both_ref
  39.3 1.0 %shard_map.121.rest_1_.rest_0_ = f32[4,32,128]{2,1,0:T(8,128)S(1)} custom-call(s32[2,12]{1,0:T(2,128)S(1)} %bitcast.6, s32[2,12]{1,0:T(2,128)S(1)} %bitcast.8, s32[2,12]{1,0:T(2,128)S(1)} %bitcast.10, s32[4,4]{1,0:T(4,128)S(1)} %bitcast.4, f32[2,16,1536]{2,1,0:T(8,128)S(1)} %copy-done.1, f32[2,16,1536]{2,1,0:T(8,128)S(1)} %collective-permute-done.12.core_ref, ...), custom_call_target="tpu_custom_call" | custom-call | flops 2000000 | bytes 1048576 | tf_op jit(solution)/shard_map/pallas_call | solution.py:358
  40.3 0.0 collective-permute-done.11.other_ref
  40.4 0.3 shard_map.122.own_ref
  40.7 0.2 shard_map.123.rest_0_.ready_ref
  40.9 0.9 %collective-permute-done.10.other_ref = f32[12,16,128]{2,1,0:T(8,128)S(1)} collective-permute-done((f32[12,16,128]{2,1,0:T(8,128)S(1)}, f32[12,16,128]{2,1,0:T(8,128)S(1)}, u32[]{:S(2)}, u32[]{:S(2)}) %collective-permute-start.10) | collective-permute-done | bytes 98336 | tf_op jit(solution)/shard_map/ppermute | solution.py:317
  41.8 0.3 shard_map.119.corner_ref
  42.1 1.3 %shard_map.124.rest_1_ = f32[8,32,128]{2,1,0:T(8,128)S(1)} custom-call(s32[2,12]{1,0:T(2,128)S(1)} %bitcast.7, s32[2,12]{1,0:T(2,128)S(1)} %bitcast.9, s32[2,12]{1,0:T(2,128)S(1)} %bitcast.11, s32[4,4]{1,0:T(4,128)S(1)} %bitcast.5, f32[2,16,1536]{2,1,0:T(8,128)S(1)} %copy-done.1, f32[2,16,1536]{2,1,0:T(8,128)S(1)} %collective-permute-done.12.core_ref, ...), custom_call_target="tpu_custom_call" | custom-call | flops 2000000 | bytes 1048576 | tf_op jit(solution)/shard_map/pallas_call | solution.py:358
  43.5 0.0 collective-permute-done.8.beside_ref
  43.5 1.3 %shard_map.125 = f32[2,16,1536]{2,1,0:T(8,128)} custom-call(s32[8,1,12]{2,1,0:T(1,128)S(1)} %get-tuple-element.37.roster_ref, f32[12,16,128]{2,1,0:T(8,128)S(1)} %collective-permute-done.8.beside_ref, f32[12,16,128]{2,1,0:T(8,128)S(1)} %shard_map.119.corner_ref, bf16[12,256,128]{2,1,0:T(8,128)(2,1)S(1)} %get-tuple-element.64.wide_ref, ...), custom_call_target="tpu_custom_call" | custom-call | flops 2000000 | bytes 1048576 | tf_op jit(solution)/shard_map/pallas_call | solution.py:430
  (6 shorter events, 0.0 us)
Async XLA Ops:
  1.8 7.4 %collective-permute-start = (f32[12,16,128]{2,1,0:T(8,128)S(1)}, f32[12,16,128]{2,1,0:T(8,128)S(1)}, u32[]{:S(2)}, u32[]{:S(2)}) collective-permute-start(f32[12,16,128]{2,1,0:T(8,128)S(1)} %get-tuple-element.38.own_ref), channel_id=1, source_target_pairs={{0,128},{1,129},{2,130},{3,131},{4,132},{5,133},{6,134},{7,135},{8... | collective-permute-start | bytes 294920 | tf_op jit(solution)/shard_map/ppermute | solution.py:317
  5.2 10.9 %copy-start.1 = (f32[2,16,1536]{2,1,0:T(8,128)S(1)}, f32[2,16,1536]{2,1,0:T(8,128)}, u32[]{:S(2)}) copy-start(f32[2,16,1536]{2,1,0:T(8,128)} %own_ref.3) | copy-start | bytes 589828
  5.2 20.6 %collective-permute-start.5 = (f32[13,64,128]{2,1,0:T(8,128)S(1)}, f32[13,64,128]{2,1,0:T(8,128)S(1)}, u32[]{:S(2)}, u32[]{:S(2)}) collective-permute-start(f32[13,64,128]{2,1,0:T(8,128)S(1)} %shard_map.113), channel_id=1, source_target_pairs={{0,32},{1,33},{2,34},{3,35},{4,36},{5,37},{6,38},{7,39},{8,40},{9,... | collective-permute-start | bytes 1277960 | tf_op jit(solution)/shard_map/ppermute | solution.py:317
  9.4 5.4 %collective-permute-start.1 = (f32[12,16,128]{2,1,0:T(8,128)S(1)}, f32[12,16,128]{2,1,0:T(8,128)S(1)}, u32[]{:S(2)}, u32[]{:S(2)}) collective-permute-start(f32[12,16,128]{2,1,0:T(8,128)S(1)} %shard_map.102.own_ref), channel_id=1, source_target_pairs={{0,64},{1,65},{2,66},{3,67},{4,68},{5,69},{6,70},{7,71},{8,72},{9,... | collective-permute-start | bytes 294920 | tf_op jit(solution)/shard_map/ppermute | solution.py:317
  11.7 24.9 %collective-permute-start.9 = (f32[13,64,128]{2,1,0:T(8,128)S(1)}, f32[13,64,128]{2,1,0:T(8,128)S(1)}, u32[]{:S(2)}, u32[]{:S(2)}) collective-permute-start(f32[13,64,128]{2,1,0:T(8,128)S(1)} %get-tuple-element.63), channel_id=1, source_target_pairs={{0,128},{1,129},{2,130},{3,131},{4,132},{5,133},{6,134},{7,135},{8... | collective-permute-start | bytes 1277960 | tf_op jit(solution)/shard_map/ppermute | solution.py:317
  15.1 5.7 %collective-permute-start.2 = (f32[12,16,128]{2,1,0:T(8,128)S(1)}, f32[12,16,128]{2,1,0:T(8,128)S(1)}, u32[]{:S(2)}, u32[]{:S(2)}) collective-permute-start(f32[12,16,128]{2,1,0:T(8,128)S(1)} %shard_map.105.after_ref.own_ref), channel_id=1, source_target_pairs={{0,32},{1,33},{2,34},{3,35},{4,36},{5,37},{6,38},{7,39},{8,40},{9,... | collective-permute-start | bytes 294920 | tf_op jit(solution)/shard_map/ppermute | solution.py:317
  16.1 9.2 %collective-permute-start.13 = (f32[2,16,1536]{2,1,0:T(8,128)S(1)}, f32[2,16,1536]{2,1,0:T(8,128)S(1)}, u32[]{:S(2)}, u32[]{:S(2)}) collective-permute-start(f32[2,16,1536]{2,1,0:T(8,128)S(1)} %copy-done.1), channel_id=1, source_target_pairs={{0,2},{1,3},{2,0},{3,1},{4,6},{5,7},{6,4},{7,5},{8,10},{9,11},{10,... | collective-permute-start | bytes 589832 | tf_op jit(solution)/shard_map/ppermute | solution.py:317
  21.0 1.4 %collective-permute-start.3 = (f32[12,16,128]{2,1,0:T(8,128)S(1)}, f32[12,16,128]{2,1,0:T(8,128)S(1)}, u32[]{:S(2)}, u32[]{:S(2)}) collective-permute-start(f32[12,16,128]{2,1,0:T(8,128)S(1)} %shard_map.108.own_ref), channel_id=1, source_target_pairs={{0,1},{1,0},{2,3},{3,2},{4,5},{5,4},{6,7},{7,6},{8,9},{9,8},{10,11... | collective-permute-start | bytes 294920 | tf_op jit(solution)/shard_map/ppermute | solution.py:317
  22.9 16.0 %copy-start.2 = (f32[12,2,64,128]{3,2,1,0:T(8,128)S(1)}, f32[12,2,64,128]{3,2,1,0:T(8,128)}, u32[]{:S(2)}) copy-start(f32[12,2,64,128]{3,2,1,0:T(8,128)} %weight_ref.3) | copy-start | bytes 2359300
  22.9 4.9 %collective-permute-start.7 = (f32[12,16,128]{2,1,0:T(8,128)S(1)}, f32[12,16,128]{2,1,0:T(8,128)S(1)}, u32[]{:S(2)}, u32[]{:S(2)}) collective-permute-start(f32[12,16,128]{2,1,0:T(8,128)S(1)} %shard_map.111.ready_ref), channel_id=1, source_target_pairs={{0,32},{1,33},{2,34},{3,35},{4,36},{5,37},{6,38},{7,39},{8,40},{9,... | collective-permute-start | bytes 294920 | tf_op jit(solution)/shard_map/ppermute | solution.py:317
  25.3 13.9 %collective-permute-start.12 = (f32[2,16,1536]{2,1,0:T(8,128)S(1)}, f32[2,16,1536]{2,1,0:T(8,128)S(1)}, u32[]{:S(2)}, u32[]{:S(2)}) collective-permute-start(f32[2,16,1536]{2,1,0:T(8,128)S(1)} %copy-done.1), channel_id=1, source_target_pairs={{0,1},{1,0},{2,3},{3,2},{4,5},{5,4},{6,7},{7,6},{8,9},{9,8},{10,11... | collective-permute-start | bytes 589832 | tf_op jit(solution)/shard_map/ppermute | solution.py:317
  25.4 13.9 %collective-permute-start.14 = (f32[2,16,1536]{2,1,0:T(8,128)S(1)}, f32[2,16,1536]{2,1,0:T(8,128)S(1)}, u32[]{:S(2)}, u32[]{:S(2)}) collective-permute-start(f32[2,16,1536]{2,1,0:T(8,128)S(1)} %collective-permute-done.13.far_ref), channel_id=1, source_target_pairs={{0,1},{1,0},{2,3},{3,2},{4,5},{5,4},{6,7},{7,6},{8,9},{9,8},{10,11... | collective-permute-start | bytes 589832 | tf_op jit(solution)/shard_map/ppermute | solution.py:317
  25.9 7.2 %collective-permute-start.6 = (f32[12,16,128]{2,1,0:T(8,128)S(1)}, f32[12,16,128]{2,1,0:T(8,128)S(1)}, u32[]{:S(2)}, u32[]{:S(2)}) collective-permute-start(f32[12,16,128]{2,1,0:T(8,128)S(1)} %shard_map.110.own_ref.after_ref), channel_id=1, source_target_pairs={{0,34},{1,35},{2,32},{3,33},{4,38},{5,39},{6,36},{7,37},{8,42},{9,... | collective-permute-start | bytes 294920 | tf_op jit(solution)/shard_map/ppermute | solution.py:317
  27.9 6.1 %collective-permute-start.4 = (f32[12,16,128]{2,1,0:T(8,128)S(1)}, f32[12,16,128]{2,1,0:T(8,128)S(1)}, u32[]{:S(2)}, u32[]{:S(2)}) collective-permute-start(f32[12,16,128]{2,1,0:T(8,128)S(1)} %shard_map.110.own_ref.after_ref), channel_id=1, source_target_pairs={{0,2},{1,3},{2,0},{3,1},{4,6},{5,7},{6,4},{7,5},{8,10},{9,11},{10,... | collective-permute-start | bytes 294920 | tf_op jit(solution)/shard_map/ppermute | solution.py:317
  32.8 6.5 %copy-start = (f32[12,2,2,128,128]{4,3,2,1,0:T(8,128)S(1)}, f32[12,2,2,128,128]{4,3,2,1,0:T(8,128)}, u32[]{:S(2)}) copy-start(f32[12,2,2,128,128]{4,3,2,1,0:T(8,128)} %weight_ref.5) | copy-start | bytes 9437188
  32.8 6.5 %copy-start.3 = (s32[1,4,4]{2,1,0:T(4,128)S(1)}, s32[1,4,4]{2,1,0:T(4,128)}, u32[]{:S(2)}) copy-start(s32[1,4,4]{2,1,0:T(4,128)} %param.19) | copy-start | bytes 196
  32.8 6.4 %copy-start.4 = (s32[12,2]{0,1:T(2,128)S(1)}, s32[12,2]{0,1:T(2,128)}, u32[]{:S(2)}) copy-start(s32[12,2]{0,1:T(2,128)} %param.16) | copy-start | bytes 292
  32.8 6.4 %copy-start.5 = (s32[12,2]{0,1:T(2,128)S(1)}, s32[12,2]{0,1:T(2,128)}, u32[]{:S(2)}) copy-start(s32[12,2]{0,1:T(2,128)} %param.17) | copy-start | bytes 292
  32.8 6.4 %copy-start.6 = (s32[12,2]{0,1:T(2,128)S(1)}, s32[12,2]{0,1:T(2,128)}, u32[]{:S(2)}) copy-start(s32[12,2]{0,1:T(2,128)} %param.18) | copy-start | bytes 292
  34.4 5.9 %collective-permute-start.11 = (f32[12,16,128]{2,1,0:T(8,128)S(1)}, f32[12,16,128]{2,1,0:T(8,128)S(1)}, u32[]{:S(2)}, u32[]{:S(2)}) collective-permute-start(f32[12,16,128]{2,1,0:T(8,128)S(1)} %shard_map.116.own_ref.after_ref.rest_0_), channel_id=1, source_target_pairs={{0,64},{1,65},{2,66},{3,67},{4,68},{5,69},{6,70},{7,71},{8,72},{9,... | collective-permute-start | bytes 294920 | tf_op jit(solution)/shard_map/ppermute | solution.py:317
  35.6 6.2 %collective-permute-start.10 = (f32[12,16,128]{2,1,0:T(8,128)S(1)}, f32[12,16,128]{2,1,0:T(8,128)S(1)}, u32[]{:S(2)}, u32[]{:S(2)}) collective-permute-start(f32[12,16,128]{2,1,0:T(8,128)S(1)} %shard_map.116.own_ref.after_ref.rest_0_), channel_id=1, source_target_pairs={{0,192},{1,193},{2,194},{3,195},{4,196},{5,197},{6,198},{7,199},{8... | collective-permute-start | bytes 294920 | tf_op jit(solution)/shard_map/ppermute | solution.py:317
  36.6 6.9 %collective-permute-start.8 = (f32[12,16,128]{2,1,0:T(8,128)S(1)}, f32[12,16,128]{2,1,0:T(8,128)S(1)}, u32[]{:S(2)}, u32[]{:S(2)}) collective-permute-start(f32[12,16,128]{2,1,0:T(8,128)S(1)} %shard_map.117.ready_ref), channel_id=1, source_target_pairs={{0,128},{1,129},{2,130},{3,131},{4,132},{5,133},{6,134},{7,135},{8... | collective-permute-start | bytes 294920 | tf_op jit(solution)/shard_map/ppermute | solution.py:317

commit v13 on v12

--- a/solution.py
+++ b/solution.py
@@ -147,12 +147,15 @@
         out_ref[k] = halves(weight_ref[k].reshape(128, 128))[1]
 
 
-def first_kernel(own_ref, weight_4, roster_ref, coupling_hbm, *refs):
-    ready_out, other_out, back_ref, own_4, other_4, *outs, weight_0, sems = refs
+def plain_weights_kernel(weight_ref, after_ref, own_out, other_out):
+    for k in range(own_out.shape[0]):
+        prepare_block(k, k, weight_ref, own_out, other_out)
+
+
+def first_kernel(own_ref, roster_ref, coupling_hbm, *refs):
+    ready_out, other_out, back_ref, *outs, weight_0, sems = refs
     pairs = zip((0, 1, 2, 6, 3), [weight_0] + outs)
     copies = started([(coupling_hbm.at[n], out) for n, out in pairs], sems)
-    for k in range(own_ref.shape[0]):
-        prepare_block(k, k, weight_4, own_4, other_4)
     copies[0].wait()
     start_level(0, own_ref, weight_0, roster_ref, ready_out, other_out, back_ref)
     finish(copies[1:])
@@ -371,12 +374,12 @@
     other = flipped(coeffs, top, 0)
     packed_4 = run(part(pack_kernel, 4), packed, [weight_4, names])
     away_4 = flipped(packed_4, top // 4, 0)
-    ready, wide_0, back_0, own_4, wide_4, weight_1, weight_2, weight_6, weight_3 = run(
+    ready, wide_0, back_0, weight_1, weight_2, weight_6, weight_3 = run(
         first_kernel,
-        [state, wide, back, wide, wide] + [level_weights] * 4,
-        [coeffs, weight_4, names, coupling_hbm],
+        [state, wide, back] + [level_weights] * 4,
+        [coeffs, names, coupling_hbm],
         scratch=[level_weights, DMA((5,))],
-        hbm=(3,),
+        hbm=(2,),
     )
     coeffs = run(level_kernel, state, [back_0, other, wide_0, ready])
 
@@ -391,8 +394,9 @@
     other = flipped(coeffs, top // 4, 0)
     far = flipped(tied(field_in, coeffs), 0, 2)
     ready = run(part(own_sorted_kernel, 2), state, [coeffs, own_2, names])
+    own_4, wide_4 = run(plain_weights_kernel, [wide, wide], [weight_4], [coeffs])
     own_3, wide_3, back_3 = run(part(sorted_kernel, 3), [wide, wide, back], [weight_3, names], [coeffs])
-    coeffs = run(level_kernel, state, [back_2, other, wide_2, ready], [own_3])
+    coeffs = run(level_kernel, state, [back_2, other, wide_2, ready], [own_3, own_4])
 
     other = flipped(coeffs, 0, 1)
     ready = run(part(own_sorted_kernel, 3), state, [coeffs, own_3, names])

time: 45.1 us -> 45.7 us (1.013)
  starting transfers between devices: 21.5 us -> 22 us
    ppermute x15, starting transfers between devices: 21.5 us -> 22 us  [flipped(): return lax.ppermute(value, ('leaf', 'sub'), pairs)]
    pallas_call x23 -> x24, Pallas kernels: 12.9 us -> 13.2 us  [run(): call(kernel, outs, spaces, [VMEM] * len(outs) if several else VMEM, scratch)]
  transfers between devices with their start and end apart: 15 -> 15, of which waited for: 7 -> 8; matrix products, arithmetic and copies ran while one was open for 0% -> 0% of each run, Pallas kernels for 30% -> 30%
where the time goes in v13:
time: 45.7 us; the launch traced here: 45.6 us
  starting transfers between devices  22 us (48%)
  Pallas kernels  16.8 us (37%)
  waiting for transfers between devices  6.19 us (14%)
  between operations  0.54 us (1%)
    ppermute x15, starting transfers between devices, flipped(): return lax.ppermute(value, ('leaf', 'sub'), pairs)  22 us
    pallas_call x24, Pallas kernels, run(): call(kernel, outs, spaces, [VMEM] * len(outs) if several else VMEM, scratch)  13.2 us
    ppermute x15, waiting for transfers between devices, flipped(): return lax.ppermute(value, ('leaf', 'sub'), pairs)  6.19 us
    pallas_call x2, Pallas kernels, near_piece(): call(functools.partial(near_kernel, begin), VMEM((count, 2 * rhs, 128), F...  2.34 us
    pallas_call x1, Pallas kernels, on_device(): call(part(last_kernel, 7), jax.ShapeDtypeStruct(field_in.shape, F32), [VM...  1.26 us
  transfers between devices with their start and end apart: 15, of which 8 were waited for; matrix products, arithmetic and copies ran while one was open for 0% of the time, Pallas kernels for 30%

profile of v13, /device:TPU:64, one launch (start us, length us, event | category | flops | bytes accessed | tf_op | source)
XLA Modules:
  0.0 45.6 jit_solution(13807156853776648505)
XLA Ops:
  0.0 1.8 %shard_map.100 = (f32[12,16,128]{2,1,0:T(8,128)S(1)}, f32[12,2,64,128]{3,2,1,0:T(8,128)S(1)}, s32[8,1,12]{2,1,0:T(1,128)S(1)}) custom-call(f32[2,16,1536]{2,1,0:T(8,128)} %own_ref.3, f32[12,2,64,128]{3,2,1,0:T(8,128)} %weight_hbm.1, f32[8,12,2,64,128]{4,3,2,1,0:T(8,128)} %coupling_hbm.5, s32[8,1,12]{2,1,0:T(1,128)} %roster_hbm.1), custom_call_target="tpu_custom_call" | custom-call | flops 2000000 | bytes 1048576 | tf_op jit(solution)/shard_map/pallas_call | solution.py:357
  1.8 3.1 %collective-permute-start = (f32[12,16,128]{2,1,0:T(8,128)S(1)}, f32[12,16,128]{2,1,0:T(8,128)S(1)}, u32[]{:S(2)}, u32[]{:S(2)}) collective-permute-start(f32[12,16,128]{2,1,0:T(8,128)S(1)} %get-tuple-element.38.own_ref), channel_id=1, source_target_pairs={{0,128},{1,129},{2,130},{3,131},{4,132},{5,133},{6,134},{7,135},{8... | collective-permute-start | bytes 294920 | tf_op jit(solution)/shard_map/ppermute | solution.py:320
  4.9 0.3 shard_map.114
  5.2 1.7 %collective-permute-start.5 = (f32[13,64,128]{2,1,0:T(8,128)S(1)}, f32[13,64,128]{2,1,0:T(8,128)S(1)}, u32[]{:S(2)}, u32[]{:S(2)}) collective-permute-start(f32[13,64,128]{2,1,0:T(8,128)S(1)} %shard_map.114), channel_id=1, source_target_pairs={{0,32},{1,33},{2,34},{3,35},{4,36},{5,37},{6,38},{7,39},{8,40},{9,... | collective-permute-start | bytes 1277960 | tf_op jit(solution)/shard_map/ppermute | solution.py:320
  6.9 2.1 %shard_map.101 = (f32[12,16,128]{2,1,0:T(8,128)S(1)}, bf16[12,256,128]{2,1,0:T(8,128)(2,1)S(1)}, s32[8,128]{1,0:T(8,128)S(1)}, f32[12,2,64,128]{3,2,1,0:T(8,128)...) custom-call(f32[12,16,128]{2,1,0:T(8,128)S(1)} %get-tuple-element.38.own_ref, ...), custom_call_target="tpu_custom_call" | custom-call | flops 2000000 | bytes 1048576 | tf_op jit(solution)/shard_map/pallas_call | solution.py:357
  9.0 0.0 collective-permute-done.other_ref
  9.0 0.2 shard_map.102.own_ref
  9.3 0.7 %collective-permute-start.1 = (f32[12,16,128]{2,1,0:T(8,128)S(1)}, f32[12,16,128]{2,1,0:T(8,128)S(1)}, u32[]{:S(2)}, u32[]{:S(2)}) collective-permute-start(f32[12,16,128]{2,1,0:T(8,128)S(1)} %shard_map.102.own_ref), channel_id=1, source_target_pairs={{0,64},{1,65},{2,66},{3,67},{4,68},{5,69},{6,70},{7,71},{8,72},{9,... | collective-permute-start | bytes 294920 | tf_op jit(solution)/shard_map/ppermute | solution.py:320
  9.9 1.0 %shard_map.103 = (f32[12,16,128]{2,1,0:T(8,128)S(1)}, bf16[12,256,128]{2,1,0:T(8,128)(2,1)S(1)}, s32[8,128]{1,0:T(8,128)S(1)}, bf16[12,256,128]{2,1,0:T(8,128)(2...) custom-call(f32[12,16,128]{2,1,0:T(8,128)S(1)} %shard_map.102.own_ref, ...), custom_call_target="tpu_custom_call" | custom-call | flops 2000000 | bytes 1048576 | tf_op jit(solution)/shard_map/pallas_call | solution.py:357
  10.9 0.5 %shard_map.104 = (bf16[12,256,128]{2,1,0:T(8,128)(2,1)S(1)}, bf16[12,256,128]{2,1,0:T(8,128)(2,1)S(1)}, f32[13,64,128]{2,1,0:T(8,128)S(1)}) custom-call(f32[12,2,64,128]{3,2,1,0:T(8,128)S(1)} %get-tuple-element.48.weight_ref, s32[8,1,12]{2,1,0:T(1,128)S(1)} %get-tuple-element.37.roster_ref, f32[12,16,128]{2,1,0:T(8,128)S(1)} %get-tuple-element.47.after_ref.ready_ref), custom_call_target="tpu_custom_call" | custom-call | flops 2000000 | bytes 1048576 | tf_op jit(solution)/shard_map/pallas_call | solution.py:357
  11.5 2.7 %collective-permute-start.9 = (f32[13,64,128]{2,1,0:T(8,128)S(1)}, f32[13,64,128]{2,1,0:T(8,128)S(1)}, u32[]{:S(2)}, u32[]{:S(2)}) collective-permute-start(f32[13,64,128]{2,1,0:T(8,128)S(1)} %get-tuple-element.63), channel_id=1, source_target_pairs={{0,128},{1,129},{2,130},{3,131},{4,132},{5,133},{6,134},{7,135},{8... | collective-permute-start | bytes 1277960 | tf_op jit(solution)/shard_map/ppermute | solution.py:320
  14.2 0.3 collective-permute-done.1.other_ref
  14.5 0.2 shard_map.105.after_ref.own_ref
  14.7 1.4 %collective-permute-start.2 = (f32[12,16,128]{2,1,0:T(8,128)S(1)}, f32[12,16,128]{2,1,0:T(8,128)S(1)}, u32[]{:S(2)}, u32[]{:S(2)}) collective-permute-start(f32[12,16,128]{2,1,0:T(8,128)S(1)} %shard_map.105.after_ref.own_ref), channel_id=1, source_target_pairs={{0,32},{1,33},{2,34},{3,35},{4,36},{5,37},{6,38},{7,39},{8,40},{9,... | collective-permute-start | bytes 294920 | tf_op jit(solution)/shard_map/ppermute | solution.py:320
  16.1 0.0 copy-done.1
  16.1 2.9 %collective-permute-start.13 = (f32[2,16,1536]{2,1,0:T(8,128)S(1)}, f32[2,16,1536]{2,1,0:T(8,128)S(1)}, u32[]{:S(2)}, u32[]{:S(2)}) collective-permute-start(f32[2,16,1536]{2,1,0:T(8,128)S(1)} %copy-done.1), channel_id=1, source_target_pairs={{0,2},{1,3},{2,0},{3,1},{4,6},{5,7},{6,4},{7,5},{8,10},{9,11},{10,... | collective-permute-start | bytes 589832 | tf_op jit(solution)/shard_map/ppermute | solution.py:320
  19.0 0.5 %shard_map.108 = (bf16[12,256,128]{2,1,0:T(8,128)(2,1)S(1)}, bf16[12,256,128]{2,1,0:T(8,128)(2,1)S(1)}) custom-call(f32[12,2,64,128]{3,2,1,0:T(8,128)S(1)} %get-tuple-element.55.weight_ref, f32[12,16,128]{2,1,0:T(8,128)S(1)} %shard_map.105.after_ref.own_ref), custom_call_target="tpu_custom_call" | custom-call | flops 2000000 | bytes 1048576 | tf_op jit(solution)/shard_map/pallas_call | solution.py:357
  19.6 0.5 %shard_map.106 = (bf16[12,256,128]{2,1,0:T(8,128)(2,1)S(1)}, bf16[12,256,128]{2,1,0:T(8,128)(2,1)S(1)}, s32[8,128]{1,0:T(8,128)S(1)}) custom-call(f32[12,2,64,128]{3,2,1,0:T(8,128)S(1)} %get-tuple-element.39.weight_ref, s32[8,1,12]{2,1,0:T(1,128)S(1)} %get-tuple-element.37.roster_ref, f32[12,16,128]{2,1,0:T(8,128)S(1)} %shard_map.105.after_ref.own_ref), custom_call_target="tpu_custom_call" | custom-call | flops 2000000 | bytes 1048576 | tf_op jit(solution)/shard_map/pallas_call | solution.py:357
  20.1 0.2 shard_map.107.ready_ref
  20.4 0.1 collective-permute-done.2.other_ref
  20.5 0.2 shard_map.109.own_ref
  20.7 0.1 collective-permute-start.3
  20.8 0.2 shard_map.110.ready_ref
  21.1 1.0 %collective-permute-done.3.other_ref = f32[12,16,128]{2,1,0:T(8,128)S(1)} collective-permute-done((f32[12,16,128]{2,1,0:T(8,128)S(1)}, f32[12,16,128]{2,1,0:T(8,128)S(1)}, u32[]{:S(2)}, u32[]{:S(2)}) %collective-permute-start.3) | collective-permute-done | bytes 98336 | tf_op jit(solution)/shard_map/ppermute | solution.py:320
  22.1 0.2 shard_map.111.own_ref.after_ref
  22.4 2.8 %collective-permute-start.6 = (f32[12,16,128]{2,1,0:T(8,128)S(1)}, f32[12,16,128]{2,1,0:T(8,128)S(1)}, u32[]{:S(2)}, u32[]{:S(2)}) collective-permute-start(f32[12,16,128]{2,1,0:T(8,128)S(1)} %shard_map.111.own_ref.after_ref), channel_id=1, source_target_pairs={{0,34},{1,35},{2,32},{3,33},{4,38},{5,39},{6,36},{7,37},{8,42},{9,... | collective-permute-start | bytes 294920 | tf_op jit(solution)/shard_map/ppermute | solution.py:320
  25.2 0.0 collective-permute-start.12
  25.2 0.1 collective-permute-done.13.far_ref
  25.3 0.4 collective-permute-start.14
  25.7 0.2 shard_map.112.ready_ref
  25.9 0.0 copy-start.2
  26.0 0.0 collective-permute-done.5.packed_ref
  26.0 0.2 collective-permute-start.7
  26.2 2.3 %collective-permute-done.6.corner_ref = f32[12,16,128]{2,1,0:T(8,128)S(1)} collective-permute-done((f32[12,16,128]{2,1,0:T(8,128)S(1)}, f32[12,16,128]{2,1,0:T(8,128)S(1)}, u32[]{:S(2)}, u32[]{:S(2)}) %collective-permute-start.6) | collective-permute-done | bytes 98336 | tf_op jit(solution)/shard_map/ppermute | solution.py:320
  28.5 1.7 %collective-permute-start.4 = (f32[12,16,128]{2,1,0:T(8,128)S(1)}, f32[12,16,128]{2,1,0:T(8,128)S(1)}, u32[]{:S(2)}, u32[]{:S(2)}) collective-permute-start(f32[12,16,128]{2,1,0:T(8,128)S(1)} %shard_map.111.own_ref.after_ref), channel_id=1, source_target_pairs={{0,2},{1,3},{2,0},{3,1},{4,6},{5,7},{6,4},{7,5},{8,10},{9,11},{10,... | collective-permute-start | bytes 294920 | tf_op jit(solution)/shard_map/ppermute | solution.py:320
  30.2 2.2 %shard_map.113 = (bf16[12,256,128]{2,1,0:T(8,128)(2,1)S(1)}, bf16[12,256,128]{2,1,0:T(8,128)(2,1)S(1)}, bf16[12,256,128]{2,1,0:T(8,128)(2,1)S(1)}, bf16[12,256,128]{2,1,0:T(8,128)(2,1)S(1)}) custom-call(f32[8,12,2,64,128]{4,3,2,1,0:T(8,128)} %coupling_hbm.5, f32[12,16,128]{2,1,0:T(8,128)S(1)} %shard_map.111.own_ref.after_ref), custom_call_target="tpu_custom_call" | custom-call | flops 2000000 | bytes 1048576 | tf_op jit(solution)/shard_map/pallas_call | solution.py:357
  32.5 0.0 copy-start
  32.5 0.0 copy-start.3
  32.5 0.0 copy-start.4
  32.5 0.0 copy-start.5
  32.5 0.0 copy-start.6
  32.5 0.2 shard_map.115.away_ref
  32.7 0.0 collective-permute-done.7.beside_ref
  32.7 0.5 %shard_map.116.side_ref = f32[12,16,128]{2,1,0:T(8,128)S(1)} custom-call(s32[8,1,12]{2,1,0:T(1,128)S(1)} %get-tuple-element.37.roster_ref, f32[13,64,128]{2,1,0:T(8,128)S(1)} %collective-permute-done.5.packed_ref, f32[12,16,128]{2,1,0:T(8,128)S(1)} %collective-permute-done.6.corner_ref, bf16[12,256,128]{2,1,0:T(8,128)(2,1)S(1)} %shard_map.115.away_ref, ...), custom_call_target="tpu_custom_call" | custom-call | flops 2000000 | bytes 1048576 | tf_op jit(solution)/shard_map/pallas_call | solution.py:357
  33.3 1.4 %collective-permute-done.4.other_ref = f32[12,16,128]{2,1,0:T(8,128)S(1)} collective-permute-done((f32[12,16,128]{2,1,0:T(8,128)S(1)}, f32[12,16,128]{2,1,0:T(8,128)S(1)}, u32[]{:S(2)}, u32[]{:S(2)}) %collective-permute-start.4) | collective-permute-done | bytes 98336 | tf_op jit(solution)/shard_map/ppermute | solution.py:320
  34.6 0.4 shard_map.117.own_ref.after_ref.rest_0_
  35.1 0.3 collective-permute-start.11
  35.4 2.3 %collective-permute-start.10 = (f32[12,16,128]{2,1,0:T(8,128)S(1)}, f32[12,16,128]{2,1,0:T(8,128)S(1)}, u32[]{:S(2)}, u32[]{:S(2)}) collective-permute-start(f32[12,16,128]{2,1,0:T(8,128)S(1)} %shard_map.117.own_ref.after_ref.rest_0_), channel_id=1, source_target_pairs={{0,192},{1,193},{2,194},{3,195},{4,196},{5,197},{6,198},{7,199},{8... | collective-permute-start | bytes 294920 | tf_op jit(solution)/shard_map/ppermute | solution.py:320
  37.7 0.2 shard_map.118.ready_ref
  38.0 0.0 collective-permute-done.9.packed_ref
  38.0 1.6 %collective-permute-start.8 = (f32[12,16,128]{2,1,0:T(8,128)S(1)}, f32[12,16,128]{2,1,0:T(8,128)S(1)}, u32[]{:S(2)}, u32[]{:S(2)}) collective-permute-start(f32[12,16,128]{2,1,0:T(8,128)S(1)} %shard_map.118.ready_ref), channel_id=1, source_target_pairs={{0,128},{1,129},{2,130},{3,131},{4,132},{5,133},{6,134},{7,135},{8... | collective-permute-start | bytes 294920 | tf_op jit(solution)/shard_map/ppermute | solution.py:320
  39.6 0.1 shard_map.121.rest_0_.expand_ref
  39.7 0.2 shard_map.119.wide_ref.rest_0_
  39.9 0.0 collective-permute-done.12.core_ref
  39.9 0.0 collective-permute-done.14.both_ref
  39.9 1.0 %shard_map.122.rest_1_.rest_0_ = f32[4,32,128]{2,1,0:T(8,128)S(1)} custom-call(s32[2,12]{1,0:T(2,128)S(1)} %bitcast.6, s32[2,12]{1,0:T(2,128)S(1)} %bitcast.8, s32[2,12]{1,0:T(2,128)S(1)} %bitcast.10, s32[4,4]{1,0:T(4,128)S(1)} %bitcast.4, f32[2,16,1536]{2,1,0:T(8,128)S(1)} %copy-done.1, f32[2,16,1536]{2,1,0:T(8,128)S(1)} %collective-permute-done.12.core_ref, ...), custom_call_target="tpu_custom_call" | custom-call | flops 2000000 | bytes 1048576 | tf_op jit(solution)/shard_map/pallas_call | solution.py:361
  41.0 0.0 collective-permute-done.11.other_ref
  41.0 0.3 shard_map.123.own_ref
  41.3 0.2 shard_map.124.rest_0_.ready_ref
  41.6 0.6 %collective-permute-done.10.other_ref = f32[12,16,128]{2,1,0:T(8,128)S(1)} collective-permute-done((f32[12,16,128]{2,1,0:T(8,128)S(1)}, f32[12,16,128]{2,1,0:T(8,128)S(1)}, u32[]{:S(2)}, u32[]{:S(2)}) %collective-permute-start.10) | collective-permute-done | bytes 98336 | tf_op jit(solution)/shard_map/ppermute | solution.py:320
  42.1 0.3 shard_map.120.corner_ref
  42.4 1.3 %shard_map.125.rest_1_ = f32[8,32,128]{2,1,0:T(8,128)S(1)} custom-call(s32[2,12]{1,0:T(2,128)S(1)} %bitcast.7, s32[2,12]{1,0:T(2,128)S(1)} %bitcast.9, s32[2,12]{1,0:T(2,128)S(1)} %bitcast.11, s32[4,4]{1,0:T(4,128)S(1)} %bitcast.5, f32[2,16,1536]{2,1,0:T(8,128)S(1)} %copy-done.1, f32[2,16,1536]{2,1,0:T(8,128)S(1)} %collective-permute-done.12.core_ref, ...), custom_call_target="tpu_custom_call" | custom-call | flops 2000000 | bytes 1048576 | tf_op jit(solution)/shard_map/pallas_call | solution.py:361
  43.8 0.3 collective-permute-done.8.beside_ref
  44.2 1.3 %shard_map.126 = f32[2,16,1536]{2,1,0:T(8,128)} custom-call(s32[8,1,12]{2,1,0:T(1,128)S(1)} %get-tuple-element.37.roster_ref, f32[12,16,128]{2,1,0:T(8,128)S(1)} %collective-permute-done.8.beside_ref, f32[12,16,128]{2,1,0:T(8,128)S(1)} %shard_map.120.corner_ref, bf16[12,256,128]{2,1,0:T(8,128)(2,1)S(1)} %get-tuple-element.64.wide_ref, ...), custom_call_target="tpu_custom_call" | custom-call | flops 2000000 | bytes 1048576 | tf_op jit(solution)/shard_map/pallas_call | solution.py:434
  (7 shorter events, 0.0 us)
Async XLA Ops:
  1.8 7.2 %collective-permute-start = (f32[12,16,128]{2,1,0:T(8,128)S(1)}, f32[12,16,128]{2,1,0:T(8,128)S(1)}, u32[]{:S(2)}, u32[]{:S(2)}) collective-permute-start(f32[12,16,128]{2,1,0:T(8,128)S(1)} %get-tuple-element.38.own_ref), channel_id=1, source_target_pairs={{0,128},{1,129},{2,130},{3,131},{4,132},{5,133},{6,134},{7,135},{8... | collective-permute-start | bytes 294920 | tf_op jit(solution)/shard_map/ppermute | solution.py:320
  4.9 11.2 %copy-start.1 = (f32[2,16,1536]{2,1,0:T(8,128)S(1)}, f32[2,16,1536]{2,1,0:T(8,128)}, u32[]{:S(2)}) copy-start(f32[2,16,1536]{2,1,0:T(8,128)} %own_ref.3) | copy-start | bytes 589828
  5.2 20.8 %collective-permute-start.5 = (f32[13,64,128]{2,1,0:T(8,128)S(1)}, f32[13,64,128]{2,1,0:T(8,128)S(1)}, u32[]{:S(2)}, u32[]{:S(2)}) collective-permute-start(f32[13,64,128]{2,1,0:T(8,128)S(1)} %shard_map.114), channel_id=1, source_target_pairs={{0,32},{1,33},{2,34},{3,35},{4,36},{5,37},{6,38},{7,39},{8,40},{9,... | collective-permute-start | bytes 1277960 | tf_op jit(solution)/shard_map/ppermute | solution.py:320
  9.3 5.2 %collective-permute-start.1 = (f32[12,16,128]{2,1,0:T(8,128)S(1)}, f32[12,16,128]{2,1,0:T(8,128)S(1)}, u32[]{:S(2)}, u32[]{:S(2)}) collective-permute-start(f32[12,16,128]{2,1,0:T(8,128)S(1)} %shard_map.102.own_ref), channel_id=1, source_target_pairs={{0,64},{1,65},{2,66},{3,67},{4,68},{5,69},{6,70},{7,71},{8,72},{9,... | collective-permute-start | bytes 294920 | tf_op jit(solution)/shard_map/ppermute | solution.py:320
  11.5 26.5 %collective-permute-start.9 = (f32[13,64,128]{2,1,0:T(8,128)S(1)}, f32[13,64,128]{2,1,0:T(8,128)S(1)}, u32[]{:S(2)}, u32[]{:S(2)}) collective-permute-start(f32[13,64,128]{2,1,0:T(8,128)S(1)} %get-tuple-element.63), channel_id=1, source_target_pairs={{0,128},{1,129},{2,130},{3,131},{4,132},{5,133},{6,134},{7,135},{8... | collective-permute-start | bytes 1277960 | tf_op jit(solution)/shard_map/ppermute | solution.py:320
  14.7 5.8 %collective-permute-start.2 = (f32[12,16,128]{2,1,0:T(8,128)S(1)}, f32[12,16,128]{2,1,0:T(8,128)S(1)}, u32[]{:S(2)}, u32[]{:S(2)}) collective-permute-start(f32[12,16,128]{2,1,0:T(8,128)S(1)} %shard_map.105.after_ref.own_ref), channel_id=1, source_target_pairs={{0,32},{1,33},{2,34},{3,35},{4,36},{5,37},{6,38},{7,39},{8,40},{9,... | collective-permute-start | bytes 294920 | tf_op jit(solution)/shard_map/ppermute | solution.py:320
  16.1 9.2 %collective-permute-start.13 = (f32[2,16,1536]{2,1,0:T(8,128)S(1)}, f32[2,16,1536]{2,1,0:T(8,128)S(1)}, u32[]{:S(2)}, u32[]{:S(2)}) collective-permute-start(f32[2,16,1536]{2,1,0:T(8,128)S(1)} %copy-done.1), channel_id=1, source_target_pairs={{0,2},{1,3},{2,0},{3,1},{4,6},{5,7},{6,4},{7,5},{8,10},{9,11},{10,... | collective-permute-start | bytes 589832 | tf_op jit(solution)/shard_map/ppermute | solution.py:320
  20.7 1.4 %collective-permute-start.3 = (f32[12,16,128]{2,1,0:T(8,128)S(1)}, f32[12,16,128]{2,1,0:T(8,128)S(1)}, u32[]{:S(2)}, u32[]{:S(2)}) collective-permute-start(f32[12,16,128]{2,1,0:T(8,128)S(1)} %shard_map.109.own_ref), channel_id=1, source_target_pairs={{0,1},{1,0},{2,3},{3,2},{4,5},{5,4},{6,7},{7,6},{8,9},{9,8},{10,11... | collective-permute-start | bytes 294920 | tf_op jit(solution)/shard_map/ppermute | solution.py:320
  22.4 6.2 %collective-permute-start.6 = (f32[12,16,128]{2,1,0:T(8,128)S(1)}, f32[12,16,128]{2,1,0:T(8,128)S(1)}, u32[]{:S(2)}, u32[]{:S(2)}) collective-permute-start(f32[12,16,128]{2,1,0:T(8,128)S(1)} %shard_map.111.own_ref.after_ref), channel_id=1, source_target_pairs={{0,34},{1,35},{2,32},{3,33},{4,38},{5,39},{6,36},{7,37},{8,42},{9,... | collective-permute-start | bytes 294920 | tf_op jit(solution)/shard_map/ppermute | solution.py:320
  25.2 14.7 %collective-permute-start.12 = (f32[2,16,1536]{2,1,0:T(8,128)S(1)}, f32[2,16,1536]{2,1,0:T(8,128)S(1)}, u32[]{:S(2)}, u32[]{:S(2)}) collective-permute-start(f32[2,16,1536]{2,1,0:T(8,128)S(1)} %copy-done.1), channel_id=1, source_target_pairs={{0,1},{1,0},{2,3},{3,2},{4,5},{5,4},{6,7},{7,6},{8,9},{9,8},{10,11... | collective-permute-start | bytes 589832 | tf_op jit(solution)/shard_map/ppermute | solution.py:320
  25.3 14.5 %collective-permute-start.14 = (f32[2,16,1536]{2,1,0:T(8,128)S(1)}, f32[2,16,1536]{2,1,0:T(8,128)S(1)}, u32[]{:S(2)}, u32[]{:S(2)}) collective-permute-start(f32[2,16,1536]{2,1,0:T(8,128)S(1)} %collective-permute-done.13.far_ref), channel_id=1, source_target_pairs={{0,1},{1,0},{2,3},{3,2},{4,5},{5,4},{6,7},{7,6},{8,9},{9,8},{10,11... | collective-permute-start | bytes 589832 | tf_op jit(solution)/shard_map/ppermute | solution.py:320
  25.9 13.6 %copy-start.2 = (f32[12,2,64,128]{3,2,1,0:T(8,128)S(1)}, f32[12,2,64,128]{3,2,1,0:T(8,128)}, u32[]{:S(2)}) copy-start(f32[12,2,64,128]{3,2,1,0:T(8,128)} %weight_ref.3) | copy-start | bytes 2359300
  26.0 6.7 %collective-permute-start.7 = (f32[12,16,128]{2,1,0:T(8,128)S(1)}, f32[12,16,128]{2,1,0:T(8,128)S(1)}, u32[]{:S(2)}, u32[]{:S(2)}) collective-permute-start(f32[12,16,128]{2,1,0:T(8,128)S(1)} %shard_map.112.ready_ref), channel_id=1, source_target_pairs={{0,32},{1,33},{2,34},{3,35},{4,36},{5,37},{6,38},{7,39},{8,40},{9,... | collective-permute-start | bytes 294920 | tf_op jit(solution)/shard_map/ppermute | solution.py:320
  28.5 6.1 %collective-permute-start.4 = (f32[12,16,128]{2,1,0:T(8,128)S(1)}, f32[12,16,128]{2,1,0:T(8,128)S(1)}, u32[]{:S(2)}, u32[]{:S(2)}) collective-permute-start(f32[12,16,128]{2,1,0:T(8,128)S(1)} %shard_map.111.own_ref.after_ref), channel_id=1, source_target_pairs={{0,2},{1,3},{2,0},{3,1},{4,6},{5,7},{6,4},{7,5},{8,10},{9,11},{10,... | collective-permute-start | bytes 294920 | tf_op jit(solution)/shard_map/ppermute | solution.py:320
  32.5 7.4 %copy-start = (f32[12,2,2,128,128]{4,3,2,1,0:T(8,128)S(1)}, f32[12,2,2,128,128]{4,3,2,1,0:T(8,128)}, u32[]{:S(2)}) copy-start(f32[12,2,2,128,128]{4,3,2,1,0:T(8,128)} %weight_ref.5) | copy-start | bytes 9437188
  32.5 7.4 %copy-start.3 = (s32[1,4,4]{2,1,0:T(4,128)S(1)}, s32[1,4,4]{2,1,0:T(4,128)}, u32[]{:S(2)}) copy-start(s32[1,4,4]{2,1,0:T(4,128)} %param.19) | copy-start | bytes 196
  32.5 7.4 %copy-start.4 = (s32[12,2]{0,1:T(2,128)S(1)}, s32[12,2]{0,1:T(2,128)}, u32[]{:S(2)}) copy-start(s32[12,2]{0,1:T(2,128)} %param.16) | copy-start | bytes 292
  32.5 7.4 %copy-start.5 = (s32[12,2]{0,1:T(2,128)S(1)}, s32[12,2]{0,1:T(2,128)}, u32[]{:S(2)}) copy-start(s32[12,2]{0,1:T(2,128)} %param.17) | copy-start | bytes 292
  32.5 7.4 %copy-start.6 = (s32[12,2]{0,1:T(2,128)S(1)}, s32[12,2]{0,1:T(2,128)}, u32[]{:S(2)}) copy-start(s32[12,2]{0,1:T(2,128)} %param.18) | copy-start | bytes 292
  35.1 5.9 %collective-permute-start.11 = (f32[12,16,128]{2,1,0:T(8,128)S(1)}, f32[12,16,128]{2,1,0:T(8,128)S(1)}, u32[]{:S(2)}, u32[]{:S(2)}) collective-permute-start(f32[12,16,128]{2,1,0:T(8,128)S(1)} %shard_map.117.own_ref.after_ref.rest_0_), channel_id=1, source_target_pairs={{0,64},{1,65},{2,66},{3,67},{4,68},{5,69},{6,70},{7,71},{8,72},{9,... | collective-permute-start | bytes 294920 | tf_op jit(solution)/shard_map/ppermute | solution.py:320
  35.4 6.7 %collective-permute-start.10 = (f32[12,16,128]{2,1,0:T(8,128)S(1)}, f32[12,16,128]{2,1,0:T(8,128)S(1)}, u32[]{:S(2)}, u32[]{:S(2)}) collective-permute-start(f32[12,16,128]{2,1,0:T(8,128)S(1)} %shard_map.117.own_ref.after_ref.rest_0_), channel_id=1, source_target_pairs={{0,192},{1,193},{2,194},{3,195},{4,196},{5,197},{6,198},{7,199},{8... | collective-permute-start | bytes 294920 | tf_op jit(solution)/shard_map/ppermute | solution.py:320
  38.0 6.2 %collective-permute-start.8 = (f32[12,16,128]{2,1,0:T(8,128)S(1)}, f32[12,16,128]{2,1,0:T(8,128)S(1)}, u32[]{:S(2)}, u32[]{:S(2)}) collective-permute-start(f32[12,16,128]{2,1,0:T(8,128)S(1)} %shard_map.118.ready_ref), channel_id=1, source_target_pairs={{0,128},{1,129},{2,130},{3,131},{4,132},{5,133},{6,134},{7,135},{8... | collective-permute-start | bytes 294920 | tf_op jit(solution)/shard_map/ppermute | solution.py:320
